TPU v7x, 128 devices: a whole 4x4x4 slice. The times are simulated.
128 devices in a mesh: dp: 8 (over z, x_hi), wide: 8 (over y, core), narrow: 2 (over x_lo).
Axes of the slice: x: 4 (x_hi: 2, x_lo: 2; x = x_hi * 2 + x_lo), y: 4, z: 4, core: 2. Of those that a mesh axis runs over, the one named last changes fastest.
Arguments:
- layer_input: bfloat16 [24576, 1536], P(('dp', 'wide'), 'narrow'), may hold values from -90 to 90
- text_states: bfloat16 [16, 64, 1536], P('dp', None, 'narrow'), may hold values from -6 to 6
- cotangent: bfloat16 [24576, 1536], P(('dp', 'wide'), 'narrow'), may hold values from -6 to 6
- first_gain: bfloat16 [1536], P('narrow'), may hold values from 0.5 to 1.5
- first_shift: bfloat16 [1536], P('narrow'), may hold values from -3 to 3
- query_weight: bfloat16 [1536, 1536], P('narrow', 'wide'), may hold values from -0.15625 to 0.15625
- key_weight: bfloat16 [1536, 1536], P('narrow', 'wide'), may hold values from -0.15625 to 0.15625
- value_weight: bfloat16 [1536, 1536], P('narrow', 'wide'), may hold values from -0.15625 to 0.15625
- output_weight: bfloat16 [1536, 1536], P('wide', 'narrow'), may hold values from -1 to 1
- second_gain: bfloat16 [1536], P('narrow'), may hold values from 0.5 to 1.5
- second_shift: bfloat16 [1536], P('narrow'), may hold values from -3 to 3
- cross_query: bfloat16 [1536, 1536], P('narrow', 'wide'), may hold values from -0.15625 to 0.15625
- cross_key: bfloat16 [1536, 1536], P('narrow', 'wide'), may hold values from -0.15625 to 0.15625
- cross_value: bfloat16 [1536, 1536], P('narrow', 'wide'), may hold values from -0.15625 to 0.15625
- cross_output: bfloat16 [1536, 1536], P('wide', 'narrow'), may hold values from -0.625 to 0.625
- third_gain: bfloat16 [1536], P('narrow'), may hold values from 0.5 to 1.5
- third_shift: bfloat16 [1536], P('narrow'), may hold values from -3 to 3
- expand_weight: bfloat16 [1536, 6144], P('narrow', 'wide'), may hold values from -0.15625 to 0.15625
- contract_weight: bfloat16 [6144, 1536], P('wide', 'narrow'), may hold values from -0.078125 to 0.078125
Outputs:
- layer_output: bfloat16 [24576, 1536], P(('dp', 'wide'), 'narrow')
- input_grad: float32 [24576, 1536], P(('dp', 'wide'), 'narrow')
- text_grad: float32 [16, 64, 1536], P('dp', None, 'narrow')
- first_gain_grad: float32 [1536], P('narrow')
- first_shift_grad: float32 [1536], P('narrow')
- query_weight_grad: float32 [1536, 1536], P('narrow', 'wide')
- key_weight_grad: float32 [1536, 1536], P('narrow', 'wide')
- value_weight_grad: float32 [1536, 1536], P('narrow', 'wide')
- output_weight_grad: float32 [1536, 1536], P('wide', 'narrow')
- second_gain_grad: float32 [1536], P('narrow')
- second_shift_grad: float32 [1536], P('narrow')
- cross_query_grad: float32 [1536, 1536], P('narrow', 'wide')
- cross_key_grad: float32 [1536, 1536], P('narrow', 'wide')
- cross_value_grad: float32 [1536, 1536], P('narrow', 'wide')
- cross_output_grad: float32 [1536, 1536], P('wide', 'narrow')
- third_gain_grad: float32 [1536], P('narrow')
- third_shift_grad: float32 [1536], P('narrow')
- expand_weight_grad: float32 [1536, 6144], P('narrow', 'wide')
- contract_weight_grad: float32 [6144, 1536], P('wide', 'narrow')
All inputs are finite; a program needn't handle non-finite values.
Results may differ from a plain program's by a relative error of at most 0.035.
Values may be sent and summed in bfloat16 or wider, within the bound.
A program may use at most 256 MiB of HBM per device.

v0:
```python
import math

import jax
import jax.numpy as jnp
from jax import lax
from jax.sharding import PartitionSpec as P

D = 1536
HDIM = 64
QBLOCK = 512


EPSILON = 1e-05
NEGATIVE = -1e30
ROOT_HALF = 0.7071067811865476
GAUSS_NORM = 0.3989422804014327


def from_everyone(x, axis):
    copies = jnp.broadcast_to(x, (lax.axis_size(axis), *x.shape))
    return lax.all_to_all(copies, axis, split_axis=0, concat_axis=0, tiled=True)


def of_everyone(x, axis):
    everything = from_everyone(x, axis)
    return jnp.sum(everything, axis=0)


def together(arrays, axis):
    flat, at, done = (jnp.concatenate([a.reshape(-1) for a in arrays]), 0, [])
    subtotal = of_everyone(flat, axis)
    for a in arrays:
        done.append(subtotal[at : at + a.size].reshape(a.shape))
        at += a.size
    return tuple(done)


def cut_along(x, dim, count):
    before, after = (x.shape[:dim], x.shape[dim + 1 :])
    return jnp.moveaxis(x.reshape(*before, count, -1, *after), dim, 0)


def sum_at_owner(x, axis, dim):
    parts = cut_along(x, dim, lax.axis_size(axis))
    arrived = lax.all_to_all(parts, axis, split_axis=0, concat_axis=0, tiled=True)
    return arrived.astype(jnp.float32).sum(axis=0)


def in_order(parts, dim):
    lengths = list(parts.shape[1:])
    lengths[dim] *= parts.shape[0]
    return jnp.moveaxis(parts, 0, dim).reshape(lengths)


def gather_directly(x, axis, dim):
    return in_order(from_everyone(x, axis), dim)


def of_everyone_2(x, axis):
    return from_everyone(x, axis).astype(jnp.float32).sum(axis=0)


def gelu_exact(values):
    return 0.5 * values * (1.0 + lax.erf(values * ROOT_HALF))


def gelu_slope(values):
    return (
        0.5 * (1.0 + lax.erf(values * ROOT_HALF))
        + values * jnp.exp(-0.5 * values * values) * GAUSS_NORM
    )


def feature_sums(first, second):
    return together((jnp.sum(first, axis=1), jnp.sum(second, axis=1)), "narrow")


def norm_forward(values, gain, shift):
    summed, squared = feature_sums(values, values * values)
    average = summed[:, None] / D
    variance = squared[:, None] / D - average * average
    factor = lax.rsqrt(variance + EPSILON)
    centred = (values - average) * factor
    return (
        centred,
        factor,
        (centred * gain.astype(jnp.float32) + shift.astype(jnp.float32)).astype(jnp.bfloat16),
    )


def norm_backward(incoming, centred, factor, gain):
    scaled = incoming * gain.astype(jnp.float32)
    summed, crossed = feature_sums(scaled, scaled * centred)
    result = factor * (scaled - summed[:, None] / D - centred * (crossed[:, None] / D))
    return (result, jnp.sum(incoming * centred, axis=0), jnp.sum(incoming, axis=0))


def contract_with(portion, weight, flipped):
    return lax.dot_general(
        portion, weight, (((1,), (flipped,)), ((), ())), preferred_element_type=jnp.float32
    )


def outer_sum(left, right):
    return lax.dot_general(
        left, right, (((0,), (0,)), ((), ())), preferred_element_type=jnp.float32
    )


def wide_to_narrow(values, weight, flipped):
    gathered = lax.all_gather(values, "wide", axis=0, tiled=True)
    return (
        gathered,
        sum_at_owner(contract_with(gathered, weight, flipped).astype(jnp.bfloat16), "narrow", 0),
    )


def narrow_to_wide(values, weight, flipped):
    gathered = lax.all_gather(values, "narrow", axis=0, tiled=True)
    own_block = lax.all_to_all(gathered, "wide", split_axis=0, concat_axis=1, tiled=True)
    whole_weight = lax.all_gather(weight, "wide", axis=flipped, tiled=True)
    return (gathered, contract_with(own_block, whole_weight, flipped))


def masked_scores(portion, split_k, offset, causal, factor):
    scores = (
        jnp.einsum("qhd,khd->hqk", portion, split_k, preferred_element_type=jnp.float32) * factor
    )
    if causal:
        row_ids = offset + lax.iota(jnp.int32, portion.shape[0])
        col_ids = lax.iota(jnp.int32, split_k.shape[0])
        scores = jnp.where((row_ids[:, None] >= col_ids[None, :])[None], scores, NEGATIVE)
    return scores


def attend(queries, keys, values, causal):
    head_count = queries.shape[1] // HDIM
    factor = 1.0 / math.sqrt(HDIM)
    block_count = queries.shape[0] // QBLOCK
    split_q = queries.reshape(block_count, QBLOCK, head_count, HDIM)
    split_k = keys.reshape(keys.shape[0], head_count, HDIM)
    split_v = values.reshape(values.shape[0], head_count, HDIM)
    offsets = lax.iota(jnp.int32, block_count) * QBLOCK

    def per_block(inputs):
        portion, offset = inputs
        scores = masked_scores(portion, split_k, offset, causal, factor)
        peak_score = jnp.max(scores, axis=2, keepdims=True)
        raised = jnp.exp(scores - peak_score)
        summed = jnp.sum(raised, axis=2, keepdims=True)
        weights = (raised / summed).astype(jnp.bfloat16)
        blended = jnp.einsum("hqk,khd->qhd", weights, split_v, preferred_element_type=jnp.float32)
        return (
            blended.reshape(QBLOCK, head_count * HDIM),
            peak_score[:, :, 0] + jnp.log(summed[:, :, 0]),
        )

    blended, log_totals = lax.map(per_block, (split_q, offsets))
    return (blended.reshape(queries.shape[0], -1), log_totals)


def attend_back(queries, keys, values, log_totals, grad_out, causal):
    head_count = queries.shape[1] // HDIM
    factor = 1.0 / math.sqrt(HDIM)
    block_count = queries.shape[0] // QBLOCK
    split_q = queries.reshape(block_count, QBLOCK, head_count, HDIM)
    split_g = grad_out.reshape(block_count, QBLOCK, head_count, HDIM)
    split_k = keys.reshape(keys.shape[0], head_count, HDIM)
    split_v = values.reshape(values.shape[0], head_count, HDIM)
    offsets = lax.iota(jnp.int32, block_count) * QBLOCK

    def per_block(carry, inputs):
        key_total, value_total = carry
        portion, grad_part, block_logs, offset = inputs
        scores = masked_scores(portion, split_k, offset, causal, factor)
        weights = jnp.exp(scores - block_logs[:, :, None])
        value_total = value_total + jnp.einsum(
            "hqk,qhd->khd",
            weights.astype(jnp.bfloat16),
            grad_part,
            preferred_element_type=jnp.float32,
        )
        grad_weights = jnp.einsum(
            "qhd,khd->hqk", grad_part, split_v, preferred_element_type=jnp.float32
        )
        row_terms = jnp.sum(weights * grad_weights, axis=2, keepdims=True)
        grad_scores = (weights * (grad_weights - row_terms)).astype(jnp.bfloat16)
        grad_query = (
            jnp.einsum("hqk,khd->qhd", grad_scores, split_k, preferred_element_type=jnp.float32)
            * factor
        )
        key_total = (
            key_total
            + jnp.einsum("hqk,qhd->khd", grad_scores, portion, preferred_element_type=jnp.float32)
            * factor
        )
        return ((key_total, value_total), grad_query.reshape(QBLOCK, head_count * HDIM))

    zero_init = jnp.zeros(split_k.shape, jnp.float32)
    (key_total, value_total), grad_query = lax.scan(
        per_block, (zero_init, zero_init), (split_q, split_g, log_totals, offsets)
    )
    key_rows = keys.shape[0]
    return (
        grad_query.reshape(queries.shape[0], -1),
        key_total.reshape(key_rows, -1),
        value_total.reshape(key_rows, -1),
    )


def on_device(
    layer_input,
    text_states,
    cotangent,
    first_gain,
    first_shift,
    query_weight,
    key_weight,
    value_weight,
    output_weight,
    second_gain,
    second_shift,
    cross_query,
    cross_key,
    cross_value,
    cross_output,
    third_gain,
    third_shift,
    expand_weight,
    contract_weight,
):
    head_cols = query_weight.shape[1]
    source = layer_input.astype(jnp.float32)
    centred_one, factor_one, normed_one = norm_forward(source, first_gain, first_shift)
    joined = jnp.concatenate((query_weight, key_weight, value_weight), axis=1)
    gathered_one, projected = wide_to_narrow(normed_one, joined, 0)
    projected = projected.astype(jnp.bfloat16)
    queries = projected[:, :head_cols]
    keys = projected[:, head_cols : 2 * head_cols]
    values = projected[:, 2 * head_cols :]
    attended, self_logs = attend(queries, keys, values, True)
    attended = attended.astype(jnp.bfloat16)
    gathered_att, self_branch = narrow_to_wide(attended, output_weight, 0)
    middle_one = source + self_branch
    centred_two, factor_two, normed_two = norm_forward(middle_one, second_gain, second_shift)
    gathered_two, cross_q = wide_to_narrow(normed_two, cross_query, 0)
    cross_q = cross_q.astype(jnp.bfloat16)
    text_pair = jnp.concatenate((cross_key, cross_value), axis=1)
    text_proj = sum_at_owner(
        jnp.einsum(
            "csd,dk->csk", text_states, text_pair, preferred_element_type=jnp.float32
        ).astype(jnp.bfloat16),
        "narrow",
        0,
    )[0].astype(jnp.bfloat16)
    text_keys = text_proj[:, :head_cols]
    text_values = text_proj[:, head_cols:]
    crossed, cross_logs = attend(cross_q, text_keys, text_values, False)
    crossed = crossed.astype(jnp.bfloat16)
    gathered_cross, cross_branch = narrow_to_wide(crossed, cross_output, 0)
    middle_two = middle_one + cross_branch
    centred_three, factor_three, normed_three = norm_forward(middle_two, third_gain, third_shift)
    gathered_three, expanded = wide_to_narrow(normed_three, expand_weight, 0)
    activated = gelu_exact(expanded).astype(jnp.bfloat16)
    gathered_act, mlp_branch = narrow_to_wide(activated, contract_weight, 0)
    layer_output = (middle_two + mlp_branch).astype(jnp.bfloat16)
    gathered_down, grad_act = wide_to_narrow(cotangent, contract_weight, 1)
    contract_grad = outer_sum(gathered_act, gathered_down)
    grad_expand = (grad_act * gelu_slope(expanded)).astype(jnp.bfloat16)
    gathered_expand, grad_norm_three = narrow_to_wide(grad_expand, expand_weight, 1)
    expand_grad = outer_sum(gathered_three, gathered_expand)
    back_three, third_gain_part, third_shift_part = norm_backward(
        grad_norm_three, centred_three, factor_three, third_gain
    )
    grad_middle_two = cotangent.astype(jnp.float32) + back_three
    gathered_mid_two, grad_crossed = wide_to_narrow(
        grad_middle_two.astype(jnp.bfloat16), cross_output, 1
    )
    cross_output_grad = outer_sum(gathered_cross, gathered_mid_two)
    grad_cross_q, grad_text_keys, grad_text_values = attend_back(
        cross_q, text_keys, text_values, cross_logs, grad_crossed.astype(jnp.bfloat16), False
    )
    gathered_cq, grad_norm_two = narrow_to_wide(grad_cross_q.astype(jnp.bfloat16), cross_query, 1)
    cross_query_grad = outer_sum(gathered_two, gathered_cq)
    text_grads = jnp.concatenate((grad_text_keys, grad_text_values), axis=1).astype(jnp.bfloat16)[
        None
    ]
    text_all = gather_directly(text_grads, "narrow", 0)
    pair_grad = jnp.einsum("csd,csk->dk", text_states, text_all, preferred_element_type=jnp.float32)
    text_part = jnp.einsum("csk,dk->csd", text_all, text_pair, preferred_element_type=jnp.float32)
    back_two, second_gain_part, second_shift_part = norm_backward(
        grad_norm_two, centred_two, factor_two, second_gain
    )
    grad_middle_one = grad_middle_two + back_two
    gathered_mid_one, grad_attended = wide_to_narrow(
        grad_middle_one.astype(jnp.bfloat16), output_weight, 1
    )
    output_grad = outer_sum(gathered_att, gathered_mid_one)
    grad_queries, grad_keys, grad_values = attend_back(
        queries, keys, values, self_logs, grad_attended.astype(jnp.bfloat16), True
    )
    grad_joined = jnp.concatenate((grad_queries, grad_keys, grad_values), axis=1).astype(
        jnp.bfloat16
    )
    gathered_joined, grad_norm_one = narrow_to_wide(grad_joined, joined, 1)
    joined_grad = outer_sum(gathered_one, gathered_joined)
    back_one, first_gain_part, first_shift_part = norm_backward(
        grad_norm_one, centred_one, factor_one, first_gain
    )
    input_grad = grad_middle_one + back_one
    (
        text_grad,
        first_gain_grad,
        first_shift_grad,
        second_gain_grad,
        second_shift_grad,
        third_gain_grad,
        third_shift_grad,
    ) = (
        of_everyone_2(text_part.astype(jnp.bfloat16), "wide").astype(jnp.float32),
        of_everyone_2(first_gain_part.astype(jnp.bfloat16), "wide").astype(jnp.float32),
        of_everyone_2(first_shift_part.astype(jnp.bfloat16), "wide").astype(jnp.float32),
        of_everyone_2(second_gain_part.astype(jnp.bfloat16), "wide").astype(jnp.float32),
        of_everyone_2(second_shift_part.astype(jnp.bfloat16), "wide").astype(jnp.float32),
        of_everyone_2(third_gain_part.astype(jnp.bfloat16), "wide").astype(jnp.float32),
        of_everyone_2(third_shift_part.astype(jnp.bfloat16), "wide").astype(jnp.float32),
    )
    (
        joined_grad,
        output_grad,
        cross_query_grad,
        pair_grad,
        cross_output_grad,
        expand_grad,
        contract_grad,
        first_gain_grad,
        first_shift_grad,
        second_gain_grad,
        second_shift_grad,
        third_gain_grad,
        third_shift_grad,
    ) = (
        lax.psum(joined_grad.astype(jnp.bfloat16), "dp").astype(jnp.float32),
        lax.psum(output_grad.astype(jnp.bfloat16), "dp").astype(jnp.float32),
        lax.psum(cross_query_grad.astype(jnp.bfloat16), "dp").astype(jnp.float32),
        lax.psum(pair_grad.astype(jnp.bfloat16), "dp").astype(jnp.float32),
        lax.psum(cross_output_grad.astype(jnp.bfloat16), "dp").astype(jnp.float32),
        lax.psum(expand_grad.astype(jnp.bfloat16), "dp").astype(jnp.float32),
        lax.psum(contract_grad.astype(jnp.bfloat16), "dp").astype(jnp.float32),
        lax.psum(first_gain_grad.astype(jnp.bfloat16), "dp").astype(jnp.float32),
        lax.psum(first_shift_grad.astype(jnp.bfloat16), "dp").astype(jnp.float32),
        lax.psum(second_gain_grad.astype(jnp.bfloat16), "dp").astype(jnp.float32),
        lax.psum(second_shift_grad.astype(jnp.bfloat16), "dp").astype(jnp.float32),
        lax.psum(third_gain_grad.astype(jnp.bfloat16), "dp").astype(jnp.float32),
        lax.psum(third_shift_grad.astype(jnp.bfloat16), "dp").astype(jnp.float32),
    )
    query_grad = joined_grad[:, :head_cols]
    key_grad = joined_grad[:, head_cols : 2 * head_cols]
    value_grad = joined_grad[:, 2 * head_cols :]
    cross_key_grad = pair_grad[:, :head_cols]
    cross_value_grad = pair_grad[:, head_cols:]
    return (
        layer_output,
        input_grad,
        text_grad,
        first_gain_grad,
        first_shift_grad,
        query_grad,
        key_grad,
        value_grad,
        output_grad,
        second_gain_grad,
        second_shift_grad,
        cross_query_grad,
        cross_key_grad,
        cross_value_grad,
        cross_output_grad,
        third_gain_grad,
        third_shift_grad,
        expand_grad,
        contract_grad,
    )


def solution(mesh):
    return jax.shard_map(
        on_device,
        mesh=mesh,
        in_specs=(
            P(("dp", "wide"), "narrow"),
            P("dp", None, "narrow"),
            P(("dp", "wide"), "narrow"),
            P("narrow"),
            P("narrow"),
            P("narrow", "wide"),
            P("narrow", "wide"),
            P("narrow", "wide"),
            P("wide", "narrow"),
            P("narrow"),
            P("narrow"),
            P("narrow", "wide"),
            P("narrow", "wide"),
            P("narrow", "wide"),
            P("wide", "narrow"),
            P("narrow"),
            P("narrow"),
            P("narrow", "wide"),
            P("wide", "narrow"),
        ),
        out_specs=(
            P(("dp", "wide"), "narrow"),
            P(("dp", "wide"), "narrow"),
            P("dp", None, "narrow"),
            P("narrow"),
            P("narrow"),
            P("narrow", "wide"),
            P("narrow", "wide"),
            P("narrow", "wide"),
            P("wide", "narrow"),
            P("narrow"),
            P("narrow"),
            P("narrow", "wide"),
            P("narrow", "wide"),
            P("narrow", "wide"),
            P("wide", "narrow"),
            P("narrow"),
            P("narrow"),
            P("narrow", "wide"),
            P("wide", "narrow"),
        ),
        check_vma=False,
    )
```

profile of v0, /device:TPU:0, one launch (start us, length us, event | category | flops | bytes accessed | tf_op | source)
XLA Modules:
  0.0 1439.7 jit_solution(10037191485992992457)
XLA Ops:
  18.7 36.8 %all-gather.19.cloned.1.call-done = bf16[3072,768]{1,0:T(8,128)(2,1)} async-done(((bf16[384,768]{1,0:T(8,128)(2,1)}), bf16[3072,768]{1,0:T(8,128)(2,1)}) %all-gather.19.cloned.1.call-update) | async-done | bytes 4718608 | tf_op jit(solution)/shard_map/all_gather | solution.py:111
  68.5 41.0 %all-to-all-done.1 = bf16[2,1536,576]{1,2,0:T(8,128)(2,1)} async-done(((bf16[2,1536,576]{1,2,0:T(8,128)(2,1)}), bf16[2,1536,576]{1,2,0:T(8,128)(2,1)}, u32[]{:S(2)}, u32[]{:S(2)}) %all-to-all-start.1) | async-done | bytes 3538976 | tf_op jit(solution)/shard_map/all_to_all | solution.py:45
  115.7 30.5 %while.54 = (s32[]{:T(128)}, bf16[3,512,192]{1,2,0:T(8,128)(2,1)S(1)}, f32[3,3,512]{2,1,0:T(4,128)S(1)}, s32[3]{0:T(128)S(1)}, bf16[3,512,3,64]{1,3,2,0:T(8,128)...) while((s32[]{:T(128)}, bf16[3,512,192]{1,2,0:T(8,128)(2,1)S(1)}, ...), condition=%wide.region_7.8_spmd, body=%wide.region_4.7_spmd.sunk | while | flops 633076736 | bytes 33482864 | solution.py:158
  148.0 24.7 %all-gather.21.cloned.1.call-done = bf16[3072,192]{0,1:T(8,128)(2,1)} async-done(((bf16[1536,192]{0,1:T(8,128)(2,1)}), bf16[3072,192]{0,1:T(8,128)(2,1)}) %all-gather.21.cloned.1.call-update) | async-done | bytes 1179664 | tf_op jit(solution)/shard_map/all_gather | solution.py:119
  179.5 28.2 %all-gather.23.cloned.1.call-done = bf16[1536,768]{1,0:T(8,128)(2,1)} async-done(((bf16[192,768]{1,0:T(8,128)(2,1)}), bf16[1536,768]{1,0:T(8,128)(2,1)}) %all-gather.23.cloned.1.call-update) | async-done | bytes 2359312 | tf_op jit(solution)/shard_map/all_gather | solution.py:121
  225.6 29.1 %all-gather.25.cloned.1.call-done = bf16[3072,768]{1,0:T(8,128)(2,1)} async-done(((bf16[384,768]{1,0:T(8,128)(2,1)}), bf16[3072,768]{1,0:T(8,128)(2,1)}) %all-gather.25.cloned.1.call-update) | async-done | bytes 4718608 | tf_op jit(solution)/shard_map/all_gather | solution.py:111
  263.9 15.2 %all-to-all-done.4 = bf16[2,1536,192]{1,2,0:T(8,128)(2,1)S(1)} async-done(((bf16[2,1536,192]{1,2,0:T(8,128)(2,1)}), bf16[2,1536,192]{1,2,0:T(8,128)(2,1)S(1)}, u32[]{:S(2)}, u32[]{:S(2)}) %all-to-all-start.4) | async-done | bytes 1179680 | tf_op jit(solution)/shard_map/all_to_all | solution.py:45
  285.8 24.1 %all-gather.27.cloned.1.call-done = bf16[3072,192]{0,1:T(8,128)(2,1)} async-done(((bf16[1536,192]{0,1:T(8,128)(2,1)}), bf16[3072,192]{0,1:T(8,128)(2,1)}) %all-gather.27.cloned.1.call-update) | async-done | bytes 1179664 | tf_op jit(solution)/shard_map/all_gather | solution.py:119
  316.6 28.2 %all-gather.29.cloned.1.call-done = bf16[1536,768]{1,0:T(8,128)(2,1)} async-done(((bf16[192,768]{1,0:T(8,128)(2,1)}), bf16[1536,768]{1,0:T(8,128)(2,1)}) %all-gather.29.cloned.1.call-update) | async-done | bytes 2359312 | tf_op jit(solution)/shard_map/all_gather | solution.py:121
  358.2 21.9 %all-gather.37.cloned.1.call-done = bf16[3072,768]{1,0:T(8,128)(2,1)} async-done(((bf16[384,768]{1,0:T(8,128)(2,1)}), bf16[3072,768]{1,0:T(8,128)(2,1)}) %all-gather.37.cloned.1.call-update) | async-done | bytes 4718608 | tf_op jit(solution)/shard_map/all_gather | solution.py:111
  395.1 21.6 %all-gather.31.cloned.1.call-done = bf16[3072,768]{1,0:T(8,128)(2,1)} async-done(((bf16[384,768]{1,0:T(8,128)(2,1)}), bf16[3072,768]{1,0:T(8,128)(2,1)}) %all-gather.31.cloned.1.call-update) | async-done | bytes 4718608 | tf_op jit(solution)/shard_map/all_gather | solution.py:111
  425.5 23.3 %all-to-all-done.10 = bf16[2,1536,768]{2,1,0:T(8,128)(2,1)} async-done(((bf16[2,1536,768]{2,1,0:T(8,128)(2,1)}), bf16[2,1536,768]{2,1,0:T(8,128)(2,1)}, u32[]{:S(2)}, u32[]{:S(2)}) %all-to-all-start.10) | async-done | bytes 4718624 | tf_op jit(solution)/shard_map/all_to_all | solution.py:45
  460.4 47.1 %all-to-all-done.8 = bf16[2,1536,768]{2,1,0:T(8,128)(2,1)} async-done(((bf16[2,1536,768]{2,1,0:T(8,128)(2,1)}), bf16[2,1536,768]{2,1,0:T(8,128)(2,1)}, u32[]{:S(2)}, u32[]{:S(2)}) %all-to-all-start.8) | async-done | bytes 4718624 | tf_op jit(solution)/shard_map/all_to_all | solution.py:45
  515.8 64.5 %all-gather.39.cloned.1.call-done = bf16[3072,768]{1,0:T(8,128)(2,1)} async-done(((bf16[1536,768]{1,0:T(8,128)(2,1)}), bf16[3072,768]{1,0:T(8,128)(2,1)}) %all-gather.39.cloned.1.call-update) | async-done | bytes 4718608 | tf_op jit(solution)/shard_map/all_gather | solution.py:119
  580.3 98.2 %all_to_all.231 = bf16[8,384,768]{2,1,0:T(8,128)(2,1)} all-to-all(bf16[8,384,768]{2,1,0:T(8,128)(2,1)} %bitcast.330), channel_id=1, replica_groups=mesh['dp'=8,'wide'=8,'narrow'=2] {'wide'}, dimensions={0} | all-to-all | bytes 9437184 | tf_op jit(solution)/shard_map/all_to_all | solution.py:120
  685.2 10.8 multiply_reduce_fusion.2
  705.2 33.6 %all-gather.43.cloned.1.call-done = bf16[3072,768]{1,0:T(8,128)(2,1)} async-done(((bf16[384,768]{1,0:T(8,128)(2,1)}), bf16[3072,768]{1,0:T(8,128)(2,1)}) %all-gather.43.cloned.1.call-update) | async-done | bytes 4718608 | tf_op jit(solution)/shard_map/all_gather | solution.py:111
  747.7 15.5 %all-to-all-done.13 = bf16[2,1536,192]{1,2,0:T(8,128)(2,1)S(1)} async-done(((bf16[2,1536,192]{1,2,0:T(8,128)(2,1)}), bf16[2,1536,192]{1,2,0:T(8,128)(2,1)S(1)}, u32[]{:S(2)}, u32[]{:S(2)}) %all-to-all-start.13) | async-done | bytes 1179680 | tf_op jit(solution)/shard_map/all_to_all | solution.py:45
  773.5 24.7 %all-gather.45.cloned.1.call-done = bf16[3072,192]{0,1:T(8,128)(2,1)} async-done(((bf16[1536,192]{0,1:T(8,128)(2,1)}), bf16[3072,192]{0,1:T(8,128)(2,1)}) %all-gather.45.cloned.1.call-update) | async-done | bytes 1179664 | tf_op jit(solution)/shard_map/all_gather | solution.py:119
  805.1 28.1 %all-gather.47.cloned.1.call-done = bf16[768,1536]{0,1:T(8,128)(2,1)} async-done(((bf16[768,192]{0,1:T(8,128)(2,1)}), bf16[768,1536]{0,1:T(8,128)(2,1)}) %all-gather.47.cloned.1.call-update) | async-done | bytes 2359312 | tf_op jit(solution)/shard_map/all_gather | solution.py:121
  848.4 33.9 %all-gather.49.cloned.1.call-done = bf16[3072,768]{1,0:T(8,128)(2,1)} async-done(((bf16[384,768]{1,0:T(8,128)(2,1)}), bf16[3072,768]{1,0:T(8,128)(2,1)}) %all-gather.49.cloned.1.call-update) | async-done | bytes 4718608 | tf_op jit(solution)/shard_map/all_gather | solution.py:111
  892.7 15.0 %all-to-all-done.16 = bf16[2,1536,192]{1,2,0:T(8,128)(2,1)} async-done(((bf16[2,1536,192]{1,2,0:T(8,128)(2,1)}), bf16[2,1536,192]{1,2,0:T(8,128)(2,1)}, u32[]{:S(2)}, u32[]{:S(2)}) %all-to-all-start.16) | async-done | bytes 1179680 | tf_op jit(solution)/shard_map/all_to_all | solution.py:45
  915.2 98.7 %while.57 = (s32[]{:T(128)}, f32[1536,3,64]{0,2,1:T(8,128)S(1)}, f32[1536,3,64]{0,2,1:T(8,128)S(1)}, bf16[3,512,192]{1,2,0:T(8,128)(2,1)}, bf16[3,512,3,64]{1,3,...) while((s32[]{:T(128)}, f32[1536,3,64]{0,2,1:T(8,128)S(1)}, ...), condition=%wide.region_35.36_spmd.clone, body=%wide.region_33.35_spmd.clone.sunk | while | flops 1533639680 | bytes 136876752 | solution.py:200
  927.8 9.4 multiply_convert_fusion.6
  960.7 9.4 multiply_convert_fusion.6
  993.6 9.4 multiply_convert_fusion.6
  1022.2 9.0 convolution_convert_fusion.7
  1033.3 44.2 %all-to-all-done.9 = bf16[8,384,768]{2,1,0:T(8,128)(2,1)} async-done(((bf16[8,384,768]{2,1,0:T(8,128)(2,1)}), bf16[8,384,768]{2,1,0:T(8,128)(2,1)}, u32[]{:S(2)}, u32[]{:S(2)}) %all-to-all-start.9) | async-done | bytes 4718624 | tf_op jit(solution)/shard_map/all_to_all | solution.py:120
  1159.6 9.8 fusion.62
  1175.5 38.7 %all-to-all-done.17 = bf16[8,384,576]{1,2,0:T(8,128)(2,1)} async-done(((bf16[8,384,576]{1,2,0:T(8,128)(2,1)}), bf16[8,384,576]{1,2,0:T(8,128)(2,1)}, u32[]{:S(2)}, u32[]{:S(2)}) %all-to-all-start.17) | async-done | bytes 3538976 | tf_op jit(solution)/shard_map/all_to_all | solution.py:120
  1264.9 44.5 %all-reduce = (bf16[768]{0:T(1024)(128)(2,1)S(1)}, bf16[768]{0:T(1024)(128)(2,1)S(1)}, bf16[768]{0:T(1024)(128)(2,1)S(1)}, bf16[768]{0:T(1024)(128)(2,1)S(1)}, b...) all-reduce(bf16[768]{0:T(1024)(128)(2,1)S(1)} %reduce_sum.438, ...), channel_id=1, replica_groups=mesh['dp'=8,'wide'=8,'narrow'=2] {'dp'}, use_global_device_ids=true, to_apply=%region_42.43 | all-reduce | flops 4608 | bytes 18432 | tf_op jit(solution)/shard_map/psum | solution.py:350
  1312.9 111.0 %all-reduce.4.cloned.1.call-done = (bf16[768,576]{0,1:T(8,128)(2,1)}, bf16[192,768]{1,0:T(8,128)(2,1)}, bf16[768,192]{0,1:T(8,128)(2,1)}, bf16[768,384]{0,1:T(8,...) async-done(((bf16[768,576]{0,1:T(8,128)(2,1)}, bf16[192,768]{1,0:T(8,128)(2,1)}, bf16[768,192]{0,1:T(8,128)(2,1)}, ...) | async-done | bytes 4718608 | tf_op jit(solution)/shard_map/psum | solution.py:343
  (467 shorter events, 480.3 us)
Async XLA Ops:
  12.5 43.0 %all-gather.19.cloned.1.call-start = ((), (), s32[]{:S(2)}) async-start(), calls=%async_computation.27 | async-start | bytes 5308416 | tf_op jit(solution)/shard_map/all_gather | solution.py:111
  63.0 46.4 %all-to-all-start.1 = ((bf16[2,1536,576]{1,2,0:T(8,128)(2,1)}), bf16[2,1536,576]{1,2,0:T(8,128)(2,1)}, u32[]{:S(2)}, u32[]{:S(2)}) async-start(bf16[2,1536,576]{1,2,0:T(8,128)(2,1)} %bitcast.324), calls=%async_computation.1 | async-start | bytes 7077888 | tf_op jit(solution)/shard_map/all_to_all | solution.py:45
  68.4 104.2 %all-gather.21.cloned.1.call-start = ((), (), s32[]{:S(2)}) async-start(), calls=%async_computation.28 | async-start | bytes 1769472 | tf_op jit(solution)/shard_map/all_gather | solution.py:119
  147.2 60.4 %all-gather.23.cloned.1.call-start = ((), (), s32[]{:S(2)}) async-start(), calls=%async_computation.29 | async-start | bytes 2654208 | tf_op jit(solution)/shard_map/all_gather | solution.py:121
  175.1 32.6 %all-to-all-start.2 = ((bf16[8,384,192]{1,2,0:T(8,128)(2,1)}), bf16[8,384,192]{1,2,0:T(8,128)(2,1)S(1)}, u32[]{:S(2)}, u32[]{:S(2)}) async-start(bf16[8,384,192]{1,2,0:T(8,128)(2,1)} %bitcast.336), calls=%async_computation.2 | async-start | bytes 2359296 | tf_op jit(solution)/shard_map/all_to_all | solution.py:120
  215.9 38.8 %all-gather.25.cloned.1.call-start = ((), (), s32[]{:S(2)}) async-start(), calls=%async_computation.30 | async-start | bytes 5308416 | tf_op jit(solution)/shard_map/all_gather | solution.py:111
  222.2 37.6 %all-to-all-start.5 = ((bf16[2,1,64,384]{3,2,1,0:T(8,128)(2,1)}), bf16[2,1,64,384]{3,2,1,0:T(8,128)(2,1)S(1)}, u32[]{:S(2)}, u32[]{:S(2)}) async-start(bf16[2,1,64,384]{3,2,1,0:T(8,128)(2,1)} %fusion.78), calls=%async_computation.5 | async-start | bytes 196608 | tf_op jit(solution)/shard_map/all_to_all | solution.py:45
  259.8 19.3 %all-to-all-start.4 = ((bf16[2,1536,192]{1,2,0:T(8,128)(2,1)}), bf16[2,1536,192]{1,2,0:T(8,128)(2,1)S(1)}, u32[]{:S(2)}, u32[]{:S(2)}) async-start(bf16[2,1536,192]{1,2,0:T(8,128)(2,1)} %bitcast.239), calls=%async_computation.4 | async-start | bytes 2359296 | tf_op jit(solution)/shard_map/all_to_all | solution.py:45
  263.4 46.5 %all-gather.27.cloned.1.call-start = ((), (), s32[]{:S(2)}) async-start(), calls=%async_computation.31 | async-start | bytes 1769472 | tf_op jit(solution)/shard_map/all_gather | solution.py:119
  284.5 60.3 %all-gather.29.cloned.1.call-start = ((), (), s32[]{:S(2)}) async-start(), calls=%async_computation.32 | async-start | bytes 2654208 | tf_op jit(solution)/shard_map/all_gather | solution.py:121
  285.0 95.1 %all-gather.37.cloned.1.call-start = ((), (), s32[]{:S(2)}) async-start(), calls=%async_computation.36 | async-start | bytes 5308416 | tf_op jit(solution)/shard_map/all_gather | solution.py:111
  312.3 32.4 %all-to-all-start.6 = ((bf16[8,384,192]{1,2,0:T(8,128)(2,1)}), bf16[8,384,192]{1,2,0:T(8,128)(2,1)S(1)}, u32[]{:S(2)}, u32[]{:S(2)}) async-start(bf16[8,384,192]{1,2,0:T(8,128)(2,1)} %bitcast.337), calls=%async_computation.6 | async-start | bytes 2359296 | tf_op jit(solution)/shard_map/all_to_all | solution.py:120
  353.3 63.5 %all-gather.31.cloned.1.call-start = ((), (), s32[]{:S(2)}) async-start(), calls=%async_computation.33 | async-start | bytes 5308416 | tf_op jit(solution)/shard_map/all_gather | solution.py:111
  388.9 59.9 %all-to-all-start.10 = ((bf16[2,1536,768]{2,1,0:T(8,128)(2,1)}), bf16[2,1536,768]{2,1,0:T(8,128)(2,1)}, u32[]{:S(2)}, u32[]{:S(2)}) async-start(bf16[2,1536,768]{2,1,0:T(8,128)(2,1)} %bitcast.334), calls=%async_computation.10 | async-start | bytes 9437184 | tf_op jit(solution)/shard_map/all_to_all | solution.py:45
  448.8 58.6 %all-to-all-start.8 = ((bf16[2,1536,768]{2,1,0:T(8,128)(2,1)}), bf16[2,1536,768]{2,1,0:T(8,128)(2,1)}, u32[]{:S(2)}, u32[]{:S(2)}) async-start(bf16[2,1536,768]{2,1,0:T(8,128)(2,1)} %bitcast.332), calls=%async_computation.8 | async-start | bytes 9437184 | tf_op jit(solution)/shard_map/all_to_all | solution.py:45
  454.5 125.7 %all-gather.39.cloned.1.call-start = ((), (), s32[]{:S(2)}) async-start(), calls=%async_computation.37 | async-start | bytes 7077888 | tf_op jit(solution)/shard_map/all_gather | solution.py:119
  515.2 170.0 %all-gather.41.cloned.1.call-start = ((), (), s32[]{:S(2)}) async-start(), calls=%async_computation.38 | async-start | bytes 10616832 | tf_op jit(solution)/shard_map/all_gather | solution.py:121
  515.8 223.1 %all-gather.43.cloned.1.call-start = ((), (), s32[]{:S(2)}) async-start(), calls=%async_computation.39 | async-start | bytes 5308416 | tf_op jit(solution)/shard_map/all_gather | solution.py:111
  744.0 19.3 %all-to-all-start.13 = ((bf16[2,1536,192]{1,2,0:T(8,128)(2,1)}), bf16[2,1536,192]{1,2,0:T(8,128)(2,1)S(1)}, u32[]{:S(2)}, u32[]{:S(2)}) async-start(bf16[2,1536,192]{1,2,0:T(8,128)(2,1)} %bitcast.335), calls=%async_computation.13 | async-start | bytes 2359296 | tf_op jit(solution)/shard_map/all_to_all | solution.py:45
  747.6 50.6 %all-gather.45.cloned.1.call-start = ((), (), s32[]{:S(2)}) async-start(), calls=%async_computation.40 | async-start | bytes 1769472 | tf_op jit(solution)/shard_map/all_gather | solution.py:119
  772.7 60.4 %all-gather.47.cloned.1.call-start = ((), (), s32[]{:S(2)}) async-start(), calls=%async_computation.41 | async-start | bytes 2654208 | tf_op jit(solution)/shard_map/all_gather | solution.py:121
  800.6 32.6 %all-to-all-start.14 = ((bf16[8,384,192]{1,2,0:T(8,128)(2,1)}), bf16[8,384,192]{1,2,0:T(8,128)(2,1)S(1)}, u32[]{:S(2)}, u32[]{:S(2)}) async-start(bf16[8,384,192]{1,2,0:T(8,128)(2,1)} %bitcast.236), calls=%async_computation.14 | async-start | bytes 2359296 | tf_op jit(solution)/shard_map/all_to_all | solution.py:120
  805.0 77.2 %all-gather.49.cloned.1.call-start = ((), (), s32[]{:S(2)}) async-start(), calls=%async_computation.42 | async-start | bytes 5308416 | tf_op jit(solution)/shard_map/all_gather | solution.py:111
  887.4 20.3 %all-to-all-start.16 = ((bf16[2,1536,192]{1,2,0:T(8,128)(2,1)}), bf16[2,1536,192]{1,2,0:T(8,128)(2,1)}, u32[]{:S(2)}, u32[]{:S(2)}) async-start(bf16[2,1536,192]{1,2,0:T(8,128)(2,1)} %bitcast.235), calls=%async_computation.16 | async-start | bytes 2359296 | tf_op jit(solution)/shard_map/all_to_all | solution.py:45
  891.8 125.7 %all-gather.33.cloned.1.call-start = ((), (), s32[]{:S(2)}) async-start(), calls=%async_computation.34 | async-start | bytes 7077888 | tf_op jit(solution)/shard_map/all_gather | solution.py:119
  892.4 236.4 %all-gather.51.cloned.1.call-start = ((), (), s32[]{:S(2)}) async-start(), calls=%async_computation.43 | async-start | bytes 5308416 | tf_op jit(solution)/shard_map/all_gather | solution.py:119
  1016.4 143.2 %all-gather.35.cloned.1.call-start = ((), (), s32[]{:S(2)}) async-start(), calls=%async_computation.35 | async-start | bytes 10616832 | tf_op jit(solution)/shard_map/all_gather | solution.py:121
  1017.0 200.6 %all-gather.53.cloned.1.call-start = ((), (), s32[]{:S(2)}) async-start(), calls=%async_computation.44 | async-start | bytes 7962624 | tf_op jit(solution)/shard_map/all_gather | solution.py:121
  1017.6 59.9 %all-to-all-start.9 = ((bf16[8,384,768]{2,1,0:T(8,128)(2,1)}), bf16[8,384,768]{2,1,0:T(8,128)(2,1)}, u32[]{:S(2)}, u32[]{:S(2)}) async-start(bf16[8,384,768]{2,1,0:T(8,128)(2,1)} %bitcast.331), calls=%async_computation.9 | async-start | bytes 9437184 | tf_op jit(solution)/shard_map/all_to_all | solution.py:120
  1111.3 29.4 %all-to-all-start.20 = ((bf16[8,2,64,768]{3,2,1,0:T(8,128)(2,1)}), bf16[8,2,64,768]{3,2,1,0:T(8,128)(2,1)S(1)}, u32[]{:S(2)}, u32[]{:S(2)}) async-start(bf16[8,2,64,768]{3,2,1,0:T(8,128)(2,1)} %broadcast_in_dim.129), calls=%async_computation.20 | async-start | bytes 3145728 | tf_op jit(solution)/shard_map/all_to_all | solution.py:21
  1140.7 73.5 %all-to-all-start.17 = ((bf16[8,384,576]{1,2,0:T(8,128)(2,1)}), bf16[8,384,576]{1,2,0:T(8,128)(2,1)}, u32[]{:S(2)}, u32[]{:S(2)}) async-start(bf16[8,384,576]{1,2,0:T(8,128)(2,1)} %bitcast.323), calls=%async_computation.17 | async-start | bytes 7077888 | tf_op jit(solution)/shard_map/all_to_all | solution.py:120
  1145.2 278.7 %all-reduce.4.cloned.1.call-start = ((), (), s32[]{:S(2)}) async-start(), calls=%async_computation.45 | async-start | bytes 9437184 | tf_op jit(solution)/shard_map/psum | solution.py:343
  (74 other events, 2110.6 us)
Sparse Core Ops, SparseCore 0:
  18.7 36.7 all-gather.18
  147.4 25.2 all-gather.20
  174.3 33.2 all-gather.22
  220.9 33.6 all-gather.24
  284.6 25.2 all-gather.26
  311.4 33.2 all-gather.28
  346.4 33.6 all-gather.36
  382.4 34.2 all-gather.30
  515.3 64.9 all-gather.38
  581.8 97.0 all-gather.40
  705.3 33.4 all-gather.42
  772.9 25.2 all-gather.44
  799.8 33.3 all-gather.46
  848.5 33.6 all-gather.48
  894.6 65.6 all-gather.32
  1016.5 52.0 all-gather.50
  1070.1 61.7 all-gather.34
  1133.4 72.2 all-gather.52
  1209.9 213.9 all-reduce.3
where the time goes:
time: 1450 us; the launch traced here: 1440 us
  waiting for transfers between devices  794 us (55%)
  matrix products  198 us (14%)
  blocking collectives  155 us (11%)
  other arithmetic  102 us (7%)
  starting transfers between devices  98.2 us (7%)
  local copies, waits for them, and re-layouts  76.9 us (5%)
  between operations  15.7 us (1%)
    all_gather x6, waiting for transfers between devices, wide_to_narrow(): gathered = lax.all_gather(values, 'wide', axis=0, tiled=True)  177 us
    all_to_all x7, waiting for transfers between devices, sum_at_owner(): lax.all_to_all(parts, axis, split_axis=0, concat_axis=0, tiled=True)  157 us
    all_gather x6, waiting for transfers between devices, narrow_to_wide(): gathered = lax.all_gather(values, 'narrow', axis=0, tiled=True)  138 us
    psum x1, waiting for transfers between devices, on_device(): lax.psum(joined_grad.astype(jnp.bfloat16), 'dp').astype(jnp.float32)  111 us
    all_to_all x1, blocking collectives, narrow_to_wide(): lax.all_to_all(gathered, 'wide', split_axis=0, concat_axis=1, tiled=True)  98.2 us
    all_gather x6, waiting for transfers between devices, narrow_to_wide(): whole_weight = lax.all_gather(weight, 'wide', axis=flipped, tiled=True)  84.4 us
    all_to_all x5, waiting for transfers between devices, narrow_to_wide(): lax.all_to_all(gathered, 'wide', split_axis=0, concat_axis=1, tiled=True)  82.9 us
    dot_general x12, matrix products, contract_with(): lax.dot_general(portion, weight, (((1,), (flipped,)), ((), ())), preferre...  76.5 us
  transfers between devices with their start and end apart: 43, of which 31 were waited for; matrix products, arithmetic and copies ran while one was open for 18% of the time, Pallas kernels for 0%

commit v1 on v0

v1 whole, which is shorter than its diff:
```python
import functools
import math

import jax
import jax.numpy as jnp
from jax import lax
from jax.experimental import pallas as pl
from jax.experimental.pallas import tpu as pltpu
from jax.sharding import PartitionSpec as P

D = 1536
HALF = 768
HDIM = 64
HEADS = 3
COLS = HEADS * HDIM
BLOCK = 192
EPSILON = 1e-05
NEGATIVE = -1e30
ROOT_HALF = 0.7071067811865476
GAUSS_NORM = 0.3989422804014327
MESH = pl.DeviceIdType.MESH
VMEM = pltpu.VMEM
ANY = pl.ANY
bf16, f32 = jnp.bfloat16, jnp.float32


def dot(a, b):
    return lax.dot_general(a, b, (((1,), (0,)), ((), ())), preferred_element_type=f32)


def dot_flip(a, b):
    return lax.dot_general(a, b, (((1,), (1,)), ((), ())), preferred_element_type=f32)


def outer(a, b):
    return lax.dot_general(a, b, (((0,), (0,)), ((), ())), preferred_element_type=f32)


class Place:
    def __init__(self):
        self.dp, self.w, self.n = (lax.axis_index(a) for a in ("dp", "wide", "narrow"))
        self.y, self.c = lax.div(self.w, 2), lax.rem(self.w, 2)
        self.z, self.s = lax.div(self.dp, 2), lax.rem(self.dp, 2)
        self.up, self.down = lax.rem(self.y + 1, 4), lax.rem(self.y + 3, 4)
        self.across = 3 - self.y
        self.moved = lax.rem(lax.div(self.y, 2) + self.n, 2)
        self.clip = lax.div(self.y, 2)

    def spot(self, y, c):
        moved = lax.rem(lax.div(y, 2) + self.n, 2)
        return (lax.rem(y + moved, 2) * 2 + c) * 2 + moved

    def rows(self, y, c, start=0, size=BLOCK):
        return pl.ds(pl.multiple_of(self.spot(y, c) * BLOCK + start, 32), size)

    def half(self, n):
        return pl.ds(pl.multiple_of(n * HALF, HALF), HALF)

    def at_y(self, y):
        return {"wide": y * 2 + self.c}

    def core(self):
        return {"wide": self.y * 2 + 1 - self.c}

    def x(self):
        return {"narrow": 1 - self.n}

    def at_z(self, k):
        return {"dp": lax.rem(self.z + k, 4) * 2 + self.s}

    def at_dp(self, k):
        return {"dp": lax.rem(self.dp + k, 8)}

    def at_x(self, ds, dn):
        return {"dp": self.z * 2 + lax.rem(self.s + ds, 2), "narrow": lax.rem(self.n + dn, 2)}


def remote(src, dst, send, recv, peer):
    return pltpu.make_async_remote_copy(
        src_ref=src, dst_ref=dst, send_sem=send, recv_sem=recv, device_id=peer, device_id_type=MESH
    )


def greet(peers):
    barrier = pltpu.get_barrier_semaphore()
    for peer in peers:
        pl.semaphore_signal(barrier, inc=1, device_id=peer, device_id_type=MESH)
    pl.semaphore_wait(barrier, len(peers))


class Swap:
    def __init__(self, array, axis):
        self.ins = [array]
        shape = list(array.shape)
        shape[axis] *= 2
        self.outs = [jax.ShapeDtypeStruct(tuple(shape), array.dtype)]
        self.axis, self.copies, self.locals = axis, 1, 1

    def peers(self, at):
        return [("x", at.x())]

    def moves(self, at, ins, outs):
        where = (slice(None),) * self.axis + (pl.ds(pl.multiple_of(at.n * ins[0].shape[self.axis], ins[0].shape[self.axis]), ins[0].shape[self.axis]),)
        dst = outs[0].at[where]
        return [(ins[0], dst, at.x())], [(ins[0], dst)]


class Text:
    def __init__(self, array, back=False):
        self.ins, self.back, self.copies, self.locals = [array], back, 1, 1
        shape = (2, 64, HALF) if back else (64, D)
        self.outs = [jax.ShapeDtypeStruct(shape, array.dtype)]

    def peers(self, at):
        return [("x", at.x())]

    def moves(self, at, ins, outs):
        src, dst = ins[0], outs[0]
        if self.back:
            there = dst.at[at.n]
            return [(src.at[:, at.half(1 - at.n)], there, at.x())], [(src.at[:, at.half(at.n)], there)]
        there = dst.at[:, at.half(at.n)]
        return [(src.at[1 - at.n], there, at.x())], [(src.at[at.n], there)]


class SumZ:
    def __init__(self, array, by_rows):
        self.by_rows, self.copies, self.locals = by_rows, 3, 0
        rows, cols = array.shape
        shape = (2, 4, rows // 8, cols) if by_rows else (4, rows // 4, cols)
        self.ins = [array.reshape(shape)]
        kept = (2, rows // 8, cols) if by_rows else (rows // 4, cols)
        self.outs = [jax.ShapeDtypeStruct((3, *kept), array.dtype)]

    def peers(self, at):
        return [(f"z{k}", at.at_z(k)) for k in (1, 2, 3)]

    def moves(self, at, ins, outs):
        out = []
        for k in (1, 2, 3):
            q = lax.rem(at.z + k, 4)
            src = ins[0].at[:, q] if self.by_rows else ins[0].at[q]
            out.append((src, outs[0].at[k - 1], at.at_z(k)))
        return out, []

    def finish(self, outs):
        z = lax.div(lax.axis_index("dp"), 2)
        own = lax.dynamic_index_in_dim(self.ins[0], z, 1 if self.by_rows else 0, False)
        return (own.astype(f32) + outs[0].astype(f32).sum(axis=0)).astype(bf16)


class SumX:
    def __init__(self, array, by_rows):
        self.by_rows, self.copies, self.locals = by_rows, 3, 0
        if by_rows:
            two, rows, cols = array.shape
            self.ins, kept = [array.reshape(2, 2, rows // 2, cols)], (rows // 2, cols)
        else:
            rows, cols = array.shape
            self.ins, kept = [array.reshape(2, rows // 2, cols)], (rows // 2, HALF)
        self.outs = [jax.ShapeDtypeStruct((3, *kept), array.dtype)]

    order = ((0, 1), (1, 0), (1, 1))

    def peers(self, at):
        return [(f"x{a}{b}", at.at_x(a, b)) for a, b in self.order]

    def moves(self, at, ins, outs):
        out = []
        for i, (a, b) in enumerate(self.order):
            s, n = lax.rem(at.s + a, 2), lax.rem(at.n + b, 2)
            src = ins[0].at[n, s] if self.by_rows else ins[0].at[s, :, at.half(n)]
            out.append((src, outs[0].at[i], at.at_x(a, b)))
        return out, []

    def finish(self, outs):
        s, n = lax.rem(lax.axis_index("dp"), 2), lax.axis_index("narrow")
        if self.by_rows:
            own = lax.dynamic_index_in_dim(lax.dynamic_index_in_dim(self.ins[0], n, 0, False), s, 0, False)
        else:
            own = lax.dynamic_slice_in_dim(lax.dynamic_index_in_dim(self.ins[0], s, 0, False), n * HALF, HALF, 1)
        return (own.astype(f32) + outs[0].astype(f32).sum(axis=0)).astype(bf16)


class Spread:
    def __init__(self, array):
        self.ins, self.copies, self.locals = [array], 7, 1
        self.outs = [jax.ShapeDtypeStruct((8, *array.shape), array.dtype)]

    def peers(self, at):
        return [(f"d{k}", at.at_dp(k)) for k in range(1, 8)]

    def moves(self, at, ins, outs):
        dst = outs[0].at[at.dp]
        return [(ins[0], dst, at.at_dp(k)) for k in range(1, 8)], [(ins[0], dst)]

    def finish(self, outs):
        eight, rows, cols = outs[0].shape
        return outs[0].reshape(eight * rows, cols).astype(f32)


class ToRing:
    def __init__(self, array):
        self.ins, self.copies, self.locals = [array], 7, 1
        self.outs = [jax.ShapeDtypeStruct((8, *array.shape), array.dtype)]

    def peers(self, at):
        return [(f"w{k}", {"wide": lax.rem(at.w + k, 8)}) for k in range(1, 8)]

    def moves(self, at, ins, outs):
        dst = outs[0].at[at.w]
        return [(ins[0], dst, peer) for _, peer in self.peers(at)], [(ins[0], dst)]


class ToClips:
    def __init__(self, array):
        self.ins, self.copies, self.locals = [array], 15, 1
        self.outs = [jax.ShapeDtypeStruct((8, 2, array.shape[0], HALF), array.dtype)]

    order = tuple((k, b) for k in range(8) for b in range(2))[1:]

    def peers(self, at):
        return [(f"c{k}{b}", {**at.at_dp(k), "narrow": lax.rem(at.n + b, 2)}) for k, b in self.order]

    def moves(self, at, ins, outs):
        dst = outs[0].at[at.dp, at.n]
        far = []
        for (k, b), (_, peer) in zip(self.order, self.peers(at)):
            far.append((ins[0].at[:, at.half(lax.rem(at.n + b, 2))], dst, peer))
        return far, [(ins[0].at[:, at.half(at.n)], dst)]


class Relay:
    def __init__(self, array, back=False):
        self.ins, self.back, self.copies, self.locals = [array], back, 2, 1
        shape = (384, HALF) if back else (BLOCK, D)
        self.outs = [jax.ShapeDtypeStruct(shape, array.dtype)]

    def peers(self, at):
        return [
            ("x", at.x()),
            ("a0", {"wide": at.across * 2 + at.c}),
            ("a1", {"wide": at.across * 2 + at.c, "narrow": 1 - at.n}),
        ]


def relay_run(relay, at, src, dst, send, recv, local, base, finish):
    mine, other = at.half(at.n), at.half(1 - at.n)
    over = at.across * 2 + at.c
    if relay.back:
        row = pl.ds(pl.multiple_of(at.moved * BLOCK, BLOCK), BLOCK)
        to = recv.at[base + at.moved]
        own = src.at[:, mine], src.at[:, other]
        land = dst.at[0:BLOCK], dst.at[BLOCK : 2 * BLOCK]
    else:
        row = mine
        to = recv.at[base + at.n]
        own = src.at[0:BLOCK], src.at[BLOCK : 2 * BLOCK]
        land = dst.at[:, at.half(0)], dst.at[:, at.half(1)]
    target = dst.at[row] if relay.back else dst.at[:, row]

    def arrive(slot, part):
        return remote(own[0], part, send.at[base], recv.at[base + slot], at.x())

    @pl.when(at.moved == 0)
    def _():
        stay = pltpu.make_async_copy(own[0], target, local)
        if relay.back:
            go = remote(own[1], target, send.at[base], to, at.x())
        else:
            go = remote(own[1], target, send.at[base], to, {"wide": over})
        if not finish:
            go.start()
            stay.start()
        else:
            stay.wait()
            go.wait_send()
            if relay.back:
                arrive(1, land[1]).wait_recv()
            else:
                arrive(1 - at.n, dst.at[:, other]).wait_recv()

    @pl.when(at.moved == 1)
    def _():
        if relay.back:
            first = remote(own[1], target, send.at[base], to, {"wide": over, "narrow": 1 - at.n})
            second = remote(own[0], target, send.at[base + 1], to, {"wide": over})
        else:
            first = remote(own[1], target, send.at[base], to, {"wide": over, "narrow": 1 - at.n})
            second = remote(own[0], target, send.at[base + 1], to, at.x())
        if not finish:
            first.start()
            second.start()
        else:
            first.wait_send()
            second.wait_send()
            arrive(0, land[0]).wait_recv()
            arrive(1, land[1]).wait_recv()


def call(body, number, ins, outs, scratch=(), beside=(), peers=None, spaces=None):
    spaces = spaces or [VMEM] * len(ins)
    copies = sum(b.copies for b in beside)
    locals_ = sum(b.locals for b in beside)
    side_ins = [a for b in beside for a in b.ins]
    side_outs = [a for b in beside for a in b.outs]
    n_in, n_out, n_scratch = len(ins), len(outs), len(scratch)

    def kernel(*refs):
        at = Place()
        refs = list(refs)

        def take(count):
            out = refs[:count]
            del refs[:count]
            return out

        main_in, side_in = take(n_in), take(len(side_ins))
        main_out, side_out, kept = take(n_out), take(len(side_outs)), take(n_scratch)
        send, recv, local = take(3)
        known = dict(peers(at)) if peers else {}
        for b in beside:
            known.update(dict(b.peers(at)))
        if known:
            greet(list(known.values()))
        slot, place, todo = 0, 0, []
        for b in beside:
            i, o = [side_in.pop(0) for _ in b.ins], [side_out.pop(0) for _ in b.outs]
            if isinstance(b, Relay):
                run = functools.partial(relay_run, b, at, i[0], o[0], send, recv, local.at[place], slot)
                run(False)
                todo.append(functools.partial(run, True))
                slot, place = slot + 2, place + 1
                continue
            far, near = b.moves(at, i, o)
            for src, dst, peer in far:
                copy = remote(src, dst, send.at[slot], recv.at[slot], peer)
                copy.start()
                todo.append(copy.wait)
                slot += 1
            for src, dst in near:
                copy = pltpu.make_async_copy(src, dst, local.at[place])
                copy.start()
                todo.append(copy.wait)
                place += 1
        if body:
            body(at, main_in, main_out, kept)
        for wait in todo:
            wait()

    results = pl.pallas_call(
        kernel,
        out_shape=tuple(outs) + tuple(side_outs),
        in_specs=[pl.BlockSpec(memory_space=s) for s in spaces] + [pl.BlockSpec(memory_space=ANY)] * len(side_ins),
        out_specs=tuple([pl.BlockSpec(memory_space=VMEM)] * len(outs) + [pl.BlockSpec(memory_space=ANY)] * len(side_outs)),
        scratch_shapes=[
            *scratch,
            pltpu.SemaphoreType.DMA((max(copies, 1),)),
            pltpu.SemaphoreType.DMA((max(copies, 1),)),
            pltpu.SemaphoreType.DMA((max(locals_, 1),)),
        ],
        compiler_params=pltpu.CompilerParams(
            collective_id=number, has_side_effects=True, vmem_limit_bytes=58 << 20
        ),
    )(*ins, *side_ins)
    results = list(results)
    main, rest = results[: len(outs)], results[len(outs) :]
    sides = []
    for b in beside:
        sides.append(rest[: len(b.outs)])
        del rest[: len(b.outs)]
    return main, sides


def ring_peers(at):
    return [("up", at.at_y(at.up)), ("down", at.at_y(at.down)), ("core", at.core())]


def gather_times(number, block, weight, flip=False, out_type=bf16, beside=(), swap=False):
    width = weight.shape[0] if flip else weight.shape[1]
    depth = weight.shape[1] if flip else weight.shape[0]

    def body(at, ins, outs, kept):
        x, w = ins
        whole, product = outs[:2]
        send, recv, local = kept[:3]
        y, c, up, down = at.y, at.c, at.up, at.down
        far = lax.rem(y + 2, 4)

        def move(slot, y_from, c_from, peer, start=0, size=BLOCK, first=False):
            rows = at.rows(y_from, c_from, start, size)
            src = x if first else whole.at[rows]
            return remote(src, whole.at[rows], send.at[slot], recv.at[slot], peer)

        to_up, to_down = at.at_y(up), at.at_y(down)
        sends = [
            move(0, y, c, to_up, first=True),
            move(1, y, c, to_down, first=True),
            move(2, y, c, at.core(), first=True),
            move(3, down, c, to_up, 0, BLOCK // 2),
            move(4, up, c, to_down, BLOCK // 2, BLOCK // 2),
            move(5, down, c, at.core()),
            move(6, up, c, at.core()),
            move(7, far, c, at.core(), 0, BLOCK // 2),
            move(8, far, c, at.core(), BLOCK // 2, BLOCK // 2),
        ]
        for i in range(3):
            sends[i].start()
        own = pltpu.make_async_copy(x, whole.at[at.rows(y, c)], local.at[0])
        own.start()
        if swap:
            full = outs[2]
            mine = pl.ds(pl.multiple_of(at.n * HALF, HALF), HALF)
            pair = remote(w, full.at[mine], send.at[9], recv.at[9], at.x())
            pair.start()
            keep = pltpu.make_async_copy(w, full.at[mine], local.at[1])
            keep.start()
        else:
            full = w
        own.wait()

        def step(s, carry):
            @pl.when(s == 1)
            def _():
                sends[2].wait_recv()
                sends[1].wait_recv()
                sends[4].start()
                sends[6].start()
                sends[0].wait_recv()
                sends[3].start()
                sends[5].start()
                if swap:
                    pair.wait_recv()
                    keep.wait()

            @pl.when(s == 3)
            def _():
                sends[6].wait_recv()

            @pl.when(s == 5)
            def _():
                sends[5].wait_recv()

            @pl.when(s == 6)
            def _():
                sends[3].wait_recv()
                sends[7].start()
                sends[4].wait_recv()
                sends[8].start()

            @pl.when(s == 7)
            def _():
                sends[7].wait_recv()
                sends[8].wait_recv()

            g = lax.div(s, 2)
            off = g + lax.div(g, 2) - 2 * lax.div(g, 3)
            rows = at.rows(lax.rem(y + off, 4), lax.rem(c + s, 2))
            product[rows, :] = (dot_flip if flip else dot)(whole[rows, :], full[...]).astype(out_type)
            return carry

        if swap:
            def early(s, carry):
                return step(s + 1, carry)

            lax.fori_loop(0, 7, early, 0)
            step(0, 0)
        else:
            lax.fori_loop(0, 8, step, 0)
        for i in range(9):
            sends[i].wait_send()
        if swap:
            pair.wait_send()

    outs = [jax.ShapeDtypeStruct((D, D), bf16), jax.ShapeDtypeStruct((D, width), out_type)]
    if swap:
        outs.append(jax.ShapeDtypeStruct((D, width), bf16))
    sems = [pltpu.SemaphoreType.DMA((10,)), pltpu.SemaphoreType.DMA((10,)), pltpu.SemaphoreType.DMA((2,))]

    def peers(at):
        return ring_peers(at) + ([("x", at.x())] if swap else [])

    return call(body, number, [block, weight], outs, sems, beside, peers)


def times_scatter(number, values, weight, flip=False, beside=()):
    def body(at, ins, outs, kept):
        v, w = ins
        result = outs[0]
        send, recv, local, out_c, in_c, own, out_y, in_y, half_out, half_in = kept
        y, c, up, down = at.y, at.c, at.up, at.down
        top, low = slice(0, BLOCK // 2), slice(BLOCK // 2, BLOCK)
        to_up, to_down = at.at_y(up), at.at_y(down)
        cores = [remote(out_c.at[g], in_c.at[g], send.at[g], recv.at[g], at.core()) for g in range(4)]
        halves = [
            remote(half_out.at[0], half_in.at[0], send.at[4], recv.at[4], to_up),
            remote(half_out.at[1], half_in.at[1], send.at[5], recv.at[5], to_down),
        ]
        blocks = [
            remote(out_y.at[0], in_y.at[0], send.at[6], recv.at[6], to_up),
            remote(out_y.at[1], in_y.at[1], send.at[7], recv.at[7], to_down),
        ]

        def step(s, carry):
            g = lax.div(s, 2)
            off = lax.rem(6 - g + 3 * lax.div(g, 2) + 2 * lax.div(g, 3), 4)
            core = lax.rem(c + 1 + s, 2)
            rows = at.rows(lax.rem(y + off, 4), core)
            part = (dot_flip if flip else dot)(v[rows, :], w[...])

            @pl.when(lax.rem(s, 2) == 0)
            def _():
                out_c[g] = part.astype(bf16)
                remote(out_c.at[g], in_c.at[g], send.at[g], recv.at[g], at.core()).start()

            @pl.when(lax.rem(s, 2) == 1)
            def _():
                own[g] = part

            @pl.when(s == 2)
            def _():
                cores[0].wait_recv()
                half_out[0] = (own[0, top] + in_c[0, top].astype(f32)).astype(bf16)
                half_out[1] = (own[0, low] + in_c[0, low].astype(f32)).astype(bf16)
                halves[0].start()
                halves[1].start()

            return carry

        lax.fori_loop(0, 8, step, 0)
        for i, kind in enumerate((top, low)):
            rest = low if i == 0 else top
            cores[1 + i].wait_recv()
            halves[i].wait_recv()
            out_y[i, rest] = (own[1 + i, rest] + in_c[1 + i, rest].astype(f32)).astype(bf16)
            out_y[i, kind] = (own[1 + i, kind] + in_c[1 + i, kind].astype(f32) + half_in[i].astype(f32)).astype(bf16)
            blocks[i].start()
        cores[3].wait_recv()
        total = own[3] + in_c[3].astype(f32)
        blocks[0].wait_recv()
        blocks[1].wait_recv()
        result[...] = total + in_y[0].astype(f32) + in_y[1].astype(f32)
        for copy in cores + halves + blocks:
            copy.wait_send()

    scratch = [
        pltpu.SemaphoreType.DMA((8,)),
        pltpu.SemaphoreType.DMA((8,)),
        pltpu.SemaphoreType.DMA((1,)),
        VMEM((4, BLOCK, D), bf16),
        VMEM((4, BLOCK, D), bf16),
        VMEM((4, BLOCK, D), f32),
        VMEM((2, BLOCK, D), bf16),
        VMEM((2, BLOCK, D), bf16),
        VMEM((2, BLOCK // 2, D), bf16),
        VMEM((2, BLOCK // 2, D), bf16),
    ]
    (total,), sides = call(body, number, [values, weight], [jax.ShapeDtypeStruct((BLOCK, D), f32)], scratch, beside, ring_peers)
    return total, sides


def causal_forward(number, joined, beside=()):
    rows_at_once = 512

    def body(at, ins, outs, kept):
        (qkv,), (out, logs) = ins, outs
        lane = lax.broadcasted_iota(jnp.int32, (rows_at_once, 128), 1)
        square = (rows_at_once, rows_at_once)
        seen = lax.broadcasted_iota(jnp.int32, square, 0) >= lax.broadcasted_iota(jnp.int32, square, 1)
        for i in range(D // rows_at_once):
            before, upto = i * rows_at_once, (i + 1) * rows_at_once
            rows = slice(before, upto)
            log_total, blended = jnp.zeros((rows_at_once, 128), f32), []
            for h in range(HEADS):
                a = h * HDIM
                q = qkv[rows, a : a + HDIM] * jnp.asarray(0.125, bf16)
                k = qkv[0:upto, COLS + a : COLS + a + HDIM]
                v = qkv[0:upto, 2 * COLS + a : 2 * COLS + a + HDIM]
                scores = dot_flip(q, k)
                last = jnp.where(seen, scores[:, before:], NEGATIVE)
                scores = jnp.concatenate((scores[:, :before], last), axis=1) if i else last
                peak = jnp.max(scores, axis=1, keepdims=True)
                raised = jnp.exp(scores - peak)
                total = jnp.sum(raised, axis=1, keepdims=True)
                blended.append(dot(raised.astype(bf16), v) / total)
                log_total = jnp.where(lane == h, peak + jnp.log(total), log_total)
            out[rows, :] = jnp.concatenate(blended, axis=1).astype(bf16)
            logs[:, rows] = log_total.T[0:8, :]

    outs = [jax.ShapeDtypeStruct((D, COLS), bf16), jax.ShapeDtypeStruct((8, D), f32)]
    return call(body, number, [joined], outs, (), beside)


def causal_backward(number, joined, grad, logs, beside=()):
    at_once = 512

    def body(at, ins, outs, kept):
        (qkv, go, log_rows), (out,), (key_sum, value_sum) = ins, outs, kept
        square = (at_once, at_once)
        seen = lax.broadcasted_iota(jnp.int32, square, 1) >= lax.broadcasted_iota(jnp.int32, square, 0)
        blocks = D // at_once
        for h in range(HEADS):
            a = h * HDIM
            turned = qkv[:, COLS + a : COLS + a + HDIM].T
            query_parts = []
            for i in reversed(range(blocks)):
                before, upto = i * at_once, (i + 1) * at_once
                rows = slice(before, upto)
                q = qkv[rows, a : a + HDIM] * jnp.asarray(0.125, bf16)
                g = go[rows, a : a + HDIM]
                k = qkv[0:upto, COLS + a : COLS + a + HDIM]
                v = qkv[0:upto, 2 * COLS + a : 2 * COLS + a + HDIM]
                p = jnp.exp(dot_flip(k, q) - log_rows[h : h + 1, rows])
                last = jnp.where(seen, p[before:], 0.0)
                p = jnp.concatenate((p[:before], last), axis=0) if i else last
                dp = dot_flip(v, g)
                ds = (p * (dp - jnp.sum(p * dp, axis=0, keepdims=True))).astype(bf16)
                value_part, key_part = dot(p.astype(bf16), g), dot(ds, q)
                if i == blocks - 1:
                    key_sum[h, 0:upto, :] = key_part
                    value_sum[h, 0:upto, :] = value_part
                else:
                    key_sum[h, 0:upto, :] += key_part
                    value_sum[h, 0:upto, :] += value_part
                query_parts.append((dot(turned[:, 0:upto], ds) * 0.125).T)
            out[:, a : a + HDIM] = jnp.concatenate(query_parts[::-1], axis=0).astype(bf16)
        for h in range(HEADS):
            a = h * HDIM
            out[:, COLS + a : COLS + a + HDIM] = key_sum[h].astype(bf16)
            out[:, 2 * COLS + a : 2 * COLS + a + HDIM] = value_sum[h].astype(bf16)

    outs = [jax.ShapeDtypeStruct((D, 3 * COLS), bf16)]
    scratch = [VMEM((HEADS, D, HDIM), f32), VMEM((HEADS, D, HDIM), f32)]
    return call(body, number, [joined, grad, logs], outs, scratch, beside)


def cross_weights(q, k):
    scores = dot_flip(k, q)
    raised = jnp.exp(scores - jnp.max(scores, axis=0, keepdims=True))
    return raised / jnp.sum(raised, axis=0, keepdims=True)


def cross_forward(queries, text_pair):
    def kernel(q_ref, kv_ref, out):
        for h in range(HEADS):
            a = h * HDIM
            q = q_ref[:, a : a + HDIM] * jnp.asarray(0.125, bf16)
            p = cross_weights(q, kv_ref[:, a : a + HDIM])
            v = kv_ref[:, COLS + a : COLS + a + HDIM].T
            out[:, a : a + HDIM] = dot(v, p.astype(bf16)).T.astype(bf16)

    return pl.pallas_call(
        kernel,
        out_shape=jax.ShapeDtypeStruct(queries.shape, bf16),
        in_specs=[pl.BlockSpec(memory_space=VMEM)] * 2,
        out_specs=pl.BlockSpec(memory_space=VMEM),
    )(queries, text_pair)


def cross_backward(queries, text_pair, grad):
    def kernel(q_ref, kv_ref, g_ref, dq_ref, dkv_ref):
        for h in range(HEADS):
            a = h * HDIM
            q = q_ref[:, a : a + HDIM] * jnp.asarray(0.125, bf16)
            k, v = kv_ref[:, a : a + HDIM], kv_ref[:, COLS + a : COLS + a + HDIM]
            g = g_ref[:, a : a + HDIM]
            p = cross_weights(q, k)
            dp = dot_flip(v, g)
            ds = (p * (dp - jnp.sum(p * dp, axis=0, keepdims=True))).astype(bf16)
            dq_ref[:, a : a + HDIM] = (dot(k.T, ds) * 0.125).T.astype(bf16)
            dkv_ref[:, a : a + HDIM] = dot(ds, q).astype(bf16)
            dkv_ref[:, COLS + a : COLS + a + HDIM] = dot(p.astype(bf16), g).astype(bf16)

    return pl.pallas_call(
        kernel,
        out_shape=(jax.ShapeDtypeStruct(queries.shape, bf16), jax.ShapeDtypeStruct(text_pair.shape, bf16)),
        in_specs=[pl.BlockSpec(memory_space=VMEM)] * 3,
        out_specs=(pl.BlockSpec(memory_space=VMEM),) * 2,
    )(queries, text_pair, grad)


def gelu_exact(v):
    return 0.5 * v * (1.0 + lax.erf(v * ROOT_HALF))


def gelu_slope(v):
    return 0.5 * (1.0 + lax.erf(v * ROOT_HALF)) + v * jnp.exp(-0.5 * v * v) * GAUSS_NORM


def norm_forward(values, gain, shift):
    average = jnp.mean(values, axis=1, keepdims=True)
    variance = jnp.mean(values * values, axis=1, keepdims=True) - average * average
    factor = lax.rsqrt(variance + EPSILON)
    centred = (values - average) * factor
    return centred, factor, (centred * gain + shift).astype(bf16)


def norm_backward(incoming, centred, factor, gain):
    scaled = incoming * gain
    first = jnp.mean(scaled, axis=1, keepdims=True)
    second = jnp.mean(scaled * centred, axis=1, keepdims=True)
    result = factor * (scaled - first - centred * second)
    return result, jnp.sum(incoming * centred, axis=0), jnp.sum(incoming, axis=0)


def on_device(
    layer_input,
    text_states,
    cotangent,
    first_gain,
    first_shift,
    query_weight,
    key_weight,
    value_weight,
    output_weight,
    second_gain,
    second_shift,
    cross_query,
    cross_key,
    cross_value,
    cross_output,
    third_gain,
    third_shift,
    expand_weight,
    contract_weight,
):
    vectors = (first_gain, first_shift, second_gain, second_shift, third_gain, third_shift)
    vectors = jnp.concatenate([jnp.stack(vectors).astype(f32), jnp.zeros((2, HALF), f32)], axis=0)
    joined = jnp.concatenate((query_weight, key_weight, value_weight), axis=1)
    pair = jnp.concatenate((cross_key, cross_value), axis=1)

    _, ((x,), (text,), (vectors,)) = call(None, 0, [], [], (), [Relay(layer_input), Text(text_states), Swap(vectors, 1)])
    gain_one, shift_one, gain_two, shift_two, gain_three, shift_three = (vectors[i : i + 1] for i in range(6))
    source = x.astype(f32)
    centred_one, factor_one, normed_one = norm_forward(source, gain_one, shift_one)
    (all_one, qkv, joined), ((out_w,),) = gather_times(1, normed_one, joined, swap=True, beside=[Swap(output_weight, 1)])
    (attended, logs), ((cq_w,), (pair,), (co_w,)) = causal_forward(
        2, qkv, [Swap(cross_query, 0), Swap(pair, 0), Swap(cross_output, 1)]
    )
    branch, ((expand,),) = times_scatter(3, attended, out_w, beside=[Swap(expand_weight, 0)])
    middle_one = source + branch
    centred_two, factor_two, normed_two = norm_forward(middle_one, gain_two, shift_two)
    (all_two, cross_q), ((contract,),) = gather_times(4, normed_two, cq_w, beside=[Swap(contract_weight, 1)])
    text_pair = dot(text, pair).astype(bf16)
    crossed = cross_forward(cross_q, text_pair)
    branch, ((down,),) = times_scatter(6, crossed, co_w, beside=[Relay(cotangent)])
    middle_two = middle_one + branch
    centred_three, factor_three, normed_three = norm_forward(middle_two, gain_three, shift_three)
    (all_three, expanded), _ = gather_times(7, normed_three, expand, out_type=f32)
    activated = gelu_exact(expanded).astype(bf16)
    (all_down, grad_act), _ = gather_times(8, down, contract, flip=True)
    branch, _ = times_scatter(9, activated, contract)
    layer_output = (middle_two + branch).astype(bf16)

    grad_expand = (grad_act.astype(f32) * gelu_slope(expanded)).astype(bf16)
    contract_leg = SumZ(outer(activated, all_down).astype(bf16), False)
    expand_leg = SumZ(outer(all_three, grad_expand).astype(bf16), True)
    grad_three, (contract_got, (layer_output,)) = times_scatter(
        10, grad_expand, expand, flip=True, beside=[contract_leg, Relay(layer_output, True)]
    )
    back, third_gain_part, third_shift_part = norm_backward(grad_three, centred_three, factor_three, gain_three)
    grad_two = down.astype(f32) + back
    contract_leg = SumX(contract_leg.finish(contract_got), False)
    (all_mid_two, grad_crossed), (expand_got, contract_got) = gather_times(
        11, grad_two.astype(bf16), co_w, flip=True, beside=[expand_leg, contract_leg]
    )
    grad_cross_q, grad_pair = cross_backward(cross_q, text_pair, grad_crossed)
    text_part = lax.psum(dot_flip(grad_pair, pair).astype(bf16), "wide")
    query_pair_leg = SumZ(
        jnp.concatenate((outer(all_two, grad_cross_q), outer(text, grad_pair)), axis=1).astype(bf16), True
    )
    cross_out_leg = SumZ(outer(crossed, all_mid_two).astype(bf16), False)
    expand_leg = SumX(expand_leg.finish(expand_got), True)
    contract_leg = Spread(contract_leg.finish(contract_got))
    grad_normed, (expand_got, contract_got, query_pair_got, cross_out_got) = times_scatter(
        13, grad_cross_q, cq_w, flip=True, beside=[expand_leg, contract_leg, query_pair_leg, cross_out_leg]
    )
    contract_grad = contract_leg.finish(contract_got)
    back, second_gain_part, second_shift_part = norm_backward(grad_normed, centred_two, factor_two, gain_two)
    grad_one = grad_two + back
    expand_leg = Spread(expand_leg.finish(expand_got))
    query_pair_leg = SumX(query_pair_leg.finish(query_pair_got), True)
    cross_out_leg = SumX(cross_out_leg.finish(cross_out_got), False)
    (all_mid_one, grad_attended), (expand_got, query_pair_got, cross_out_got) = gather_times(
        14, grad_one.astype(bf16), out_w, flip=True, beside=[expand_leg, query_pair_leg, cross_out_leg]
    )
    expand_grad = expand_leg.finish(expand_got)
    output_leg = SumZ(outer(attended, all_mid_one).astype(bf16), False)
    query_pair_leg = Spread(query_pair_leg.finish(query_pair_got))
    cross_out_leg = Spread(cross_out_leg.finish(cross_out_got))
    (grad_qkv,), (output_got, query_pair_got, cross_out_got) = causal_backward(
        15, qkv, grad_attended, logs, [output_leg, query_pair_leg, cross_out_leg]
    )
    query_pair_grad = query_pair_leg.finish(query_pair_got)
    cross_output_grad = cross_out_leg.finish(cross_out_got)
    joined_leg = SumZ(outer(all_one, grad_qkv).astype(bf16), True)
    output_leg = SumX(output_leg.finish(output_got), False)
    grad_normed, (joined_got, output_got) = times_scatter(
        16, grad_qkv, joined, flip=True, beside=[joined_leg, output_leg]
    )
    back, first_gain_part, first_shift_part = norm_backward(grad_normed, centred_one, factor_one, gain_one)
    input_grad = (grad_one + back).astype(bf16)
    parts = jnp.stack(
        (first_gain_part, first_shift_part, second_gain_part, second_shift_part, third_gain_part, third_shift_part)
    )
    parts = jnp.concatenate([parts, jnp.zeros((2, D), f32)], axis=0)
    joined_leg = SumX(joined_leg.finish(joined_got), True)
    output_leg = Spread(output_leg.finish(output_got))
    _, ((input_grad,), joined_got, output_got, (text_grad,), (parts,)) = call(
        None, 17, [], [], (), [Relay(input_grad, True), joined_leg, output_leg, Text(text_part, True), ToRing(parts)]
    )
    output_grad = output_leg.finish(output_got)
    joined_leg = Spread(joined_leg.finish(joined_got))
    _, (joined_got, (parts,)) = call(None, 18, [], [], (), [joined_leg, ToClips(jnp.sum(parts, axis=0))])
    joined_grad = joined_leg.finish(joined_got)
    parts = jnp.sum(parts, axis=(0, 1))
    return (
        layer_output,
        input_grad.astype(f32),
        text_grad.astype(f32),
        parts[0],
        parts[1],
        joined_grad[:, :COLS],
        joined_grad[:, COLS : 2 * COLS],
        joined_grad[:, 2 * COLS :],
        output_grad,
        parts[2],
        parts[3],
        query_pair_grad[:, :COLS],
        query_pair_grad[:, COLS : 2 * COLS],
        query_pair_grad[:, 2 * COLS :],
        cross_output_grad,
        parts[4],
        parts[5],
        expand_grad,
        contract_grad,
    )


def solution(mesh):
    return jax.shard_map(
        on_device,
        mesh=mesh,
        in_specs=(
            P(("dp", "wide"), "narrow"),
            P("dp", None, "narrow"),
            P(("dp", "wide"), "narrow"),
            P("narrow"),
            P("narrow"),
            P("narrow", "wide"),
            P("narrow", "wide"),
            P("narrow", "wide"),
            P("wide", "narrow"),
            P("narrow"),
            P("narrow"),
            P("narrow", "wide"),
            P("narrow", "wide"),
            P("narrow", "wide"),
            P("wide", "narrow"),
            P("narrow"),
            P("narrow"),
            P("narrow", "wide"),
            P("wide", "narrow"),
        ),
        out_specs=(
            P(("dp", "wide"), "narrow"),
            P(("dp", "wide"), "narrow"),
            P("dp", None, "narrow"),
            P("narrow"),
            P("narrow"),
            P("narrow", "wide"),
            P("narrow", "wide"),
            P("narrow", "wide"),
            P("wide", "narrow"),
            P("narrow"),
            P("narrow"),
            P("narrow", "wide"),
            P("narrow", "wide"),
            P("narrow", "wide"),
            P("wide", "narrow"),
            P("narrow"),
            P("narrow"),
            P("narrow", "wide"),
            P("wide", "narrow"),
        ),
        check_vma=False,
    )
```

time: 1450 us -> 747 us (0.52)
  waiting for transfers between devices: 794 us -> 0.02 us
  Pallas kernels: 0 us -> 589 us
  matrix products: 198 us -> 38 us
  blocking collectives: 155 us -> 0 us
  starting transfers between devices: 98.2 us -> 0.04 us
  local copies, waits for them, and re-layouts: 76.9 us -> 28.8 us
  other arithmetic: 102 us -> 71.2 us
    pallas_call x0 -> x19, Pallas kernels: none -> 589 us  [the longest x17 581 us: call(): pl.pallas_call(kernel, out_shape=tuple(outs) + tuple(side_outs), in_specs...]
    all_gather x18 -> x0, waiting for transfers between devices: 399 us -> none  [the longest x6 177 us: wide_to_narrow(): gathered = lax.all_gather(values, 'wide', axis=0, tiled=True)]
    all_to_all x24 -> x0, waiting for transfers between devices: 278 us -> none  [the longest x7 157 us: sum_at_owner(): lax.all_to_all(parts, axis, split_axis=0, concat_axis=0, tiled=True)]
    dot_general x63 -> x9, matrix products: 198 us -> 38 us  [the longest x7 35 us: outer(): lax.dot_general(a, b, (((0,), (0,)), ((), ())), preferred_element_type=f32)]
    psum x1, waiting for transfers between devices: 111 us -> 0.01 us  [on_device(): text_part = lax.psum(dot_flip(grad_pair, pair).astype(bf16), 'wide')]
    all_to_all x3 -> x0, blocking collectives: 111 us -> none  [the longest x1 98.2 us: narrow_to_wide(): lax.all_to_all(gathered, 'wide', split_axis=0, concat_axis=1, tiled=True)]
    all_to_all x24 -> x0, starting transfers between devices: 96.8 us -> none  [the longest x12 42.3 us: from_everyone(): return lax.all_to_all(copies, axis, split_axis=0, concat_axis=0, tiled=True)]
    psum x1 -> x0, blocking collectives: 44.5 us -> none  [on_device(): lax.psum(first_gain_grad.astype(jnp.bfloat16), 'dp').astype(jnp.float32)]
  transfers between devices with their start and end apart: 43 -> 1, of which waited for: 31 -> 0; matrix products, arithmetic and copies ran while one was open for 18% -> 9% of each run, Pallas kernels for 0% -> 19%
where the time goes in v1:
time: 747 us; the launch traced here: 742 us
  Pallas kernels  589 us (79%)
  other arithmetic  71.2 us (10%)
  matrix products  38 us (5%)
  local copies, waits for them, and re-layouts  28.8 us (4%)
  between operations  15.1 us (2%)
    pallas_call x17, Pallas kernels, call(): pl.pallas_call(kernel, out_shape=tuple(outs) + tuple(side_outs), in_specs...  581 us
    dot_general x7, matrix products, outer(): lax.dot_general(a, b, (((0,), (0,)), ((), ())), preferred_element_type=f32)  35 us
  transfers between devices with their start and end apart: 1, of which 0 were waited for; matrix products, arithmetic and copies ran while one was open for 9% of the time, Pallas kernels for 19%

profile of v1, /device:TPU:0, one launch (start us, length us, event | category | flops | bytes accessed | tf_op | source)
XLA Modules:
  0.0 741.8 jit_solution(1524753794895334156)
XLA Ops:
  12.1 20.7 %shard_map.330 = (bf16[192,1536]{1,0:T(8,128)(2,1)}, bf16[64,1536]{1,0:T(8,128)(2,1)}, f32[8,1536]{1,0:T(8,128)}) custom-call(bf16[384,768]{1,0:T(8,128)(2,1)} %refs_0_.1, bf16[2,64,768]{2,1,0:T(8,128)(2,1)} %refs_1_.2, f32[8,768]{1,0:T(8,128)} %pad_convert_fusion.refs_2_), custom_call_target="tpu_custom_call" | custom-call | tf_op jit(solution)/shard_map/pallas_call | solution.py:351
  41.3 39.6 %shard_map.331 = (bf16[1536,1536]{1,0:T(8,128)(2,1)}, bf16[1536,576]{1,0:T(8,128)(2,1)}, bf16[1536,576]{1,0:T(8,128)(2,1)}, bf16[192,1536]{1,0:T(8,128)(2,1)}) custom-call(bf16[192,1536]{1,0:T(8,128)(2,1)} %fusion.12.refs_0_, bf16[768,576]{1,0:T(8,128)(2,1)} %pad_maximum_fusion.1.refs_1_, bf16[192,768]{1,0:T(8,128)(2,1)} %refs_2_.4), custom_call_target="tpu_custom_call" | custom-call | tf_op jit(solution)/shard_map/pallas_call | solution.py:351
  80.8 44.8 %shard_map.332 = (bf16[1536,192]{1,0:T(8,128)(2,1)}, f32[8,1536]{1,0:T(8,128)}, bf16[1536,192]{1,0:T(8,128)(2,1)}, bf16[1536,384]{1,0:T(8,128)(2,1)}, bf16[192,1536]{1,0:T(8,128)(2,1)}) custom-call(bf16[1536,576]{1,0:T(8,128)(2,1)} %get-tuple-element.77.refs_0_, bf16[768,192]{1,0:T(8,128)(2,1)} %copy.43.refs_1_, bf16[768,384]{1,0:T(8,128)(2,1)} %pad_maximum_fusion.2.refs_2_, ...), custom_call_target="tpu_custom_call" | custom-call | tf_op jit(solution)/shard_map/pallas_call | solution.py:351
  125.6 40.2 %shard_map.333 = (f32[192,1536]{1,0:T(8,128)}, bf16[1536,768]{1,0:T(8,128)(2,1)}) custom-call(bf16[1536,192]{1,0:T(8,128)(2,1)} %get-tuple-element.78.refs_0_, bf16[192,1536]{1,0:T(8,128)(2,1)} %get-tuple-element.79.refs_1_, bf16[768,768]{1,0:T(8,128)(2,1)} %refs_2_.5), custom_call_target="tpu_custom_call" | custom-call | tf_op jit(solution)/shard_map/pallas_call | solution.py:351
  169.6 43.2 %shard_map.334 = (bf16[1536,1536]{1,0:T(8,128)(2,1)}, bf16[1536,192]{1,0:T(8,128)(2,1)}, bf16[768,1536]{1,0:T(8,128)(2,1)}) custom-call(bf16[192,1536]{1,0:T(8,128)(2,1)} %add_convert_fusion.2.refs_0_, bf16[1536,192]{1,0:T(8,128)(2,1)} %get-tuple-element.81.refs_1_, bf16[768,768]{1,0:T(8,128)(2,1)} %refs_2_.6), custom_call_target="tpu_custom_call" | custom-call | tf_op jit(solution)/shard_map/pallas_call | solution.py:351
  212.8 3.4 shard_map.335.refs_0_
  216.2 35.8 %shard_map.336 = (f32[192,1536]{1,0:T(8,128)}, bf16[192,1536]{1,0:T(8,128)(2,1)}) custom-call(bf16[1536,192]{1,0:T(8,128)(2,1)} %shard_map.335.refs_0_, bf16[192,1536]{1,0:T(8,128)(2,1)} %get-tuple-element.85.refs_1_, bf16[384,768]{1,0:T(8,128)(2,1)} %refs_2_.7), custom_call_target="tpu_custom_call" | custom-call | tf_op jit(solution)/shard_map/pallas_call | solution.py:351
  253.6 33.7 %shard_map.337 = (bf16[1536,1536]{1,0:T(8,128)(2,1)}, bf16[1536,768]{1,0:T(8,128)(2,1)}) custom-call(bf16[192,1536]{1,0:T(8,128)(2,1)} %get-tuple-element.86.refs_0_, bf16[768,1536]{1,0:T(8,128)(2,1)} %get-tuple-element.87.refs_1_), custom_call_target="tpu_custom_call" | custom-call | tf_op jit(solution)/shard_map/pallas_call | solution.py:351
  288.4 31.8 %shard_map.338 = (bf16[1536,1536]{1,0:T(8,128)(2,1)}, f32[1536,768]{1,0:T(8,128)}) custom-call(bf16[192,1536]{1,0:T(8,128)(2,1)} %add_convert_fusion.1.refs_0_, bf16[1536,768]{1,0:T(8,128)(2,1)} %get-tuple-element.90.refs_1_), custom_call_target="tpu_custom_call" | custom-call | tf_op jit(solution)/shard_map/pallas_call | solution.py:351
  320.2 6.7 multiply_convert_fusion
  326.9 31.7 %shard_map.339 = f32[192,1536]{1,0:T(8,128)} custom-call(bf16[1536,768]{1,0:T(8,128)(2,1)} %get-tuple-element.167.refs_0_, bf16[768,1536]{1,0:T(8,128)(2,1)} %get-tuple-element.87.refs_1_), custom_call_target="tpu_custom_call" | custom-call | tf_op jit(solution)/shard_map/pallas_call | solution.py:351
  358.7 2.4 add_convert_fusion.refs_3_
  361.0 7.4 %convolution_convert_fusion.1 = bf16[768,1536]{1,0:T(8,128)(2,1)} fusion(bf16[1536,768]{1,0:T(8,128)(2,1)S(1)} %copy-done.2, bf16[1536,1536]{1,0:T(8,128)(2,1)} %get-tuple-element.92), kind=kOutput, calls=%fused_computation.12 | convolution fusion | flops 3625058304 | bytes 9437184 | tf_op jit(solution)/shard_map/dot_general | solution.py:36
  368.4 38.8 %shard_map.340 = (f32[192,1536]{1,0:T(8,128)}, bf16[3,192,1536]{2,1,0:T(8,128)(2,1)}, bf16[384,768]{1,0:T(8,128)(2,1)}) custom-call(bf16[1536,768]{1,0:T(8,128)(2,1)} %get-tuple-element.168.refs_0_, bf16[1536,768]{1,0:T(8,128)(2,1)} %get-tuple-element.90.refs_1_, bf16[4,192,1536]{2,1,0:T(8,128)(2,1)} %bitcast.91, bf16[192,1536]{1,0:T(8,128)(2,1)} %add_convert_fusion.refs_3_), custom_call_target="tpu_custom_call" | custom-call | tf_op jit(solution)/shard_map/pallas_call | solution.py:351
  407.2 2.9 convert_reduce_fusion.1
  411.2 8.5 %convolution_convert_fusion = bf16[1536,768]{1,0:T(8,128)(2,1)} fusion(bf16[1536,1536]{1,0:T(8,128)(2,1)} %get-tuple-element.95, bf16[1536,768]{1,0:T(8,128)(2,1)} %get-tuple-element.168.refs_0_), kind=kOutput, calls=%fused_computation.11 | convolution fusion | flops 3625058304 | bytes 9437184 | tf_op jit(solution)/shard_map/dot_general | solution.py:36
  423.8 34.7 %shard_map.341 = (bf16[1536,1536]{1,0:T(8,128)(2,1)}, bf16[1536,192]{1,0:T(8,128)(2,1)}, bf16[3,2,192,768]{3,2,1,0:T(8,128)(2,1)}, bf16[3,96,768]{2,1,0:T(8,128)(2,1)}) custom-call(bf16[192,1536]{1,0:T(8,128)(2,1)} %get-tuple-element.163.refs_0_, bf16[192,1536]{1,0:T(8,128)(2,1)} %get-tuple-element.85.refs_1_, bf16[2,4,192,768]{3,2,1,0:T(8,128)(2,1)} %bitcast.89, ...), custom_call_target="tpu_custom_call" | custom-call | tf_op jit(solution)/shard_map/pallas_call | solution.py:351
  458.5 4.3 shard_map.342
  466.7 4.3 convolution_convert_fusion.6
  471.0 2.2 copy.44
  473.3 3.3 pad_maximum_fusion.refs_4_
  477.6 3.8 convolution_convert_fusion.5
  486.7 48.2 %shard_map.343 = (f32[192,1536]{1,0:T(8,128)}, bf16[3,96,768]{2,1,0:T(8,128)(2,1)}, bf16[8,96,768]{2,1,0:T(8,128)(2,1)}, bf16[3,2,192,576]{3,2,1,0:T(8,128)(2,1)}, bf16[3,48,1536]{2,1,0:T(8,128)(2,1)}) custom-call(bf16[1536,192]{1,0:T(8,128)(2,1)} %get-tuple-element.98.refs_0_, bf16[1536,192]{1,0:T(8,128)(2,1)} %get-tuple-element.81.refs_1_, ...), custom_call_target="tpu_custom_call" | custom-call | tf_op jit(solution)/shard_map/pallas_call | solution.py:351
  536.0 2.8 convert_reduce_fusion.3
  545.8 31.5 %shard_map.344 = (bf16[1536,1536]{1,0:T(8,128)(2,1)}, bf16[1536,192]{1,0:T(8,128)(2,1)}, bf16[8,96,768]{2,1,0:T(8,128)(2,1)}, bf16[3,96,576]{2,1,0:T(8,128)(2,1)}, bf16[3,24,768]{2,1,0:T(8,128)(2,1)}) custom-call(bf16[192,1536]{1,0:T(8,128)(2,1)} %get-tuple-element.161.refs_0_, bf16[192,1536]{1,0:T(8,128)(2,1)} %get-tuple-element.79.refs_1_, ...), custom_call_target="tpu_custom_call" | custom-call | tf_op jit(solution)/shard_map/pallas_call | solution.py:351
  582.5 3.4 convolution_convert_fusion.4
  586.8 30.6 %shard_map.345 = (bf16[1536,576]{1,0:T(8,128)(2,1)}, bf16[3,48,1536]{2,1,0:T(8,128)(2,1)}, bf16[8,96,576]{2,1,0:T(8,128)(2,1)}, bf16[8,24,768]{2,1,0:T(8,128)(2,1)}) custom-call(bf16[1536,576]{1,0:T(8,128)(2,1)} %get-tuple-element.77.refs_0_, bf16[1536,192]{1,0:T(8,128)(2,1)} %get-tuple-element.108.refs_1_, f32[8,1536]{1,0:T(8,128)} %get-tuple-element.109.refs_2_, ...), custom_call_target="tpu_custom_call" | custom-call | tf_op jit(solution)/shard_map/pallas_call | solution.py:351
  618.5 7.2 convolution_convert_fusion.2
  625.6 2.7 copy.45
  629.7 30.9 %shard_map.346 = (f32[192,1536]{1,0:T(8,128)}, bf16[3,2,192,576]{3,2,1,0:T(8,128)(2,1)}, bf16[3,24,768]{2,1,0:T(8,128)(2,1)}) custom-call(bf16[1536,576]{1,0:T(8,128)(2,1)} %get-tuple-element.113.refs_0_, bf16[1536,576]{1,0:T(8,128)(2,1)} %get-tuple-element.114.refs_1_, bf16[2,4,192,576]{3,2,1,0:T(8,128)(2,1)} %bitcast.82, bf16[2,24,1536]{2,1,0:T(8,128)(2,1)} %fusion.25.refs_3_), custom_call_target="tpu_custom_call" | custom-call | tf_op jit(solution)/shard_map/pallas_call | solution.py:351
  677.6 23.9 %shard_map.347 = (bf16[384,768]{1,0:T(8,128)(2,1)}, bf16[3,96,576]{2,1,0:T(8,128)(2,1)}, bf16[8,24,768]{2,1,0:T(8,128)(2,1)}, bf16[2,64,768]{2,1,0:T(8,128)(2,1)}, f32[8,8,1536]{2,1,0:T(8,128)}) custom-call(bf16[192,1536]{1,0:T(8,128)(2,1)} %fusion.17.refs_0_, bf16[2,2,96,576]{3,2,1,0:T(8,128)(2,1)} %fusion.22.refs_1_, bf16[24,768]{1,0:T(8,128)(2,1)} %fusion.31.refs_2_, ...), custom_call_target="tpu_custom_call" | custom-call | tf_op jit(solution)/shard_map/pallas_call | solution.py:351
  704.8 20.7 %shard_map.348 = (bf16[8,96,576]{2,1,0:T(8,128)(2,1)}, f32[8,2,8,768]{3,2,1,0:T(8,128)}) custom-call(bf16[96,576]{1,0:T(8,128)(2,1)} %fusion.29.refs_0_, f32[8,1536]{1,0:T(8,128)} %reduce_sum.336.refs_1_), custom_call_target="tpu_custom_call" | custom-call | tf_op jit(solution)/shard_map/pallas_call | solution.py:351
  (209 shorter events, 80.6 us)
Async XLA Ops:
  7.2 28.2 %copy-start.34 = (bf16[768,192]{0,1:T(8,128)(2,1)S(1)}, bf16[768,192]{0,1:T(8,128)(2,1)}, u32[]{:S(2)}) copy-start(bf16[768,192]{0,1:T(8,128)(2,1)} %param.24) | copy-start | bytes 884740
  7.2 28.4 %copy-start.35 = (bf16[768,192]{0,1:T(8,128)(2,1)S(1)}, bf16[768,192]{0,1:T(8,128)(2,1)}, u32[]{:S(2)}) copy-start(bf16[768,192]{0,1:T(8,128)(2,1)} %param.25) | copy-start | bytes 884740
  7.2 670.4 %all-reduce.3.cloned.1.call-start = ((), (), s32[]{:S(2)}) async-start(), calls=%async_computation | async-start | bytes 393216 | tf_op jit(solution)/shard_map/psum | solution.py:768
  32.8 3.0 copy-start.36
  37.7 2.3 copy-start.51
  37.7 2.3 copy-start.53
  167.5 2.1 copy-start.47
  167.6 2.1 copy-start.49
  288.4 31.8 %copy-start.13 = (bf16[1536,768]{1,0:T(8,128)(2,1)S(1)}, bf16[1536,768]{1,0:T(8,128)(2,1)}, u32[]{:S(2)}) copy-start(bf16[1536,768]{1,0:T(8,128)(2,1)} %get-tuple-element.88) | copy-start | bytes 7077892
  358.6 2.4 copy-start.2
  411.2 8.5 %copy-start.6 = (f32[192,1536]{1,0:T(8,128)S(1)}, f32[192,1536]{1,0:T(8,128)}, u32[]{:S(2)}) copy-start(f32[192,1536]{1,0:T(8,128)} %get-tuple-element.94) | copy-start | bytes 3538948
  458.5 4.3 copy-start.5
  462.8 2.1 copy-start.40
  473.3 3.3 copy-start.3
  477.6 3.8 copy-start.28
  536.0 2.8 copy-start.29
  536.0 2.8 copy-start.7
  538.9 2.7 copy-start.12
  538.9 2.7 copy-start.15
  541.6 2.5 copy-start.10
  541.6 2.5 copy-start.48
  541.6 2.5 copy-start.50
  577.3 5.2 copy-start.23
  629.7 31.0 %copy-start.52 = (f32[192]{0:T(256)S(1)}, f32[192]{0:T(256)}, u32[]{:S(2)}) copy-start(f32[192]{0:T(256)} %copy-done.51) | copy-start | bytes 2308
  629.7 31.0 %copy-start.54 = (f32[192]{0:T(256)S(1)}, f32[192]{0:T(256)}, u32[]{:S(2)}) copy-start(f32[192]{0:T(256)} %copy-done.53) | copy-start | bytes 2308
  667.6 2.6 copy-start.11
  670.7 2.8 copy-start.46
  670.7 2.9 copy-start.45
  670.7 2.9 copy-start.44
  670.7 2.9 copy-start.43
  701.5 2.7 copy-start.31
  728.3 2.1 copy-start.30
  (24 other events, 36.7 us)
Sparse Core Ops, SparseCore 0:
  465.0 60.9 all-reduce.2

commit v2 on v1

v2 whole, which is shorter than its diff:
```python
import functools
import math

import jax
import jax.numpy as jnp
from jax import lax
from jax.experimental import pallas as pl
from jax.experimental.pallas import tpu as pltpu
from jax.sharding import PartitionSpec as P

D = 1536
HALF = 768
HDIM = 64
HEADS = 3
COLS = HEADS * HDIM
BLOCK = 192
EPSILON = 1e-05
NEGATIVE = -1e30
ROOT_HALF = 0.7071067811865476
GAUSS_NORM = 0.3989422804014327
MESH = pl.DeviceIdType.MESH
VMEM = pltpu.VMEM
ANY = pl.ANY
bf16, f32 = jnp.bfloat16, jnp.float32


def dot(a, b):
    return lax.dot_general(a, b, (((1,), (0,)), ((), ())), preferred_element_type=f32)


def dot_flip(a, b):
    return lax.dot_general(a, b, (((1,), (1,)), ((), ())), preferred_element_type=f32)


def outer(a, b):
    return lax.dot_general(a, b, (((0,), (0,)), ((), ())), preferred_element_type=f32)


class Place:
    def __init__(self):
        self.dp, self.w, self.n = (lax.axis_index(a) for a in ("dp", "wide", "narrow"))
        self.y, self.c = lax.div(self.w, 2), lax.rem(self.w, 2)
        self.z, self.s = lax.div(self.dp, 2), lax.rem(self.dp, 2)
        self.up, self.down = lax.rem(self.y + 1, 4), lax.rem(self.y + 3, 4)
        self.across = 3 - self.y
        self.moved = lax.rem(lax.div(self.y, 2) + self.n, 2)
        self.clip = lax.div(self.y, 2)

    def spot(self, y, c):
        moved = lax.rem(lax.div(y, 2) + self.n, 2)
        return (lax.rem(y + moved, 2) * 2 + c) * 2 + moved

    def rows(self, y, c, start=0, size=BLOCK):
        return pl.ds(pl.multiple_of(self.spot(y, c) * BLOCK + start, 32), size)

    def half(self, n):
        return pl.ds(pl.multiple_of(n * HALF, HALF), HALF)

    def at_y(self, y):
        return {"wide": y * 2 + self.c}

    def core(self):
        return {"wide": self.y * 2 + 1 - self.c}

    def x(self):
        return {"narrow": 1 - self.n}

    def at_z(self, k):
        return {"dp": lax.rem(self.z + k, 4) * 2 + self.s}

    def at_dp(self, k):
        return {"dp": lax.rem(self.dp + k, 8)}

    def at_x(self, ds, dn):
        return {"dp": self.z * 2 + lax.rem(self.s + ds, 2), "narrow": lax.rem(self.n + dn, 2)}


def remote(src, dst, send, recv, peer):
    return pltpu.make_async_remote_copy(
        src_ref=src, dst_ref=dst, send_sem=send, recv_sem=recv, device_id=peer, device_id_type=MESH
    )


def greet(peers):
    barrier = pltpu.get_barrier_semaphore()
    for peer in peers:
        pl.semaphore_signal(barrier, inc=1, device_id=peer, device_id_type=MESH)
    pl.semaphore_wait(barrier, len(peers))


class Give:
    def __init__(self, array):
        self.ins, self.copies, self.locals = [array], 1, 0
        self.outs = [jax.ShapeDtypeStruct(array.shape, array.dtype)]

    def peers(self, at):
        return [("x", at.x())]

    def moves(self, at, ins, outs):
        return [(ins[0], outs[0], at.x())], []


class GiveClip(Give):
    def __init__(self, array):
        super().__init__(array)
        self.outs = [jax.ShapeDtypeStruct(array.shape[1:], array.dtype)]

    def moves(self, at, ins, outs):
        return [(ins[0].at[1 - at.n], outs[0], at.x())], []


class SumZ:
    def __init__(self, array, by_rows):
        self.by_rows, self.copies, self.locals = by_rows, 3, 0
        rows, cols = array.shape
        shape = (2, 4, rows // 8, cols) if by_rows else (4, rows // 4, cols)
        self.ins = [array.reshape(shape)]
        kept = (2, rows // 8, cols) if by_rows else (rows // 4, cols)
        self.outs = [jax.ShapeDtypeStruct((3, *kept), array.dtype)]

    def peers(self, at):
        return [(f"z{k}", at.at_z(k)) for k in (1, 2, 3)]

    def moves(self, at, ins, outs):
        out = []
        for k in (1, 2, 3):
            q = lax.rem(at.z + k, 4)
            src = ins[0].at[:, q] if self.by_rows else ins[0].at[q]
            out.append((src, outs[0].at[k - 1], at.at_z(k)))
        return out, []

    def finish(self, outs):
        z = lax.div(lax.axis_index("dp"), 2)
        own = lax.dynamic_index_in_dim(self.ins[0], z, 1 if self.by_rows else 0, False)
        return (own.astype(f32) + outs[0].astype(f32).sum(axis=0)).astype(bf16)


class SumX:
    def __init__(self, array, by_rows):
        self.by_rows, self.copies, self.locals = by_rows, 3, 0
        if by_rows:
            two, rows, cols = array.shape
            self.ins, kept = [array.reshape(2, 2, rows // 2, cols)], (rows // 2, cols)
        else:
            rows, cols = array.shape
            self.ins, kept = [array.reshape(2, rows // 2, cols)], (rows // 2, HALF)
        self.outs = [jax.ShapeDtypeStruct((3, *kept), array.dtype)]

    order = ((0, 1), (1, 0), (1, 1))

    def peers(self, at):
        return [(f"x{a}{b}", at.at_x(a, b)) for a, b in self.order]

    def moves(self, at, ins, outs):
        out = []
        for i, (a, b) in enumerate(self.order):
            s, n = lax.rem(at.s + a, 2), lax.rem(at.n + b, 2)
            src = ins[0].at[n, s] if self.by_rows else ins[0].at[s, :, at.half(n)]
            out.append((src, outs[0].at[i], at.at_x(a, b)))
        return out, []

    def finish(self, outs):
        s, n = lax.rem(lax.axis_index("dp"), 2), lax.axis_index("narrow")
        if self.by_rows:
            own = lax.dynamic_index_in_dim(lax.dynamic_index_in_dim(self.ins[0], n, 0, False), s, 0, False)
        else:
            own = lax.dynamic_slice_in_dim(lax.dynamic_index_in_dim(self.ins[0], s, 0, False), n * HALF, HALF, 1)
        return (own.astype(f32) + outs[0].astype(f32).sum(axis=0)).astype(bf16)


class Spread:
    def __init__(self, array):
        self.ins, self.copies, self.locals = [array], 7, 1
        self.outs = [jax.ShapeDtypeStruct((8, *array.shape), array.dtype)]

    def peers(self, at):
        return [(f"d{k}", at.at_dp(k)) for k in range(1, 8)]

    def moves(self, at, ins, outs):
        dst = outs[0].at[at.dp]
        return [(ins[0], dst, at.at_dp(k)) for k in range(1, 8)], [(ins[0], dst)]

    def finish(self, outs):
        eight, rows, cols = outs[0].shape
        return outs[0].reshape(eight * rows, cols).astype(f32)


class ToRing:
    def __init__(self, array):
        self.ins, self.copies, self.locals = [array], 7, 1
        self.outs = [jax.ShapeDtypeStruct((8, *array.shape), array.dtype)]

    def peers(self, at):
        return [(f"w{k}", {"wide": lax.rem(at.w + k, 8)}) for k in range(1, 8)]

    def moves(self, at, ins, outs):
        dst = outs[0].at[at.w]
        return [(ins[0], dst, peer) for _, peer in self.peers(at)], [(ins[0], dst)]


class ToClips:
    def __init__(self, array):
        self.ins, self.copies, self.locals = [array], 15, 1
        self.outs = [jax.ShapeDtypeStruct((8, 2, array.shape[0], HALF), array.dtype)]

    order = tuple((k, b) for k in range(8) for b in range(2))[1:]

    def peers(self, at):
        return [(f"c{k}{b}", {**at.at_dp(k), "narrow": lax.rem(at.n + b, 2)}) for k, b in self.order]

    def moves(self, at, ins, outs):
        dst = outs[0].at[at.dp, at.n]
        far = []
        for (k, b), (_, peer) in zip(self.order, self.peers(at)):
            far.append((ins[0].at[:, at.half(lax.rem(at.n + b, 2))], dst, peer))
        return far, [(ins[0].at[:, at.half(at.n)], dst)]


class Relay:
    def __init__(self, array, back=False):
        self.ins, self.back, self.copies, self.locals = [array], back, 2, 1
        shape = (384, HALF) if back else (BLOCK, D)
        self.outs = [jax.ShapeDtypeStruct(shape, array.dtype)]

    def peers(self, at):
        return [
            ("x", at.x()),
            ("a0", {"wide": at.across * 2 + at.c}),
            ("a1", {"wide": at.across * 2 + at.c, "narrow": 1 - at.n}),
        ]


def relay_run(relay, at, src, dst, send, recv, local, base, finish):
    mine, other = at.half(at.n), at.half(1 - at.n)
    over = at.across * 2 + at.c
    if relay.back:
        row = pl.ds(pl.multiple_of(at.moved * BLOCK, BLOCK), BLOCK)
        to = recv.at[base + at.moved]
        own = src.at[:, mine], src.at[:, other]
        land = dst.at[0:BLOCK], dst.at[BLOCK : 2 * BLOCK]
    else:
        row = mine
        to = recv.at[base + at.n]
        own = src.at[0:BLOCK], src.at[BLOCK : 2 * BLOCK]
        land = dst.at[:, at.half(0)], dst.at[:, at.half(1)]
    target = dst.at[row] if relay.back else dst.at[:, row]

    def arrive(slot, part):
        return remote(own[0], part, send.at[base], recv.at[base + slot], at.x())

    @pl.when(at.moved == 0)
    def _():
        stay = pltpu.make_async_copy(own[0], target, local)
        if relay.back:
            go = remote(own[1], target, send.at[base], to, at.x())
        else:
            go = remote(own[1], target, send.at[base], to, {"wide": over})
        if not finish:
            go.start()
            stay.start()
        else:
            stay.wait()
            go.wait_send()
            if relay.back:
                arrive(1, land[1]).wait_recv()
            else:
                arrive(1 - at.n, dst.at[:, other]).wait_recv()

    @pl.when(at.moved == 1)
    def _():
        if relay.back:
            first = remote(own[1], target, send.at[base], to, {"wide": over, "narrow": 1 - at.n})
            second = remote(own[0], target, send.at[base + 1], to, {"wide": over})
        else:
            first = remote(own[1], target, send.at[base], to, {"wide": over, "narrow": 1 - at.n})
            second = remote(own[0], target, send.at[base + 1], to, at.x())
        if not finish:
            first.start()
            second.start()
        else:
            first.wait_send()
            second.wait_send()
            arrive(0, land[0]).wait_recv()
            arrive(1, land[1]).wait_recv()


def call(body, number, ins, outs, scratch=(), beside=(), peers=None, spaces=None, out_spaces=None):
    spaces = spaces or [VMEM] * len(ins)
    out_spaces = out_spaces or [VMEM] * len(outs)
    copies = sum(b.copies for b in beside)
    locals_ = sum(b.locals for b in beside)
    side_ins = [a for b in beside for a in b.ins]
    side_outs = [a for b in beside for a in b.outs]
    n_in, n_out, n_scratch = len(ins), len(outs), len(scratch)

    def kernel(*refs):
        at = Place()
        refs = list(refs)

        def take(count):
            out = refs[:count]
            del refs[:count]
            return out

        main_in, side_in = take(n_in), take(len(side_ins))
        main_out, side_out, kept = take(n_out), take(len(side_outs)), take(n_scratch)
        send, recv, local = take(3)
        known = dict(peers(at)) if peers else {}
        for b in beside:
            known.update(dict(b.peers(at)))
        if known:
            greet(list(known.values()))
        slot, place, todo = 0, 0, []
        for b in beside:
            i, o = [side_in.pop(0) for _ in b.ins], [side_out.pop(0) for _ in b.outs]
            if isinstance(b, Relay):
                run = functools.partial(relay_run, b, at, i[0], o[0], send, recv, local.at[place], slot)
                run(False)
                todo.append(functools.partial(run, True))
                slot, place = slot + 2, place + 1
                continue
            far, near = b.moves(at, i, o)
            for src, dst, peer in far:
                copy = remote(src, dst, send.at[slot], recv.at[slot], peer)
                copy.start()
                todo.append(copy.wait)
                slot += 1
            for src, dst in near:
                copy = pltpu.make_async_copy(src, dst, local.at[place])
                copy.start()
                todo.append(copy.wait)
                place += 1
        if body:
            body(at, main_in, main_out, kept)
        for wait in todo:
            wait()

    results = pl.pallas_call(
        kernel,
        out_shape=tuple(outs) + tuple(side_outs),
        in_specs=[pl.BlockSpec(memory_space=s) for s in spaces] + [pl.BlockSpec(memory_space=ANY)] * len(side_ins),
        out_specs=tuple(pl.BlockSpec(memory_space=m) for m in out_spaces + [ANY] * len(side_outs)),
        scratch_shapes=[
            *scratch,
            pltpu.SemaphoreType.DMA((max(copies, 1),)),
            pltpu.SemaphoreType.DMA((max(copies, 1),)),
            pltpu.SemaphoreType.DMA((max(locals_, 1),)),
        ],
        compiler_params=pltpu.CompilerParams(
            collective_id=number, has_side_effects=True, vmem_limit_bytes=58 << 20
        ),
    )(*ins, *side_ins)
    results = list(results)
    main, rest = results[: len(outs)], results[len(outs) :]
    sides = []
    for b in beside:
        sides.append(rest[: len(b.outs)])
        del rest[: len(b.outs)]
    return main, sides


def ring_peers(at):
    return [("up", at.at_y(at.up)), ("down", at.at_y(at.down)), ("core", at.core())]


def sems(count):
    return [pltpu.SemaphoreType.DMA((count,)), pltpu.SemaphoreType.DMA((count,)), pltpu.SemaphoreType.DMA((count,))]


def by_rows(count, size, work, carry=None):
    def step(i, carry):
        return work(pl.ds(pl.multiple_of(i * size, size), size), carry)

    return lax.fori_loop(0, count // size, step, carry)


class Whole:
    def __init__(self, at, own, got, full, sem, axis):
        size = own.shape[axis]
        self.copies = []
        for i, (part, n) in enumerate(((own, at.n), (got, 1 - at.n))):
            where = pl.ds(pl.multiple_of(n * size, size), size)
            target = full.at[where] if axis == 0 else full.at[:, where]
            self.copies.append(pltpu.make_async_copy(part, target, sem.at[i]))
            self.copies[-1].start()

    def wait(self):
        for copy in self.copies:
            copy.wait()


class Gather:
    slots = 9

    def __init__(self, at, x, whole, send, recv, local):
        self.at, self.x, self.whole = at, x, whole
        y, c, up, down = at.y, at.c, at.up, at.down
        far = lax.rem(y + 2, 4)
        half = BLOCK // 2

        def move(slot, y_from, peer, start=0, size=BLOCK, first=False):
            rows = at.rows(y_from, c, start, size)
            return remote(x if first else whole.at[rows], whole.at[rows], send.at[slot], recv.at[slot], peer)

        to_up, to_down, core = at.at_y(up), at.at_y(down), at.core()
        self.sends = [
            move(0, y, to_up, first=True),
            move(1, y, to_down, first=True),
            move(2, y, core, first=True),
            move(3, down, to_up, 0, half),
            move(4, up, to_down, half, half),
            move(5, down, core),
            move(6, up, core),
            move(7, far, core, 0, half),
            move(8, far, core, half, half),
        ]
        self.own = pltpu.make_async_copy(x, whole.at[at.rows(y, c)], local)

    def begin(self):
        for i in range(3):
            self.sends[i].start()
        self.own.start()
        self.own.wait()

    def pass_on(self):
        s = self.sends
        s[1].wait_recv()
        s[4].start()
        s[6].start()
        s[0].wait_recv()
        s[3].start()
        s[5].start()

    def pass_far(self):
        s = self.sends
        s[3].wait_recv()
        s[7].start()
        s[4].wait_recv()
        s[8].start()

    def got(self, *slots):
        for i in slots:
            self.sends[i].wait_recv()

    def end(self):
        for copy in self.sends:
            copy.wait_send()

    def each(self, work, before_last=None):
        at = self.at

        def step(s, carry):
            @pl.when(s == 1)
            def _():
                self.got(2)

            @pl.when(s == 2)
            def _():
                self.pass_on()

            @pl.when(s == 3)
            def _():
                self.got(6)

            @pl.when(s == 5)
            def _():
                self.got(5)

            @pl.when(s == 6)
            def _():
                self.pass_far()

            @pl.when(s == 7)
            def _():
                self.got(7, 8)

            g = lax.div(s, 2)
            off = g + lax.div(g, 2) - 2 * lax.div(g, 3)
            work(s, at.rows(lax.rem(at.y + off, 4), lax.rem(at.c + s, 2)))
            return carry

        lax.fori_loop(0, 8, step, 0)
        self.end()


class Scatter:
    slots = 8
    scratch = [
        VMEM((4, BLOCK, D), bf16),
        VMEM((4, BLOCK, D), bf16),
        VMEM((4, BLOCK, D), f32),
        VMEM((2, BLOCK, D), bf16),
        VMEM((2, BLOCK, D), bf16),
        VMEM((2, BLOCK // 2, D), bf16),
        VMEM((2, BLOCK // 2, D), bf16),
    ]

    def __init__(self, at, send, recv, refs):
        self.at, self.send, self.recv = at, send, recv
        self.out_c, self.in_c, self.own, self.out_y, self.in_y, self.half_out, self.half_in = refs
        to_up, to_down = at.at_y(at.up), at.at_y(at.down)
        self.cores = [self.core(g) for g in range(4)]
        self.halves = [
            remote(self.half_out.at[0], self.half_in.at[0], send.at[4], recv.at[4], to_up),
            remote(self.half_out.at[1], self.half_in.at[1], send.at[5], recv.at[5], to_down),
        ]
        self.blocks = [
            remote(self.out_y.at[0], self.in_y.at[0], send.at[6], recv.at[6], to_up),
            remote(self.out_y.at[1], self.in_y.at[1], send.at[7], recv.at[7], to_down),
        ]

    def core(self, g):
        return remote(self.out_c.at[g], self.in_c.at[g], self.send.at[g], self.recv.at[g], self.at.core())

    def both(self, g, rows):
        return self.own[g, rows] + self.in_c[g, rows].astype(f32)

    def products(self, product):
        at = self.at
        half = BLOCK // 2

        def step(s, carry):
            g = lax.div(s, 2)
            off = lax.rem(6 - g + 3 * lax.div(g, 2) + 2 * lax.div(g, 3), 4)
            part = product(at.rows(lax.rem(at.y + off, 4), lax.rem(at.c + 1 + s, 2)))

            @pl.when(lax.rem(s, 2) == 0)
            def _():
                self.out_c[g] = part.astype(bf16)
                self.core(g).start()

            @pl.when(lax.rem(s, 2) == 1)
            def _():
                self.own[g] = part

            @pl.when(s == 2)
            def _():
                self.cores[0].wait_recv()
                for i in range(2):

                    def add(rows, carry, i=i):
                        low = pl.ds(pl.multiple_of(rows.start + i * half, 32), 32)
                        self.half_out[i, rows] = self.both(0, low).astype(bf16)

                    by_rows(half, 32, add)
                    self.halves[i].start()

            return carry

        lax.fori_loop(0, 8, step, 0)

    def middle(self):
        half = BLOCK // 2
        for i in range(2):
            self.cores[1 + i].wait_recv()
            self.halves[i].wait_recv()

            def add(rows, carry, i=i):
                here = pl.ds(pl.multiple_of(rows.start + i * half, 32), 32)
                there = pl.ds(pl.multiple_of(rows.start + (1 - i) * half, 32), 32)
                self.out_y[i, here] = (self.both(1 + i, here) + self.half_in[i, rows].astype(f32)).astype(bf16)
                self.out_y[i, there] = self.both(1 + i, there).astype(bf16)

            by_rows(half, 32, add)
            self.blocks[i].start()

    def arrive(self):
        self.cores[3].wait_recv()
        self.blocks[0].wait_recv()
        self.blocks[1].wait_recv()

    def total(self, rows):
        return self.both(3, rows) + self.in_y[0, rows].astype(f32) + self.in_y[1, rows].astype(f32)

    def end(self):
        for copy in self.cores + self.halves + self.blocks:
            copy.wait_send()


def standard(values):
    average = jnp.mean(values, axis=1, keepdims=True)
    variance = jnp.mean(values * values, axis=1, keepdims=True) - average * average
    factor = lax.rsqrt(variance + EPSILON)
    return (values - average) * factor, factor


def norm_back(incoming, centred, factor, gain):
    scaled = incoming * gain
    first = jnp.mean(scaled, axis=1, keepdims=True)
    second = jnp.mean(scaled * centred, axis=1, keepdims=True)
    return factor * (scaled - first - centred * second)


def two_sums(incoming, centred, carry):
    gains, shifts = carry
    return gains + jnp.sum(incoming * centred, axis=0, keepdims=True), shifts + jnp.sum(incoming, axis=0, keepdims=True)


def no_sums():
    return jnp.zeros((1, D), f32), jnp.zeros((1, D), f32)


def head(ref, rows, start):
    return ref[rows, start : start + HDIM]


def cross_weights(q, k):
    scores = dot_flip(k, q)
    raised = jnp.exp(scores - jnp.max(scores, axis=0, keepdims=True))
    return raised / jnp.sum(raised, axis=0, keepdims=True)


EIGHTH = 0.125


def shape(*dims, dtype=bf16):
    return jax.ShapeDtypeStruct(dims, dtype)


def enter(number, layer_input, vectors, joined, beside):
    relay = Relay(layer_input)

    def body(at, ins, outs, kept):
        (source, own_vectors, own_weight), (x, vectors, weight, all_rows, qkv) = ins, outs
        normed, whole, send, recv, local = kept
        half = at.half(at.n)
        moving = functools.partial(relay_run, relay, at, source, x, send, recv, local.at[0], 9)
        moving(False)
        stay = [
            pltpu.make_async_copy(own_vectors, vectors.at[:, half], local.at[1]),
            pltpu.make_async_copy(own_weight, weight.at[half], local.at[2]),
        ]
        go = [
            remote(own_vectors, vectors.at[:, half], send.at[11], recv.at[11], at.x()),
            remote(own_weight, weight.at[half], send.at[12], recv.at[12], at.x()),
        ]
        for copy in stay + go:
            copy.start()
        stay[0].wait()
        go[0].wait_recv()
        moving(True)

        def norm(rows, carry):
            centred, _ = standard(x[rows].astype(f32))
            normed[rows] = (centred * vectors[0:1] + vectors[1:2]).astype(bf16)

        by_rows(BLOCK, 32, norm)
        gather = Gather(at, normed, whole, send, recv, local.at[3])
        gather.begin()

        def work(s, rows):
            @pl.when(s == 7)
            def _():
                stay[1].wait()
                go[1].wait_recv()

            pltpu.make_async_copy(whole.at[rows], all_rows.at[rows], local.at[4 + s]).start()

        gather.each(work)

        def times(rows, carry):
            qkv[rows] = dot(whole[rows], weight[...]).astype(bf16)

        by_rows(D, BLOCK, times)
        for s in range(8):
            pltpu.make_async_copy(whole.at[0:BLOCK], all_rows.at[0:BLOCK], local.at[4 + s]).wait()
        for copy in go:
            copy.wait_send()

    return call(
        body,
        number,
        [layer_input, vectors, joined],
        [shape(BLOCK, D), shape(8, D, dtype=f32), shape(D, 3 * COLS), shape(D, D), shape(D, 3 * COLS)],
        [VMEM((BLOCK, D), bf16), VMEM((D, D), bf16), *sems(16)],
        beside,
        lambda at: ring_peers(at) + relay.peers(at) + [("x", at.x())],
        out_spaces=[VMEM, VMEM, VMEM, ANY, VMEM],
    )


def self_to_cross(number, attended, out_w, x, vectors, query_w, text_pair, beside):
    def body(at, ins, outs, kept):
        values, out_own, out_got, x, vectors, query_own, query_got, pair = ins
        middle, all_rows, queries, crossed = outs
        *refs, normed, whole, out_full, query_full, send, recv, local = kept
        weight = Whole(at, out_own, out_got, out_full, local.at[pl.ds(0, 2)], 1)
        later = Whole(at, query_own, query_got, query_full, local.at[pl.ds(2, 2)], 0)
        weight.wait()
        scatter = Scatter(at, send, recv, refs)
        scatter.products(lambda rows: dot(values[rows], out_full[...]))
        scatter.middle()
        later.wait()
        scatter.arrive()

        def norm(rows, carry):
            total = x[rows].astype(f32) + scatter.total(rows)
            middle[rows] = total
            centred, _ = standard(total)
            normed[rows] = (centred * vectors[2:3] + vectors[3:4]).astype(bf16)

        by_rows(BLOCK, 32, norm)
        gather = Gather(at, normed, whole, send.at[pl.ds(8, 9)], recv.at[pl.ds(8, 9)], local.at[4])
        gather.begin()

        def work(s, rows):
            pltpu.make_async_copy(whole.at[rows], all_rows.at[rows], local.at[5 + s]).start()
            q_all = dot(whole[rows], query_full[...]).astype(bf16)
            queries[rows] = q_all
            parts = []
            for h in range(HEADS):
                a = h * HDIM
                p = cross_weights(q_all[:, a : a + HDIM] * EIGHTH, pair[:, a : a + HDIM])
                v = pair[:, COLS + a : COLS + a + HDIM].T
                parts.append(dot(v, p.astype(bf16)).T)
            crossed[rows] = jnp.concatenate(parts, axis=1).astype(bf16)

        gather.each(work)
        for s in range(8):
            pltpu.make_async_copy(whole.at[0:BLOCK], all_rows.at[0:BLOCK], local.at[5 + s]).wait()
        scatter.end()

    return call(
        body,
        number,
        [attended, *out_w, x, vectors, *query_w, text_pair],
        [shape(BLOCK, D, dtype=f32), shape(D, D), shape(D, COLS), shape(D, COLS)],
        [*Scatter.scratch, VMEM((BLOCK, D), bf16), VMEM((D, D), bf16), VMEM((COLS, D), bf16), VMEM((D, COLS), bf16), *sems(17)],
        beside,
        ring_peers,
        spaces=[VMEM, ANY, ANY, VMEM, VMEM, ANY, ANY, VMEM],
        out_spaces=[VMEM, ANY, VMEM, VMEM],
    )


def feed_forward(number, crossed, cross_w, middle, vectors, expand_w, contract_w, all_down, beside):
    def body(at, ins, outs, kept):
        values, cross_own, cross_got, middle, vectors, expand_own, expand_got, contract_own, contract_got, all_down = ins
        after, all_rows, activated, grad = outs
        *refs, normed, whole, down, cross_full, expand_full, contract_full, send, recv, local = kept
        weight = Whole(at, cross_own, cross_got, cross_full, local.at[pl.ds(0, 2)], 1)
        later = [
            Whole(at, expand_own, expand_got, expand_full, local.at[pl.ds(2, 2)], 0),
            Whole(at, contract_own, contract_got, contract_full, local.at[pl.ds(4, 2)], 1),
            pltpu.make_async_copy(all_down, down, local.at[6]),
        ]
        later[2].start()
        weight.wait()
        scatter = Scatter(at, send, recv, refs)
        scatter.products(lambda rows: dot(values[rows], cross_full[...]))
        scatter.middle()
        for copy in later:
            copy.wait()
        scatter.arrive()

        def norm(rows, carry):
            total = middle[rows] + scatter.total(rows)
            after[rows] = total
            centred, _ = standard(total)
            normed[rows] = (centred * vectors[4:5] + vectors[5:6]).astype(bf16)

        by_rows(BLOCK, 32, norm)
        gather = Gather(at, normed, whole, send.at[pl.ds(8, 9)], recv.at[pl.ds(8, 9)], local.at[7])
        gather.begin()

        def work(s, rows):
            pltpu.make_async_copy(whole.at[rows], all_rows.at[rows], local.at[8 + s]).start()
            hidden = dot(whole[rows], expand_full[...])
            back = dot_flip(down[rows], contract_full[...])
            bell = 0.5 * (1.0 + lax.erf(hidden * ROOT_HALF))
            activated[rows] = (hidden * bell).astype(bf16)
            grad[rows] = (back * (bell + hidden * jnp.exp(-0.5 * hidden * hidden) * GAUSS_NORM)).astype(bf16)

        gather.each(work)
        for s in range(8):
            pltpu.make_async_copy(whole.at[0:BLOCK], all_rows.at[0:BLOCK], local.at[8 + s]).wait()
        scatter.end()

    return call(
        body,
        number,
        [crossed, *cross_w, middle, vectors, *expand_w, *contract_w, all_down],
        [shape(BLOCK, D, dtype=f32), shape(D, D), shape(D, HALF), shape(D, HALF)],
        [
            *Scatter.scratch,
            VMEM((BLOCK, D), bf16),
            VMEM((D, D), bf16),
            VMEM((D, D), bf16),
            VMEM((COLS, D), bf16),
            VMEM((D, HALF), bf16),
            VMEM((HALF, D), bf16),
            *sems(17),
        ],
        beside,
        ring_peers,
        spaces=[VMEM, ANY, ANY, VMEM, VMEM, ANY, ANY, ANY, ANY, ANY],
        out_spaces=[VMEM, ANY, VMEM, VMEM],
    )


def feed_forward_back(number, grad, expand_w, after, vectors, down, cross_w, queries, text_pair, beside):
    def body(at, ins, outs, kept):
        grad, expand_own, expand_got, after, vectors, down, cross_own, cross_got, queries, pair = ins
        grad_rows, all_rows, grad_queries, grad_pair, grad_vectors = outs
        *refs, rounded, whole, expand_full, cross_full, pair_sum, send, recv, local = kept
        weight = Whole(at, expand_own, expand_got, expand_full, local.at[pl.ds(0, 2)], 0)
        later = Whole(at, cross_own, cross_got, cross_full, local.at[pl.ds(2, 2)], 1)
        weight.wait()
        scatter = Scatter(at, send, recv, refs)
        scatter.products(lambda rows: dot_flip(grad[rows], expand_full[...]))
        scatter.middle()
        later.wait()
        scatter.arrive()

        def norm(rows, carry):
            incoming = scatter.total(rows)
            centred, factor = standard(after[rows])
            total = down[rows].astype(f32) + norm_back(incoming, centred, factor, vectors[4:5])
            grad_rows[rows] = total
            rounded[rows] = total.astype(bf16)
            return two_sums(incoming, centred, carry)

        gains, shifts = by_rows(BLOCK, 32, norm, no_sums())
        grad_vectors[0:1] = gains
        grad_vectors[1:2] = shifts
        gather = Gather(at, rounded, whole, send.at[pl.ds(8, 9)], recv.at[pl.ds(8, 9)], local.at[4])
        gather.begin()
        pair_sum[...] = jnp.zeros_like(pair_sum)

        def work(s, rows):
            pltpu.make_async_copy(whole.at[rows], all_rows.at[rows], local.at[5 + s]).start()
            back = dot_flip(whole[rows], cross_full[...]).astype(bf16)
            parts = []
            for h in range(HEADS):
                a = h * HDIM
                q = head(queries, rows, a) * EIGHTH
                k, v = pair[:, a : a + HDIM], pair[:, COLS + a : COLS + a + HDIM]
                g = back[:, a : a + HDIM]
                p = cross_weights(q, k)
                dp = dot_flip(v, g)
                ds = (p * (dp - jnp.sum(p * dp, axis=0, keepdims=True))).astype(bf16)
                parts.append((dot(k.T, ds) * 0.125).T)
                pair_sum[h] += dot(ds, q)
                pair_sum[HEADS + h] += dot(p.astype(bf16), g)
            grad_queries[rows] = jnp.concatenate(parts, axis=1).astype(bf16)

        gather.each(work)
        grad_pair[...] = jnp.concatenate([pair_sum[i] for i in range(2 * HEADS)], axis=1).astype(bf16)
        for s in range(8):
            pltpu.make_async_copy(whole.at[0:BLOCK], all_rows.at[0:BLOCK], local.at[5 + s]).wait()
        scatter.end()

    return call(
        body,
        number,
        [grad, *expand_w, after, vectors, down, *cross_w, queries, text_pair],
        [shape(BLOCK, D, dtype=f32), shape(D, D), shape(D, COLS), shape(64, 2 * COLS), shape(8, D, dtype=f32)],
        [
            *Scatter.scratch,
            VMEM((BLOCK, D), bf16),
            VMEM((D, D), bf16),
            VMEM((D, HALF), bf16),
            VMEM((COLS, D), bf16),
            VMEM((2 * HEADS, 64, HDIM), f32),
            *sems(17),
        ],
        beside,
        ring_peers,
        spaces=[VMEM, ANY, ANY, VMEM, VMEM, VMEM, ANY, ANY, VMEM, VMEM],
        out_spaces=[VMEM, ANY, VMEM, VMEM, VMEM],
    )


def cross_to_self_back(number, grad, query_w, middle, vectors, grad_rows, out_w, beside):
    def body(at, ins, outs, kept):
        grad, query_own, query_got, middle, vectors, before, out_own, out_got = ins
        grad_rows, all_rows, grad_values, grad_vectors = outs
        *refs, rounded, whole, query_full, out_full, send, recv, local = kept
        weight = Whole(at, query_own, query_got, query_full, local.at[pl.ds(0, 2)], 0)
        later = Whole(at, out_own, out_got, out_full, local.at[pl.ds(2, 2)], 1)
        weight.wait()
        scatter = Scatter(at, send, recv, refs)
        scatter.products(lambda rows: dot_flip(grad[rows], query_full[...]))
        scatter.middle()
        later.wait()
        scatter.arrive()

        def norm(rows, carry):
            incoming = scatter.total(rows)
            centred, factor = standard(middle[rows])
            total = before[rows] + norm_back(incoming, centred, factor, vectors[2:3])
            grad_rows[rows] = total
            rounded[rows] = total.astype(bf16)
            return two_sums(incoming, centred, carry)

        gains, shifts = by_rows(BLOCK, 32, norm, no_sums())
        grad_vectors[0:1] = gains
        grad_vectors[1:2] = shifts
        gather = Gather(at, rounded, whole, send.at[pl.ds(8, 9)], recv.at[pl.ds(8, 9)], local.at[4])
        gather.begin()

        def work(s, rows):
            pltpu.make_async_copy(whole.at[rows], all_rows.at[rows], local.at[5 + s]).start()
            grad_values[rows] = dot_flip(whole[rows], out_full[...]).astype(bf16)

        gather.each(work)
        for s in range(8):
            pltpu.make_async_copy(whole.at[0:BLOCK], all_rows.at[0:BLOCK], local.at[5 + s]).wait()
        scatter.end()

    return call(
        body,
        number,
        [grad, *query_w, middle, vectors, grad_rows, *out_w],
        [shape(BLOCK, D, dtype=f32), shape(D, D), shape(D, COLS), shape(8, D, dtype=f32)],
        [*Scatter.scratch, VMEM((BLOCK, D), bf16), VMEM((D, D), bf16), VMEM((D, COLS), bf16), VMEM((COLS, D), bf16), *sems(17)],
        beside,
        ring_peers,
        spaces=[VMEM, ANY, ANY, VMEM, VMEM, VMEM, ANY, ANY],
        out_spaces=[VMEM, ANY, VMEM, VMEM],
    )


def leave(number, grad, joined, x, vectors, grad_rows, beside):
    relay = Relay(jax.ShapeDtypeStruct((BLOCK, D), bf16), True)

    def body(at, ins, outs, kept):
        grad, weight, x, vectors, before = ins
        result, grad_vectors = outs
        *refs, rounded, send, recv, local = kept
        scatter = Scatter(at, send, recv, refs)
        scatter.products(lambda rows: dot_flip(grad[rows], weight[...]))
        scatter.middle()
        scatter.arrive()

        def norm(rows, carry):
            incoming = scatter.total(rows)
            centred, factor = standard(x[rows].astype(f32))
            total = before[rows] + norm_back(incoming, centred, factor, vectors[0:1])
            rounded[rows] = total.astype(bf16)
            return two_sums(incoming, centred, carry)

        gains, shifts = by_rows(BLOCK, 32, norm, no_sums())
        moving = functools.partial(relay_run, relay, at, rounded, result, send, recv, local.at[0], 8)
        moving(False)
        grad_vectors[0:1] = gains
        grad_vectors[1:2] = shifts
        moving(True)
        scatter.end()

    return call(
        body,
        number,
        [grad, joined, x, vectors, grad_rows],
        [shape(384, HALF), shape(8, D, dtype=f32)],
        [*Scatter.scratch, VMEM((BLOCK, D), bf16), *sems(10)],
        beside,
        lambda at: ring_peers(at) + relay.peers(at),
        out_spaces=[ANY, VMEM],
    )


def causal_forward(number, joined, down, beside):
    at_once = 512

    def body(at, ins, outs, kept):
        (qkv, block), (out, logs, all_rows), (send, recv, local) = ins, outs, kept
        gather = Gather(at, block, all_rows, send, recv, local.at[0])
        gather.begin()
        lane = lax.broadcasted_iota(jnp.int32, (at_once, 128), 1)
        square = (at_once, at_once)
        seen = lax.broadcasted_iota(jnp.int32, square, 0) >= lax.broadcasted_iota(jnp.int32, square, 1)
        for i in reversed(range(D // at_once)):
            before, upto = i * at_once, (i + 1) * at_once
            rows = slice(before, upto)
            log_total, blended = jnp.zeros((at_once, 128), f32), []
            for h in range(HEADS):
                a = h * HDIM
                q = head(qkv, rows, a) * EIGHTH
                k = head(qkv, slice(0, upto), COLS + a)
                v = head(qkv, slice(0, upto), 2 * COLS + a)
                scores = dot_flip(q, k)
                last = jnp.where(seen, scores[:, before:], NEGATIVE)
                scores = jnp.concatenate((scores[:, :before], last), axis=1) if i else last
                peak = jnp.max(scores, axis=1, keepdims=True)
                raised = jnp.exp(scores - peak)
                total = jnp.sum(raised, axis=1, keepdims=True)
                blended.append(dot(raised.astype(bf16), v) / total)
                log_total = jnp.where(lane == h, peak + jnp.log(total), log_total)
            out[rows, :] = jnp.concatenate(blended, axis=1).astype(bf16)
            logs[:, rows] = log_total.T[0:8, :]
            if i == 1:
                gather.pass_on()
        gather.pass_far()
        gather.got(2, 5, 6, 7, 8)
        gather.end()

    return call(
        body,
        number,
        [joined, down],
        [shape(D, COLS), shape(8, D, dtype=f32), shape(D, D)],
        sems(9),
        beside,
        ring_peers,
        out_spaces=[VMEM, VMEM, ANY],
    )


def causal_backward(number, joined, grad, logs, activated, contract_w, after, beside):
    at_once = 512

    def body(at, ins, outs, kept):
        (qkv, go, log_rows, activated, contract_own, contract_got, after), (out, result) = ins, outs
        *refs, contract_full, key_sum, value_sum, send, recv, local = kept
        weight = Whole(at, contract_own, contract_got, contract_full, local, 1)
        weight.wait()
        scatter = Scatter(at, send, recv, refs)
        scatter.products(lambda rows: dot(activated[rows], contract_full[...]))
        square = (at_once, at_once)
        seen = lax.broadcasted_iota(jnp.int32, square, 1) >= lax.broadcasted_iota(jnp.int32, square, 0)
        blocks = D // at_once
        for h in range(HEADS):
            a = h * HDIM
            turned = head(qkv, slice(0, D), COLS + a).T
            query_parts = []
            for i in reversed(range(blocks)):
                before, upto = i * at_once, (i + 1) * at_once
                rows = slice(before, upto)
                q = head(qkv, rows, a) * EIGHTH
                g = head(go, rows, a)
                k = head(qkv, slice(0, upto), COLS + a)
                v = head(qkv, slice(0, upto), 2 * COLS + a)
                p = jnp.exp(dot_flip(k, q) - log_rows[h : h + 1, rows])
                last = jnp.where(seen, p[before:], 0.0)
                p = jnp.concatenate((p[:before], last), axis=0) if i else last
                dp = dot_flip(v, g)
                ds = (p * (dp - jnp.sum(p * dp, axis=0, keepdims=True))).astype(bf16)
                value_part, key_part = dot(p.astype(bf16), g), dot(ds, q)
                if i == blocks - 1:
                    key_sum[h, 0:upto, :] = key_part
                    value_sum[h, 0:upto, :] = value_part
                else:
                    key_sum[h, 0:upto, :] += key_part
                    value_sum[h, 0:upto, :] += value_part
                query_parts.append((dot(turned[:, 0:upto], ds) * 0.125).T)
            out[:, a : a + HDIM] = jnp.concatenate(query_parts[::-1], axis=0).astype(bf16)
            if h == 0:
                scatter.middle()
        for h in range(HEADS):
            a = h * HDIM
            out[:, COLS + a : COLS + a + HDIM] = key_sum[h].astype(bf16)
            out[:, 2 * COLS + a : 2 * COLS + a + HDIM] = value_sum[h].astype(bf16)
        scatter.arrive()

        def finish(rows, carry):
            result[rows] = (after[rows] + scatter.total(rows)).astype(bf16)

        by_rows(BLOCK, 32, finish)
        scatter.end()

    return call(
        body,
        number,
        [joined, grad, logs, activated, *contract_w, after],
        [shape(D, 3 * COLS), shape(BLOCK, D)],
        [*Scatter.scratch, VMEM((HALF, D), bf16), VMEM((HEADS, D, HDIM), f32), VMEM((HEADS, D, HDIM), f32), *sems(8)],
        beside,
        ring_peers,
        spaces=[VMEM, VMEM, VMEM, VMEM, ANY, ANY, VMEM],
    )


def on_device(
    layer_input,
    text_states,
    cotangent,
    first_gain,
    first_shift,
    query_weight,
    key_weight,
    value_weight,
    output_weight,
    second_gain,
    second_shift,
    cross_query,
    cross_key,
    cross_value,
    cross_output,
    third_gain,
    third_shift,
    expand_weight,
    contract_weight,
):
    vectors = (first_gain, first_shift, second_gain, second_shift, third_gain, third_shift)
    vectors = jnp.concatenate([jnp.stack(vectors).astype(f32), jnp.zeros((2, HALF), f32)], axis=0)
    joined = jnp.concatenate((query_weight, key_weight, value_weight), axis=1)
    pair = jnp.concatenate((cross_key, cross_value), axis=1)
    n = lax.axis_index("narrow")

    (x, vectors, joined, all_one, qkv), ((down,), (text_got,)) = enter(
        1, layer_input, vectors, joined, [Relay(cotangent), GiveClip(text_states)]
    )
    text_parts = jnp.einsum("csd,dk->csk", text_states, pair, preferred_element_type=f32)
    (attended, logs, all_down), ((text_pair_got,), (out_got,), (query_got,), (cross_got,)) = causal_forward(
        2, qkv, down, [GiveClip(text_parts), Give(output_weight), Give(cross_query), Give(cross_output)]
    )
    out_w, query_w, cross_w = (output_weight, out_got), (cross_query, query_got), (cross_output, cross_got)
    text_pair = (lax.dynamic_index_in_dim(text_parts, n, 0, False) + text_pair_got).astype(bf16)
    (middle, all_two, cross_q, crossed), ((expand_got,), (contract_got,)) = self_to_cross(
        3, attended, out_w, x, vectors, query_w, text_pair, [Give(expand_weight), Give(contract_weight)]
    )
    expand_w, contract_w = (expand_weight, expand_got), (contract_weight, contract_got)
    (after, all_three, activated, grad_expand), _ = feed_forward(
        4, crossed, cross_w, middle, vectors, expand_w, contract_w, all_down, []
    )

    contract_leg = SumZ(outer(activated, all_down).astype(bf16), False)
    expand_leg = SumZ(outer(all_three, grad_expand).astype(bf16), True)
    (grad_two, all_mid_two, grad_cross_q, grad_pair, third), (contract_sum, expand_sum) = feed_forward_back(
        5, grad_expand, expand_w, after, vectors, down, cross_w, cross_q, text_pair, [contract_leg, expand_leg]
    )
    own_text = lax.dynamic_index_in_dim(text_states, n, 0, False)
    first_half, second_half = jnp.where(n == 0, own_text, text_got), jnp.where(n == 0, text_got, own_text)
    text = jnp.concatenate((first_half, second_half), axis=1)
    query_pair_leg = SumZ(
        jnp.concatenate((outer(all_two, grad_cross_q), outer(text, grad_pair)), axis=1).astype(bf16), True
    )
    cross_leg = SumZ(outer(crossed, all_mid_two).astype(bf16), False)
    contract_leg, expand_leg = SumX(contract_leg.finish(contract_sum), False), SumX(expand_leg.finish(expand_sum), True)
    (grad_one, all_mid_one, grad_attended, second), sums = cross_to_self_back(
        6,
        grad_cross_q,
        query_w,
        middle,
        vectors,
        grad_two,
        out_w,
        [contract_leg, expand_leg, query_pair_leg, cross_leg, Give(grad_pair)],
    )
    contract_sum, expand_sum, query_pair_sum, cross_sum, (grad_pair_got,) = sums
    pairs = jnp.where(n == 0, jnp.stack((grad_pair, grad_pair_got)), jnp.stack((grad_pair_got, grad_pair)))
    text_grad = lax.psum(
        jnp.einsum("csk,dk->csd", pairs, pair, preferred_element_type=f32).astype(bf16), "wide"
    ).astype(f32)
    contract_leg, expand_leg = Spread(contract_leg.finish(contract_sum)), Spread(expand_leg.finish(expand_sum))
    query_pair_leg, cross_leg = SumX(query_pair_leg.finish(query_pair_sum), True), SumX(cross_leg.finish(cross_sum), False)
    output_leg = SumZ(outer(attended, all_mid_one).astype(bf16), False)
    (grad_qkv, layer_output), sums = causal_backward(
        7,
        qkv,
        grad_attended,
        logs,
        activated,
        contract_w,
        after,
        [contract_leg, expand_leg, query_pair_leg, cross_leg, output_leg],
    )
    contract_sum, expand_sum, query_pair_sum, cross_sum, output_sum = sums
    contract_grad, expand_grad = contract_leg.finish(contract_sum), expand_leg.finish(expand_sum)
    joined_leg = SumZ(outer(all_one, grad_qkv).astype(bf16), True)
    query_pair_leg, cross_leg = Spread(query_pair_leg.finish(query_pair_sum)), Spread(cross_leg.finish(cross_sum))
    output_leg = SumX(output_leg.finish(output_sum), False)
    (input_grad, first), sums = leave(
        8,
        grad_qkv,
        joined,
        x,
        vectors,
        grad_one,
        [joined_leg, output_leg, query_pair_leg, cross_leg, Relay(layer_output, True)],
    )
    joined_sum, output_sum, query_pair_sum, cross_sum, (layer_output,) = sums
    query_pair_grad, cross_output_grad = query_pair_leg.finish(query_pair_sum), cross_leg.finish(cross_sum)
    parts = jnp.concatenate((first[0:2], second[0:2], third[0:2], jnp.zeros((2, D), f32)), axis=0)
    joined_leg, output_leg = SumX(joined_leg.finish(joined_sum), True), Spread(output_leg.finish(output_sum))
    _, (joined_sum, output_sum, (parts,)) = call(None, 9, [], [], (), [joined_leg, output_leg, ToRing(parts)])
    output_grad = output_leg.finish(output_sum)
    joined_leg = Spread(joined_leg.finish(joined_sum))
    _, (joined_sum, (parts,)) = call(None, 10, [], [], (), [joined_leg, ToClips(jnp.sum(parts, axis=0))])
    joined_grad = joined_leg.finish(joined_sum)
    parts = jnp.sum(parts, axis=(0, 1))
    return (
        layer_output,
        input_grad.astype(f32),
        text_grad,
        parts[0],
        parts[1],
        joined_grad[:, :COLS],
        joined_grad[:, COLS : 2 * COLS],
        joined_grad[:, 2 * COLS :],
        output_grad,
        parts[2],
        parts[3],
        query_pair_grad[:, :COLS],
        query_pair_grad[:, COLS : 2 * COLS],
        query_pair_grad[:, 2 * COLS :],
        cross_output_grad,
        parts[4],
        parts[5],
        expand_grad,
        contract_grad,
    )


def solution(mesh):
    return jax.shard_map(
        on_device,
        mesh=mesh,
        in_specs=(
            P(("dp", "wide"), "narrow"),
            P("dp", None, "narrow"),
            P(("dp", "wide"), "narrow"),
            P("narrow"),
            P("narrow"),
            P("narrow", "wide"),
            P("narrow", "wide"),
            P("narrow", "wide"),
            P("wide", "narrow"),
            P("narrow"),
            P("narrow"),
            P("narrow", "wide"),
            P("narrow", "wide"),
            P("narrow", "wide"),
            P("wide", "narrow"),
            P("narrow"),
            P("narrow"),
            P("narrow", "wide"),
            P("wide", "narrow"),
        ),
        out_specs=(
            P(("dp", "wide"), "narrow"),
            P(("dp", "wide"), "narrow"),
            P("dp", None, "narrow"),
            P("narrow"),
            P("narrow"),
            P("narrow", "wide"),
            P("narrow", "wide"),
            P("narrow", "wide"),
            P("wide", "narrow"),
            P("narrow"),
            P("narrow"),
            P("narrow", "wide"),
            P("narrow", "wide"),
            P("narrow", "wide"),
            P("wide", "narrow"),
            P("narrow"),
            P("narrow"),
            P("narrow", "wide"),
            P("wide", "narrow"),
        ),
        check_vma=False,
    )
```

time: 747 us -> 603 us (0.81)
  Pallas kernels: 589 us -> 476 us
  other arithmetic: 71.2 us -> 42.9 us
    pallas_call x17 -> x10, Pallas kernels: 581 us -> 476 us  [call(): pl.pallas_call(kernel, out_shape=tuple(outs) + tuple(side_outs), in_specs...]
    convert_element_type x9 -> x2, other arithmetic: 18 us -> 3.23 us  [the longest x1 1.7 us: on_device(): text_grad = lax.psum(jnp.einsum('csk,dk->csd', pairs, pair, preferred_ele...]
    reduce_sum x6 -> x0, other arithmetic: 9.56 us -> none  [the longest x3 4.99 us: norm_backward(): jnp.sum(incoming * centred, axis=0)]
    pallas_call x2 -> x0, Pallas kernels: 7.76 us -> none  [the longest x1 4.33 us: cross_backward(): pl.pallas_call(kernel, out_shape=(jax.ShapeDtypeStruct(queries.shape, bf1...]
  transfers between devices with their start and end apart: 1 -> 1, of which waited for: 0 -> 0; matrix products, arithmetic and copies ran while one was open for 9% -> 9% of each run, Pallas kernels for 19% -> 23%
where the time goes in v2:
time: 603 us; the launch traced here: 592 us
  Pallas kernels  476 us (79%)
  other arithmetic  42.9 us (7%)
  matrix products  35.2 us (6%)
  local copies, waits for them, and re-layouts  22.8 us (4%)
  between operations  15.2 us (3%)
    pallas_call x10, Pallas kernels, call(): pl.pallas_call(kernel, out_shape=tuple(outs) + tuple(side_outs), in_specs...  476 us
    dot_general x7, matrix products, outer(): lax.dot_general(a, b, (((0,), (0,)), ((), ())), preferred_element_type=f32)  32.2 us
    convert_element_type x12, other arithmetic, finish(): return (own.astype(f32) + outs[0].astype(f32).sum(axis=0)).astype(bf16)  14.6 us
    unnamed x93, local copies, waits for them, and re-layouts  13.2 us
  transfers between devices with their start and end apart: 1, of which 0 were waited for; matrix products, arithmetic and copies ran while one was open for 9% of the time, Pallas kernels for 23%

profile of v2, /device:TPU:0, one launch (start us, length us, event | category | flops | bytes accessed | tf_op | source)
XLA Modules:
  0.0 592.0 jit_solution(14062544234963509286)
XLA Ops:
  15.3 67.0 %shard_map.330 = (bf16[192,1536]{1,0:T(8,128)(2,1)}, f32[8,1536]{1,0:T(8,128)}, bf16[1536,576]{1,0:T(8,128)(2,1)}, bf16[1536,1536]{1,0:T(8,128)(2,1)}, bf16[1536...) custom-call(bf16[384,768]{1,0:T(8,128)(2,1)} %refs_0_.1, f32[8,768]{1,0:T(8,128)} %pad_convert_fusion.refs_1_, ...), custom_call_target="tpu_custom_call" | custom-call | tf_op jit(solution)/shard_map/pallas_call | solution.py:338
  82.3 29.5 %shard_map.331 = (bf16[1536,192]{1,0:T(8,128)(2,1)}, f32[8,1536]{1,0:T(8,128)}, bf16[1536,1536]{1,0:T(8,128)(2,1)}, f32[64,384]{1,0:T(8,128)}, bf16[192,768]{1,0...) custom-call(bf16[1536,576]{1,0:T(8,128)(2,1)} %get-tuple-element.78.refs_0_, ...), custom_call_target="tpu_custom_call" | custom-call | tf_op jit(solution)/shard_map/pallas_call | solution.py:338
  111.8 1.5 fusion.20.refs_7_.refs_9_
  113.3 57.9 %shard_map.332 = (f32[192,1536]{1,0:T(8,128)}, bf16[1536,1536]{1,0:T(8,128)(2,1)}, bf16[1536,192]{1,0:T(8,128)(2,1)}, bf16[1536,192]{1,0:T(8,128)(2,1)}, bf16[76...) custom-call(bf16[1536,192]{1,0:T(8,128)(2,1)} %get-tuple-element.80.refs_0_, bf16[192,768]{1,0:T(8,128)(2,1)} %refs_6_.3, ...), custom_call_target="tpu_custom_call" | custom-call | tf_op jit(solution)/shard_map/pallas_call | solution.py:338
  171.2 59.8 %shard_map.333 = (f32[192,1536]{1,0:T(8,128)}, bf16[1536,1536]{1,0:T(8,128)(2,1)}, bf16[1536,768]{1,0:T(8,128)(2,1)}, bf16[1536,768]{1,0:T(8,128)(2,1)}) custom-call(bf16[1536,192]{1,0:T(8,128)(2,1)} %get-tuple-element.86.refs_0_, bf16[192,768]{1,0:T(8,128)(2,1)} %refs_6_.2, bf16[192,768]{1,0:T(8,128)(2,1)} %get-tuple-element.87.refs_2_.refs_7_, ...), custom_call_target="tpu_custom_call" | custom-call | tf_op jit(solution)/shard_map/pallas_call | solution.py:338
  231.1 6.8 %convolution_convert_fusion.1 = bf16[768,1536]{1,0:T(8,128)(2,1)} fusion(bf16[1536,768]{1,0:T(8,128)(2,1)} %get-tuple-element.95.refs_3_, bf16[1536,1536]{1,0:T(8,128)(2,1)S(1)} %bitcast.98), kind=kOutput, calls=%fused_computation.3 | convolution fusion | flops 3625058304 | bytes 9437184 | tf_op jit(solution)/shard_map/dot_general | solution.py:36
  237.9 7.0 %convolution_convert_fusion = bf16[1536,768]{1,0:T(8,128)(2,1)S(1)} fusion(bf16[1536,1536]{1,0:T(8,128)(2,1)} %get-tuple-element.96, bf16[1536,768]{1,0:T(8,128)(2,1)} %get-tuple-element.92.refs_0_), kind=kOutput, calls=%fused_computation.2 | convolution fusion | flops 3625058304 | bytes 9437184 | tf_op jit(solution)/shard_map/dot_general | solution.py:36
  245.0 1.5 constant_dynamic-slice_fusion.4
  246.6 64.0 %shard_map.334 = (f32[192,1536]{1,0:T(8,128)}, bf16[1536,1536]{1,0:T(8,128)(2,1)}, bf16[1536,192]{1,0:T(8,128)(2,1)}, bf16[64,384]{1,0:T(8,128)(2,1)}, f32[8,153...) custom-call(bf16[1536,768]{1,0:T(8,128)(2,1)} %get-tuple-element.92.refs_0_, ...), custom_call_target="tpu_custom_call" | custom-call | tf_op jit(solution)/shard_map/pallas_call | solution.py:338
  310.6 4.3 convolution_convert_fusion.5
  315.0 3.5 convolution_convert_fusion.6
  318.7 2.0 convert_reduce_fusion
  322.2 2.1 pad_maximum_fusion.refs_10_
  326.2 58.9 %shard_map.335 = (f32[192,1536]{1,0:T(8,128)}, bf16[1536,1536]{1,0:T(8,128)(2,1)}, bf16[1536,192]{1,0:T(8,128)(2,1)}, f32[8,1536]{1,0:T(8,128)}, bf16[3,96,768]{...) custom-call(bf16[1536,192]{1,0:T(8,128)(2,1)} %get-tuple-element.97., ...), custom_call_target="tpu_custom_call" | custom-call | tf_op jit(solution)/shard_map/pallas_call | solution.py:338
  385.2 2.0 convolution_convert_fusion.7
  387.5 3.6 convolution_convert_fusion.4
  395.3 1.6 fusion.7.refs_8_
  396.9 1.7 fusion.8.refs_7_
  398.6 45.9 %shard_map.336 = (bf16[1536,576]{1,0:T(8,128)(2,1)}, bf16[192,1536]{1,0:T(8,128)(2,1)}, bf16[8,96,768]{2,1,0:T(8,128)(2,1)}, bf16[8,96,768]{2,1,0:T(8,128)(2,1)}...) custom-call(bf16[1536,576]{1,0:T(8,128)(2,1)} %get-tuple-element.78.refs_0_, ...), custom_call_target="tpu_custom_call" | custom-call | tf_op jit(solution)/shard_map/pallas_call | solution.py:338
  445.6 1.5 fusion.23.refs_8_
  448.1 1.6 fusion.11.refs_7_
  450.8 6.5 %convolution_convert_fusion.2 = bf16[1536,576]{0,1:T(8,128)(2,1)} fusion(bf16[1536,1536]{1,0:T(8,128)(2,1)} %get-tuple-element.115, bf16[1536,576]{1,0:T(8,128)(2,1)S(1)} %copy-done.2), kind=kOutput, calls=%fused_computation.4 | convolution fusion | flops 2718793728 | bytes 8257536 | tf_op jit(solution)/shard_map/dot_general | solution.py:36
  457.3 2.7 copy.47
  461.4 60.0 %shard_map.337 = (bf16[384,768]{1,0:T(8,128)(2,1)}, f32[8,1536]{1,0:T(8,128)}, bf16[3,2,192,576]{3,2,1,0:T(8,128)(2,1)}, bf16[3,24,768]{2,1,0:T(8,128)(2,1)}, bf...) custom-call(bf16[1536,576]{1,0:T(8,128)(2,1)} %get-tuple-element.112.refs_0_, ...), custom_call_target="tpu_custom_call" | custom-call | tf_op jit(solution)/shard_map/pallas_call | solution.py:338
  526.2 1.7 convert_reduce_fusion.2
  529.6 14.1 %shard_map.338 = (bf16[3,96,576]{2,1,0:T(8,128)(2,1)}, bf16[8,24,768]{2,1,0:T(8,128)(2,1)}, f32[8,8,1536]{2,1,0:T(8,128)}) custom-call(bf16[2,2,96,576]{3,2,1,0:T(8,128)(2,1)} %fusion.2.refs_0_, bf16[24,768]{1,0:T(8,128)(2,1)} %fusion.22.refs_1_, f32[8,1536]{1,0:T(8,128)} %maximum_maximum_fusion.refs_2_), custom_call_target="tpu_custom_call" | custom-call | tf_op jit(solution)/shard_map/pallas_call | solution.py:338
  544.8 1.6 fusion.10.refs_0_
  546.4 1.6 reduce_sum.156.refs_1_
  548.0 18.7 %shard_map.339 = (bf16[8,96,576]{2,1,0:T(8,128)(2,1)}, f32[8,2,8,768]{3,2,1,0:T(8,128)}) custom-call(bf16[96,576]{1,0:T(8,128)(2,1)} %fusion.10.refs_0_, f32[8,1536]{1,0:T(8,128)} %reduce_sum.156.refs_1_), custom_call_target="tpu_custom_call" | custom-call | tf_op jit(solution)/shard_map/pallas_call | solution.py:338
  578.3 1.7 bitcast_convert_fusion
  579.9 1.7 bitcast_convert_fusion.1
  582.2 1.7 convert_element_type.266
  (145 shorter events, 41.0 us)
Async XLA Ops:
  7.2 3.6 copy-start.32
  7.2 3.6 copy-start.33
  7.2 3.7 copy-start.34
  7.2 3.7 copy-start.35
  7.2 3.7 copy-start.36
  7.2 3.7 copy-start.37
  7.3 4.4 copy-start.26
  7.3 4.5 copy-start.27
  7.3 4.7 copy-start.28
  7.3 575.0 %all-reduce.3.cloned.1.call-start = ((), (), s32[]{:S(2)}) async-start(), calls=%async_computation | async-start | bytes 393216 | tf_op jit(solution)/shard_map/psum | solution.py:1143
  11.6 2.6 copy-start.16
  11.8 3.4 copy-start.20
  12.0 3.3 copy-start.22
  82.3 29.5 %copy-start.14 = (f32[384,2,64]{0,2,1:T(8,128)S(1)}, f32[384,2,64]{0,2,1:T(8,128)}, u32[]{:S(2)}) copy-start(f32[384,2,64]{0,2,1:T(8,128)} %fusion.9) | copy-start | bytes 589828
  113.3 117.8 %slice-start = ((s8[4718592]{0:T(1024)(128)(4,1)}), s8[4194304]{0:T(1024)(128)(4,1)S(1)}, s32[]{:S(2)}) async-start(s8[4718592]{0:T(1024)(128)(4,1)} %bitcast.97), calls=%async_computation.1 | async-start | bytes 8388608
  171.2 59.9 %slice-start.1 = ((s8[4718592]{0:T(1024)(128)(4,1)}), s8[524288]{0:T(1024)(128)(4,1)S(1)}, s32[]{:S(2)}) async-start(s8[4718592]{0:T(1024)(128)(4,1)} %bitcast.97), calls=%async_computation.2 | async-start | bytes 1048576
  246.6 64.1 %copy-start.11 = (bf16[1536,192]{1,0:T(8,128)(2,1)S(1)}, bf16[1536,192]{1,0:T(8,128)(2,1)}, u32[]{:S(2)}) copy-start(bf16[1536,192]{1,0:T(8,128)(2,1)} %get-tuple-element.86.refs_0_) | copy-start | bytes 1769476
  310.6 4.4 copy-start.10
  326.2 58.9 %copy-start.21 = (bf16[768,192]{1,0:T(8,128)(2,1)S(1)}, bf16[768,192]{1,0:T(8,128)(2,1)}, u32[]{:S(2)}) copy-start(bf16[768,192]{1,0:T(8,128)(2,1)} %copy-done.20) | copy-start | bytes 884740
  326.2 59.0 %copy-start.23 = (bf16[768,192]{1,0:T(8,128)(2,1)S(1)}, bf16[768,192]{1,0:T(8,128)(2,1)}, u32[]{:S(2)}) copy-start(bf16[768,192]{1,0:T(8,128)(2,1)} %copy-done.22) | copy-start | bytes 884740
  326.2 59.0 %copy-start.30 = (bf16[64,384]{1,0:T(8,128)(2,1)S(1)}, bf16[64,384]{1,0:T(8,128)(2,1)}, u32[]{:S(2)}) copy-start(bf16[64,384]{1,0:T(8,128)(2,1)} %get-tuple-element.103.refs_12_) | copy-start | bytes 147460
  385.2 2.3 copy-start.9
  387.5 4.7 copy-start.18
  387.5 4.8 copy-start.4
  444.5 6.3 %copy-start.2 = (bf16[1536,576]{1,0:T(8,128)(2,1)S(1)}, bf16[1536,576]{1,0:T(8,128)(2,1)}, u32[]{:S(2)}) copy-start(bf16[1536,576]{1,0:T(8,128)(2,1)} %get-tuple-element.112.refs_0_) | copy-start | bytes 5308420
  568.4 3.2 copy-start.19
  568.4 3.2 copy-start.25
  569.5 3.1 copy-start.7
  573.1 3.2 copy-start.12
  574.2 3.2 copy-start.24
  575.2 3.0 copy-start.6
  579.9 4.0 copy-start.13
  (9 other events, 13.5 us)
Sparse Core Ops, SparseCore 0:
  387.3 60.2 all-reduce.2

commit v3 on v2

v3 whole, which is shorter than its diff:
```python
import functools
import math

import jax
import jax.numpy as jnp
from jax import lax
from jax.experimental import pallas as pl
from jax.experimental.pallas import tpu as pltpu
from jax.sharding import PartitionSpec as P

D = 1536
HALF = 768
HDIM = 64
HEADS = 3
COLS = HEADS * HDIM
BLOCK = 192
EPSILON = 1e-05
NEGATIVE = -1e30
ROOT_HALF = 0.7071067811865476
GAUSS_NORM = 0.3989422804014327
MESH = pl.DeviceIdType.MESH
VMEM = pltpu.VMEM
ANY = pl.ANY
bf16, f32 = jnp.bfloat16, jnp.float32


def dot(a, b):
    return lax.dot_general(a, b, (((1,), (0,)), ((), ())), preferred_element_type=f32)


def dot_flip(a, b):
    return lax.dot_general(a, b, (((1,), (1,)), ((), ())), preferred_element_type=f32)


def outer(a, b):
    return lax.dot_general(a, b, (((0,), (0,)), ((), ())), preferred_element_type=f32)


class Place:
    def __init__(self):
        self.dp, self.w, self.n = (lax.axis_index(a) for a in ("dp", "wide", "narrow"))
        self.y, self.c = lax.div(self.w, 2), lax.rem(self.w, 2)
        self.z, self.s = lax.div(self.dp, 2), lax.rem(self.dp, 2)
        self.up, self.down = lax.rem(self.y + 1, 4), lax.rem(self.y + 3, 4)
        self.across = 3 - self.y
        self.moved = lax.rem(lax.div(self.y, 2) + self.n, 2)
        self.clip = lax.div(self.y, 2)

    def spot(self, y, c):
        moved = lax.rem(lax.div(y, 2) + self.n, 2)
        return (lax.rem(y + moved, 2) * 2 + c) * 2 + moved

    def rows(self, y, c, start=0, size=BLOCK):
        return pl.ds(pl.multiple_of(self.spot(y, c) * BLOCK + start, 32), size)

    def half(self, n):
        return pl.ds(pl.multiple_of(n * HALF, HALF), HALF)

    def at_y(self, y):
        return {"wide": y * 2 + self.c}

    def core(self):
        return {"wide": self.y * 2 + 1 - self.c}

    def x(self):
        return {"narrow": 1 - self.n}

    def at_z(self, k):
        return {"dp": lax.rem(self.z + k, 4) * 2 + self.s}

    def at_dp(self, k):
        return {"dp": lax.rem(self.dp + k, 8)}

    def at_x(self, ds, dn):
        return {"dp": self.z * 2 + lax.rem(self.s + ds, 2), "narrow": lax.rem(self.n + dn, 2)}


def remote(src, dst, send, recv, peer):
    return pltpu.make_async_remote_copy(
        src_ref=src, dst_ref=dst, send_sem=send, recv_sem=recv, device_id=peer, device_id_type=MESH
    )


def greet(peers):
    barrier = pltpu.get_barrier_semaphore()
    for peer in peers:
        pl.semaphore_signal(barrier, inc=1, device_id=peer, device_id_type=MESH)
    pl.semaphore_wait(barrier, len(peers))


class Give:
    def __init__(self, array):
        self.ins, self.copies, self.locals = [array], 1, 0
        self.outs = [jax.ShapeDtypeStruct(array.shape, array.dtype)]

    def peers(self, at):
        return [("x", at.x())]

    def moves(self, at, ins, outs):
        return [(ins[0], outs[0], at.x())], []


class GiveClip(Give):
    def __init__(self, array):
        super().__init__(array)
        self.outs = [jax.ShapeDtypeStruct(array.shape[1:], array.dtype)]

    def moves(self, at, ins, outs):
        return [(ins[0].at[1 - at.n], outs[0], at.x())], []


class SumZ:
    def __init__(self, array, by_rows):
        self.by_rows, self.copies, self.locals = by_rows, 3, 0
        rows, cols = array.shape
        shape = (2, 4, rows // 8, cols) if by_rows else (4, rows // 4, cols)
        self.ins = [array.reshape(shape)]
        kept = (2, rows // 8, cols) if by_rows else (rows // 4, cols)
        self.outs = [jax.ShapeDtypeStruct((3, *kept), array.dtype)]

    def peers(self, at):
        return [(f"z{k}", at.at_z(k)) for k in (1, 2, 3)]

    def moves(self, at, ins, outs):
        out = []
        for k in (1, 2, 3):
            q = lax.rem(at.z + k, 4)
            src = ins[0].at[:, q] if self.by_rows else ins[0].at[q]
            out.append((src, outs[0].at[k - 1], at.at_z(k)))
        return out, []

    def finish(self, outs):
        z = lax.div(lax.axis_index("dp"), 2)
        own = lax.dynamic_index_in_dim(self.ins[0], z, 1 if self.by_rows else 0, False)
        return (own.astype(f32) + outs[0].astype(f32).sum(axis=0)).astype(bf16)


class SumX:
    def __init__(self, array, by_rows):
        self.by_rows, self.copies, self.locals = by_rows, 3, 0
        if by_rows:
            two, rows, cols = array.shape
            self.ins, kept = [array.reshape(2, 2, rows // 2, cols)], (rows // 2, cols)
        else:
            rows, cols = array.shape
            self.ins, kept = [array.reshape(2, rows // 2, cols)], (rows // 2, HALF)
        self.outs = [jax.ShapeDtypeStruct((3, *kept), array.dtype)]

    order = ((0, 1), (1, 0), (1, 1))

    def peers(self, at):
        return [(f"x{a}{b}", at.at_x(a, b)) for a, b in self.order]

    def moves(self, at, ins, outs):
        out = []
        for i, (a, b) in enumerate(self.order):
            s, n = lax.rem(at.s + a, 2), lax.rem(at.n + b, 2)
            src = ins[0].at[n, s] if self.by_rows else ins[0].at[s, :, at.half(n)]
            out.append((src, outs[0].at[i], at.at_x(a, b)))
        return out, []

    def finish(self, outs):
        s, n = lax.rem(lax.axis_index("dp"), 2), lax.axis_index("narrow")
        if self.by_rows:
            own = lax.dynamic_index_in_dim(lax.dynamic_index_in_dim(self.ins[0], n, 0, False), s, 0, False)
        else:
            own = lax.dynamic_slice_in_dim(lax.dynamic_index_in_dim(self.ins[0], s, 0, False), n * HALF, HALF, 1)
        return (own.astype(f32) + outs[0].astype(f32).sum(axis=0)).astype(bf16)


class Spread:
    def __init__(self, array):
        self.ins, self.copies, self.locals = [array], 7, 1
        self.outs = [jax.ShapeDtypeStruct((8, *array.shape), array.dtype)]

    def peers(self, at):
        return [(f"d{k}", at.at_dp(k)) for k in range(1, 8)]

    def moves(self, at, ins, outs):
        dst = outs[0].at[at.dp]
        return [(ins[0], dst, at.at_dp(k)) for k in range(1, 8)], [(ins[0], dst)]

    def finish(self, outs):
        eight, rows, cols = outs[0].shape
        return outs[0].reshape(eight * rows, cols).astype(f32)


class ToRing:
    def __init__(self, array):
        self.ins, self.copies, self.locals = [array], 7, 1
        self.outs = [jax.ShapeDtypeStruct((8, *array.shape), array.dtype)]

    def peers(self, at):
        return [(f"w{k}", {"wide": lax.rem(at.w + k, 8)}) for k in range(1, 8)]

    def moves(self, at, ins, outs):
        dst = outs[0].at[at.w]
        return [(ins[0], dst, peer) for _, peer in self.peers(at)], [(ins[0], dst)]


class Trade:
    def __init__(self, array):
        self.ins, self.copies, self.locals = [array], 7, 1
        self.outs = [jax.ShapeDtypeStruct(array.shape, array.dtype)]

    def others(self, at):
        return [lax.rem(at.w + k, 8) for k in range(1, 8)]

    def peers(self, at):
        return [(f"w{k + 1}", {"wide": w}) for k, w in enumerate(self.others(at))]

    def moves(self, at, ins, outs):
        mine = at.spot(at.y, at.c)
        dst = outs[0].at[mine]
        far = [(ins[0].at[at.spot(lax.div(w, 2), lax.rem(w, 2))], dst, {"wide": w}) for w in self.others(at)]
        return far, [(ins[0].at[mine], dst)]


class ToSpots(ToRing):
    def moves(self, at, ins, outs):
        dst = outs[0].at[at.spot(at.y, at.c)]
        return [(ins[0], dst, peer) for _, peer in self.peers(at)], [(ins[0], dst)]


class ToClips:
    def __init__(self, array):
        self.ins, self.copies, self.locals = [array], 15, 1
        self.outs = [jax.ShapeDtypeStruct((8, 2, array.shape[0], HALF), array.dtype)]

    order = tuple((k, b) for k in range(8) for b in range(2))[1:]

    def peers(self, at):
        return [(f"c{k}{b}", {**at.at_dp(k), "narrow": lax.rem(at.n + b, 2)}) for k, b in self.order]

    def moves(self, at, ins, outs):
        dst = outs[0].at[at.dp, at.n]
        far = []
        for (k, b), (_, peer) in zip(self.order, self.peers(at)):
            far.append((ins[0].at[:, at.half(lax.rem(at.n + b, 2))], dst, peer))
        return far, [(ins[0].at[:, at.half(at.n)], dst)]


class Relay:
    def __init__(self, array, back=False):
        self.ins, self.back, self.copies, self.locals = [array], back, 2, 1
        shape = (384, HALF) if back else (BLOCK, D)
        self.outs = [jax.ShapeDtypeStruct(shape, array.dtype)]

    def peers(self, at):
        return [
            ("x", at.x()),
            ("a0", {"wide": at.across * 2 + at.c}),
            ("a1", {"wide": at.across * 2 + at.c, "narrow": 1 - at.n}),
        ]


def relay_run(relay, at, src, dst, send, recv, local, base, finish):
    mine, other = at.half(at.n), at.half(1 - at.n)
    over = at.across * 2 + at.c
    if relay.back:
        row = pl.ds(pl.multiple_of(at.moved * BLOCK, BLOCK), BLOCK)
        to = recv.at[base + at.moved]
        own = src.at[:, mine], src.at[:, other]
        land = dst.at[0:BLOCK], dst.at[BLOCK : 2 * BLOCK]
    else:
        row = mine
        to = recv.at[base + at.n]
        own = src.at[0:BLOCK], src.at[BLOCK : 2 * BLOCK]
        land = dst.at[:, at.half(0)], dst.at[:, at.half(1)]
    target = dst.at[row] if relay.back else dst.at[:, row]

    def arrive(slot, part):
        return remote(own[0], part, send.at[base], recv.at[base + slot], at.x())

    @pl.when(at.moved == 0)
    def _():
        stay = pltpu.make_async_copy(own[0], target, local)
        if relay.back:
            go = remote(own[1], target, send.at[base], to, at.x())
        else:
            go = remote(own[1], target, send.at[base], to, {"wide": over})
        if not finish:
            go.start()
            stay.start()
        else:
            stay.wait()
            go.wait_send()
            if relay.back:
                arrive(1, land[1]).wait_recv()
            else:
                arrive(1 - at.n, dst.at[:, other]).wait_recv()

    @pl.when(at.moved == 1)
    def _():
        if relay.back:
            first = remote(own[1], target, send.at[base], to, {"wide": over, "narrow": 1 - at.n})
            second = remote(own[0], target, send.at[base + 1], to, {"wide": over})
        else:
            first = remote(own[1], target, send.at[base], to, {"wide": over, "narrow": 1 - at.n})
            second = remote(own[0], target, send.at[base + 1], to, at.x())
        if not finish:
            first.start()
            second.start()
        else:
            first.wait_send()
            second.wait_send()
            arrive(0, land[0]).wait_recv()
            arrive(1, land[1]).wait_recv()


def call(body, number, ins, outs, scratch=(), beside=(), peers=None, spaces=None, out_spaces=None, late=False):
    spaces = spaces or [VMEM] * len(ins)
    out_spaces = out_spaces or [VMEM] * len(outs)
    copies = sum(b.copies for b in beside)
    locals_ = sum(b.locals for b in beside)
    side_ins = [a for b in beside for a in b.ins]
    side_outs = [a for b in beside for a in b.outs]
    n_in, n_out, n_scratch = len(ins), len(outs), len(scratch)

    def kernel(*refs):
        at = Place()
        refs = list(refs)

        def take(count):
            out = refs[:count]
            del refs[:count]
            return out

        main_in, side_in = take(n_in), take(len(side_ins))
        main_out, side_out, kept = take(n_out), take(len(side_outs)), take(n_scratch)
        send, recv, local = take(3)
        known = dict(peers(at)) if peers else {}
        for b in beside:
            known.update(dict(b.peers(at)))
        if known:
            greet(list(known.values()))
        side_refs = [([side_in.pop(0) for _ in b.ins], [side_out.pop(0) for _ in b.outs]) for b in beside]
        todo = []

        def start():
            slot, place = 0, 0
            for b, (i, o) in zip(beside, side_refs):
                if isinstance(b, Relay):
                    run = functools.partial(relay_run, b, at, i[0], o[0], send, recv, local.at[place], slot)
                    run(False)
                    todo.append(functools.partial(run, True))
                    slot, place = slot + 2, place + 1
                    continue
                far, near = b.moves(at, i, o)
                for src, dst, peer in far:
                    copy = remote(src, dst, send.at[slot], recv.at[slot], peer)
                    copy.start()
                    todo.append(copy.wait)
                    slot += 1
                for src, dst in near:
                    copy = pltpu.make_async_copy(src, dst, local.at[place])
                    copy.start()
                    todo.append(copy.wait)
                    place += 1

        at.start_beside = start
        if not late:
            start()
        if body:
            body(at, main_in, main_out, kept)
        for wait in todo:
            wait()

    results = pl.pallas_call(
        kernel,
        out_shape=tuple(outs) + tuple(side_outs),
        in_specs=[pl.BlockSpec(memory_space=s) for s in spaces] + [pl.BlockSpec(memory_space=ANY)] * len(side_ins),
        out_specs=tuple(pl.BlockSpec(memory_space=m) for m in out_spaces + [ANY] * len(side_outs)),
        scratch_shapes=[
            *scratch,
            pltpu.SemaphoreType.DMA((max(copies, 1),)),
            pltpu.SemaphoreType.DMA((max(copies, 1),)),
            pltpu.SemaphoreType.DMA((max(locals_, 1),)),
        ],
        compiler_params=pltpu.CompilerParams(
            collective_id=number, has_side_effects=True, vmem_limit_bytes=58 << 20
        ),
    )(*ins, *side_ins)
    results = list(results)
    main, rest = results[: len(outs)], results[len(outs) :]
    sides = []
    for b in beside:
        sides.append(rest[: len(b.outs)])
        del rest[: len(b.outs)]
    return main, sides


def ring_peers(at):
    return [("up", at.at_y(at.up)), ("down", at.at_y(at.down)), ("core", at.core())]


def sems(count):
    return [pltpu.SemaphoreType.DMA((count,)), pltpu.SemaphoreType.DMA((count,)), pltpu.SemaphoreType.DMA((count,))]


def by_rows(count, size, work, carry=None):
    def step(i, carry):
        return work(pl.ds(pl.multiple_of(i * size, size), size), carry)

    return lax.fori_loop(0, count // size, step, carry)


class Whole:
    def __init__(self, at, own, got, full, sem, axis):
        size = own.shape[axis]
        self.copies = []
        for i, (part, n) in enumerate(((own, at.n), (got, 1 - at.n))):
            where = pl.ds(pl.multiple_of(n * size, size), size)
            target = full.at[where] if axis == 0 else full.at[:, where]
            self.copies.append(pltpu.make_async_copy(part, target, sem.at[i]))
            self.copies[-1].start()

    def wait(self):
        for copy in self.copies:
            copy.wait()


class Gather:
    slots = 11

    def __init__(self, at, x, whole, send, recv, local, base=0):
        self.at, self.x, self.whole = at, x, whole
        y, c, up, down = at.y, at.c, at.up, at.down
        far = lax.rem(y + 2, 4)
        half = BLOCK // 2

        def move(slot, y_from, peer, start=0, size=BLOCK, first=False):
            rows = at.rows(y_from, c, start, size)
            src = whole.at[rows]
            if first:
                src = x if size == BLOCK else x.at[start : start + size]
            return remote(src, whole.at[rows], send.at[base + slot], recv.at[base + slot], peer)

        to_up, to_down, core = at.at_y(up), at.at_y(down), at.core()
        self.sends = [
            move(0, y, to_up, 0, half, first=True),
            move(1, y, to_up, half, half, first=True),
            move(2, y, to_down, half, half, first=True),
            move(3, y, to_down, 0, half, first=True),
            move(4, y, core, first=True),
            move(5, down, to_up, 0, half),
            move(6, up, to_down, half, half),
            move(7, down, core),
            move(8, up, core),
            move(9, far, core, 0, half),
            move(10, far, core, half, half),
        ]
        self.own = pltpu.make_async_copy(x, whole.at[at.rows(y, c)], local)

    def begin(self):
        for i in (0, 2, 1, 3, 4):
            self.sends[i].start()
        self.own.start()
        self.own.wait()

    def chain(self, *pairs):
        for arrived, leaving in pairs:
            self.sends[arrived].wait_recv()
            self.sends[leaving].start()

    def pass_on(self):
        self.chain((0, 5), (2, 6))

    def pass_near(self):
        self.chain((1, 7), (3, 8))

    def pass_far(self):
        self.chain((5, 9), (6, 10))

    def got(self, *slots):
        for i in slots:
            self.sends[i].wait_recv()

    def end(self):
        for copy in self.sends:
            copy.wait_send()

    def finish(self):
        self.pass_on()
        self.pass_near()
        self.pass_far()
        self.got(4, 7, 8, 9, 10)
        self.end()

    def each(self, work):
        at = self.at

        def step(s, carry):
            @pl.when(s == 1)
            def _():
                self.got(4)
                self.pass_on()

            @pl.when(s == 2)
            def _():
                self.pass_near()

            @pl.when(s == 3)
            def _():
                self.got(8)

            @pl.when(s == 5)
            def _():
                self.got(7)

            @pl.when(s == 6)
            def _():
                self.pass_far()

            @pl.when(s == 7)
            def _():
                self.got(9, 10)

            g = lax.div(s, 2)
            off = g + lax.div(g, 2) - 2 * lax.div(g, 3)
            work(s, at.rows(lax.rem(at.y + off, 4), lax.rem(at.c + s, 2)))
            return carry

        lax.fori_loop(0, 8, step, 0)
        self.end()


class Scatter:
    slots = 10
    scratch = [
        VMEM((4, BLOCK, D), bf16),
        VMEM((4, BLOCK, D), bf16),
        VMEM((4, BLOCK, D), f32),
        VMEM((2, BLOCK, D), bf16),
        VMEM((2, BLOCK, D), bf16),
        VMEM((2, BLOCK // 2, D), bf16),
        VMEM((2, BLOCK // 2, D), bf16),
    ]

    def __init__(self, at, send, recv, refs, base=0):
        self.at, self.send, self.recv, self.base = at, send, recv, base
        self.out_c, self.in_c, self.own, self.out_y, self.in_y, self.half_out, self.half_in = refs
        half = BLOCK // 2
        peers = at.at_y(at.up), at.at_y(at.down)

        def move(slot, src, dst, peer):
            return remote(src, dst, send.at[base + slot], recv.at[base + slot], peer)

        self.cores = [self.core(g) for g in range(4)]
        self.halves = [move(4 + i, self.half_out.at[i], self.half_in.at[i], peers[i]) for i in range(2)]
        free = [pl.ds((1 - i) * half, half) for i in range(2)]
        bound = [pl.ds(i * half, half) for i in range(2)]
        self.free = [move(6 + i, self.out_y.at[i, free[i]], self.in_y.at[i, free[i]], peers[i]) for i in range(2)]
        self.bound = [move(8 + i, self.out_y.at[i, bound[i]], self.in_y.at[i, bound[i]], peers[i]) for i in range(2)]

    def core(self, g):
        slot = self.base + g
        return remote(self.out_c.at[g], self.in_c.at[g], self.send.at[slot], self.recv.at[slot], self.at.core())

    def both(self, g, rows):
        return self.own[g, rows] + self.in_c[g, rows].astype(f32)

    def products(self, product):
        at = self.at
        half = BLOCK // 2

        def part_rows(rows, i):
            return pl.ds(pl.multiple_of(rows.start + i * half, 32), 32)

        def send_free(i):
            self.cores[1 + i].wait_recv()

            def add(rows, carry):
                there = part_rows(rows, 1 - i)
                self.out_y[i, there] = self.both(1 + i, there).astype(bf16)

            by_rows(half, 32, add)
            self.free[i].start()

        def step(s, carry):
            g = lax.div(s, 2)
            off = lax.rem(6 - g + 3 * lax.div(g, 2) + 2 * lax.div(g, 3), 4)
            part = product(at.rows(lax.rem(at.y + off, 4), lax.rem(at.c + 1 + s, 2)))

            @pl.when(lax.rem(s, 2) == 0)
            def _():
                self.out_c[g] = part.astype(bf16)
                self.core(g).start()

            @pl.when(lax.rem(s, 2) == 1)
            def _():
                self.own[g] = part

            @pl.when(s == 2)
            def _():
                self.cores[0].wait_recv()
                for i in range(2):

                    def add(rows, carry, i=i):
                        self.half_out[i, rows] = self.both(0, part_rows(rows, i)).astype(bf16)

                    by_rows(half, 32, add)
                    self.halves[i].start()

            @pl.when(s == 4)
            def _():
                send_free(0)

            @pl.when(s == 6)
            def _():
                send_free(1)

            return carry

        lax.fori_loop(0, 8, step, 0)

    def middle(self):
        half = BLOCK // 2
        for i in range(2):
            self.halves[i].wait_recv()

            def add(rows, carry, i=i):
                here = pl.ds(pl.multiple_of(rows.start + i * half, 32), 32)
                self.out_y[i, here] = (self.both(1 + i, here) + self.half_in[i, rows].astype(f32)).astype(bf16)

            by_rows(half, 32, add)
            self.bound[i].start()

    def arrive(self):
        self.cores[3].wait_recv()
        for copy in self.free + self.bound:
            copy.wait_recv()

    def total(self, rows):
        return self.both(3, rows) + self.in_y[0, rows].astype(f32) + self.in_y[1, rows].astype(f32)

    def end(self):
        for copy in self.cores + self.halves + self.free + self.bound:
            copy.wait_send()


def standard(values):
    average = jnp.mean(values, axis=1, keepdims=True)
    variance = jnp.mean(values * values, axis=1, keepdims=True) - average * average
    factor = lax.rsqrt(variance + EPSILON)
    return (values - average) * factor, factor


def norm_back(incoming, centred, factor, gain):
    scaled = incoming * gain
    first = jnp.mean(scaled, axis=1, keepdims=True)
    second = jnp.mean(scaled * centred, axis=1, keepdims=True)
    return factor * (scaled - first - centred * second)


def two_sums(incoming, centred, carry):
    gains, shifts = carry
    return gains + jnp.sum(incoming * centred, axis=0, keepdims=True), shifts + jnp.sum(incoming, axis=0, keepdims=True)


def no_sums():
    return jnp.zeros((1, D), f32), jnp.zeros((1, D), f32)


EIGHTH = 0.125


def shape(*dims, dtype=bf16):
    return jax.ShapeDtypeStruct(dims, dtype)


class Keep:
    def __init__(self, whole, out, sem, base):
        self.whole, self.out, self.sem, self.base = whole, out, sem, base

    def block(self, s, rows):
        pltpu.make_async_copy(self.whole.at[rows], self.out.at[rows], self.sem.at[self.base + s]).start()

    def wait(self):
        for s in range(8):
            some = pl.ds(0, BLOCK)
            pltpu.make_async_copy(self.whole.at[some], self.out.at[some], self.sem.at[self.base + s]).wait()


def enter(number, layer_input, vectors, weights, beside):
    relay = Relay(layer_input)

    def body(at, ins, outs, kept):
        (source, own_vectors, *own_weights), (x, vectors, weight, all_rows, qkv) = ins, outs
        normed, whole, send, recv, local = kept
        half = at.half(at.n)
        moving = functools.partial(relay_run, relay, at, source, x, send, recv, local.at[0], 11)
        moving(False)
        stay, go = [], []
        for i, (own, target) in enumerate(
            [(own_vectors, vectors.at[:, half])]
            + [(own, weight.at[j * COLS : (j + 1) * COLS, half]) for j, own in enumerate(own_weights)]
        ):
            stay.append(pltpu.make_async_copy(own, target, local.at[1 + i]))
            go.append(remote(own, target, send.at[13 + i], recv.at[13 + i], at.x()))
        stay[0].start()
        go[0].start()
        stay[0].wait()
        go[0].wait_recv()
        moving(True)
        for copy in stay[1:] + go[1:]:
            copy.start()

        def norm(rows, carry):
            centred, _ = standard(x[rows].astype(f32))
            normed[rows] = (centred * vectors[0:1] + vectors[1:2]).astype(bf16)

        by_rows(BLOCK, 32, norm)
        gather = Gather(at, normed, whole, send, recv, local.at[5])
        gather.begin()
        at.start_beside()
        keep = Keep(whole, all_rows, local, 6)
        gather.each(keep.block)
        for copy in stay[1:]:
            copy.wait()
        for copy in go[1:]:
            copy.wait_recv()

        def times(rows, carry):
            qkv[rows] = dot_flip(whole[rows], weight[...]).astype(bf16)

        by_rows(D, BLOCK, times)
        keep.wait()
        for copy in go:
            copy.wait_send()

    return call(
        body,
        number,
        [layer_input, vectors, *weights],
        [shape(BLOCK, D), shape(8, D, dtype=f32), shape(3 * COLS, D), shape(D, D), shape(D, 3 * COLS)],
        [VMEM((BLOCK, D), bf16), VMEM((D, D), bf16), *sems(17)],
        beside,
        lambda at: ring_peers(at) + relay.peers(at) + [("x", at.x())],
        out_spaces=[VMEM, VMEM, VMEM, ANY, VMEM],
        late=True,
    )


def causal_forward(number, joined, query_w, out_w, text_pair, beside):
    at_once = 512

    def body(at, ins, outs, kept):
        (qkv, query_own, query_got, out_own, out_got, pair), (out, logs, all_keys, all_values) = ins, outs
        parts, mixed, keys, values, send, recv, local = kept
        half, other = at.half(at.n), at.half(1 - at.n)
        for own, got, target, axis in ((query_own, query_got, keys, 0), (out_own, out_got, values, 1)):
            for cols, ref in ((half, own), (other, got)):
                for h in range(HEADS):
                    rows = slice(h * HDIM, (h + 1) * HDIM)
                    text = pair[:, axis * COLS + h * HDIM : axis * COLS + (h + 1) * HDIM]
                    product = dot(text, ref[rows, :])
                    target[rows, cols] = (product * EIGHTH if axis == 0 else product).astype(bf16)
        first = Gather(at, keys, all_keys, send, recv, local.at[0])
        second = Gather(at, values, all_values, send, recv, local.at[1], 11)
        first.begin()
        for i in range(3):
            for h in range(HEADS):
                a = i * COLS + h * HDIM
                piece = qkv[:, a : a + HDIM]
                parts[i, h] = piece * EIGHTH if i == 0 else piece
        square = (at_once, at_once)
        seen = lax.broadcasted_iota(jnp.int32, square, 0) >= lax.broadcasted_iota(jnp.int32, square, 1)

        def one(h, carry):
            for i in reversed(range(D // at_once)):
                before, upto = i * at_once, (i + 1) * at_once
                rows = slice(before, upto)
                scores = dot_flip(parts[0, h, rows], parts[1, h, 0:upto])
                last = jnp.where(seen, scores[:, before:], NEGATIVE)
                scores = jnp.concatenate((scores[:, :before], last), axis=1) if i else last
                peak = jnp.max(scores, axis=1, keepdims=True)
                raised = jnp.exp(scores - peak)
                total = jnp.sum(raised, axis=1, keepdims=True)
                mixed[h, rows] = (dot(raised.astype(bf16), parts[2, h, 0:upto]) / total).astype(bf16)
                column = jnp.broadcast_to(peak + jnp.log(total), (at_once, 128))
                logs[pl.ds(h, 1), rows] = column.T[0:1, :]

            @pl.when(h == 0)
            def _():
                first.pass_on()
                second.begin()
                first.pass_near()

            @pl.when(h == 1)
            def _():
                first.pass_far()
                second.pass_on()

            return carry

        lax.fori_loop(0, HEADS, one, 0)
        second.pass_near()
        out[...] = jnp.concatenate([mixed[h] for h in range(HEADS)], axis=1)
        second.pass_far()
        for gather in (first, second):
            gather.got(4, 7, 8, 9, 10)
            gather.end()

    return call(
        body,
        number,
        [joined, *query_w, *out_w, text_pair],
        [shape(D, COLS), shape(8, D, dtype=f32), shape(D, D), shape(D, D)],
        [VMEM((3, HEADS, D, HDIM), bf16), VMEM((HEADS, D, HDIM), bf16), VMEM((BLOCK, D), bf16), VMEM((BLOCK, D), bf16), *sems(22)],
        beside,
        ring_peers,
        out_spaces=[VMEM, VMEM, ANY, ANY],
    )


def forward_rest(number, attended, out_w, x, vectors, keys, values, down, expand_w, contract):
    def body(at, ins, outs, kept):
        mixed, out_own, out_got, x, vectors, keys, values, down, expand_own, expand_got, contract_own = ins
        middle, after, normed_two, weights, all_rows, all_down, activated, grad, contract_out = outs
        *refs, normed, whole, downs, out_full, expand_full, contract_full, key_full, value_full, branch, send, recv, local = kept
        half = at.half(at.n)
        weight = Whole(at, out_own, out_got, out_full, local.at[pl.ds(0, 2)], 1)
        swap = remote(contract_own, contract_full.at[:, half], send.at[32], recv.at[32], at.x())
        swap.start()
        later = [
            pltpu.make_async_copy(keys, key_full, local.at[2]),
            pltpu.make_async_copy(values, value_full, local.at[3]),
            pltpu.make_async_copy(contract_own, contract_full.at[:, half], local.at[4]),
        ]
        for copy in later:
            copy.start()
        later.append(Whole(at, expand_own, expand_got, expand_full, local.at[pl.ds(5, 2)], 0))
        weight.wait()
        scatter = Scatter(at, send, recv, refs)
        scatter.products(lambda rows: dot(mixed[rows], out_full[...]))
        scatter.middle()
        for copy in later:
            copy.wait()
        scatter.arrive()
        cotangents = Gather(at, down, downs, send, recv, local.at[7], 10)
        cotangents.begin()

        def norm_two(rows, carry):
            total = x[rows].astype(f32) + scatter.total(rows)
            middle[rows] = total
            centred, _ = standard(total)
            normed_two[rows] = (centred * vectors[2:3] + vectors[3:4]).astype(bf16)

        by_rows(BLOCK, 32, norm_two)

        def cross(b, carry):
            rows = pl.ds(pl.multiple_of(b * BLOCK, BLOCK), BLOCK)
            scores = dot_flip(key_full[rows], normed_two[...]).reshape(HEADS, 64, BLOCK)
            raised = jnp.exp(scores - jnp.max(scores, axis=1, keepdims=True))
            p = raised / jnp.sum(raised, axis=1, keepdims=True)
            p = p.reshape(BLOCK, BLOCK).T.astype(bf16)
            weights[b] = p
            part = dot(p, value_full[rows])

            @pl.when(b == 0)
            def _():
                branch[...] = part

            @pl.when(b > 0)
            def _():
                branch[...] += part

            @pl.when(b == 3)
            def _():
                cotangents.pass_on()
                cotangents.pass_near()

            return carry

        lax.fori_loop(0, 8, cross, 0)

        def norm_three(rows, carry):
            total = middle[rows] + branch[rows]
            after[rows] = total
            centred, _ = standard(total)
            normed[rows] = (centred * vectors[4:5] + vectors[5:6]).astype(bf16)

        by_rows(BLOCK, 32, norm_three)
        gather = Gather(at, normed, whole, send, recv, local.at[8], 21)
        gather.begin()
        cotangents.pass_far()
        cotangents.got(4, 7, 8, 9, 10)
        keep_down = pltpu.make_async_copy(downs, all_down, local.at[9])
        keep_down.start()
        swap.wait_recv()
        keep_contract = pltpu.make_async_copy(contract_full, contract_out, local.at[10])
        keep_contract.start()
        keep = Keep(whole, all_rows, local, 11)

        def work(s, rows):
            keep.block(s, rows)
            hidden = dot(whole[rows], expand_full[...])
            back = dot_flip(downs[rows], contract_full[...])
            bell = 0.5 * (1.0 + lax.erf(hidden * ROOT_HALF))
            activated[rows] = (hidden * bell).astype(bf16)
            grad[rows] = (back * (bell + hidden * jnp.exp(-0.5 * hidden * hidden) * GAUSS_NORM)).astype(bf16)

        gather.each(work)
        keep.wait()
        keep_down.wait()
        keep_contract.wait()
        cotangents.end()
        scatter.end()
        swap.wait_send()

    results, _ = call(
        body,
        number,
        [attended, *out_w, x, vectors, keys, values, down, *expand_w, contract],
        [
            shape(BLOCK, D, dtype=f32),
            shape(BLOCK, D, dtype=f32),
            shape(BLOCK, D),
            shape(8, BLOCK, BLOCK),
            shape(D, D),
            shape(D, D),
            shape(D, HALF),
            shape(D, HALF),
            shape(HALF, D),
        ],
        [
            *Scatter.scratch,
            VMEM((BLOCK, D), bf16),
            VMEM((D, D), bf16),
            VMEM((D, D), bf16),
            VMEM((COLS, D), bf16),
            VMEM((D, HALF), bf16),
            VMEM((HALF, D), bf16),
            VMEM((D, D), bf16),
            VMEM((D, D), bf16),
            VMEM((BLOCK, D), f32),
            *sems(33),
        ],
        (),
        lambda at: ring_peers(at) + [("x", at.x())],
        spaces=[VMEM, ANY, ANY, VMEM, VMEM, ANY, ANY, VMEM, ANY, ANY, ANY],
        out_spaces=[VMEM, VMEM, VMEM, VMEM, ANY, ANY, VMEM, VMEM, ANY],
    )
    return results


def backward_rest(number, grad, expand_w, after, middle, vectors, down, keys, values, weights, normed_two, out_w, beside):
    def body(at, ins, outs, kept):
        grad, expand_own, expand_got, after, middle, vectors, down, keys, values, weights, normed_two, out_own, out_got = ins
        grad_rows, rounded_two, grad_scores, all_two, all_rows, grad_mixed, grad_vectors = outs
        *refs, rounded, whole, second, out_full, expand_full, key_full, value_full, send, recv, local = kept
        weight = Whole(at, expand_own, expand_got, expand_full, local.at[pl.ds(0, 2)], 0)
        later = [
            pltpu.make_async_copy(keys, key_full, local.at[2]),
            pltpu.make_async_copy(values, value_full, local.at[3]),
        ]
        for copy in later:
            copy.start()
        later.append(Whole(at, out_own, out_got, out_full, local.at[pl.ds(4, 2)], 1))
        weight.wait()
        scatter = Scatter(at, send, recv, refs)
        scatter.products(lambda rows: dot_flip(grad[rows], expand_full[...]))
        scatter.middle()
        for copy in later:
            copy.wait()
        scatter.arrive()
        before = Gather(at, normed_two, all_two, send, recv, local.at[6], 10)
        before.begin()

        def norm_three(rows, carry):
            incoming = scatter.total(rows)
            centred, factor = standard(after[rows])
            total = down[rows].astype(f32) + norm_back(incoming, centred, factor, vectors[4:5])
            grad_rows[rows] = total
            rounded_two[rows] = total.astype(bf16)
            return two_sums(incoming, centred, carry)

        gains, shifts = by_rows(BLOCK, 32, norm_three, no_sums())
        grad_vectors[4:5] = gains
        grad_vectors[5:6] = shifts

        def cross(b, carry):
            rows = pl.ds(pl.multiple_of(b * BLOCK, BLOCK), BLOCK)
            p = weights[b].astype(f32).T.reshape(HEADS, 64, BLOCK)
            dp = dot_flip(value_full[rows], rounded_two[...]).reshape(HEADS, 64, BLOCK)
            ds = p * (dp - jnp.sum(p * dp, axis=1, keepdims=True))
            ds = ds.reshape(BLOCK, BLOCK).T.astype(bf16)
            grad_scores[b] = ds
            part = dot(ds, key_full[rows])

            @pl.when(b == 0)
            def _():
                second[...] = part

            @pl.when(b > 0)
            def _():
                second[...] += part

            @pl.when(b == 3)
            def _():
                before.pass_on()
                before.pass_near()

            return carry

        lax.fori_loop(0, 8, cross, 0)

        def norm_two(rows, carry):
            incoming = second[rows]
            centred, factor = standard(middle[rows])
            total = grad_rows[rows] + norm_back(incoming, centred, factor, vectors[2:3])
            grad_rows[rows] = total
            rounded[rows] = total.astype(bf16)
            return two_sums(incoming, centred, carry)

        gains, shifts = by_rows(BLOCK, 32, norm_two, no_sums())
        grad_vectors[2:3] = gains
        grad_vectors[3:4] = shifts
        gather = Gather(at, rounded, whole, send, recv, local.at[7], 21)
        gather.begin()
        before.pass_far()
        keep = Keep(whole, all_rows, local, 8)

        def work(s, rows):
            keep.block(s, rows)
            grad_mixed[rows] = dot_flip(whole[rows], out_full[...]).astype(bf16)

        gather.each(work)
        before.got(4, 7, 8, 9, 10)
        before.end()
        keep.wait()
        scatter.end()

    return call(
        body,
        number,
        [grad, *expand_w, after, middle, vectors, down, keys, values, weights, normed_two, *out_w],
        [
            shape(BLOCK, D, dtype=f32),
            shape(BLOCK, D),
            shape(8, BLOCK, BLOCK),
            shape(D, D),
            shape(D, D),
            shape(D, COLS),
            shape(8, D, dtype=f32),
        ],
        [
            *Scatter.scratch,
            VMEM((BLOCK, D), bf16),
            VMEM((D, D), bf16),
            VMEM((BLOCK, D), f32),
            VMEM((COLS, D), bf16),
            VMEM((D, HALF), bf16),
            VMEM((D, D), bf16),
            VMEM((D, D), bf16),
            *sems(32),
        ],
        beside,
        ring_peers,
        spaces=[VMEM, ANY, ANY, VMEM, VMEM, VMEM, VMEM, ANY, ANY, VMEM, VMEM, ANY, ANY],
        out_spaces=[VMEM, VMEM, VMEM, ANY, ANY, VMEM, VMEM],
    )


def causal_backward(number, joined, grad, logs, activated, contract, after, rounded_two, beside):
    at_once = 512

    def body(at, ins, outs, kept):
        (qkv, go, log_rows, activated, contract, after, block), (out, result, all_rows) = ins, outs
        *refs, parts, key_sum, value_sum, send, recv, local = kept
        scatter = Scatter(at, send, recv, refs)
        scatter.products(lambda rows: dot(activated[rows], contract[...]))
        gather = Gather(at, block, all_rows, send, recv, local.at[0], 10)
        for i in range(4):
            for h in range(HEADS):
                a = i * COLS + h * HDIM
                piece = qkv[:, a : a + HDIM] if i < 3 else go[:, h * HDIM : (h + 1) * HDIM]
                parts[i, h] = piece * EIGHTH if i == 0 else piece
        square = (at_once, at_once)
        seen = lax.broadcasted_iota(jnp.int32, square, 1) >= lax.broadcasted_iota(jnp.int32, square, 0)
        blocks = D // at_once

        def one(h, carry):
            turned = parts[1, h].T
            query_parts = []
            for i in reversed(range(blocks)):
                before, upto = i * at_once, (i + 1) * at_once
                rows = slice(before, upto)
                q, g = parts[0, h, rows], parts[3, h, rows]
                k, v = parts[1, h, 0:upto], parts[2, h, 0:upto]
                p = jnp.exp(dot_flip(k, q) - log_rows[pl.ds(h, 1), rows])
                last = jnp.where(seen, p[before:], 0.0)
                p = jnp.concatenate((p[:before], last), axis=0) if i else last
                dp = dot_flip(v, g)
                ds = (p * (dp - jnp.sum(p * dp, axis=0, keepdims=True))).astype(bf16)
                value_part, key_part = dot(p.astype(bf16), g), dot(ds, q)
                if i == blocks - 1:
                    key_sum[0:upto, :] = key_part
                    value_sum[0:upto, :] = value_part
                else:
                    key_sum[0:upto, :] += key_part
                    value_sum[0:upto, :] += value_part
                query_parts.append((dot(turned[:, 0:upto], ds) * EIGHTH).T)
            parts[0, h] = jnp.concatenate(query_parts[::-1], axis=0).astype(bf16)
            parts[1, h] = key_sum[...].astype(bf16)
            parts[2, h] = value_sum[...].astype(bf16)

            @pl.when(h == 0)
            def _():
                scatter.middle()
                gather.begin()

            @pl.when(h == 1)
            def _():
                gather.pass_on()
                gather.pass_near()

            return carry

        lax.fori_loop(0, HEADS, one, 0)
        gather.pass_far()
        for i in range(3):
            out[:, i * COLS : (i + 1) * COLS] = jnp.concatenate([parts[i, h] for h in range(HEADS)], axis=1)
        scatter.arrive()

        def finish(rows, carry):
            result[rows] = (after[rows] + scatter.total(rows)).astype(bf16)

        by_rows(BLOCK, 32, finish)
        gather.got(4, 7, 8, 9, 10)
        gather.end()
        scatter.end()

    return call(
        body,
        number,
        [joined, grad, logs, activated, contract, after, rounded_two],
        [shape(D, 3 * COLS), shape(BLOCK, D), shape(D, D)],
        [*Scatter.scratch, VMEM((4, HEADS, D, HDIM), bf16), VMEM((D, HDIM), f32), VMEM((D, HDIM), f32), *sems(21)],
        beside,
        ring_peers,
        out_spaces=[VMEM, VMEM, ANY],
    )


def leave(number, grad, joined, x, vectors, grad_rows, beside):
    relay = Relay(jax.ShapeDtypeStruct((BLOCK, D), bf16), True)

    def body(at, ins, outs, kept):
        grad, weight, x, vectors, before = ins
        result, grad_vectors = outs
        *refs, rounded, send, recv, local = kept
        scatter = Scatter(at, send, recv, refs)
        scatter.products(lambda rows: dot(grad[rows], weight[...]))
        scatter.middle()
        scatter.arrive()

        def norm(rows, carry):
            incoming = scatter.total(rows)
            centred, factor = standard(x[rows].astype(f32))
            total = before[rows] + norm_back(incoming, centred, factor, vectors[0:1])
            rounded[rows] = total.astype(bf16)
            return two_sums(incoming, centred, carry)

        gains, shifts = by_rows(BLOCK, 32, norm, no_sums())
        moving = functools.partial(relay_run, relay, at, rounded, result, send, recv, local.at[0], 10)
        moving(False)
        grad_vectors[0:1] = gains
        grad_vectors[1:2] = shifts
        moving(True)
        scatter.end()

    return call(
        body,
        number,
        [grad, joined, x, vectors, grad_rows],
        [shape(384, HALF), shape(8, D, dtype=f32)],
        [*Scatter.scratch, VMEM((BLOCK, D), bf16), *sems(12)],
        beside,
        lambda at: ring_peers(at) + relay.peers(at),
        out_spaces=[ANY, VMEM],
    )


def on_device(
    layer_input,
    text_states,
    cotangent,
    first_gain,
    first_shift,
    query_weight,
    key_weight,
    value_weight,
    output_weight,
    second_gain,
    second_shift,
    cross_query,
    cross_key,
    cross_value,
    cross_output,
    third_gain,
    third_shift,
    expand_weight,
    contract_weight,
):
    vectors = (first_gain, first_shift, second_gain, second_shift, third_gain, third_shift)
    vectors = jnp.concatenate([jnp.stack(vectors).astype(f32), jnp.zeros((2, HALF), f32)], axis=0)
    weights = [query_weight.T, key_weight.T, value_weight.T]
    query_t = cross_query.T
    pair_t = jnp.concatenate((cross_key.T, cross_value.T), axis=0)
    n = lax.axis_index("narrow")

    text_parts = dot_flip(text_states.reshape(128, HALF), pair_t).reshape(2, 64, 2 * COLS)
    (x, vectors, joined, all_one, qkv), ((text_pair_got,), (query_got,), (cross_got,), (text_got,)) = enter(
        1, layer_input, vectors, weights, [GiveClip(text_parts), Give(query_t), Give(cross_output), GiveClip(text_states)]
    )
    text_pair = (lax.dynamic_index_in_dim(text_parts, n, 0, False) + text_pair_got).astype(bf16)
    (attended, logs, all_keys, all_values), ((down,), (out_got,), (expand_got,)) = causal_forward(
        2,
        qkv,
        (query_t, query_got),
        (cross_output, cross_got),
        text_pair,
        [Relay(cotangent), Give(output_weight), Give(expand_weight)],
    )
    out_w, expand_w = (output_weight, out_got), (expand_weight, expand_got)
    middle, after, normed_two, cross_p, all_three, all_down, activated, grad_expand, contract = forward_rest(
        3, attended, out_w, x, vectors, all_keys, all_values, down, expand_w, contract_weight
    )

    contract_leg = SumZ(outer(activated, all_down).astype(bf16), False)
    expand_leg = SumZ(outer(all_three, grad_expand).astype(bf16), True)
    (grad_one, rounded_two, grad_scores, all_two, all_mid_one, grad_attended, late), sums = backward_rest(
        4,
        grad_expand,
        expand_w,
        after,
        middle,
        vectors,
        down,
        all_keys,
        all_values,
        cross_p,
        normed_two,
        out_w,
        [contract_leg, expand_leg, Trade(cross_p)],
    )
    contract_sum, expand_sum, (cross_p,) = sums
    contract_leg, expand_leg = SumX(contract_leg.finish(contract_sum), False), SumX(expand_leg.finish(expand_sum), True)
    output_leg = SumZ(outer(attended, all_mid_one).astype(bf16), False)
    (grad_qkv, layer_output, all_mid_two), sums = causal_backward(
        5,
        qkv,
        grad_attended,
        logs,
        activated,
        contract,
        after,
        rounded_two,
        [contract_leg, expand_leg, output_leg, Trade(grad_scores)],
    )
    contract_sum, expand_sum, output_sum, (grad_scores,) = sums

    joined_leg = SumZ(outer(grad_qkv, all_one).astype(bf16), False)
    grad_keys = outer(grad_scores.reshape(D, COLS), all_two).astype(bf16).reshape(HEADS, 64, D)
    grad_values = outer(cross_p.reshape(D, COLS), all_mid_two).astype(bf16).reshape(HEADS, 64, D)
    own_first = n == 0

    def whole(own, got):
        return jnp.concatenate((jnp.where(own_first, own, got), jnp.where(own_first, got, own)), axis=1)

    text = whole(lax.dynamic_index_in_dim(text_states, n, 0, False), text_got)
    heads_query = whole(query_t, query_got).reshape(HEADS, HDIM, D)
    heads_out = whole(cross_output, cross_got).reshape(HEADS, HDIM, D)
    text_heads = text_pair.reshape(64, 2, HEADS, HDIM)

    def heads(what, a, b):
        return jnp.einsum(what, a, b, preferred_element_type=f32)

    grad_text_keys = heads("hkf,hdf->khd", grad_keys, heads_query) * EIGHTH
    grad_text_values = heads("hkf,hdf->khd", grad_values, heads_out)
    grad_pair = jnp.stack((grad_text_keys, grad_text_values), axis=1).reshape(64, 2 * COLS).astype(bf16)
    grad_query = heads("khd,hkf->hdf", text_heads[:, 0], grad_keys).reshape(COLS, D) * EIGHTH
    grad_cross = heads("khd,hkf->hdf", text_heads[:, 1], grad_values).reshape(COLS, D)
    cross_leg = SumZ(jnp.concatenate((grad_query, outer(grad_pair, text), grad_cross), axis=0).astype(bf16), False)

    contract_leg, expand_leg = Spread(contract_leg.finish(contract_sum)), Spread(expand_leg.finish(expand_sum))
    output_leg = SumX(output_leg.finish(output_sum), False)
    (input_grad, first), sums = leave(
        6,
        grad_qkv,
        joined,
        x,
        vectors,
        grad_one,
        [joined_leg, cross_leg, contract_leg, expand_leg, output_leg, Relay(layer_output, True), Give(grad_pair)],
    )
    joined_sum, cross_sum, contract_sum, expand_sum, output_sum, (layer_output,), (grad_pair_got,) = sums
    contract_grad, expand_grad = contract_leg.finish(contract_sum), expand_leg.finish(expand_sum)
    parts = jnp.concatenate((first[0:2], late[2:6], jnp.zeros((2, D), f32)), axis=0)
    pairs = jnp.concatenate((jnp.where(own_first, grad_pair, grad_pair_got), jnp.where(own_first, grad_pair_got, grad_pair)), axis=0)
    text_part = dot(pairs, pair_t).astype(bf16).reshape(8, 16, HALF)
    joined_leg, cross_leg = SumX(joined_leg.finish(joined_sum), False), SumX(cross_leg.finish(cross_sum), False)
    output_leg = Spread(output_leg.finish(output_sum))
    _, (joined_sum, cross_sum, output_sum, (parts,), (text_part,)) = call(
        None, 7, [], [], (), [joined_leg, cross_leg, output_leg, ToRing(parts), Trade(text_part)]
    )
    output_grad = output_leg.finish(output_sum)
    joined_leg, cross_leg = Spread(joined_leg.finish(joined_sum)), Spread(cross_leg.finish(cross_sum))
    text_part = jnp.sum(text_part.astype(f32), axis=0).astype(bf16)
    _, (joined_sum, cross_sum, (parts,), (text_grad,)) = call(
        None, 8, [], [], (), [joined_leg, cross_leg, ToClips(jnp.sum(parts, axis=0)), ToSpots(text_part)]
    )
    joined_grad, cross_grad = joined_leg.finish(joined_sum), cross_leg.finish(cross_sum)
    parts = jnp.sum(parts, axis=(0, 1))
    return (
        layer_output,
        input_grad.astype(f32),
        text_grad.reshape(2, 64, HALF).astype(f32),
        parts[0],
        parts[1],
        joined_grad[:COLS].T,
        joined_grad[COLS : 2 * COLS].T,
        joined_grad[2 * COLS :].T,
        output_grad,
        parts[2],
        parts[3],
        cross_grad[:COLS].T,
        cross_grad[COLS : 2 * COLS].T,
        cross_grad[2 * COLS : 3 * COLS].T,
        cross_grad[3 * COLS :],
        parts[4],
        parts[5],
        expand_grad,
        contract_grad,
    )


def solution(mesh):
    return jax.shard_map(
        on_device,
        mesh=mesh,
        in_specs=(
            P(("dp", "wide"), "narrow"),
            P("dp", None, "narrow"),
            P(("dp", "wide"), "narrow"),
            P("narrow"),
            P("narrow"),
            P("narrow", "wide"),
            P("narrow", "wide"),
            P("narrow", "wide"),
            P("wide", "narrow"),
            P("narrow"),
            P("narrow"),
            P("narrow", "wide"),
            P("narrow", "wide"),
            P("narrow", "wide"),
            P("wide", "narrow"),
            P("narrow"),
            P("narrow"),
            P("narrow", "wide"),
            P("wide", "narrow"),
        ),
        out_specs=(
            P(("dp", "wide"), "narrow"),
            P(("dp", "wide"), "narrow"),
            P("dp", None, "narrow"),
            P("narrow"),
            P("narrow"),
            P("narrow", "wide"),
            P("narrow", "wide"),
            P("narrow", "wide"),
            P("wide", "narrow"),
            P("narrow"),
            P("narrow"),
            P("narrow", "wide"),
            P("narrow", "wide"),
            P("narrow", "wide"),
            P("wide", "narrow"),
            P("narrow"),
            P("narrow"),
            P("narrow", "wide"),
            P("wide", "narrow"),
        ),
        check_vma=False,
    )
```

time: 603 us -> 572 us (0.949)
  between operations: 15.2 us -> 1.43 us
  other arithmetic: 42.9 us -> 33.3 us
    unnamed x93 -> x65, local copies, waits for them, and re-layouts: 13.2 us -> 2.96 us
    convert_element_type x12 -> x10, other arithmetic: 14.6 us -> 12.6 us  [finish(): return (own.astype(f32) + outs[0].astype(f32).sum(axis=0)).astype(bf16)]
    pallas_call x10 -> x8, Pallas kernels: 476 us -> 476 us  [call(): pl.pallas_call(kernel, out_shape=tuple(outs) + tuple(side_outs), in_specs...]
  transfers between devices with their start and end apart: 1 -> 0, of which waited for: 0 -> 0; matrix products, arithmetic and copies ran while one was open for 9% -> 0% of each run, Pallas kernels for 23% -> 0%
where the time goes in v3:
time: 572 us; the launch traced here: 565 us
  Pallas kernels  476 us (83%)
  matrix products  36.2 us (6%)
  other arithmetic  33.3 us (6%)
  local copies, waits for them, and re-layouts  17.8 us (3%)
    pallas_call x8, Pallas kernels, call(): pl.pallas_call(kernel, out_shape=tuple(outs) + tuple(side_outs), in_specs...  476 us
    dot_general x7, matrix products, outer(): lax.dot_general(a, b, (((0,), (0,)), ((), ())), preferred_element_type=f32)  32 us
    convert_element_type x10, other arithmetic, finish(): return (own.astype(f32) + outs[0].astype(f32).sum(axis=0)).astype(bf16)  12.6 us

profile of v3, /device:TPU:0, one launch (start us, length us, event | category | flops | bytes accessed | tf_op | source)
XLA Modules:
  0.0 564.9 jit_solution(1488298913628548038)
XLA Ops:
  0.7 2.1 fusion.8
  7.6 58.9 %shard_map.330 = (bf16[192,1536]{1,0:T(8,128)(2,1)}, f32[8,1536]{1,0:T(8,128)}, bf16[576,1536]{1,0:T(8,128)(2,1)}, bf16[1536,1536]{1,0:T(8,128)(2,1)}, bf16[1536...) custom-call(bf16[384,768]{1,0:T(8,128)(2,1)} %refs_0_.1, ...), custom_call_target="tpu_custom_call" | custom-call | tf_op jit(solution)/shard_map/pallas_call | solution.py:369
  66.5 1.5 fusion.20.refs_5_
  68.0 57.6 %shard_map.331 = (bf16[1536,192]{1,0:T(8,128)(2,1)}, f32[8,1536]{1,0:T(8,128)}, bf16[1536,1536]{1,0:T(8,128)(2,1)}, bf16[1536,1536]{1,0:T(8,128)(2,1)}, bf16[192...) custom-call(bf16[1536,576]{1,0:T(8,128)(2,1)} %get-tuple-element.79.refs_0_, ...), custom_call_target="tpu_custom_call" | custom-call | tf_op jit(solution)/shard_map/pallas_call | solution.py:369
  125.6 82.4 %shard_map.332 = (f32[192,1536]{1,0:T(8,128)}, f32[192,1536]{1,0:T(8,128)}, bf16[192,1536]{1,0:T(8,128)(2,1)}, bf16[8,192,192]{2,1,0:T(8,128)(2,1)}, bf16[1536,1...) custom-call(bf16[1536,192]{1,0:T(8,128)(2,1)} %get-tuple-element.83., ...), custom_call_target="tpu_custom_call" | custom-call | tf_op jit(solution)/shard_map/pallas_call | solution.py:369
  207.9 8.5 %convolution_convert_fusion = bf16[1536,768]{1,0:T(8,128)(2,1)} fusion(bf16[1536,1536]{1,0:T(8,128)(2,1)} %get-tuple-element.98, bf16[1536,768]{1,0:T(8,128)(2,1)} %get-tuple-element.91.refs_0_), kind=kOutput, calls=%fused_computation.3 | convolution fusion | flops 3625058304 | bytes 9437184 | tf_op jit(solution)/shard_map/dot_general | solution.py:36
  216.5 5.1 convolution_convert_fusion.1
  221.6 84.5 %shard_map.333 = (f32[192,1536]{1,0:T(8,128)}, bf16[192,1536]{1,0:T(8,128)(2,1)}, bf16[8,192,192]{2,1,0:T(8,128)(2,1)}, bf16[1536,1536]{1,0:T(8,128)(2,1)}, bf16...) custom-call(bf16[1536,768]{1,0:T(8,128)(2,1)} %get-tuple-element.91., ...), custom_call_target="tpu_custom_call" | custom-call | tf_op jit(solution)/shard_map/pallas_call | solution.py:369
  306.1 4.4 convolution_convert_fusion.7
  310.8 1.2 constant_dynamic-slice_fusion.3
  313.2 1.1 constant_dynamic-slice_fusion.4
  315.3 59.2 %shard_map.334 = (bf16[1536,576]{1,0:T(8,128)(2,1)}, bf16[192,1536]{1,0:T(8,128)(2,1)}, bf16[1536,1536]{1,0:T(8,128)(2,1)}, bf16[3,96,768]{2,1,0:T(8,128)(2,1)},...) custom-call(bf16[1536,576]{1,0:T(8,128)(2,1)} %get-tuple-element.79.refs_0_, ...), custom_call_target="tpu_custom_call" | custom-call | tf_op jit(solution)/shard_map/pallas_call | solution.py:369
  377.3 1.3 convert_reduce_fusion.6
  378.7 1.6 fusion.11.refs_8_
  380.3 1.7 fusion.12.refs_7_
  382.0 3.5 convolution_convert_fusion.6
  387.2 3.4 convolution_convert_fusion.5
  392.4 1.6 pad_maximum_fusion
  394.8 6.5 %convolution_convert_fusion.2 = bf16[576,1536]{1,0:T(8,128)(2,1)} fusion(bf16[1536,576]{1,0:T(8,128)(2,1)S(1)} %copy-done.4, bf16[1536,1536]{1,0:T(8,128)(2,1)} %get-tuple-element.110), kind=kOutput, calls=%fused_computation.5 | convolution fusion | flops 2718793728 | bytes 8257536 | tf_op jit(solution)/shard_map/dot_general | solution.py:36
  401.3 80.7 %shard_map.335 = (bf16[384,768]{1,0:T(8,128)(2,1)}, f32[8,1536]{1,0:T(8,128)}, bf16[3,144,1536]{2,1,0:T(8,128)(2,1)}, bf16[3,192,1536]{2,1,0:T(8,128)(2,1)}, bf1...) custom-call(bf16[1536,576]{1,0:T(8,128)(2,1)} %get-tuple-element.107, ...), custom_call_target="tpu_custom_call" | custom-call | tf_op jit(solution)/shard_map/pallas_call | solution.py:369
  486.5 1.5 fusion.21.refs_2_
  488.2 1.2 constant_dynamic-slice_fusion
  492.5 20.5 %shard_map.336 = (bf16[3,72,768]{2,1,0:T(8,128)(2,1)}, bf16[3,96,768]{2,1,0:T(8,128)(2,1)}, bf16[8,24,768]{2,1,0:T(8,128)(2,1)}, f32[8,8,1536]{2,1,0:T(8,128)}, bf16[8,16,768]{2,1,0:T(8,128)(2,1)}) custom-call(bf16[2,72,1536]{2,1,0:T(8,128)(2,1)} %fusion.7.refs_0_, bf16[2,96,1536]{2,1,0:T(8,128)(2,1)} %fusion.1.refs_1_, bf16[24,768]{1,0:T(8,128)(2,1)} %fusion.21.refs_2_, ...), custom_call_target="tpu_custom_call" | custom-call | tf_op jit(solution)/shard_map/pallas_call | solution.py:369
  513.0 1.2 convert_reduce_fusion.4
  514.2 1.7 fusion.9.refs_1_
  516.9 1.7 fusion.13.refs_0_
  519.9 32.5 %shard_map.337 = (bf16[8,72,768]{2,1,0:T(8,128)(2,1)}, bf16[8,96,768]{2,1,0:T(8,128)(2,1)}, f32[8,2,8,768]{3,2,1,0:T(8,128)}, bf16[8,16,768]{2,1,0:T(8,128)(2,1)}) custom-call(bf16[72,768]{1,0:T(8,128)(2,1)} %fusion.13.refs_0_, bf16[96,768]{1,0:T(8,128)(2,1)} %fusion.9.refs_1_, f32[8,1536]{1,0:T(8,128)} %reduce_sum.145.refs_2_, ...), custom_call_target="tpu_custom_call" | custom-call | tf_op jit(solution)/shard_map/pallas_call | solution.py:369
  552.4 1.3 bitcast_convert_fusion.2
  553.7 1.2 slice_bitcast_fusion
  555.6 1.4 fusion.25
  559.4 1.7 bitcast_convert_fusion
  561.0 1.7 bitcast_convert_fusion.1
  (113 shorter events, 29.1 us)
Async XLA Ops:
  2.8 63.7 %copy-start.19 = (f32[384,128]{0,1:T(8,128)S(1)}, f32[384,128]{0,1:T(8,128)}, u32[]{:S(2)}) copy-start(f32[384,128]{0,1:T(8,128)} %fusion.8) | copy-start | bytes 589828
  207.9 8.6 %copy-start.3 = (bf16[1536,768]{1,0:T(8,128)(2,1)S(1)}, bf16[1536,768]{1,0:T(8,128)(2,1)}, u32[]{:S(2)}) copy-start(bf16[1536,768]{1,0:T(8,128)(2,1)} %get-tuple-element.96.refs_3_) | copy-start | bytes 7077892
  207.9 8.6 %copy-start.27 = (bf16[1536,1536]{1,0:T(8,128)(2,1)S(1)}, bf16[1536,1536]{1,0:T(8,128)(2,1)}, u32[]{:S(2)}) copy-start(bf16[1536,1536]{1,0:T(8,128)(2,1)} %get-tuple-element.97) | copy-start | bytes 14155780
  221.6 84.5 %copy-start.13 = (bf16[1536,192]{1,0:T(8,128)(2,1)S(1)}, bf16[1536,192]{1,0:T(8,128)(2,1)}, u32[]{:S(2)}) copy-start(bf16[1536,192]{1,0:T(8,128)(2,1)} %get-tuple-element.83.refs_0_) | copy-start | bytes 1769476
  306.1 4.4 copy-start.7
  310.8 2.2 copy-start.5
  375.6 6.3 %copy-start.29 = (bf16[8,192,192]{2,1,0:T(8,128)(2,1)S(1)}, bf16[8,192,192]{2,1,0:T(8,128)(2,1)}, u32[]{:S(2)}) copy-start(bf16[8,192,192]{2,1,0:T(8,128)(2,1)} %get-tuple-element.111) | copy-start | bytes 1769476
  382.0 3.6 copy-start.17
  382.0 4.0 copy-start.1
  382.0 4.0 copy-start.2
  382.0 4.0 copy-start.9
  382.0 4.0 copy-start.10
  386.0 1.1 copy-start.28
  390.6 0.9 copy-start.18
  390.6 1.0 copy-start.25
  392.4 2.4 copy-start.4
  401.3 80.8 %copy-start.16 = (bf16[64,384]{1,0:T(8,128)(2,1)S(1)}, bf16[64,384]{1,0:T(8,128)(2,1)}, u32[]{:S(2)}) copy-start(bf16[64,384]{1,0:T(8,128)(2,1)} %copy.44.refs_11_) | copy-start | bytes 147460
  401.3 81.7 %copy-start.30 = (bf16[768,192]{0,1:T(8,128)(2,1)S(1)}, bf16[768,192]{0,1:T(8,128)(2,1)}, u32[]{:S(2)}) copy-start(bf16[768,192]{0,1:T(8,128)(2,1)} %param.32) | copy-start | bytes 884740
  401.3 81.7 %copy-start.31 = (bf16[768,192]{0,1:T(8,128)(2,1)S(1)}, bf16[768,192]{0,1:T(8,128)(2,1)}, u32[]{:S(2)}) copy-start(bf16[768,192]{0,1:T(8,128)(2,1)} %param.31) | copy-start | bytes 884740
  401.3 83.5 %copy-start.26 = (f32[8,1536]{1,0:T(8,128)S(1)}, f32[8,1536]{1,0:T(8,128)}, u32[]{:S(2)}) copy-start(f32[8,1536]{1,0:T(8,128)} %get-tuple-element.126) | copy-start | bytes 147460
  482.0 5.9 %copy-start.6 = (bf16[3,192,1536]{2,1,0:T(8,128)(2,1)S(1)}, bf16[3,192,1536]{2,1,0:T(8,128)(2,1)}, u32[]{:S(2)}) copy-start(bf16[3,192,1536]{2,1,0:T(8,128)(2,1)} %get-tuple-element.123) | copy-start | bytes 5308420
  488.2 2.2 copy-start.8
  513.0 5.6 copy-start.21
  513.0 6.2 %copy-start.23 = (bf16[8,16,768]{2,1,0:T(8,128)(2,1)S(1)}, bf16[8,16,768]{2,1,0:T(8,128)(2,1)}, u32[]{:S(2)}) copy-start(bf16[8,16,768]{2,1,0:T(8,128)(2,1)} %get-tuple-element.131) | copy-start | bytes 589828
  553.7 1.9 copy-start
  555.6 1.4 copy-start.24
  555.6 2.2 copy-start.20
  555.6 2.9 copy-start.22
  557.0 2.3 copy-start.12
  559.4 1.7 copy-start.11
  561.0 1.7 copy-start.14
  561.0 2.8 copy-start.15

commit v4 on v3

--- a/solution.py
+++ b/solution.py
@@ -109,95 +109,6 @@
         return [(ins[0].at[1 - at.n], outs[0], at.x())], []
 
 
-class SumZ:
-    def __init__(self, array, by_rows):
-        self.by_rows, self.copies, self.locals = by_rows, 3, 0
-        rows, cols = array.shape
-        shape = (2, 4, rows // 8, cols) if by_rows else (4, rows // 4, cols)
-        self.ins = [array.reshape(shape)]
-        kept = (2, rows // 8, cols) if by_rows else (rows // 4, cols)
-        self.outs = [jax.ShapeDtypeStruct((3, *kept), array.dtype)]
-
-    def peers(self, at):
-        return [(f"z{k}", at.at_z(k)) for k in (1, 2, 3)]
-
-    def moves(self, at, ins, outs):
-        out = []
-        for k in (1, 2, 3):
-            q = lax.rem(at.z + k, 4)
-            src = ins[0].at[:, q] if self.by_rows else ins[0].at[q]
-            out.append((src, outs[0].at[k - 1], at.at_z(k)))
-        return out, []
-
-    def finish(self, outs):
-        z = lax.div(lax.axis_index("dp"), 2)
-        own = lax.dynamic_index_in_dim(self.ins[0], z, 1 if self.by_rows else 0, False)
-        return (own.astype(f32) + outs[0].astype(f32).sum(axis=0)).astype(bf16)
-
-
-class SumX:
-    def __init__(self, array, by_rows):
-        self.by_rows, self.copies, self.locals = by_rows, 3, 0
-        if by_rows:
-            two, rows, cols = array.shape
-            self.ins, kept = [array.reshape(2, 2, rows // 2, cols)], (rows // 2, cols)
-        else:
-            rows, cols = array.shape
-            self.ins, kept = [array.reshape(2, rows // 2, cols)], (rows // 2, HALF)
-        self.outs = [jax.ShapeDtypeStruct((3, *kept), array.dtype)]
-
-    order = ((0, 1), (1, 0), (1, 1))
-
-    def peers(self, at):
-        return [(f"x{a}{b}", at.at_x(a, b)) for a, b in self.order]
-
-    def moves(self, at, ins, outs):
-        out = []
-        for i, (a, b) in enumerate(self.order):
-            s, n = lax.rem(at.s + a, 2), lax.rem(at.n + b, 2)
-            src = ins[0].at[n, s] if self.by_rows else ins[0].at[s, :, at.half(n)]
-            out.append((src, outs[0].at[i], at.at_x(a, b)))
-        return out, []
-
-    def finish(self, outs):
-        s, n = lax.rem(lax.axis_index("dp"), 2), lax.axis_index("narrow")
-        if self.by_rows:
-            own = lax.dynamic_index_in_dim(lax.dynamic_index_in_dim(self.ins[0], n, 0, False), s, 0, False)
-        else:
-            own = lax.dynamic_slice_in_dim(lax.dynamic_index_in_dim(self.ins[0], s, 0, False), n * HALF, HALF, 1)
-        return (own.astype(f32) + outs[0].astype(f32).sum(axis=0)).astype(bf16)
-
-
-class Spread:
-    def __init__(self, array):
-        self.ins, self.copies, self.locals = [array], 7, 1
-        self.outs = [jax.ShapeDtypeStruct((8, *array.shape), array.dtype)]
-
-    def peers(self, at):
-        return [(f"d{k}", at.at_dp(k)) for k in range(1, 8)]
-
-    def moves(self, at, ins, outs):
-        dst = outs[0].at[at.dp]
-        return [(ins[0], dst, at.at_dp(k)) for k in range(1, 8)], [(ins[0], dst)]
-
-    def finish(self, outs):
-        eight, rows, cols = outs[0].shape
-        return outs[0].reshape(eight * rows, cols).astype(f32)
-
-
-class ToRing:
-    def __init__(self, array):
-        self.ins, self.copies, self.locals = [array], 7, 1
-        self.outs = [jax.ShapeDtypeStruct((8, *array.shape), array.dtype)]
-
-    def peers(self, at):
-        return [(f"w{k}", {"wide": lax.rem(at.w + k, 8)}) for k in range(1, 8)]
-
-    def moves(self, at, ins, outs):
-        dst = outs[0].at[at.w]
-        return [(ins[0], dst, peer) for _, peer in self.peers(at)], [(ins[0], dst)]
-
-
 class Trade:
     def __init__(self, array):
         self.ins, self.copies, self.locals = [array], 7, 1
@@ -214,30 +125,6 @@
         dst = outs[0].at[mine]
         far = [(ins[0].at[at.spot(lax.div(w, 2), lax.rem(w, 2))], dst, {"wide": w}) for w in self.others(at)]
         return far, [(ins[0].at[mine], dst)]
-
-
-class ToSpots(ToRing):
-    def moves(self, at, ins, outs):
-        dst = outs[0].at[at.spot(at.y, at.c)]
-        return [(ins[0], dst, peer) for _, peer in self.peers(at)], [(ins[0], dst)]
-
-
-class ToClips:
-    def __init__(self, array):
-        self.ins, self.copies, self.locals = [array], 15, 1
-        self.outs = [jax.ShapeDtypeStruct((8, 2, array.shape[0], HALF), array.dtype)]
-
-    order = tuple((k, b) for k in range(8) for b in range(2))[1:]
-
-    def peers(self, at):
-        return [(f"c{k}{b}", {**at.at_dp(k), "narrow": lax.rem(at.n + b, 2)}) for k, b in self.order]
-
-    def moves(self, at, ins, outs):
-        dst = outs[0].at[at.dp, at.n]
-        far = []
-        for (k, b), (_, peer) in zip(self.order, self.peers(at)):
-            far.append((ins[0].at[:, at.half(lax.rem(at.n + b, 2))], dst, peer))
-        return far, [(ins[0].at[:, at.half(at.n)], dst)]
 
 
 class Relay:
@@ -420,6 +307,106 @@
             copy.wait()
 
 
+class Reduce:
+    slots, locals_, deep = 10, 2, 96
+
+    @staticmethod
+    def scratch(x_first, by_rows=False):
+        deep = Reduce.deep
+        first = (4, deep, HALF) if x_first else (2, 2, deep, HALF) if by_rows else (2, deep, D)
+        return [VMEM((3, *first), bf16), VMEM(first, bf16), VMEM((3, deep, HALF), bf16), VMEM((2, deep, HALF), bf16)]
+
+    @staticmethod
+    def peers(at):
+        return [(f"z{k}", at.at_z(k)) for k in (1, 2, 3)] + [(f"x{a}{b}", at.at_x(a, b)) for a, b in ((0, 1), (1, 0), (1, 1))]
+
+    def __init__(self, at, src, out, refs, send, recv, local, base, place, x_first, by_rows=False):
+        self.at, self.src, self.out = at, src, out
+        self.land, self.total, self.land_two, self.last = refs
+        self.x_first, self.by_rows = x_first, by_rows
+        z_steps = [(at.at_z(k), lax.rem(at.z + k, 4)) for k in (1, 2, 3)]
+        x_steps = [
+            (at.at_x(a, b), (lax.rem(at.s + a, 2), lax.rem(at.n + b, 2))) for a, b in ((0, 1), (1, 0), (1, 1))
+        ]
+        first, second = (x_steps, z_steps) if x_first else (z_steps, x_steps)
+
+        def move(slot, source, target, peer):
+            return remote(source, target, send.at[base + slot], recv.at[base + slot], peer)
+
+        self.one = [move(i, self.piece(where), self.land.at[i], peer) for i, (peer, where) in enumerate(first)]
+        self.own = pltpu.make_async_copy(
+            self.piece((at.s, at.n) if x_first else at.z), self.total, local.at[place]
+        )
+        self.two = [move(3 + i, self.part(where), self.land_two.at[i], peer) for i, (peer, where) in enumerate(second)]
+        self.mine = at.z if x_first else (at.s, at.n)
+        self.three = move(6, self.last.at[at.s], self.last.at[at.s], at.at_x(1, 0))
+        target = out.at[at.z]
+        self.four = [move(7 + i, self.last, target, peer) for i, (peer, _) in enumerate(z_steps)]
+        self.stay = pltpu.make_async_copy(self.last, target, local.at[place + 1])
+
+    def piece(self, where):
+        if self.x_first:
+            s, n = where
+            return self.src.at[n, :, s] if self.by_rows else self.src.at[:, s, :, self.at.half(n)]
+        return self.src.at[:, where] if self.by_rows else self.src.at[where]
+
+    def part(self, where):
+        if self.x_first:
+            return self.total.at[where]
+        s, n = where
+        return self.total.at[n, s] if self.by_rows else self.total.at[s, :, self.at.half(n)]
+
+    def first(self):
+        for copy in self.one + [self.own]:
+            copy.start()
+
+    def second(self):
+        self.own.wait()
+        for copy in self.one:
+            copy.wait_recv()
+        lead = self.total.shape[:-2]
+        count = math.prod(lead)
+
+        def add(i, carry):
+            at_lead = (i,) if len(lead) == 1 else (lax.div(i, lead[1]), lax.rem(i, lead[1]))
+            for start in range(0, self.deep, 32):
+                where = (*at_lead, slice(start, start + 32))
+                got = self.total[where].astype(f32)
+                for k in range(3):
+                    got += self.land[(k, *where)].astype(f32)
+                self.total[where] = got.astype(bf16)
+            return carry
+
+        lax.fori_loop(0, count, add, 0)
+        for copy in self.two:
+            copy.start()
+
+    def third(self):
+        for copy in self.two:
+            copy.wait_recv()
+        own = self.part(self.mine)
+        s = self.at.s
+        for start in range(0, self.deep, 32):
+            rows = slice(start, start + 32)
+            got = own[rows].astype(f32)
+            for k in range(3):
+                got += self.land_two[k, rows].astype(f32)
+            self.last[s, rows] = got.astype(bf16)
+        self.three.start()
+
+    def fourth(self):
+        self.three.wait_recv()
+        for copy in self.four + [self.stay]:
+            copy.start()
+
+    def end(self):
+        for copy in self.four:
+            copy.wait()
+        for copy in self.one + self.two + [self.three]:
+            copy.wait_send()
+        self.stay.wait()
+
+
 class Gather:
     slots = 11
 
@@ -516,13 +503,16 @@
             def _():
                 self.got(9, 10)
 
-            g = lax.div(s, 2)
-            off = g + lax.div(g, 2) - 2 * lax.div(g, 3)
-            work(s, at.rows(lax.rem(at.y + off, 4), lax.rem(at.c + s, 2)))
+            work(s, self.place(s))
             return carry
 
         lax.fori_loop(0, 8, step, 0)
         self.end()
+
+    def place(self, s):
+        g = lax.div(s, 2)
+        off = g + lax.div(g, 2) - 2 * lax.div(g, 3)
+        return self.at.rows(lax.rem(self.at.y + off, 4), lax.rem(self.at.c + s, 2))
 
 
 class Scatter:
@@ -715,16 +705,31 @@
         gather.begin()
         at.start_beside()
         keep = Keep(whole, all_rows, local, 6)
-        gather.each(keep.block)
-        for copy in stay[1:]:
-            copy.wait()
-        for copy in go[1:]:
-            copy.wait_recv()
-
-        def times(rows, carry):
+
+        def times(rows):
             qkv[rows] = dot_flip(whole[rows], weight[...]).astype(bf16)
 
-        by_rows(D, BLOCK, times)
+        def work(s, rows):
+            keep.block(s, rows)
+
+            @pl.when(s == 4)
+            def _():
+                for copy in stay[1:]:
+                    copy.wait()
+                for copy in go[1:]:
+                    copy.wait_recv()
+
+            @pl.when(s >= 4)
+            def _():
+                times(rows)
+
+        gather.each(work)
+
+        def rest(s, carry):
+            times(gather.place(s))
+            return carry
+
+        lax.fori_loop(0, 4, rest, 0)
         keep.wait()
         for copy in go:
             copy.wait_send()
@@ -945,11 +950,20 @@
     return results
 
 
-def backward_rest(number, grad, expand_w, after, middle, vectors, down, keys, values, weights, normed_two, out_w, beside):
+def backward_rest(
+    number, grad, expand_w, after, middle, vectors, down, keys, values, weights, normed_two, out_w, contract_sum, expand_sum, beside
+):
     def body(at, ins, outs, kept):
-        grad, expand_own, expand_got, after, middle, vectors, down, keys, values, weights, normed_two, out_own, out_got = ins
-        grad_rows, rounded_two, grad_scores, all_two, all_rows, grad_mixed, grad_vectors = outs
+        grad, expand_own, expand_got, after, middle, vectors, down, keys, values, weights, normed_two, out_own, out_got = ins[:13]
+        grad_rows, rounded_two, grad_scores, all_two, all_rows, grad_mixed, grad_vectors = outs[:7]
         *refs, rounded, whole, second, out_full, expand_full, key_full, value_full, send, recv, local = kept
+        reduces = [
+            Reduce(at, ins[13], outs[7], refs[7:11], send, recv, local, 32, 16, False),
+            Reduce(at, ins[14], outs[8], refs[11:15], send, recv, local, 42, 18, True, True),
+        ]
+        refs = refs[:7]
+        for reduce in reduces:
+            reduce.first()
         weight = Whole(at, expand_own, expand_got, expand_full, local.at[pl.ds(0, 2)], 0)
         later = [
             pltpu.make_async_copy(keys, key_full, local.at[2]),
@@ -967,6 +981,8 @@
         scatter.arrive()
         before = Gather(at, normed_two, all_two, send, recv, local.at[6], 10)
         before.begin()
+        for reduce in reduces:
+            reduce.second()
 
         def norm_three(rows, carry):
             incoming = scatter.total(rows)
@@ -1006,6 +1022,9 @@
 
         lax.fori_loop(0, 8, cross, 0)
 
+        for reduce in reduces:
+            reduce.third()
+
         def norm_two(rows, carry):
             incoming = second[rows]
             centred, factor = standard(middle[rows])
@@ -1019,6 +1038,8 @@
         grad_vectors[3:4] = shifts
         gather = Gather(at, rounded, whole, send, recv, local.at[7], 21)
         gather.begin()
+        for reduce in reduces:
+            reduce.fourth()
         before.pass_far()
         keep = Keep(whole, all_rows, local, 8)
 
@@ -1031,11 +1052,13 @@
         before.end()
         keep.wait()
         scatter.end()
+        for reduce in reduces:
+            reduce.end()
 
     return call(
         body,
         number,
-        [grad, *expand_w, after, middle, vectors, down, keys, values, weights, normed_two, *out_w],
+        [grad, *expand_w, after, middle, vectors, down, keys, values, weights, normed_two, *out_w, contract_sum, expand_sum],
         [
             shape(BLOCK, D, dtype=f32),
             shape(BLOCK, D),
@@ -1044,9 +1067,13 @@
             shape(D, D),
             shape(D, COLS),
             shape(8, D, dtype=f32),
+            shape(4, 2, Reduce.deep, HALF),
+            shape(4, 2, Reduce.deep, HALF),
         ],
         [
             *Scatter.scratch,
+            *Reduce.scratch(False),
+            *Reduce.scratch(True, True),
             VMEM((BLOCK, D), bf16),
             VMEM((D, D), bf16),
             VMEM((BLOCK, D), f32),
@@ -1054,12 +1081,12 @@
             VMEM((D, HALF), bf16),
             VMEM((D, D), bf16),
             VMEM((D, D), bf16),
-            *sems(32),
+            *sems(52),
         ],
         beside,
-        ring_peers,
-        spaces=[VMEM, ANY, ANY, VMEM, VMEM, VMEM, VMEM, ANY, ANY, VMEM, VMEM, ANY, ANY],
-        out_spaces=[VMEM, VMEM, VMEM, ANY, ANY, VMEM, VMEM],
+        lambda at: ring_peers(at) + Reduce.peers(at),
+        spaces=[VMEM, ANY, ANY, VMEM, VMEM, VMEM, VMEM, ANY, ANY, VMEM, VMEM, ANY, ANY, ANY, ANY],
+        out_spaces=[VMEM, VMEM, VMEM, ANY, ANY, VMEM, VMEM, ANY, ANY],
     )
 
 
@@ -1144,16 +1171,83 @@
     )
 
 
-def leave(number, grad, joined, x, vectors, grad_rows, beside):
+def leave(number, grad, joined, x, vectors, grad_rows, sums, late, text_part, beside):
     relay = Relay(jax.ShapeDtypeStruct((BLOCK, D), bf16), True)
+    some = 64 // 8
+
+    def ring(at):
+        return [{"wide": lax.rem(at.w + k, 8)} for k in range(1, 8)]
+
+    def clips(at):
+        return [(k, b, {**at.at_dp(k), "narrow": lax.rem(at.n + b, 2)}) for k in range(8) for b in range(2)][1:]
+
+    def group(at):
+        return [(b, {"wide": lax.rem(at.w + k, 8), "narrow": lax.rem(at.n + b, 2)}) for k in range(8) for b in range(2)][1:]
+
+    def peers(at):
+        known = ring_peers(at) + relay.peers(at) + Reduce.peers(at)
+        known += [(f"r{i}", peer) for i, peer in enumerate(ring(at))]
+        known += [(f"c{i}", peer) for i, (_, _, peer) in enumerate(clips(at))]
+        return known + [(f"g{i}", peer) for i, (_, peer) in enumerate(group(at))]
 
     def body(at, ins, outs, kept):
-        grad, weight, x, vectors, before = ins
-        result, grad_vectors = outs
-        *refs, rounded, send, recv, local = kept
+        grad, weight, x, vectors, before, late, text, one, two = ins
+        result, out_one, out_two, vector_sums, text_out = outs
+        refs, kept = kept[:7], kept[7:]
+        reduces = [
+            Reduce(at, one, out_one, kept[0:4], kept[-3], kept[-2], kept[-1], 12, 1, False),
+            Reduce(at, two, out_two, kept[4:8], kept[-3], kept[-2], kept[-1], 22, 3, True),
+        ]
+        rounded, parts, ring_parts, ring_sum, clip_parts, text_parts, text_sum, send, recv, local = kept[8:]
+        me = at.spot(at.y, at.c)
+
+        def move(slot, source, target, peer):
+            return remote(source, target, send.at[slot], recv.at[slot], peer)
+
+        to_ring, to_clips, to_group = ring(at), clips(at), group(at)
+        slot = 32
+        trades = []
+        for peer in to_ring:
+            there = at.spot(lax.div(peer["wide"], 2), lax.rem(peer["wide"], 2))
+            trades.append(move(slot, text.at[there], text_parts.at[me], peer))
+            slot += 1
+        text_own = pltpu.make_async_copy(text.at[me], text_parts.at[me], local.at[5])
+        texts = []
+        for b, peer in to_group:
+            n = lax.rem(at.n + b, 2)
+            texts.append(move(slot, text_sum.at[:, at.half(n)], text_out.at[at.n, me], peer))
+            slot += 1
+        text_stay = pltpu.make_async_copy(text_sum.at[:, at.half(at.n)], text_out.at[at.n, me], local.at[6])
+        rings = []
+        for peer in to_ring:
+            rings.append(move(slot, parts, ring_parts.at[at.w], peer))
+            slot += 1
+        ring_own = pltpu.make_async_copy(parts, ring_parts.at[at.w], local.at[7])
+        spreads = []
+        for _, b, peer in to_clips:
+            n = lax.rem(at.n + b, 2)
+            spreads.append(move(slot, ring_sum.at[:, at.half(n)], clip_parts.at[at.dp, at.n], peer))
+            slot += 1
+        clip_own = pltpu.make_async_copy(ring_sum.at[:, at.half(at.n)], clip_parts.at[at.dp, at.n], local.at[8])
+
+        for reduce in reduces:
+            reduce.first()
+        text_own.start()
+        for copy in trades:
+            copy.start()
         scatter = Scatter(at, send, recv, refs)
         scatter.products(lambda rows: dot(grad[rows], weight[...]))
         scatter.middle()
+        text_own.wait()
+        for copy in trades:
+            copy.wait_recv()
+        total = text_parts[0].astype(f32)
+        for i in range(1, 8):
+            total += text_parts[i].astype(f32)
+        text_sum[...] = total.astype(bf16)
+        text_stay.start()
+        for copy in texts:
+            copy.start()
         scatter.arrive()
 
         def norm(rows, carry):
@@ -1166,20 +1260,75 @@
         gains, shifts = by_rows(BLOCK, 32, norm, no_sums())
         moving = functools.partial(relay_run, relay, at, rounded, result, send, recv, local.at[0], 10)
         moving(False)
-        grad_vectors[0:1] = gains
-        grad_vectors[1:2] = shifts
+        parts[0:1] = gains
+        parts[1:2] = shifts
+        parts[2:6] = late[2:6]
+        parts[6:8] = jnp.zeros((2, D), f32)
+        ring_own.start()
+        for copy in rings:
+            copy.start()
+        for reduce in reduces:
+            reduce.second()
+        ring_own.wait()
+        for copy in rings:
+            copy.wait_recv()
+        total = ring_parts[0]
+        for i in range(1, 8):
+            total += ring_parts[i]
+        ring_sum[...] = total
+        clip_own.start()
+        for copy in spreads:
+            copy.start()
+        for reduce in reduces:
+            reduce.third()
+        for reduce in reduces:
+            reduce.fourth()
+        clip_own.wait()
+        for copy in spreads:
+            copy.wait_recv()
+        total = clip_parts[0, 0] + clip_parts[0, 1]
+        for i in range(1, 8):
+            total += clip_parts[i, 0] + clip_parts[i, 1]
+        vector_sums[...] = total
         moving(True)
+        text_stay.wait()
+        for copy in texts:
+            copy.wait()
+        for copy in trades + rings + spreads:
+            copy.wait_send()
         scatter.end()
-
+        for reduce in reduces:
+            reduce.end()
+
+    deep = Reduce.deep
     return call(
         body,
         number,
-        [grad, joined, x, vectors, grad_rows],
-        [shape(384, HALF), shape(8, D, dtype=f32)],
-        [*Scatter.scratch, VMEM((BLOCK, D), bf16), *sems(12)],
+        [grad, joined, x, vectors, grad_rows, late, text_part, *sums],
+        [
+            shape(384, HALF),
+            shape(4, 2, deep, HALF),
+            shape(4, 2, deep, HALF),
+            shape(8, HALF, dtype=f32),
+            shape(2, 8, some, HALF),
+        ],
+        [
+            *Scatter.scratch,
+            *Reduce.scratch(False),
+            *Reduce.scratch(True),
+            VMEM((BLOCK, D), bf16),
+            VMEM((8, D), f32),
+            VMEM((8, 8, D), f32),
+            VMEM((8, D), f32),
+            VMEM((8, 2, 8, HALF), f32),
+            VMEM((8, some, D), bf16),
+            VMEM((some, D), bf16),
+            *sems(32 + 7 + 15 + 7 + 15),
+        ],
         beside,
-        lambda at: ring_peers(at) + relay.peers(at),
-        out_spaces=[ANY, VMEM],
+        peers,
+        spaces=[VMEM, VMEM, VMEM, VMEM, VMEM, VMEM, ANY, ANY, ANY],
+        out_spaces=[ANY, ANY, ANY, VMEM, ANY],
     )
 
 
@@ -1229,9 +1378,10 @@
         3, attended, out_w, x, vectors, all_keys, all_values, down, expand_w, contract_weight
     )
 
-    contract_leg = SumZ(outer(activated, all_down).astype(bf16), False)
-    expand_leg = SumZ(outer(all_three, grad_expand).astype(bf16), True)
-    (grad_one, rounded_two, grad_scores, all_two, all_mid_one, grad_attended, late), sums = backward_rest(
+    deep = Reduce.deep
+    contract_part = outer(activated, all_down).astype(bf16).reshape(4, 2, deep, D)
+    expand_part = outer(all_three, grad_expand).astype(bf16).reshape(2, 4, 2, deep, HALF)
+    results, ((cross_p,),) = backward_rest(
         4,
         grad_expand,
         expand_w,
@@ -1244,25 +1394,16 @@
         cross_p,
         normed_two,
         out_w,
-        [contract_leg, expand_leg, Trade(cross_p)],
+        contract_part,
+        expand_part,
+        [Trade(cross_p)],
     )
-    contract_sum, expand_sum, (cross_p,) = sums
-    contract_leg, expand_leg = SumX(contract_leg.finish(contract_sum), False), SumX(expand_leg.finish(expand_sum), True)
-    output_leg = SumZ(outer(attended, all_mid_one).astype(bf16), False)
-    (grad_qkv, layer_output, all_mid_two), sums = causal_backward(
-        5,
-        qkv,
-        grad_attended,
-        logs,
-        activated,
-        contract,
-        after,
-        rounded_two,
-        [contract_leg, expand_leg, output_leg, Trade(grad_scores)],
+    grad_one, rounded_two, grad_scores, all_two, all_mid_one, grad_attended, late, contract_grad, expand_grad = results
+    (grad_qkv, layer_output, all_mid_two), ((grad_scores,), (pair_got,)) = causal_backward(
+        5, qkv, grad_attended, logs, activated, contract, after, rounded_two, [Trade(grad_scores), Give(pair_t)]
     )
-    contract_sum, expand_sum, output_sum, (grad_scores,) = sums
-
-    joined_leg = SumZ(outer(grad_qkv, all_one).astype(bf16), False)
+
+    joined_part = jnp.concatenate((outer(grad_qkv, all_one), outer(attended, all_mid_one)), axis=0)
     grad_keys = outer(grad_scores.reshape(D, COLS), all_two).astype(bf16).reshape(HEADS, 64, D)
     grad_values = outer(cross_p.reshape(D, COLS), all_mid_two).astype(bf16).reshape(HEADS, 64, D)
     own_first = n == 0
@@ -1283,37 +1424,24 @@
     grad_pair = jnp.stack((grad_text_keys, grad_text_values), axis=1).reshape(64, 2 * COLS).astype(bf16)
     grad_query = heads("khd,hkf->hdf", text_heads[:, 0], grad_keys).reshape(COLS, D) * EIGHTH
     grad_cross = heads("khd,hkf->hdf", text_heads[:, 1], grad_values).reshape(COLS, D)
-    cross_leg = SumZ(jnp.concatenate((grad_query, outer(grad_pair, text), grad_cross), axis=0).astype(bf16), False)
-
-    contract_leg, expand_leg = Spread(contract_leg.finish(contract_sum)), Spread(expand_leg.finish(expand_sum))
-    output_leg = SumX(output_leg.finish(output_sum), False)
-    (input_grad, first), sums = leave(
+    cross_part = jnp.concatenate((grad_query, outer(grad_pair, text), grad_cross), axis=0)
+    text_part = dot(grad_pair, whole(pair_t, pair_got)).astype(bf16).reshape(8, 8, D)
+
+    (input_grad, joined_grad, cross_grad, parts, text_grad), ((layer_output,),) = leave(
         6,
         grad_qkv,
         joined,
         x,
         vectors,
         grad_one,
-        [joined_leg, cross_leg, contract_leg, expand_leg, output_leg, Relay(layer_output, True), Give(grad_pair)],
+        [part.astype(bf16).reshape(4, 2, deep, D) for part in (joined_part, cross_part)],
+        late,
+        text_part,
+        [Relay(layer_output, True)],
     )
-    joined_sum, cross_sum, contract_sum, expand_sum, output_sum, (layer_output,), (grad_pair_got,) = sums
-    contract_grad, expand_grad = contract_leg.finish(contract_sum), expand_leg.finish(expand_sum)
-    parts = jnp.concatenate((first[0:2], late[2:6], jnp.zeros((2, D), f32)), axis=0)
-    pairs = jnp.concatenate((jnp.where(own_first, grad_pair, grad_pair_got), jnp.where(own_first, grad_pair_got, grad_pair)), axis=0)
-    text_part = dot(pairs, pair_t).astype(bf16).reshape(8, 16, HALF)
-    joined_leg, cross_leg = SumX(joined_leg.finish(joined_sum), False), SumX(cross_leg.finish(cross_sum), False)
-    output_leg = Spread(output_leg.finish(output_sum))
-    _, (joined_sum, cross_sum, output_sum, (parts,), (text_part,)) = call(
-        None, 7, [], [], (), [joined_leg, cross_leg, output_leg, ToRing(parts), Trade(text_part)]
+    joined_grad, cross_grad, expand_grad, contract_grad = (
+        grad.reshape(HALF, HALF).astype(f32) for grad in (joined_grad, cross_grad, expand_grad, contract_grad)
     )
-    output_grad = output_leg.finish(output_sum)
-    joined_leg, cross_leg = Spread(joined_leg.finish(joined_sum)), Spread(cross_leg.finish(cross_sum))
-    text_part = jnp.sum(text_part.astype(f32), axis=0).astype(bf16)
-    _, (joined_sum, cross_sum, (parts,), (text_grad,)) = call(
-        None, 8, [], [], (), [joined_leg, cross_leg, ToClips(jnp.sum(parts, axis=0)), ToSpots(text_part)]
-    )
-    joined_grad, cross_grad = joined_leg.finish(joined_sum), cross_leg.finish(cross_sum)
-    parts = jnp.sum(parts, axis=(0, 1))
     return (
         layer_output,
         input_grad.astype(f32),
@@ -1322,8 +1450,8 @@
         parts[1],
         joined_grad[:COLS].T,
         joined_grad[COLS : 2 * COLS].T,
-        joined_grad[2 * COLS :].T,
-        output_grad,
+        joined_grad[2 * COLS : 3 * COLS].T,
+        joined_grad[3 * COLS :],
         parts[2],
         parts[3],
         cross_grad[:COLS].T,

time: 572 us -> 507 us (0.89)
  Pallas kernels: 476 us -> 442 us
  other arithmetic: 33.3 us -> 12.6 us
  matrix products: 36.2 us -> 28.8 us
    pallas_call x8 -> x6, Pallas kernels: 476 us -> 442 us  [call(): pl.pallas_call(kernel, out_shape=tuple(outs) + tuple(side_outs), in_specs...]
    convert_element_type x14 -> x1, other arithmetic: 18 us -> 4.23 us  [on_device(): grad.reshape(HALF, HALF).astype(f32)]
    reduce_sum x12 -> x0, other arithmetic: 7.83 us -> none  [the longest x9 6.52 us: finish(): return (own.astype(f32) + outs[0].astype(f32).sum(axis=0)).astype(bf16)]
    dot_general x7, matrix products: 32 us -> 24.5 us  [outer(): lax.dot_general(a, b, (((0,), (0,)), ((), ())), preferred_element_type=f32)]
where the time goes in v4:
time: 507 us; the launch traced here: 499 us
  Pallas kernels  442 us (87%)
  matrix products  28.8 us (6%)
  local copies, waits for them, and re-layouts  13.3 us (3%)
  other arithmetic  12.6 us (2%)
    pallas_call x6, Pallas kernels, call(): pl.pallas_call(kernel, out_shape=tuple(outs) + tuple(side_outs), in_specs...  442 us
    dot_general x7, matrix products, outer(): lax.dot_general(a, b, (((0,), (0,)), ((), ())), preferred_element_type=f32)  24.5 us

profile of v4, /device:TPU:0, one launch (start us, length us, event | category | flops | bytes accessed | tf_op | source)
XLA Modules:
  0.0 498.7 jit_solution(4737286452663353728)
XLA Ops:
  0.7 2.1 fusion.14
  2.8 0.7 stack.33
  3.5 0.7 stack.34
  4.2 0.7 stack.35
  4.9 0.7 stack.36
  5.5 0.7 stack.37
  6.2 0.7 stack.38
  7.6 58.9 %shard_map.330 = (bf16[192,1536]{1,0:T(8,128)(2,1)}, f32[8,1536]{1,0:T(8,128)}, bf16[576,1536]{1,0:T(8,128)(2,1)}, bf16[1536,1536]{1,0:T(8,128)(2,1)}, bf16[1536...) custom-call(bf16[384,768]{1,0:T(8,128)(2,1)} %refs_0_.1, ...), custom_call_target="tpu_custom_call" | custom-call | tf_op jit(solution)/shard_map/pallas_call | solution.py:256
  66.5 1.5 fusion.11.refs_5_
  68.0 57.5 %shard_map.331 = (bf16[1536,192]{1,0:T(8,128)(2,1)}, f32[8,1536]{1,0:T(8,128)}, bf16[1536,1536]{1,0:T(8,128)(2,1)}, bf16[1536,1536]{1,0:T(8,128)(2,1)}, bf16[192...) custom-call(bf16[1536,576]{1,0:T(8,128)(2,1)} %get-tuple-element.65.refs_0_, ...), custom_call_target="tpu_custom_call" | custom-call | tf_op jit(solution)/shard_map/pallas_call | solution.py:256
  125.5 82.0 %shard_map.332 = (f32[192,1536]{1,0:T(8,128)}, f32[192,1536]{1,0:T(8,128)}, bf16[192,1536]{1,0:T(8,128)(2,1)}, bf16[8,192,192]{2,1,0:T(8,128)(2,1)}, bf16[1536,1...) custom-call(bf16[1536,192]{1,0:T(8,128)(2,1)} %get-tuple-element.69., ...), custom_call_target="tpu_custom_call" | custom-call | tf_op jit(solution)/shard_map/pallas_call | solution.py:256
  207.5 8.5 %convolution_convert_fusion = bf16[1536,768]{1,0:T(8,128)(2,1)} fusion(bf16[1536,1536]{1,0:T(8,128)(2,1)} %get-tuple-element.84, bf16[1536,768]{1,0:T(8,128)(2,1)} %get-tuple-element.77.refs_0_), kind=kOutput, calls=%fused_computation | convolution fusion | flops 3625058304 | bytes 9437184 | tf_op jit(solution)/shard_map/dot_general | solution.py:36
  216.1 5.1 %convolution_convert_fusion.1 = bf16[768,1536]{1,0:T(8,128)(2,1)} fusion(bf16[1536,768]{1,0:T(8,128)(2,1)S(1)} %copy-done.3, bf16[1536,1536]{1,0:T(8,128)(2,1)S(1)} %copy-done.20), kind=kOutput, calls=%fused_computation.1 | convolution fusion | flops 3625058304 | bytes 9437184 | tf_op jit(solution)/shard_map/dot_general | solution.py:36
  221.2 92.3 %shard_map.333 = (f32[192,1536]{1,0:T(8,128)}, bf16[192,1536]{1,0:T(8,128)(2,1)}, bf16[8,192,192]{2,1,0:T(8,128)(2,1)}, bf16[1536,1536]{1,0:T(8,128)(2,1)}, bf16...) custom-call(bf16[1536,768]{1,0:T(8,128)(2,1)} %get-tuple-element.77., ...), custom_call_target="tpu_custom_call" | custom-call | tf_op jit(solution)/shard_map/pallas_call | solution.py:256
  313.5 4.2 bitcast_convert_fusion
  317.8 0.9 pad_maximum_fusion.2.refs_8_
  318.6 59.0 %shard_map.334 = (bf16[1536,576]{1,0:T(8,128)(2,1)}, bf16[192,1536]{1,0:T(8,128)(2,1)}, bf16[1536,1536]{1,0:T(8,128)(2,1)}, bf16[8,192,192]{2,1,0:T(8,128)(2,1)}, bf16[384,768]{1,0:T(8,128)(2,1)}) custom-call(bf16[1536,576]{1,0:T(8,128)(2,1)} %get-tuple-element.65.refs_0_, bf16[1536,192]{1,0:T(8,128)(2,1)} %get-tuple-element.85.refs_1_, ...), custom_call_target="tpu_custom_call" | custom-call | tf_op jit(solution)/shard_map/pallas_call | solution.py:256
  377.6 3.8 convolution_convert_fusion.7
  382.4 1.9 copy-done.19
  384.2 2.5 convolution_convert_fusion.6
  388.5 1.6 pad_maximum_fusion.1
  390.1 0.8 copy-done.4
  390.9 2.9 convolution_convert_fusion.2
  393.9 1.1 convolution_convert_fusion.5
  395.0 1.6 pad_maximum_fusion
  396.8 1.0 fusion.1.refs_6_
  397.9 92.8 %shard_map.335 = (bf16[384,768]{1,0:T(8,128)(2,1)}, bf16[4,2,96,768]{3,2,1,0:T(8,128)(2,1)}, bf16[4,2,96,768]{3,2,1,0:T(8,128)(2,1)}, f32[8,768]{1,0:T(8,128)}, ...) custom-call(bf16[1536,576]{1,0:T(8,128)(2,1)} %get-tuple-element.90.refs_0_, ...), custom_call_target="tpu_custom_call" | custom-call | tf_op jit(solution)/shard_map/pallas_call | solution.py:256
  490.7 2.8 fusion.16
  493.5 1.4 fusion.15
  494.9 1.1 convert_element_type.71
  496.0 0.8 bitcast_convert_fusion.2
  497.4 0.8 copy.44
  (65 shorter events, 4.1 us)
Async XLA Ops:
  2.8 63.7 %copy-start.15 = (f32[384,128]{0,1:T(8,128)S(1)}, f32[384,128]{0,1:T(8,128)}, u32[]{:S(2)}) copy-start(f32[384,128]{0,1:T(8,128)} %fusion.14) | copy-start | bytes 589828
  207.5 8.6 %copy-start.3 = (bf16[1536,768]{1,0:T(8,128)(2,1)S(1)}, bf16[1536,768]{1,0:T(8,128)(2,1)}, u32[]{:S(2)}) copy-start(bf16[1536,768]{1,0:T(8,128)(2,1)} %get-tuple-element.82.refs_3_) | copy-start | bytes 7077892
  207.5 8.6 %copy-start.20 = (bf16[1536,1536]{1,0:T(8,128)(2,1)S(1)}, bf16[1536,1536]{1,0:T(8,128)(2,1)}, u32[]{:S(2)}) copy-start(bf16[1536,1536]{1,0:T(8,128)(2,1)} %get-tuple-element.83) | copy-start | bytes 14155780
  313.5 4.3 copy-start.7
  313.5 4.2 copy-start.8
  377.6 3.8 copy-start.13
  377.6 4.3 copy-start.1
  377.6 4.3 copy-start.2
  377.6 4.3 copy-start.5
  377.6 4.3 copy-start.6
  381.9 2.3 copy-start.19
  382.0 8.1 %slice-start = ((s8[4718592]{0:T(1024)(128)(4,1)}), s8[4194304]{0:T(1024)(128)(4,1)S(1)}, s32[]{:S(2)}) async-start(s8[4718592]{0:T(1024)(128)(4,1)} %bitcast.137), calls=%async_computation | async-start | bytes 8388608
  386.8 0.9 copy-start.14
  386.8 1.0 copy-start.17
  386.8 3.3 slice-start.1
  388.5 2.4 copy-start.4
  388.5 5.3 %slice-start.2 = ((s8[4718592]{0:T(1024)(128)(4,1)}), s8[4194304]{0:T(1024)(128)(4,1)S(1)}, s32[]{:S(2)}) async-start(s8[4718592]{0:T(1024)(128)(4,1)} %bitcast.139), calls=%async_computation.2 | async-start | bytes 8388608
  390.9 3.0 copy-start.9
  390.9 3.0 slice-start.3
  395.0 1.6 copy-start.10
  490.7 2.8 copy-start
  493.5 1.5 copy-start.11
  493.5 2.5 copy-start.16
  494.9 1.9 copy-start.18
  494.9 2.5 copy-start.12

commit v5 on v4

--- a/solution.py
+++ b/solution.py
@@ -125,6 +125,19 @@
         dst = outs[0].at[mine]
         far = [(ins[0].at[at.spot(lax.div(w, 2), lax.rem(w, 2))], dst, {"wide": w}) for w in self.others(at)]
         return far, [(ins[0].at[mine], dst)]
+
+
+class ToSpots:
+    def __init__(self, array):
+        self.ins, self.copies, self.locals = [array], 7, 1
+        self.outs = [jax.ShapeDtypeStruct((8, *array.shape), array.dtype)]
+
+    def peers(self, at):
+        return [(f"w{k}", {"wide": lax.rem(at.w + k, 8)}) for k in range(1, 8)]
+
+    def moves(self, at, ins, outs):
+        dst = outs[0].at[at.spot(at.y, at.c)]
+        return [(ins[0], dst, peer) for _, peer in self.peers(at)], [(ins[0], dst)]
 
 
 class Relay:
@@ -308,11 +321,8 @@
 
 
 class Reduce:
-    slots, locals_, deep = 10, 2, 96
-
     @staticmethod
-    def scratch(x_first, by_rows=False):
-        deep = Reduce.deep
+    def scratch(deep, x_first, by_rows=False):
         first = (4, deep, HALF) if x_first else (2, 2, deep, HALF) if by_rows else (2, deep, D)
         return [VMEM((3, *first), bf16), VMEM(first, bf16), VMEM((3, deep, HALF), bf16), VMEM((2, deep, HALF), bf16)]
 
@@ -324,6 +334,8 @@
         self.at, self.src, self.out = at, src, out
         self.land, self.total, self.land_two, self.last = refs
         self.x_first, self.by_rows = x_first, by_rows
+        self.deep = self.last.shape[1]
+        self.chunk = 32 if self.deep % 32 == 0 else 24
         z_steps = [(at.at_z(k), lax.rem(at.z + k, 4)) for k in (1, 2, 3)]
         x_steps = [
             (at.at_x(a, b), (lax.rem(at.s + a, 2), lax.rem(at.n + b, 2))) for a, b in ((0, 1), (1, 0), (1, 1))
@@ -369,8 +381,8 @@
 
         def add(i, carry):
             at_lead = (i,) if len(lead) == 1 else (lax.div(i, lead[1]), lax.rem(i, lead[1]))
-            for start in range(0, self.deep, 32):
-                where = (*at_lead, slice(start, start + 32))
+            for start in range(0, self.deep, self.chunk):
+                where = (*at_lead, slice(start, start + self.chunk))
                 got = self.total[where].astype(f32)
                 for k in range(3):
                     got += self.land[(k, *where)].astype(f32)
@@ -386,8 +398,8 @@
             copy.wait_recv()
         own = self.part(self.mine)
         s = self.at.s
-        for start in range(0, self.deep, 32):
-            rows = slice(start, start + 32)
+        for start in range(0, self.deep, self.chunk):
+            rows = slice(start, start + self.chunk)
             got = own[rows].astype(f32)
             for k in range(3):
                 got += self.land_two[k, rows].astype(f32)
@@ -515,6 +527,55 @@
         return self.at.rows(lax.rem(self.at.y + off, 4), lax.rem(self.at.c + s, 2))
 
 
+QUARTER = 384
+
+
+class GatherZ(Gather):
+    def __init__(self, at, quarter, full, send, recv, local, base=0):
+        self.at = at
+        z, up, down, far = at.z, lax.rem(at.z + 1, 4), lax.rem(at.z + 3, 4), lax.rem(at.z + 2, 4)
+        half = QUARTER
+
+        def move(slot, z_from, peer, start=0, size=2 * QUARTER, first=False):
+            rows = pl.ds(pl.multiple_of(at.c * 2 * QUARTER + start, QUARTER), size)
+            target = full.at[rows, self.columns(z_from)]
+            return remote(quarter.at[rows] if first else target, target, send.at[base + slot], recv.at[base + slot], peer)
+
+        to_up, to_down, core = at.at_z(1), at.at_z(3), at.core()
+        self.sends = {
+            0: move(0, z, to_up, 0, half, first=True),
+            1: move(1, z, to_up, half, half, first=True),
+            2: move(2, z, to_down, half, half, first=True),
+            3: move(3, z, to_down, 0, half, first=True),
+            5: move(5, down, to_up, 0, half),
+            6: move(6, up, to_down, half, half),
+            7: move(7, down, core),
+            8: move(8, up, core),
+            9: move(9, far, core, 0, half),
+            10: move(10, far, core, half, half),
+        }
+        self.own = pltpu.make_async_copy(quarter, full.at[:, self.columns(z)], local)
+
+    @staticmethod
+    def columns(z):
+        return pl.ds(pl.multiple_of(z * QUARTER, QUARTER), QUARTER)
+
+    @staticmethod
+    def peers(at):
+        return [("z1", at.at_z(1)), ("z3", at.at_z(3)), ("core", at.core())]
+
+    def begin(self):
+        for i in (0, 2, 1, 3):
+            self.sends[i].start()
+        self.own.start()
+
+    def end(self):
+        self.got(7, 8, 9, 10)
+        self.own.wait()
+        for copy in self.sends.values():
+            copy.wait_send()
+
+
 class Scatter:
     slots = 10
     scratch = [
@@ -672,15 +733,33 @@
             pltpu.make_async_copy(self.whole.at[some], self.out.at[some], self.sem.at[self.base + s]).wait()
 
 
-def enter(number, layer_input, vectors, weights, beside):
+def enter(number, layer_input, vectors, weights, query_t, cross_out, beside):
     relay = Relay(layer_input)
 
     def body(at, ins, outs, kept):
-        (source, own_vectors, *own_weights), (x, vectors, weight, all_rows, qkv) = ins, outs
-        normed, whole, send, recv, local = kept
+        source, own_vectors, *own_weights, query_own, out_own = ins
+        x, vectors, weight, all_rows, qkv, query_all, out_quarter = outs
+        normed, whole, query_part, out_part, query_quarter, send, recv, local = kept
         half = at.half(at.n)
         moving = functools.partial(relay_run, relay, at, source, x, send, recv, local.at[0], 11)
         moving(False)
+        columns = GatherZ.columns(lax.rem(at.z, 2))
+        holds = at.n == lax.div(at.z, 2)
+        quarters = []
+        for i, (own, part) in enumerate(((query_own, query_part), (out_own, out_part))):
+            quarters.append(
+                (
+                    pltpu.make_async_copy(own.at[:, columns], part, local.at[14 + i]),
+                    remote(own.at[:, columns], part, send.at[17 + i], recv.at[17 + i], at.x()),
+                )
+            )
+
+        @pl.when(holds)
+        def _():
+            for stay, go in quarters:
+                go.start()
+                stay.start()
+
         stay, go = [], []
         for i, (own, target) in enumerate(
             [(own_vectors, vectors.at[:, half])]
@@ -690,11 +769,28 @@
             go.append(remote(own, target, send.at[13 + i], recv.at[13 + i], at.x()))
         stay[0].start()
         go[0].start()
+
+        @pl.when(holds)
+        def _():
+            for near, far in quarters:
+                near.wait()
+                far.wait_send()
+
+        @pl.when(jnp.logical_not(holds))
+        def _():
+            for near, far in quarters:
+                far.wait_recv()
+
+        queries = Gather(at, query_part, query_quarter, send, recv, local.at[16], 19)
+        outputs = Gather(at, out_part, out_quarter, send, recv, local.at[17], 30)
+        queries.begin()
         stay[0].wait()
         go[0].wait_recv()
         moving(True)
         for copy in stay[1:] + go[1:]:
             copy.start()
+        queries.pass_on()
+        queries.pass_near()
 
         def norm(rows, carry):
             centred, _ = standard(x[rows].astype(f32))
@@ -703,6 +799,10 @@
         by_rows(BLOCK, 32, norm)
         gather = Gather(at, normed, whole, send, recv, local.at[5])
         gather.begin()
+        queries.pass_far()
+        queries.got(4, 7, 8, 9, 10)
+        around = GatherZ(at, query_quarter, query_all, send, recv, local.at[18], 41)
+        around.begin()
         at.start_beside()
         keep = Keep(whole, all_rows, local, 6)
 
@@ -723,46 +823,68 @@
             def _():
                 times(rows)
 
+            @pl.when(s == 6)
+            def _():
+                outputs.begin()
+                around.pass_on()
+
         gather.each(work)
+        around.pass_near()
+        outputs.pass_on()
+        outputs.pass_near()
 
         def rest(s, carry):
             times(gather.place(s))
             return carry
 
         lax.fori_loop(0, 4, rest, 0)
+        outputs.pass_far()
+        around.pass_far()
+        outputs.got(4, 7, 8, 9, 10)
         keep.wait()
         for copy in go:
             copy.wait_send()
+        outputs.end()
+        queries.end()
+        around.end()
 
     return call(
         body,
         number,
-        [layer_input, vectors, *weights],
-        [shape(BLOCK, D), shape(8, D, dtype=f32), shape(3 * COLS, D), shape(D, D), shape(D, 3 * COLS)],
-        [VMEM((BLOCK, D), bf16), VMEM((D, D), bf16), *sems(17)],
+        [layer_input, vectors, *weights, query_t, cross_out],
+        [
+            shape(BLOCK, D),
+            shape(8, D, dtype=f32),
+            shape(3 * COLS, D),
+            shape(D, D),
+            shape(D, 3 * COLS),
+            shape(D, D),
+            shape(D, QUARTER),
+        ],
+        [
+            VMEM((BLOCK, D), bf16),
+            VMEM((D, D), bf16),
+            VMEM((COLS, QUARTER), bf16),
+            VMEM((COLS, QUARTER), bf16),
+            VMEM((D, QUARTER), bf16),
+            *sems(52),
+        ],
         beside,
-        lambda at: ring_peers(at) + relay.peers(at) + [("x", at.x())],
-        out_spaces=[VMEM, VMEM, VMEM, ANY, VMEM],
+        lambda at: ring_peers(at) + relay.peers(at) + [("x", at.x())] + GatherZ.peers(at),
+        out_spaces=[VMEM, VMEM, VMEM, ANY, VMEM, ANY, VMEM],
         late=True,
     )
 
 
-def causal_forward(number, joined, query_w, out_w, text_pair, beside):
+def causal_forward(number, joined, down, out_quarter, beside):
     at_once = 512
 
     def body(at, ins, outs, kept):
-        (qkv, query_own, query_got, out_own, out_got, pair), (out, logs, all_keys, all_values) = ins, outs
-        parts, mixed, keys, values, send, recv, local = kept
-        half, other = at.half(at.n), at.half(1 - at.n)
-        for own, got, target, axis in ((query_own, query_got, keys, 0), (out_own, out_got, values, 1)):
-            for cols, ref in ((half, own), (other, got)):
-                for h in range(HEADS):
-                    rows = slice(h * HDIM, (h + 1) * HDIM)
-                    text = pair[:, axis * COLS + h * HDIM : axis * COLS + (h + 1) * HDIM]
-                    product = dot(text, ref[rows, :])
-                    target[rows, cols] = (product * EIGHTH if axis == 0 else product).astype(bf16)
-        first = Gather(at, keys, all_keys, send, recv, local.at[0])
-        second = Gather(at, values, all_values, send, recv, local.at[1], 11)
+        (qkv, block, quarter), (out, logs, all_down, out_all) = ins, outs
+        parts, mixed, send, recv, local = kept
+        first = Gather(at, block, all_down, send, recv, local.at[0])
+        second = GatherZ(at, quarter, out_all, send, recv, local.at[1], 11)
+        second.begin()
         first.begin()
         for i in range(3):
             for h in range(HEADS):
@@ -786,52 +908,53 @@
                 column = jnp.broadcast_to(peak + jnp.log(total), (at_once, 128))
                 logs[pl.ds(h, 1), rows] = column.T[0:1, :]
 
-            @pl.when(h == 0)
+            @pl.when(h == 1)
             def _():
                 first.pass_on()
-                second.begin()
-                first.pass_near()
-
-            @pl.when(h == 1)
-            def _():
-                first.pass_far()
                 second.pass_on()
 
             return carry
 
         lax.fori_loop(0, HEADS, one, 0)
+        first.pass_near()
         second.pass_near()
         out[...] = jnp.concatenate([mixed[h] for h in range(HEADS)], axis=1)
+        first.pass_far()
         second.pass_far()
-        for gather in (first, second):
-            gather.got(4, 7, 8, 9, 10)
-            gather.end()
+        first.got(4, 7, 8, 9, 10)
+        first.end()
+        second.end()
 
     return call(
         body,
         number,
-        [joined, *query_w, *out_w, text_pair],
+        [joined, down, out_quarter],
         [shape(D, COLS), shape(8, D, dtype=f32), shape(D, D), shape(D, D)],
-        [VMEM((3, HEADS, D, HDIM), bf16), VMEM((HEADS, D, HDIM), bf16), VMEM((BLOCK, D), bf16), VMEM((BLOCK, D), bf16), *sems(22)],
+        [VMEM((3, HEADS, D, HDIM), bf16), VMEM((HEADS, D, HDIM), bf16), *sems(22)],
         beside,
-        ring_peers,
+        lambda at: ring_peers(at) + GatherZ.peers(at),
         out_spaces=[VMEM, VMEM, ANY, ANY],
     )
 
 
-def forward_rest(number, attended, out_w, x, vectors, keys, values, down, expand_w, contract):
+def forward_rest(number, attended, out_w, x, vectors, query_all, out_all, texts, all_down, expand_w, contract):
     def body(at, ins, outs, kept):
-        mixed, out_own, out_got, x, vectors, keys, values, down, expand_own, expand_got, contract_own = ins
-        middle, after, normed_two, weights, all_rows, all_down, activated, grad, contract_out = outs
+        mixed, out_own, out_got, x, vectors, query_all, out_all, texts, all_down, expand_own, expand_got, contract_own = ins
+        middle, after, normed_two, weights, all_rows, activated, grad, contract_out, keys_out, values_out = outs
         *refs, normed, whole, downs, out_full, expand_full, contract_full, key_full, value_full, branch, send, recv, local = kept
         half = at.half(at.n)
         weight = Whole(at, out_own, out_got, out_full, local.at[pl.ds(0, 2)], 1)
-        swap = remote(contract_own, contract_full.at[:, half], send.at[32], recv.at[32], at.x())
+        swap = remote(contract_own, contract_full.at[:, half], send.at[21], recv.at[21], at.x())
         swap.start()
+        factors = [
+            pltpu.make_async_copy(query_all, key_full, local.at[2]),
+            pltpu.make_async_copy(out_all, value_full, local.at[3]),
+        ]
+        for copy in factors:
+            copy.start()
         later = [
-            pltpu.make_async_copy(keys, key_full, local.at[2]),
-            pltpu.make_async_copy(values, value_full, local.at[3]),
             pltpu.make_async_copy(contract_own, contract_full.at[:, half], local.at[4]),
+            pltpu.make_async_copy(all_down, downs, local.at[7]),
         ]
         for copy in later:
             copy.start()
@@ -839,12 +962,29 @@
         weight.wait()
         scatter = Scatter(at, send, recv, refs)
         scatter.products(lambda rows: dot(mixed[rows], out_full[...]))
+        for copy in factors:
+            copy.wait()
+
+        def make(b, carry):
+            for h in range(HEADS):
+                rows = pl.ds(pl.multiple_of(b * BLOCK + h * 64, 64), 64)
+                text_keys = texts[b, :, h * HDIM : (h + 1) * HDIM]
+                text_values = texts[b, :, COLS + h * HDIM : COLS + (h + 1) * HDIM]
+                key_full[rows] = (dot(text_keys, key_full[rows]) * EIGHTH).astype(bf16)
+                value_full[rows] = dot(text_values, value_full[rows]).astype(bf16)
+            return carry
+
+        lax.fori_loop(0, 8, make, 0)
+        made = [
+            pltpu.make_async_copy(key_full, keys_out, local.at[8]),
+            pltpu.make_async_copy(value_full, values_out, local.at[9]),
+        ]
+        for copy in made:
+            copy.start()
         scatter.middle()
         for copy in later:
             copy.wait()
         scatter.arrive()
-        cotangents = Gather(at, down, downs, send, recv, local.at[7], 10)
-        cotangents.begin()
 
         def norm_two(rows, carry):
             total = x[rows].astype(f32) + scatter.total(rows)
@@ -871,11 +1011,6 @@
             def _():
                 branch[...] += part
 
-            @pl.when(b == 3)
-            def _():
-                cotangents.pass_on()
-                cotangents.pass_near()
-
             return carry
 
         lax.fori_loop(0, 8, cross, 0)
@@ -887,47 +1022,49 @@
             normed[rows] = (centred * vectors[4:5] + vectors[5:6]).astype(bf16)
 
         by_rows(BLOCK, 32, norm_three)
-        gather = Gather(at, normed, whole, send, recv, local.at[8], 21)
+        gather = Gather(at, normed, whole, send, recv, local.at[10], 10)
         gather.begin()
-        cotangents.pass_far()
-        cotangents.got(4, 7, 8, 9, 10)
-        keep_down = pltpu.make_async_copy(downs, all_down, local.at[9])
-        keep_down.start()
         swap.wait_recv()
-        keep_contract = pltpu.make_async_copy(contract_full, contract_out, local.at[10])
+        keep_contract = pltpu.make_async_copy(contract_full, contract_out, local.at[11])
         keep_contract.start()
-        keep = Keep(whole, all_rows, local, 11)
+        keep = Keep(whole, all_rows, local, 12)
+
+        def ahead(rows, carry):
+            grad[rows] = dot_flip(downs[rows], contract_full[...]).astype(bf16)
+
+        by_rows(D, BLOCK, ahead)
 
         def work(s, rows):
             keep.block(s, rows)
             hidden = dot(whole[rows], expand_full[...])
-            back = dot_flip(downs[rows], contract_full[...])
             bell = 0.5 * (1.0 + lax.erf(hidden * ROOT_HALF))
             activated[rows] = (hidden * bell).astype(bf16)
-            grad[rows] = (back * (bell + hidden * jnp.exp(-0.5 * hidden * hidden) * GAUSS_NORM)).astype(bf16)
+            slope = bell + hidden * jnp.exp(-0.5 * hidden * hidden) * GAUSS_NORM
+            grad[rows] = (grad[rows].astype(f32) * slope).astype(bf16)
 
         gather.each(work)
         keep.wait()
-        keep_down.wait()
         keep_contract.wait()
-        cotangents.end()
+        for copy in made:
+            copy.wait()
         scatter.end()
         swap.wait_send()
 
     results, _ = call(
         body,
         number,
-        [attended, *out_w, x, vectors, keys, values, down, *expand_w, contract],
+        [attended, *out_w, x, vectors, query_all, out_all, texts, all_down, *expand_w, contract],
         [
             shape(BLOCK, D, dtype=f32),
             shape(BLOCK, D, dtype=f32),
             shape(BLOCK, D),
             shape(8, BLOCK, BLOCK),
             shape(D, D),
-            shape(D, D),
             shape(D, HALF),
             shape(D, HALF),
             shape(HALF, D),
+            shape(D, D),
+            shape(D, D),
         ],
         [
             *Scatter.scratch,
@@ -940,26 +1077,26 @@
             VMEM((D, D), bf16),
             VMEM((D, D), bf16),
             VMEM((BLOCK, D), f32),
-            *sems(33),
+            *sems(22),
         ],
         (),
         lambda at: ring_peers(at) + [("x", at.x())],
-        spaces=[VMEM, ANY, ANY, VMEM, VMEM, ANY, ANY, VMEM, ANY, ANY, ANY],
-        out_spaces=[VMEM, VMEM, VMEM, VMEM, ANY, ANY, VMEM, VMEM, ANY],
+        spaces=[VMEM, ANY, ANY, VMEM, VMEM, ANY, ANY, VMEM, ANY, ANY, ANY, ANY],
+        out_spaces=[VMEM, VMEM, VMEM, VMEM, ANY, VMEM, VMEM, ANY, ANY, ANY],
     )
     return results
 
 
 def backward_rest(
-    number, grad, expand_w, after, middle, vectors, down, keys, values, weights, normed_two, out_w, contract_sum, expand_sum, beside
+    number, grad, expand_w, after, middle, vectors, down, keys, values, weights, out_w, contract_sum, expand_sum, beside
 ):
     def body(at, ins, outs, kept):
-        grad, expand_own, expand_got, after, middle, vectors, down, keys, values, weights, normed_two, out_own, out_got = ins[:13]
+        grad, expand_own, expand_got, after, middle, vectors, down, keys, values, weights, out_own, out_got = ins[:12]
         grad_rows, rounded_two, grad_scores, all_two, all_rows, grad_mixed, grad_vectors = outs[:7]
         *refs, rounded, whole, second, out_full, expand_full, key_full, value_full, send, recv, local = kept
         reduces = [
-            Reduce(at, ins[13], outs[7], refs[7:11], send, recv, local, 32, 16, False),
-            Reduce(at, ins[14], outs[8], refs[11:15], send, recv, local, 42, 18, True, True),
+            Reduce(at, ins[12], outs[7], refs[7:11], send, recv, local, 32, 16, False),
+            Reduce(at, ins[13], outs[8], refs[11:15], send, recv, local, 42, 18, True, True),
         ]
         refs = refs[:7]
         for reduce in reduces:
@@ -979,10 +1116,6 @@
         for copy in later:
             copy.wait()
         scatter.arrive()
-        before = Gather(at, normed_two, all_two, send, recv, local.at[6], 10)
-        before.begin()
-        for reduce in reduces:
-            reduce.second()
 
         def norm_three(rows, carry):
             incoming = scatter.total(rows)
@@ -993,6 +1126,10 @@
             return two_sums(incoming, centred, carry)
 
         gains, shifts = by_rows(BLOCK, 32, norm_three, no_sums())
+        before = Gather(at, rounded_two, all_two, send, recv, local.at[6], 10)
+        before.begin()
+        for reduce in reduces:
+            reduce.second()
         grad_vectors[4:5] = gains
         grad_vectors[5:6] = shifts
 
@@ -1058,7 +1195,7 @@
     return call(
         body,
         number,
-        [grad, *expand_w, after, middle, vectors, down, keys, values, weights, normed_two, *out_w, contract_sum, expand_sum],
+        [grad, *expand_w, after, middle, vectors, down, keys, values, weights, *out_w, contract_sum, expand_sum],
         [
             shape(BLOCK, D, dtype=f32),
             shape(BLOCK, D),
@@ -1067,13 +1204,13 @@
             shape(D, D),
             shape(D, COLS),
             shape(8, D, dtype=f32),
-            shape(4, 2, Reduce.deep, HALF),
-            shape(4, 2, Reduce.deep, HALF),
+            shape(4, 2, 96, HALF),
+            shape(4, 2, 96, HALF),
         ],
         [
             *Scatter.scratch,
-            *Reduce.scratch(False),
-            *Reduce.scratch(True, True),
+            *Reduce.scratch(96, False),
+            *Reduce.scratch(96, True, True),
             VMEM((BLOCK, D), bf16),
             VMEM((D, D), bf16),
             VMEM((BLOCK, D), f32),
@@ -1085,18 +1222,20 @@
         ],
         beside,
         lambda at: ring_peers(at) + Reduce.peers(at),
-        spaces=[VMEM, ANY, ANY, VMEM, VMEM, VMEM, VMEM, ANY, ANY, VMEM, VMEM, ANY, ANY, ANY, ANY],
+        spaces=[VMEM, ANY, ANY, VMEM, VMEM, VMEM, VMEM, ANY, ANY, VMEM, ANY, ANY, ANY, ANY],
         out_spaces=[VMEM, VMEM, VMEM, ANY, ANY, VMEM, VMEM, ANY, ANY],
     )
 
 
-def causal_backward(number, joined, grad, logs, activated, contract, after, rounded_two, beside):
+def causal_backward(number, joined, grad, logs, activated, contract, after, normed_two, part, beside):
     at_once = 512
 
     def body(at, ins, outs, kept):
-        (qkv, go, log_rows, activated, contract, after, block), (out, result, all_rows) = ins, outs
+        (qkv, go, log_rows, activated, contract, after, block, part), (out, result, all_rows, summed) = ins, outs
         *refs, parts, key_sum, value_sum, send, recv, local = kept
-        scatter = Scatter(at, send, recv, refs)
+        reduce = Reduce(at, part, summed, refs[7:], send, recv, local, 21, 1, False)
+        reduce.first()
+        scatter = Scatter(at, send, recv, refs[:7])
         scatter.products(lambda rows: dot(activated[rows], contract[...]))
         gather = Gather(at, block, all_rows, send, recv, local.at[0], 10)
         for i in range(4):
@@ -1137,15 +1276,18 @@
             def _():
                 scatter.middle()
                 gather.begin()
+                reduce.second()
 
             @pl.when(h == 1)
             def _():
                 gather.pass_on()
                 gather.pass_near()
+                reduce.third()
 
             return carry
 
         lax.fori_loop(0, HEADS, one, 0)
+        reduce.fourth()
         gather.pass_far()
         for i in range(3):
             out[:, i * COLS : (i + 1) * COLS] = jnp.concatenate([parts[i, h] for h in range(HEADS)], axis=1)
@@ -1158,16 +1300,25 @@
         gather.got(4, 7, 8, 9, 10)
         gather.end()
         scatter.end()
+        reduce.end()
 
     return call(
         body,
         number,
-        [joined, grad, logs, activated, contract, after, rounded_two],
-        [shape(D, 3 * COLS), shape(BLOCK, D), shape(D, D)],
-        [*Scatter.scratch, VMEM((4, HEADS, D, HDIM), bf16), VMEM((D, HDIM), f32), VMEM((D, HDIM), f32), *sems(21)],
+        [joined, grad, logs, activated, contract, after, normed_two, part],
+        [shape(D, 3 * COLS), shape(BLOCK, D), shape(D, D), shape(4, 2, 72, HALF)],
+        [
+            *Scatter.scratch,
+            *Reduce.scratch(72, False),
+            VMEM((4, HEADS, D, HDIM), bf16),
+            VMEM((D, HDIM), f32),
+            VMEM((D, HDIM), f32),
+            *sems(31),
+        ],
         beside,
-        ring_peers,
-        out_spaces=[VMEM, VMEM, ANY],
+        lambda at: ring_peers(at) + Reduce.peers(at),
+        spaces=[VMEM] * 7 + [ANY],
+        out_spaces=[VMEM, VMEM, ANY, ANY],
     )
 
 
@@ -1238,6 +1389,9 @@
         scatter = Scatter(at, send, recv, refs)
         scatter.products(lambda rows: dot(grad[rows], weight[...]))
         scatter.middle()
+        for reduce in reduces:
+            reduce.second()
+        at.start_beside()
         text_own.wait()
         for copy in trades:
             copy.wait_recv()
@@ -1268,7 +1422,7 @@
         for copy in rings:
             copy.start()
         for reduce in reduces:
-            reduce.second()
+            reduce.third()
         ring_own.wait()
         for copy in rings:
             copy.wait_recv()
@@ -1279,8 +1433,6 @@
         clip_own.start()
         for copy in spreads:
             copy.start()
-        for reduce in reduces:
-            reduce.third()
         for reduce in reduces:
             reduce.fourth()
         clip_own.wait()
@@ -1300,22 +1452,21 @@
         for reduce in reduces:
             reduce.end()
 
-    deep = Reduce.deep
     return call(
         body,
         number,
         [grad, joined, x, vectors, grad_rows, late, text_part, *sums],
         [
             shape(384, HALF),
-            shape(4, 2, deep, HALF),
-            shape(4, 2, deep, HALF),
+            shape(4, 2, 72, HALF),
+            shape(4, 2, 48, HALF),
             shape(8, HALF, dtype=f32),
             shape(2, 8, some, HALF),
         ],
         [
             *Scatter.scratch,
-            *Reduce.scratch(False),
-            *Reduce.scratch(True),
+            *Reduce.scratch(72, False),
+            *Reduce.scratch(48, True),
             VMEM((BLOCK, D), bf16),
             VMEM((8, D), f32),
             VMEM((8, 8, D), f32),
@@ -1329,6 +1480,7 @@
         peers,
         spaces=[VMEM, VMEM, VMEM, VMEM, VMEM, VMEM, ANY, ANY, ANY],
         out_spaces=[ANY, ANY, ANY, VMEM, ANY],
+        late=True,
     )
 
 
@@ -1361,26 +1513,27 @@
     n = lax.axis_index("narrow")
 
     text_parts = dot_flip(text_states.reshape(128, HALF), pair_t).reshape(2, 64, 2 * COLS)
-    (x, vectors, joined, all_one, qkv), ((text_pair_got,), (query_got,), (cross_got,), (text_got,)) = enter(
-        1, layer_input, vectors, weights, [GiveClip(text_parts), Give(query_t), Give(cross_output), GiveClip(text_states)]
+    results, ((text_pair_got,), (down,), (query_got,), (cross_got,), (text_got,)) = enter(
+        1,
+        layer_input,
+        vectors,
+        weights,
+        query_t,
+        cross_output,
+        [GiveClip(text_parts), Relay(cotangent), Give(query_t), Give(cross_output), GiveClip(text_states)],
     )
+    x, vectors, joined, all_one, qkv, query_all, out_quarter = results
     text_pair = (lax.dynamic_index_in_dim(text_parts, n, 0, False) + text_pair_got).astype(bf16)
-    (attended, logs, all_keys, all_values), ((down,), (out_got,), (expand_got,)) = causal_forward(
-        2,
-        qkv,
-        (query_t, query_got),
-        (cross_output, cross_got),
-        text_pair,
-        [Relay(cotangent), Give(output_weight), Give(expand_weight)],
+    (attended, logs, all_down, out_all), ((texts,), (out_got,), (expand_got,)) = causal_forward(
+        2, qkv, down, out_quarter, [ToSpots(text_pair), Give(output_weight), Give(expand_weight)]
     )
     out_w, expand_w = (output_weight, out_got), (expand_weight, expand_got)
-    middle, after, normed_two, cross_p, all_three, all_down, activated, grad_expand, contract = forward_rest(
-        3, attended, out_w, x, vectors, all_keys, all_values, down, expand_w, contract_weight
+    middle, after, normed_two, cross_p, all_three, activated, grad_expand, contract, all_keys, all_values = forward_rest(
+        3, attended, out_w, x, vectors, query_all, out_all, texts, all_down, expand_w, contract_weight
     )
 
-    deep = Reduce.deep
-    contract_part = outer(activated, all_down).astype(bf16).reshape(4, 2, deep, D)
-    expand_part = outer(all_three, grad_expand).astype(bf16).reshape(2, 4, 2, deep, HALF)
+    contract_part = outer(activated, all_down).astype(bf16).reshape(4, 2, 96, D)
+    expand_part = outer(all_three, grad_expand).astype(bf16).reshape(2, 4, 2, 96, HALF)
     results, ((cross_p,),) = backward_rest(
         4,
         grad_expand,
@@ -1392,55 +1545,64 @@
         all_keys,
         all_values,
         cross_p,
-        normed_two,
         out_w,
         contract_part,
         expand_part,
         [Trade(cross_p)],
     )
-    grad_one, rounded_two, grad_scores, all_two, all_mid_one, grad_attended, late, contract_grad, expand_grad = results
-    (grad_qkv, layer_output, all_mid_two), ((grad_scores,), (pair_got,)) = causal_backward(
-        5, qkv, grad_attended, logs, activated, contract, after, rounded_two, [Trade(grad_scores), Give(pair_t)]
-    )
-
-    joined_part = jnp.concatenate((outer(grad_qkv, all_one), outer(attended, all_mid_one)), axis=0)
-    grad_keys = outer(grad_scores.reshape(D, COLS), all_two).astype(bf16).reshape(HEADS, 64, D)
-    grad_values = outer(cross_p.reshape(D, COLS), all_mid_two).astype(bf16).reshape(HEADS, 64, D)
+    grad_one, _, grad_scores, all_mid_two, all_mid_one, grad_attended, late, contract_grad, expand_grad = results
+
     own_first = n == 0
 
     def whole(own, got):
         return jnp.concatenate((jnp.where(own_first, own, got), jnp.where(own_first, got, own)), axis=1)
 
-    text = whole(lax.dynamic_index_in_dim(text_states, n, 0, False), text_got)
-    heads_query = whole(query_t, query_got).reshape(HEADS, HDIM, D)
-    heads_out = whole(cross_output, cross_got).reshape(HEADS, HDIM, D)
-    text_heads = text_pair.reshape(64, 2, HEADS, HDIM)
-
     def heads(what, a, b):
         return jnp.einsum(what, a, b, preferred_element_type=f32)
 
-    grad_text_keys = heads("hkf,hdf->khd", grad_keys, heads_query) * EIGHTH
-    grad_text_values = heads("hkf,hdf->khd", grad_values, heads_out)
-    grad_pair = jnp.stack((grad_text_keys, grad_text_values), axis=1).reshape(64, 2 * COLS).astype(bf16)
+    text = whole(lax.dynamic_index_in_dim(text_states, n, 0, False), text_got)
+    text_heads = text_pair.reshape(64, 2, HEADS, HDIM)
+    grad_values = outer(cross_p.reshape(D, COLS), all_mid_two).astype(bf16).reshape(HEADS, 64, D)
+    heads_out = whole(cross_output, cross_got).reshape(HEADS, HDIM, D)
+    grad_text_values = heads("hkf,hdf->khd", grad_values, heads_out).reshape(64, COLS).astype(bf16)
+    grad_cross = heads("khd,hkf->hdf", text_heads[:, 1], grad_values).reshape(COLS, D)
+    value_part = jnp.concatenate((grad_cross, outer(grad_text_values, text), outer(attended, all_mid_one)), axis=0)
+    (grad_qkv, layer_output, all_two, value_grad), ((grad_scores,), (pair_got,)) = causal_backward(
+        5,
+        qkv,
+        grad_attended,
+        logs,
+        activated,
+        contract,
+        after,
+        normed_two,
+        value_part.astype(bf16).reshape(4, 2, 72, D),
+        [Trade(grad_scores), Give(pair_t)],
+    )
+
+    joined_part = outer(grad_qkv, all_one).astype(bf16).reshape(4, 2, 72, D)
+    grad_keys = outer(grad_scores.reshape(D, COLS), all_two).astype(bf16).reshape(HEADS, 64, D)
+    heads_query = whole(query_t, query_got).reshape(HEADS, HDIM, D)
+    grad_text_keys = (heads("hkf,hdf->khd", grad_keys, heads_query) * EIGHTH).reshape(64, COLS).astype(bf16)
     grad_query = heads("khd,hkf->hdf", text_heads[:, 0], grad_keys).reshape(COLS, D) * EIGHTH
-    grad_cross = heads("khd,hkf->hdf", text_heads[:, 1], grad_values).reshape(COLS, D)
-    cross_part = jnp.concatenate((grad_query, outer(grad_pair, text), grad_cross), axis=0)
+    key_part = jnp.concatenate((grad_query, outer(grad_text_keys, text)), axis=0).astype(bf16).reshape(4, 2, 48, D)
+    grad_pair = jnp.concatenate((grad_text_keys, grad_text_values), axis=1)
     text_part = dot(grad_pair, whole(pair_t, pair_got)).astype(bf16).reshape(8, 8, D)
 
-    (input_grad, joined_grad, cross_grad, parts, text_grad), ((layer_output,),) = leave(
+    (input_grad, joined_grad, key_grad, parts, text_grad), ((layer_output,),) = leave(
         6,
         grad_qkv,
         joined,
         x,
         vectors,
         grad_one,
-        [part.astype(bf16).reshape(4, 2, deep, D) for part in (joined_part, cross_part)],
+        (joined_part, key_part),
         late,
         text_part,
         [Relay(layer_output, True)],
     )
-    joined_grad, cross_grad, expand_grad, contract_grad = (
-        grad.reshape(HALF, HALF).astype(f32) for grad in (joined_grad, cross_grad, expand_grad, contract_grad)
+    joined_grad, key_grad, value_grad, expand_grad, contract_grad = (
+        grad.reshape(-1, HALF).astype(f32) for grad in (joined_grad, key_grad, value_grad, expand_grad, contract_grad)
     )
     return (
         layer_output,
@@ -1450,14 +1612,14 @@
         parts[1],
         joined_grad[:COLS].T,
         joined_grad[COLS : 2 * COLS].T,
-        joined_grad[2 * COLS : 3 * COLS].T,
-        joined_grad[3 * COLS :],
+        joined_grad[2 * COLS :].T,
+        value_grad[2 * COLS :],
         parts[2],
         parts[3],
-        cross_grad[:COLS].T,
-        cross_grad[COLS : 2 * COLS].T,
-        cross_grad[2 * COLS : 3 * COLS].T,
-        cross_grad[3 * COLS :],
+        key_grad[:COLS].T,
+        key_grad[COLS:].T,
+        value_grad[COLS : 2 * COLS].T,
+        value_grad[:COLS],
         parts[4],
         parts[5],
         expand_grad,

time: 507 us -> 489 us (0.964)
  Pallas kernels: 442 us -> 423 us
    pallas_call x6, Pallas kernels: 442 us -> 423 us  [call(): pl.pallas_call(kernel, out_shape=tuple(outs) + tuple(side_outs), in_specs...]
    dot_general x7 -> x8, matrix products: 24.5 us -> 26.8 us  [outer(): lax.dot_general(a, b, (((0,), (0,)), ((), ())), preferred_element_type=f32)]
where the time goes in v5:
time: 489 us; the launch traced here: 480 us
  Pallas kernels  423 us (87%)
  matrix products  31.1 us (6%)
  other arithmetic  13.5 us (3%)
  local copies, waits for them, and re-layouts  11.6 us (2%)
    pallas_call x6, Pallas kernels, call(): pl.pallas_call(kernel, out_shape=tuple(outs) + tuple(side_outs), in_specs...  423 us
    dot_general x8, matrix products, outer(): lax.dot_general(a, b, (((0,), (0,)), ((), ())), preferred_element_type=f32)  26.8 us

profile of v5, /device:TPU:0, one launch (start us, length us, event | category | flops | bytes accessed | tf_op | source)
XLA Modules:
  0.0 480.5 jit_solution(6007663970037062800)
XLA Ops:
  0.7 2.1 fusion.13
  2.8 0.7 stack.21
  3.5 0.7 stack.22
  4.9 0.7 stack.24
  5.5 0.7 stack.25
  6.2 0.7 stack.26
  7.6 81.6 %shard_map.330 = (bf16[192,1536]{1,0:T(8,128)(2,1)}, f32[8,1536]{1,0:T(8,128)}, bf16[576,1536]{1,0:T(8,128)(2,1)}, bf16[1536,1536]{1,0:T(8,128)(2,1)}, bf16[1536...) custom-call(bf16[384,768]{1,0:T(8,128)(2,1)} %refs_0_.1, ...), custom_call_target="tpu_custom_call" | custom-call | tf_op jit(solution)/shard_map/pallas_call | solution.py:269
  89.2 1.5 fusion.9.refs_3_
  90.7 40.6 %shard_map.331 = (bf16[1536,192]{1,0:T(8,128)(2,1)}, f32[8,1536]{1,0:T(8,128)}, bf16[1536,1536]{1,0:T(8,128)(2,1)}, bf16[1536,1536]{1,0:T(8,128)(2,1)}, bf16[8,6...) custom-call(bf16[1536,576]{1,0:T(8,128)(2,1)} %get-tuple-element.69.refs_0_, ...), custom_call_target="tpu_custom_call" | custom-call | tf_op jit(solution)/shard_map/pallas_call | solution.py:269
  131.3 65.6 %shard_map.332 = (f32[192,1536]{1,0:T(8,128)}, f32[192,1536]{1,0:T(8,128)}, bf16[192,1536]{1,0:T(8,128)(2,1)}, bf16[8,192,192]{2,1,0:T(8,128)(2,1)}, bf16[1536,1...) custom-call(bf16[1536,192]{1,0:T(8,128)(2,1)} %get-tuple-element.73., ...), custom_call_target="tpu_custom_call" | custom-call | tf_op jit(solution)/shard_map/pallas_call | solution.py:269
  197.0 8.5 %convolution_convert_fusion = bf16[1536,768]{1,0:T(8,128)(2,1)} fusion(bf16[1536,1536]{1,0:T(8,128)(2,1)} %get-tuple-element.89, bf16[1536,768]{1,0:T(8,128)(2,1)} %get-tuple-element.82.refs_0_), kind=kOutput, calls=%fused_computation | convolution fusion | flops 3625058304 | bytes 9437184 | tf_op jit(solution)/shard_map/dot_general | solution.py:36
  205.5 5.2 %convolution_convert_fusion.1 = bf16[768,1536]{1,0:T(8,128)(2,1)} fusion(bf16[1536,768]{1,0:T(8,128)(2,1)S(1)} %copy-done.3, bf16[1536,1536]{1,0:T(8,128)(2,1)S(1)} %bitcast.100), kind=kOutput, calls=%fused_computation.1 | convolution fusion | flops 3625058304 | bytes 9437184 | tf_op jit(solution)/shard_map/dot_general | solution.py:36
  210.7 92.9 %shard_map.333 = (f32[192,1536]{1,0:T(8,128)}, bf16[192,1536]{1,0:T(8,128)(2,1)}, bf16[8,192,192]{2,1,0:T(8,128)(2,1)}, bf16[1536,1536]{1,0:T(8,128)(2,1)}, bf16...) custom-call(bf16[1536,768]{1,0:T(8,128)(2,1)} %get-tuple-element.82., ...), custom_call_target="tpu_custom_call" | custom-call | tf_op jit(solution)/shard_map/pallas_call | solution.py:269
  303.6 4.3 bitcast_convert_fusion
  308.0 1.1 convolution_convert_fusion.8
  310.9 1.2 copy-done.20
  312.3 1.1 convolution_convert_fusion.5
  313.4 1.3 pad_maximum_fusion
  314.8 0.9 pad_maximum_fusion.2.refs_9_
  315.6 67.6 %shard_map.334 = (bf16[1536,576]{1,0:T(8,128)(2,1)}, bf16[192,1536]{1,0:T(8,128)(2,1)}, bf16[1536,1536]{1,0:T(8,128)(2,1)}, bf16[4,2,72,768]{3,2,1,0:T(8,128)(2,...) custom-call(bf16[1536,576]{1,0:T(8,128)(2,1)} %get-tuple-element.69.refs_0_, ...), custom_call_target="tpu_custom_call" | custom-call | tf_op jit(solution)/shard_map/pallas_call | solution.py:269
  383.3 3.7 convolution_convert_fusion.4
  387.9 1.1 pad_maximum_fusion.1
  389.0 6.6 %convolution_convert_fusion.2 = bf16[576,1536]{1,0:T(8,128)(2,1)} fusion(bf16[1536,576]{1,0:T(8,128)(2,1)S(1)} %copy-done.4, bf16[1536,1536]{1,0:T(8,128)(2,1)} %get-tuple-element.108), kind=kOutput, calls=%fused_computation.2 | convolution fusion | flops 2718793728 | bytes 8257536 | tf_op jit(solution)/shard_map/dot_general | solution.py:36
  395.9 1.0 fusion.1.refs_6_
  396.9 74.5 %shard_map.335 = (bf16[384,768]{1,0:T(8,128)(2,1)}, bf16[4,2,72,768]{3,2,1,0:T(8,128)(2,1)}, bf16[4,2,48,768]{3,2,1,0:T(8,128)(2,1)}, f32[8,768]{1,0:T(8,128)}, ...) custom-call(bf16[1536,576]{1,0:T(8,128)(2,1)} %get-tuple-element.100.refs_0_, ...), custom_call_target="tpu_custom_call" | custom-call | tf_op jit(solution)/shard_map/pallas_call | solution.py:269
  471.4 1.3 bitcast_convert_fusion.3
  472.7 1.2 slice_bitcast_fusion.1
  474.1 1.1 fusion.15
  475.2 1.1 convert_element_type.102
  476.3 0.8 bitcast_convert_fusion.4
  477.9 1.2 fusion.14
  479.2 0.8 copy.44
  (67 shorter events, 5.5 us)
Async XLA Ops:
  2.8 86.4 %copy-start.14 = (f32[384,128]{0,1:T(8,128)S(1)}, f32[384,128]{0,1:T(8,128)}, u32[]{:S(2)}) copy-start(f32[384,128]{0,1:T(8,128)} %fusion.13) | copy-start | bytes 589828
  131.3 74.2 %slice-start = ((s8[4718592]{0:T(1024)(128)(4,1)}), s8[524288]{0:T(1024)(128)(4,1)S(1)}, s32[]{:S(2)}) async-start(s8[4718592]{0:T(1024)(128)(4,1)} %bitcast.99), calls=%async_computation | async-start | bytes 1048576
  196.9 8.6 %slice-start.1 = ((s8[4718592]{0:T(1024)(128)(4,1)}), s8[4194304]{0:T(1024)(128)(4,1)S(1)}, s32[]{:S(2)}) async-start(s8[4718592]{0:T(1024)(128)(4,1)} %bitcast.99), calls=%async_computation.1 | async-start | bytes 8388608
  196.9 8.6 %copy-start.3 = (bf16[1536,768]{1,0:T(8,128)(2,1)S(1)}, bf16[1536,768]{1,0:T(8,128)(2,1)}, u32[]{:S(2)}) copy-start(bf16[1536,768]{1,0:T(8,128)(2,1)} %get-tuple-element.88.refs_3_) | copy-start | bytes 7077892
  303.6 4.3 copy-start.21
  303.6 4.3 copy-start.22
  308.0 1.2 copy-start.12
  308.0 1.6 copy-start
  308.0 1.6 copy-start.1
  308.0 1.6 copy-start.15
  308.0 1.6 copy-start.16
  309.6 0.9 copy-start.13
  309.6 1.0 copy-start.18
  309.6 2.5 copy-start.20
  309.7 2.6 copy-start.8
  313.4 1.3 copy-start.5
  313.4 1.3 copy-start.6
  387.3 1.7 copy-start.4
  389.0 6.6 %copy-start.9 = (bf16[384,768]{1,0:T(8,128)(2,1)S(1)}, bf16[384,768]{1,0:T(8,128)(2,1)}, u32[]{:S(2)}) copy-start(bf16[384,768]{1,0:T(8,128)(2,1)} %get-tuple-element.107) | copy-start | bytes 1769476
  472.7 1.3 copy-start.2
  474.0 1.2 copy-start.10
  474.1 2.2 copy-start.17
  474.1 3.0 copy-start.19
  474.1 3.6 copy-start.7
  477.9 1.3 copy-start.11

commit v6 on v5

--- a/solution.py
+++ b/solution.py
@@ -235,28 +235,30 @@
         if known:
             greet(list(known.values()))
         side_refs = [([side_in.pop(0) for _ in b.ins], [side_out.pop(0) for _ in b.outs]) for b in beside]
-        todo = []
+        begin, todo = [], []
+        slot, place = 0, 0
+        for b, (i, o) in zip(beside, side_refs):
+            if isinstance(b, Relay):
+                run = functools.partial(relay_run, b, at, i[0], o[0], send, recv, local.at[place], slot)
+                begin.append(functools.partial(run, False))
+                todo.append(functools.partial(run, True))
+                slot, place = slot + 2, place + 1
+                continue
+            far, near = b.moves(at, i, o)
+            for src, dst, peer in far:
+                copy = remote(src, dst, send.at[slot], recv.at[slot], peer)
+                begin.append(copy.start)
+                todo.append(copy.wait)
+                slot += 1
+            for src, dst in near:
+                copy = pltpu.make_async_copy(src, dst, local.at[place])
+                begin.append(copy.start)
+                todo.append(copy.wait)
+                place += 1
 
         def start():
-            slot, place = 0, 0
-            for b, (i, o) in zip(beside, side_refs):
-                if isinstance(b, Relay):
-                    run = functools.partial(relay_run, b, at, i[0], o[0], send, recv, local.at[place], slot)
-                    run(False)
-                    todo.append(functools.partial(run, True))
-                    slot, place = slot + 2, place + 1
-                    continue
-                far, near = b.moves(at, i, o)
-                for src, dst, peer in far:
-                    copy = remote(src, dst, send.at[slot], recv.at[slot], peer)
-                    copy.start()
-                    todo.append(copy.wait)
-                    slot += 1
-                for src, dst in near:
-                    copy = pltpu.make_async_copy(src, dst, local.at[place])
-                    copy.start()
-                    todo.append(copy.wait)
-                    place += 1
+            for go in begin:
+                go()
 
         at.start_beside = start
         if not late:
@@ -733,16 +735,20 @@
             pltpu.make_async_copy(self.whole.at[some], self.out.at[some], self.sem.at[self.base + s]).wait()
 
 
-def enter(number, layer_input, vectors, weights, query_t, cross_out, beside):
+def enter(number, layer_input, gains, weights, query_t, cross_out, texts, pair_t, beside):
     relay = Relay(layer_input)
 
     def body(at, ins, outs, kept):
-        source, own_vectors, *own_weights, query_own, out_own = ins
-        x, vectors, weight, all_rows, qkv, query_all, out_quarter = outs
-        normed, whole, query_part, out_part, query_quarter, send, recv, local = kept
+        source, *gains = ins[:7]
+        *own_weights, query_own, out_own, own_texts, pair = ins[7:]
+        x, vectors, weight, all_rows, qkv, query_all, out_quarter, text_pair = outs
+        normed, whole, query_part, out_part, query_quarter, text_parts, text_got, own_vectors, send, recv, local = kept
         half = at.half(at.n)
         moving = functools.partial(relay_run, relay, at, source, x, send, recv, local.at[0], 11)
         moving(False)
+        own_vectors[...] = jnp.zeros_like(own_vectors)
+        for i, ref in enumerate(gains):
+            own_vectors[i : i + 1] = ref[...].astype(f32).reshape(1, HALF)
         columns = GatherZ.columns(lax.rem(at.z, 2))
         holds = at.n == lax.div(at.z, 2)
         quarters = []
@@ -781,6 +787,10 @@
             for near, far in quarters:
                 far.wait_recv()
 
+        for clip in range(2):
+            text_parts[clip] = dot_flip(own_texts[clip], pair[...])
+        text_go = remote(text_parts.at[1 - at.n], text_got, send.at[52], recv.at[52], at.x())
+        text_go.start()
         queries = Gather(at, query_part, query_quarter, send, recv, local.at[16], 19)
         outputs = Gather(at, out_part, out_quarter, send, recv, local.at[17], 30)
         queries.begin()
@@ -803,7 +813,6 @@
         queries.got(4, 7, 8, 9, 10)
         around = GatherZ(at, query_quarter, query_all, send, recv, local.at[18], 41)
         around.begin()
-        at.start_beside()
         keep = Keep(whole, all_rows, local, 6)
 
         def times(rows):
@@ -818,6 +827,7 @@
                     copy.wait()
                 for copy in go[1:]:
                     copy.wait_recv()
+                at.start_beside()
 
             @pl.when(s >= 4)
             def _():
@@ -840,6 +850,8 @@
         lax.fori_loop(0, 4, rest, 0)
         outputs.pass_far()
         around.pass_far()
+        text_go.wait()
+        text_pair[...] = (text_parts[at.n] + text_got[...]).astype(bf16)
         outputs.got(4, 7, 8, 9, 10)
         keep.wait()
         for copy in go:
@@ -851,7 +863,7 @@
     return call(
         body,
         number,
-        [layer_input, vectors, *weights, query_t, cross_out],
+        [layer_input, *gains, *weights, query_t, cross_out, texts, pair_t],
         [
             shape(BLOCK, D),
             shape(8, D, dtype=f32),
@@ -860,6 +872,7 @@
             shape(D, 3 * COLS),
             shape(D, D),
             shape(D, QUARTER),
+            shape(64, 2 * COLS),
         ],
         [
             VMEM((BLOCK, D), bf16),
@@ -867,11 +880,14 @@
             VMEM((COLS, QUARTER), bf16),
             VMEM((COLS, QUARTER), bf16),
             VMEM((D, QUARTER), bf16),
-            *sems(52),
+            VMEM((2, 64, 2 * COLS), f32),
+            VMEM((64, 2 * COLS), f32),
+            VMEM((8, HALF), f32),
+            *sems(53),
         ],
         beside,
         lambda at: ring_peers(at) + relay.peers(at) + [("x", at.x())] + GatherZ.peers(at),
-        out_spaces=[VMEM, VMEM, VMEM, ANY, VMEM, ANY, VMEM],
+        out_spaces=[VMEM, VMEM, VMEM, ANY, VMEM, ANY, VMEM, VMEM],
         late=True,
     )
 
@@ -1235,9 +1251,11 @@
         *refs, parts, key_sum, value_sum, send, recv, local = kept
         reduce = Reduce(at, part, summed, refs[7:], send, recv, local, 21, 1, False)
         reduce.first()
+        gather = Gather(at, block, all_rows, send, recv, local.at[0], 10)
+        gather.begin()
         scatter = Scatter(at, send, recv, refs[:7])
         scatter.products(lambda rows: dot(activated[rows], contract[...]))
-        gather = Gather(at, block, all_rows, send, recv, local.at[0], 10)
+        gather.pass_on()
         for i in range(4):
             for h in range(HEADS):
                 a = i * COLS + h * HDIM
@@ -1268,27 +1286,33 @@
                     key_sum[0:upto, :] += key_part
                     value_sum[0:upto, :] += value_part
                 query_parts.append((dot(turned[:, 0:upto], ds) * EIGHTH).T)
+                if i == blocks - 1:
+
+                    @pl.when(h == 1)
+                    def _():
+                        reduce.second()
+
+                    @pl.when(h == 2)
+                    def _():
+                        reduce.fourth()
+
             parts[0, h] = jnp.concatenate(query_parts[::-1], axis=0).astype(bf16)
             parts[1, h] = key_sum[...].astype(bf16)
             parts[2, h] = value_sum[...].astype(bf16)
 
             @pl.when(h == 0)
             def _():
+                gather.pass_near()
+
+            @pl.when(h == 1)
+            def _():
                 scatter.middle()
-                gather.begin()
-                reduce.second()
-
-            @pl.when(h == 1)
-            def _():
-                gather.pass_on()
-                gather.pass_near()
+                gather.pass_far()
                 reduce.third()
 
             return carry
 
         lax.fori_loop(0, HEADS, one, 0)
-        reduce.fourth()
-        gather.pass_far()
         for i in range(3):
             out[:, i * COLS : (i + 1) * COLS] = jnp.concatenate([parts[i, h] for h in range(HEADS)], axis=1)
         scatter.arrive()
@@ -1388,10 +1412,10 @@
             copy.start()
         scatter = Scatter(at, send, recv, refs)
         scatter.products(lambda rows: dot(grad[rows], weight[...]))
+        at.start_beside()
         scatter.middle()
         for reduce in reduces:
             reduce.second()
-        at.start_beside()
         text_own.wait()
         for copy in trades:
             copy.wait_recv()
@@ -1505,25 +1529,24 @@
     expand_weight,
     contract_weight,
 ):
-    vectors = (first_gain, first_shift, second_gain, second_shift, third_gain, third_shift)
-    vectors = jnp.concatenate([jnp.stack(vectors).astype(f32), jnp.zeros((2, HALF), f32)], axis=0)
+    gains = (first_gain, first_shift, second_gain, second_shift, third_gain, third_shift)
     weights = [query_weight.T, key_weight.T, value_weight.T]
     query_t = cross_query.T
     pair_t = jnp.concatenate((cross_key.T, cross_value.T), axis=0)
     n = lax.axis_index("narrow")
 
-    text_parts = dot_flip(text_states.reshape(128, HALF), pair_t).reshape(2, 64, 2 * COLS)
-    results, ((text_pair_got,), (down,), (query_got,), (cross_got,), (text_got,)) = enter(
+    results, ((down,), (text_got,)) = enter(
         1,
         layer_input,
-        vectors,
+        gains,
         weights,
         query_t,
         cross_output,
-        [GiveClip(text_parts), Relay(cotangent), Give(query_t), Give(cross_output), GiveClip(text_states)],
+        text_states,
+        pair_t,
+        [Relay(cotangent), GiveClip(text_states)],
     )
-    x, vectors, joined, all_one, qkv, query_all, out_quarter = results
-    text_pair = (lax.dynamic_index_in_dim(text_parts, n, 0, False) + text_pair_got).astype(bf16)
+    x, vectors, joined, all_one, qkv, query_all, out_quarter, text_pair = results
     (attended, logs, all_down, out_all), ((texts,), (out_got,), (expand_got,)) = causal_forward(
         2, qkv, down, out_quarter, [ToSpots(text_pair), Give(output_weight), Give(expand_weight)]
     )
@@ -1534,7 +1557,7 @@
 
     contract_part = outer(activated, all_down).astype(bf16).reshape(4, 2, 96, D)
     expand_part = outer(all_three, grad_expand).astype(bf16).reshape(2, 4, 2, 96, HALF)
-    results, ((cross_p,),) = backward_rest(
+    results, ((cross_p,), (query_got,), (cross_got,)) = backward_rest(
         4,
         grad_expand,
         expand_w,
@@ -1548,7 +1571,7 @@
         out_w,
         contract_part,
         expand_part,
-        [Trade(cross_p)],
+        [Trade(cross_p), Give(query_t), Give(cross_output)],
     )
     grad_one, _, grad_scores, all_mid_two, all_mid_one, grad_attended, late, contract_grad, expand_grad = results
 

time: 489 us -> 482 us (0.986)
  local copies, waits for them, and re-layouts: 11.6 us -> 5.98 us
where the time goes in v6:
time: 482 us; the launch traced here: 473 us
  Pallas kernels  422 us (88%)
  matrix products  31.4 us (7%)
  other arithmetic  12.4 us (3%)
  local copies, waits for them, and re-layouts  5.98 us (1%)
    pallas_call x6, Pallas kernels, call(): pl.pallas_call(kernel, out_shape=tuple(outs) + tuple(side_outs), in_specs...  422 us
    dot_general x8, matrix products, outer(): lax.dot_general(a, b, (((0,), (0,)), ((), ())), preferred_element_type=f32)  29.2 us

profile of v6, /device:TPU:0, one launch (start us, length us, event | category | flops | bytes accessed | tf_op | source)
XLA Modules:
  0.0 473.5 jit_solution(17383982409563744707)
XLA Ops:
  0.7 1.9 pad_maximum_fusion.2.refs_13_.refs_9_
  2.6 71.0 %shard_map.330 = (bf16[192,1536]{1,0:T(8,128)(2,1)}, f32[8,1536]{1,0:T(8,128)}, bf16[576,1536]{1,0:T(8,128)(2,1)}, bf16[1536,1536]{1,0:T(8,128)(2,1)}, bf16[1536...) custom-call(bf16[384,768]{1,0:T(8,128)(2,1)} %refs_0_.1, ...), custom_call_target="tpu_custom_call" | custom-call | tf_op jit(solution)/shard_map/pallas_call | solution.py:271
  73.6 46.8 %shard_map.331 = (bf16[1536,192]{1,0:T(8,128)(2,1)}, f32[8,1536]{1,0:T(8,128)}, bf16[1536,1536]{1,0:T(8,128)(2,1)}, bf16[1536,1536]{1,0:T(8,128)(2,1)}, bf16[8,6...) custom-call(bf16[1536,576]{1,0:T(8,128)(2,1)} %get-tuple-element.69.refs_0_, ...), custom_call_target="tpu_custom_call" | custom-call | tf_op jit(solution)/shard_map/pallas_call | solution.py:271
  120.4 66.5 %shard_map.332 = (f32[192,1536]{1,0:T(8,128)}, f32[192,1536]{1,0:T(8,128)}, bf16[192,1536]{1,0:T(8,128)(2,1)}, bf16[8,192,192]{2,1,0:T(8,128)(2,1)}, bf16[1536,1...) custom-call(bf16[1536,192]{1,0:T(8,128)(2,1)} %get-tuple-element.73., ...), custom_call_target="tpu_custom_call" | custom-call | tf_op jit(solution)/shard_map/pallas_call | solution.py:271
  186.9 8.5 %convolution_convert_fusion = bf16[1536,768]{1,0:T(8,128)(2,1)} fusion(bf16[1536,1536]{1,0:T(8,128)(2,1)} %get-tuple-element.89, bf16[1536,768]{1,0:T(8,128)(2,1)} %get-tuple-element.82.refs_0_), kind=kOutput, calls=%fused_computation | convolution fusion | flops 3625058304 | bytes 9437184 | tf_op jit(solution)/shard_map/dot_general | solution.py:36
  195.5 5.2 %convolution_convert_fusion.1 = bf16[768,1536]{1,0:T(8,128)(2,1)} fusion(bf16[1536,768]{1,0:T(8,128)(2,1)S(1)} %copy-done.3, bf16[1536,1536]{1,0:T(8,128)(2,1)S(1)} %bitcast.91), kind=kOutput, calls=%fused_computation.1 | convolution fusion | flops 3625058304 | bytes 9437184 | tf_op jit(solution)/shard_map/dot_general | solution.py:36
  200.6 93.4 %shard_map.333 = (f32[192,1536]{1,0:T(8,128)}, bf16[192,1536]{1,0:T(8,128)(2,1)}, bf16[8,192,192]{2,1,0:T(8,128)(2,1)}, bf16[1536,1536]{1,0:T(8,128)(2,1)}, bf16...) custom-call(bf16[1536,768]{1,0:T(8,128)(2,1)} %get-tuple-element.82., ...), custom_call_target="tpu_custom_call" | custom-call | tf_op jit(solution)/shard_map/pallas_call | solution.py:271
  294.0 4.3 bitcast_convert_fusion
  298.4 1.1 convolution_convert_fusion.8
  299.7 0.3 convolution_convert_fusion.7
  300.2 0.3 convolution_convert_fusion.10
  300.5 0.5 copy-done.5
  301.0 0.3 convolution_convert_fusion.6
  301.3 3.4 convolution_convert_fusion.5
  304.8 1.3 pad_maximum_fusion
  306.1 66.0 %shard_map.334 = (bf16[1536,576]{1,0:T(8,128)(2,1)}, bf16[192,1536]{1,0:T(8,128)(2,1)}, bf16[1536,1536]{1,0:T(8,128)(2,1)}, bf16[4,2,72,768]{3,2,1,0:T(8,128)(2,...) custom-call(bf16[1536,576]{1,0:T(8,128)(2,1)} %get-tuple-element.69.refs_0_, ...), custom_call_target="tpu_custom_call" | custom-call | tf_op jit(solution)/shard_map/pallas_call | solution.py:271
  372.1 3.7 convolution_convert_fusion.4
  375.8 0.3 fusion
  376.2 0.3 fusion.5
  376.5 0.3 convolution_convert_fusion.3
  376.8 1.1 pad_maximum_fusion.1
  377.9 6.6 %convolution_convert_fusion.2 = bf16[576,1536]{1,0:T(8,128)(2,1)} fusion(bf16[1536,576]{1,0:T(8,128)(2,1)S(1)} %copy-done.4, bf16[1536,1536]{1,0:T(8,128)(2,1)} %get-tuple-element.108), kind=kOutput, calls=%fused_computation.2 | convolution fusion | flops 2718793728 | bytes 8257536 | tf_op jit(solution)/shard_map/dot_general | solution.py:36
  384.7 1.0 fusion.1.refs_6_
  385.7 78.7 %shard_map.335 = (bf16[384,768]{1,0:T(8,128)(2,1)}, bf16[4,2,72,768]{3,2,1,0:T(8,128)(2,1)}, bf16[4,2,48,768]{3,2,1,0:T(8,128)(2,1)}, f32[8,768]{1,0:T(8,128)}, ...) custom-call(bf16[1536,576]{1,0:T(8,128)(2,1)} %get-tuple-element.100.refs_0_, ...), custom_call_target="tpu_custom_call" | custom-call | tf_op jit(solution)/shard_map/pallas_call | solution.py:271
  464.4 1.3 bitcast_convert_fusion.3
  465.7 1.2 slice_bitcast_fusion.1
  467.1 1.1 fusion.13
  468.2 1.1 convert_element_type.97
  469.3 0.8 bitcast_convert_fusion.4
  470.1 0.6 slice_reduce_fusion
  470.9 1.2 fusion.12
  472.2 0.8 copy.44
  (53 shorter events, 1.0 us)
Async XLA Ops:
  120.4 75.1 %slice-start = ((s8[4718592]{0:T(1024)(128)(4,1)}), s8[524288]{0:T(1024)(128)(4,1)S(1)}, s32[]{:S(2)}) async-start(s8[4718592]{0:T(1024)(128)(4,1)} %bitcast.90), calls=%async_computation | async-start | bytes 1048576
  186.9 8.6 %slice-start.1 = ((s8[4718592]{0:T(1024)(128)(4,1)}), s8[4194304]{0:T(1024)(128)(4,1)S(1)}, s32[]{:S(2)}) async-start(s8[4718592]{0:T(1024)(128)(4,1)} %bitcast.90), calls=%async_computation.1 | async-start | bytes 8388608
  186.9 8.6 %copy-start.3 = (bf16[1536,768]{1,0:T(8,128)(2,1)S(1)}, bf16[1536,768]{1,0:T(8,128)(2,1)}, u32[]{:S(2)}) copy-start(bf16[1536,768]{1,0:T(8,128)(2,1)} %get-tuple-element.88.refs_3_) | copy-start | bytes 7077892
  294.0 4.3 copy-start.19
  294.0 4.3 copy-start.20
  298.4 1.2 copy-start.15
  298.4 1.6 copy-start
  298.4 1.6 copy-start.1
  298.4 1.6 copy-start.13
  298.4 1.6 copy-start.14
  300.0 0.9 copy-start.5
  300.0 1.0 copy-start.17
  300.1 1.2 copy-start.9
  376.2 1.7 copy-start.4
  377.9 6.6 %copy-start.6 = (bf16[768,192]{0,1:T(8,128)(2,1)S(1)}, bf16[768,192]{0,1:T(8,128)(2,1)}, u32[]{:S(2)}) copy-start(bf16[768,192]{0,1:T(8,128)(2,1)} %param.32) | copy-start | bytes 884740
  377.9 6.6 %copy-start.7 = (bf16[768,192]{0,1:T(8,128)(2,1)S(1)}, bf16[768,192]{0,1:T(8,128)(2,1)}, u32[]{:S(2)}) copy-start(bf16[768,192]{0,1:T(8,128)(2,1)} %param.31) | copy-start | bytes 884740
  377.9 6.6 %copy-start.10 = (bf16[384,768]{1,0:T(8,128)(2,1)S(1)}, bf16[384,768]{1,0:T(8,128)(2,1)}, u32[]{:S(2)}) copy-start(bf16[384,768]{1,0:T(8,128)(2,1)} %get-tuple-element.107) | copy-start | bytes 1769476
  465.7 1.3 copy-start.2
  467.0 1.2 copy-start.11
  467.1 2.2 copy-start.16
  467.1 3.0 copy-start.18
  467.1 3.6 copy-start.8
  470.9 1.3 copy-start.12

commit v7 on v6

--- a/solution.py
+++ b/solution.py
@@ -118,7 +118,7 @@
         return [lax.rem(at.w + k, 8) for k in range(1, 8)]
 
     def peers(self, at):
-        return [(f"w{k + 1}", {"wide": w}) for k, w in enumerate(self.others(at))]
+        return [(f"w{k}", {"wide": w}) for k, w in enumerate(self.others(at), 1)]
 
     def moves(self, at, ins, outs):
         mine = at.spot(at.y, at.c)
@@ -216,6 +216,9 @@
     side_ins = [a for b in beside for a in b.ins]
     side_outs = [a for b in beside for a in b.outs]
     n_in, n_out, n_scratch = len(ins), len(outs), len(scratch)
+    loaded = [i for i, m in enumerate(spaces) if m is VMEM]
+    stored = [i for i, m in enumerate(out_spaces) if m is VMEM]
+    buffers = [VMEM(ins[i].shape, ins[i].dtype) for i in loaded] + [VMEM(outs[i].shape, outs[i].dtype) for i in stored]
 
     def kernel(*refs):
         at = Place()
@@ -228,10 +231,31 @@
 
         main_in, side_in = take(n_in), take(len(side_ins))
         main_out, side_out, kept = take(n_out), take(len(side_outs)), take(n_scratch)
-        send, recv, local = take(3)
+        in_buffers, out_buffers = take(len(loaded)), take(len(stored))
+        send, recv, local, passing = take(4)
+        loads, stores = [], {}
+        for k, i in enumerate(loaded):
+            loads.append(pltpu.make_async_copy(main_in[i], in_buffers[k], passing.at[k]))
+            loads[-1].start()
+            main_in[i] = in_buffers[k]
+        for k, i in enumerate(stored):
+            stores[i] = pltpu.make_async_copy(out_buffers[k], main_out[i], passing.at[len(loaded) + k])
+            main_out[i] = out_buffers[k]
+        waiting = dict(stores)
+
+        def flush(*which):
+            for i in which or list(waiting):
+                waiting.pop(i).start()
+
+        at.flush = flush
         known = dict(peers(at)) if peers else {}
         for b in beside:
             known.update(dict(b.peers(at)))
+        if "w1" in known:
+            for name in ("up", "down", "core", "a0"):
+                known.pop(name, None)
+        if "x01" in known:
+            known.pop("x", None)
         if known:
             greet(list(known.values()))
         side_refs = [([side_in.pop(0) for _ in b.ins], [side_out.pop(0) for _ in b.outs]) for b in beside]
@@ -263,21 +287,29 @@
         at.start_beside = start
         if not late:
             start()
+        for copy in loads:
+            copy.wait()
         if body:
             body(at, main_in, main_out, kept)
+        flush()
         for wait in todo:
             wait()
+        for copy in stores.values():
+            copy.wait()
 
     results = pl.pallas_call(
         kernel,
         out_shape=tuple(outs) + tuple(side_outs),
-        in_specs=[pl.BlockSpec(memory_space=s) for s in spaces] + [pl.BlockSpec(memory_space=ANY)] * len(side_ins),
-        out_specs=tuple(pl.BlockSpec(memory_space=m) for m in out_spaces + [ANY] * len(side_outs)),
+        in_specs=[pl.BlockSpec(memory_space=VMEM if m == PLAIN else ANY) for m in spaces]
+        + [pl.BlockSpec(memory_space=ANY)] * len(side_ins),
+        out_specs=(pl.BlockSpec(memory_space=ANY),) * (len(outs) + len(side_outs)),
         scratch_shapes=[
             *scratch,
+            *buffers,
             pltpu.SemaphoreType.DMA((max(copies, 1),)),
             pltpu.SemaphoreType.DMA((max(copies, 1),)),
             pltpu.SemaphoreType.DMA((max(locals_, 1),)),
+            pltpu.SemaphoreType.DMA((max(len(buffers), 1),)),
         ],
         compiler_params=pltpu.CompilerParams(
             collective_id=number, has_side_effects=True, vmem_limit_bytes=58 << 20
@@ -290,6 +322,9 @@
         sides.append(rest[: len(b.outs)])
         del rest[: len(b.outs)]
     return main, sides
+
+
+PLAIN = "plain"
 
 
 def ring_peers(at):
@@ -828,6 +863,7 @@
                 for copy in go[1:]:
                     copy.wait_recv()
                 at.start_beside()
+                at.flush(0, 1, 2)
 
             @pl.when(s >= 4)
             def _():
@@ -848,6 +884,7 @@
             return carry
 
         lax.fori_loop(0, 4, rest, 0)
+        at.flush(4)
         outputs.pass_far()
         around.pass_far()
         text_go.wait()
@@ -887,6 +924,7 @@
         ],
         beside,
         lambda at: ring_peers(at) + relay.peers(at) + [("x", at.x())] + GatherZ.peers(at),
+        spaces=[ANY] + [PLAIN] * 6 + [VMEM] * 7,
         out_spaces=[VMEM, VMEM, VMEM, ANY, VMEM, ANY, VMEM, VMEM],
         late=True,
     )
@@ -935,6 +973,7 @@
         first.pass_near()
         second.pass_near()
         out[...] = jnp.concatenate([mixed[h] for h in range(HEADS)], axis=1)
+        at.flush()
         first.pass_far()
         second.pass_far()
         first.got(4, 7, 8, 9, 10)
@@ -1040,6 +1079,7 @@
         by_rows(BLOCK, 32, norm_three)
         gather = Gather(at, normed, whole, send, recv, local.at[10], 10)
         gather.begin()
+        at.flush(0, 1, 2, 3)
         swap.wait_recv()
         keep_contract = pltpu.make_async_copy(contract_full, contract_out, local.at[11])
         keep_contract.start()
@@ -1059,6 +1099,7 @@
             grad[rows] = (grad[rows].astype(f32) * slope).astype(bf16)
 
         gather.each(work)
+        at.flush()
         keep.wait()
         keep_contract.wait()
         for copy in made:
@@ -1169,14 +1210,18 @@
             @pl.when(b == 3)
             def _():
                 before.pass_on()
-                before.pass_near()
+
+            @pl.when(b == 5)
+            def _():
+                for reduce in reduces:
+                    reduce.third()
 
             return carry
 
         lax.fori_loop(0, 8, cross, 0)
-
+        at.flush(1, 2)
         for reduce in reduces:
-            reduce.third()
+            reduce.fourth()
 
         def norm_two(rows, carry):
             incoming = second[rows]
@@ -1190,9 +1235,9 @@
         grad_vectors[2:3] = gains
         grad_vectors[3:4] = shifts
         gather = Gather(at, rounded, whole, send, recv, local.at[7], 21)
+        before.pass_near()
         gather.begin()
-        for reduce in reduces:
-            reduce.fourth()
+        at.flush(0, 6)
         before.pass_far()
         keep = Keep(whole, all_rows, local, 8)
 
@@ -1201,6 +1246,7 @@
             grad_mixed[rows] = dot_flip(whole[rows], out_full[...]).astype(bf16)
 
         gather.each(work)
+        at.flush()
         before.got(4, 7, 8, 9, 10)
         before.end()
         keep.wait()
@@ -1320,7 +1366,9 @@
         def finish(rows, carry):
             result[rows] = (after[rows] + scatter.total(rows)).astype(bf16)
 
+        at.flush(0)
         by_rows(BLOCK, 32, finish)
+        at.flush(1)
         gather.got(4, 7, 8, 9, 10)
         gather.end()
         scatter.end()
@@ -1353,17 +1401,15 @@
     def ring(at):
         return [{"wide": lax.rem(at.w + k, 8)} for k in range(1, 8)]
 
-    def clips(at):
-        return [(k, b, {**at.at_dp(k), "narrow": lax.rem(at.n + b, 2)}) for k in range(8) for b in range(2)][1:]
+    x_steps = ((0, 1), (1, 0), (1, 1))
 
     def group(at):
         return [(b, {"wide": lax.rem(at.w + k, 8), "narrow": lax.rem(at.n + b, 2)}) for k in range(8) for b in range(2)][1:]
 
     def peers(at):
         known = ring_peers(at) + relay.peers(at) + Reduce.peers(at)
-        known += [(f"r{i}", peer) for i, peer in enumerate(ring(at))]
-        known += [(f"c{i}", peer) for i, (_, _, peer) in enumerate(clips(at))]
-        return known + [(f"g{i}", peer) for i, (_, peer) in enumerate(group(at))]
+        known += [(f"w{k}", peer) for k, peer in enumerate(ring(at), 1)]
+        return known + [(f"g{i}", peer) for i, (b, peer) in enumerate(group(at)) if b]
 
     def body(at, ins, outs, kept):
         grad, weight, x, vectors, before, late, text, one, two = ins
@@ -1373,13 +1419,13 @@
             Reduce(at, one, out_one, kept[0:4], kept[-3], kept[-2], kept[-1], 12, 1, False),
             Reduce(at, two, out_two, kept[4:8], kept[-3], kept[-2], kept[-1], 22, 3, True),
         ]
-        rounded, parts, ring_parts, ring_sum, clip_parts, text_parts, text_sum, send, recv, local = kept[8:]
+        rounded, parts, ring_parts, ring_sum, x_parts, x_sum, z_parts, text_parts, text_sum, send, recv, local = kept[8:]
         me = at.spot(at.y, at.c)
 
         def move(slot, source, target, peer):
             return remote(source, target, send.at[slot], recv.at[slot], peer)
 
-        to_ring, to_clips, to_group = ring(at), clips(at), group(at)
+        to_ring, to_group = ring(at), group(at)
         slot = 32
         trades = []
         for peer in to_ring:
@@ -1399,11 +1445,15 @@
             slot += 1
         ring_own = pltpu.make_async_copy(parts, ring_parts.at[at.w], local.at[7])
         spreads = []
-        for _, b, peer in to_clips:
-            n = lax.rem(at.n + b, 2)
-            spreads.append(move(slot, ring_sum.at[:, at.half(n)], clip_parts.at[at.dp, at.n], peer))
+        for a, b in x_steps:
+            half = ring_sum.at[:, at.half(lax.rem(at.n + b, 2))]
+            spreads.append(move(slot, half, x_parts.at[at.s, at.n], at.at_x(a, b)))
             slot += 1
-        clip_own = pltpu.make_async_copy(ring_sum.at[:, at.half(at.n)], clip_parts.at[at.dp, at.n], local.at[8])
+        x_own = pltpu.make_async_copy(ring_sum.at[:, at.half(at.n)], x_parts.at[at.s, at.n], local.at[8])
+        lasts = []
+        for k in (1, 2, 3):
+            lasts.append(move(slot, x_sum, z_parts.at[at.z], at.at_z(k)))
+            slot += 1
 
         for reduce in reduces:
             reduce.first()
@@ -1454,23 +1504,28 @@
         for i in range(1, 8):
             total += ring_parts[i]
         ring_sum[...] = total
-        clip_own.start()
+        x_own.start()
         for copy in spreads:
             copy.start()
         for reduce in reduces:
             reduce.fourth()
-        clip_own.wait()
+        x_own.wait()
         for copy in spreads:
             copy.wait_recv()
-        total = clip_parts[0, 0] + clip_parts[0, 1]
-        for i in range(1, 8):
-            total += clip_parts[i, 0] + clip_parts[i, 1]
-        vector_sums[...] = total
+        total = x_parts[0, 0] + x_parts[0, 1] + x_parts[1, 0] + x_parts[1, 1]
+        x_sum[...] = total
+        for copy in lasts:
+            copy.start()
+        z_parts[pl.ds(at.z, 1)] = total.reshape(1, 8, HALF)
+        for copy in lasts:
+            copy.wait_recv()
+        vector_sums[...] = z_parts[0] + z_parts[1] + z_parts[2] + z_parts[3]
+        at.flush()
         moving(True)
         text_stay.wait()
         for copy in texts:
             copy.wait()
-        for copy in trades + rings + spreads:
+        for copy in trades + rings + spreads + lasts:
             copy.wait_send()
         scatter.end()
         for reduce in reduces:
@@ -1495,10 +1550,12 @@
             VMEM((8, D), f32),
             VMEM((8, 8, D), f32),
             VMEM((8, D), f32),
-            VMEM((8, 2, 8, HALF), f32),
+            VMEM((2, 2, 8, HALF), f32),
+            VMEM((8, HALF), f32),
+            VMEM((4, 8, HALF), f32),
             VMEM((8, some, D), bf16),
             VMEM((some, D), bf16),
-            *sems(32 + 7 + 15 + 7 + 15),
+            *sems(32 + 7 + 15 + 7 + 6),
         ],
         beside,
         peers,

time: 482 us -> 458 us (0.950)
  Pallas kernels: 422 us -> 398 us
    pallas_call x6, Pallas kernels: 422 us -> 398 us  [call(): pl.pallas_call(kernel, out_shape=tuple(outs) + tuple(side_outs), in_specs...]
where the time goes in v7:
time: 458 us; the launch traced here: 449 us
  Pallas kernels  398 us (87%)
  matrix products  31.4 us (7%)
  other arithmetic  12.4 us (3%)
  local copies, waits for them, and re-layouts  5.98 us (1%)
    pallas_call x6, Pallas kernels, call(): pl.pallas_call(kernel, out_shape=tuple(outs) + tuple(side_outs), in_specs...  398 us
    dot_general x8, matrix products, outer(): lax.dot_general(a, b, (((0,), (0,)), ((), ())), preferred_element_type=f32)  29.2 us

profile of v7, /device:TPU:0, one launch (start us, length us, event | category | flops | bytes accessed | tf_op | source)
XLA Modules:
  0.0 449.5 jit_solution(9970967997721624977)
XLA Ops:
  0.7 1.9 pad_maximum_fusion.2.refs_13_.refs_9_
  2.6 68.9 %shard_map.330 = (bf16[192,1536]{1,0:T(8,128)(2,1)}, f32[8,1536]{1,0:T(8,128)}, bf16[576,1536]{1,0:T(8,128)(2,1)}, bf16[1536,1536]{1,0:T(8,128)(2,1)}, bf16[1536...) custom-call(bf16[384,768]{1,0:T(8,128)(2,1)} %refs_0_.1, ...), custom_call_target="tpu_custom_call" | custom-call | tf_op jit(solution)/shard_map/pallas_call | solution.py:300
  71.5 43.9 %shard_map.331 = (bf16[1536,192]{1,0:T(8,128)(2,1)}, f32[8,1536]{1,0:T(8,128)}, bf16[1536,1536]{1,0:T(8,128)(2,1)}, bf16[1536,1536]{1,0:T(8,128)(2,1)}, bf16[8,6...) custom-call(bf16[1536,576]{1,0:T(8,128)(2,1)} %get-tuple-element.69.refs_0_, ...), custom_call_target="tpu_custom_call" | custom-call | tf_op jit(solution)/shard_map/pallas_call | solution.py:300
  115.4 64.0 %shard_map.332 = (f32[192,1536]{1,0:T(8,128)}, f32[192,1536]{1,0:T(8,128)}, bf16[192,1536]{1,0:T(8,128)(2,1)}, bf16[8,192,192]{2,1,0:T(8,128)(2,1)}, bf16[1536,1...) custom-call(bf16[1536,192]{1,0:T(8,128)(2,1)} %get-tuple-element.73., ...), custom_call_target="tpu_custom_call" | custom-call | tf_op jit(solution)/shard_map/pallas_call | solution.py:300
  179.4 8.5 %convolution_convert_fusion = bf16[1536,768]{1,0:T(8,128)(2,1)} fusion(bf16[1536,1536]{1,0:T(8,128)(2,1)} %get-tuple-element.89, bf16[1536,768]{1,0:T(8,128)(2,1)} %get-tuple-element.82.refs_0_), kind=kOutput, calls=%fused_computation | convolution fusion | flops 3625058304 | bytes 9437184 | tf_op jit(solution)/shard_map/dot_general | solution.py:36
  188.0 5.2 %convolution_convert_fusion.1 = bf16[768,1536]{1,0:T(8,128)(2,1)} fusion(bf16[1536,768]{1,0:T(8,128)(2,1)S(1)} %copy-done.3, bf16[1536,1536]{1,0:T(8,128)(2,1)S(1)} %bitcast.91), kind=kOutput, calls=%fused_computation.1 | convolution fusion | flops 3625058304 | bytes 9437184 | tf_op jit(solution)/shard_map/dot_general | solution.py:36
  193.1 87.2 %shard_map.333 = (f32[192,1536]{1,0:T(8,128)}, bf16[192,1536]{1,0:T(8,128)(2,1)}, bf16[8,192,192]{2,1,0:T(8,128)(2,1)}, bf16[1536,1536]{1,0:T(8,128)(2,1)}, bf16...) custom-call(bf16[1536,768]{1,0:T(8,128)(2,1)} %get-tuple-element.82., ...), custom_call_target="tpu_custom_call" | custom-call | tf_op jit(solution)/shard_map/pallas_call | solution.py:300
  280.4 4.3 bitcast_convert_fusion
  284.7 1.1 convolution_convert_fusion.8
  286.0 0.3 convolution_convert_fusion.7
  286.5 0.3 convolution_convert_fusion.10
  286.8 0.5 copy-done.5
  287.4 0.3 convolution_convert_fusion.6
  287.7 3.5 convolution_convert_fusion.5
  291.1 1.3 pad_maximum_fusion
  292.5 63.1 %shard_map.334 = (bf16[1536,576]{1,0:T(8,128)(2,1)}, bf16[192,1536]{1,0:T(8,128)(2,1)}, bf16[1536,1536]{1,0:T(8,128)(2,1)}, bf16[4,2,72,768]{3,2,1,0:T(8,128)(2,...) custom-call(bf16[1536,576]{1,0:T(8,128)(2,1)} %get-tuple-element.69.refs_0_, ...), custom_call_target="tpu_custom_call" | custom-call | tf_op jit(solution)/shard_map/pallas_call | solution.py:300
  355.5 3.7 convolution_convert_fusion.4
  359.2 0.3 fusion
  359.6 0.3 fusion.5
  359.9 0.3 convolution_convert_fusion.3
  360.2 1.1 pad_maximum_fusion.1
  361.3 6.6 %convolution_convert_fusion.2 = bf16[576,1536]{1,0:T(8,128)(2,1)} fusion(bf16[1536,576]{1,0:T(8,128)(2,1)S(1)} %copy-done.4, bf16[1536,1536]{1,0:T(8,128)(2,1)} %get-tuple-element.108), kind=kOutput, calls=%fused_computation.2 | convolution fusion | flops 2718793728 | bytes 8257536 | tf_op jit(solution)/shard_map/dot_general | solution.py:36
  368.1 1.0 fusion.1.refs_6_
  369.2 71.3 %shard_map.335 = (bf16[384,768]{1,0:T(8,128)(2,1)}, bf16[4,2,72,768]{3,2,1,0:T(8,128)(2,1)}, bf16[4,2,48,768]{3,2,1,0:T(8,128)(2,1)}, f32[8,768]{1,0:T(8,128)}, ...) custom-call(bf16[1536,576]{1,0:T(8,128)(2,1)} %get-tuple-element.100.refs_0_, ...), custom_call_target="tpu_custom_call" | custom-call | tf_op jit(solution)/shard_map/pallas_call | solution.py:300
  440.4 1.3 bitcast_convert_fusion.3
  441.7 1.2 slice_bitcast_fusion.1
  443.1 1.1 fusion.13
  444.2 1.1 convert_element_type.97
  445.3 0.8 bitcast_convert_fusion.4
  446.1 0.6 slice_reduce_fusion
  446.9 1.2 fusion.12
  448.2 0.8 copy.44
  (53 shorter events, 1.0 us)
Async XLA Ops:
  115.4 72.6 %slice-start = ((s8[4718592]{0:T(1024)(128)(4,1)}), s8[524288]{0:T(1024)(128)(4,1)S(1)}, s32[]{:S(2)}) async-start(s8[4718592]{0:T(1024)(128)(4,1)} %bitcast.90), calls=%async_computation | async-start | bytes 1048576
  179.4 8.6 %slice-start.1 = ((s8[4718592]{0:T(1024)(128)(4,1)}), s8[4194304]{0:T(1024)(128)(4,1)S(1)}, s32[]{:S(2)}) async-start(s8[4718592]{0:T(1024)(128)(4,1)} %bitcast.90), calls=%async_computation.1 | async-start | bytes 8388608
  179.4 8.6 %copy-start.3 = (bf16[1536,768]{1,0:T(8,128)(2,1)S(1)}, bf16[1536,768]{1,0:T(8,128)(2,1)}, u32[]{:S(2)}) copy-start(bf16[1536,768]{1,0:T(8,128)(2,1)} %get-tuple-element.88.refs_3_) | copy-start | bytes 7077892
  280.4 4.3 copy-start.19
  280.4 4.3 copy-start.20
  284.7 1.2 copy-start.15
  284.7 1.6 copy-start
  284.7 1.6 copy-start.1
  284.7 1.6 copy-start.13
  284.7 1.6 copy-start.14
  286.3 0.9 copy-start.5
  286.4 1.0 copy-start.17
  286.5 1.2 copy-start.9
  359.6 1.7 copy-start.4
  361.3 6.6 %copy-start.6 = (bf16[768,192]{0,1:T(8,128)(2,1)S(1)}, bf16[768,192]{0,1:T(8,128)(2,1)}, u32[]{:S(2)}) copy-start(bf16[768,192]{0,1:T(8,128)(2,1)} %param.32) | copy-start | bytes 884740
  361.3 6.6 %copy-start.7 = (bf16[768,192]{0,1:T(8,128)(2,1)S(1)}, bf16[768,192]{0,1:T(8,128)(2,1)}, u32[]{:S(2)}) copy-start(bf16[768,192]{0,1:T(8,128)(2,1)} %param.31) | copy-start | bytes 884740
  361.3 6.6 %copy-start.10 = (bf16[384,768]{1,0:T(8,128)(2,1)S(1)}, bf16[384,768]{1,0:T(8,128)(2,1)}, u32[]{:S(2)}) copy-start(bf16[384,768]{1,0:T(8,128)(2,1)} %get-tuple-element.107) | copy-start | bytes 1769476
  441.7 1.3 copy-start.2
  443.0 1.2 copy-start.11
  443.1 2.2 copy-start.16
  443.1 3.0 copy-start.18
  443.1 3.6 copy-start.8
  446.9 1.3 copy-start.12

commit v8 on v7

--- a/solution.py
+++ b/solution.py
@@ -107,24 +107,6 @@
 
     def moves(self, at, ins, outs):
         return [(ins[0].at[1 - at.n], outs[0], at.x())], []
-
-
-class Trade:
-    def __init__(self, array):
-        self.ins, self.copies, self.locals = [array], 7, 1
-        self.outs = [jax.ShapeDtypeStruct(array.shape, array.dtype)]
-
-    def others(self, at):
-        return [lax.rem(at.w + k, 8) for k in range(1, 8)]
-
-    def peers(self, at):
-        return [(f"w{k}", {"wide": w}) for k, w in enumerate(self.others(at), 1)]
-
-    def moves(self, at, ins, outs):
-        mine = at.spot(at.y, at.c)
-        dst = outs[0].at[mine]
-        far = [(ins[0].at[at.spot(lax.div(w, 2), lax.rem(w, 2))], dst, {"wide": w}) for w in self.others(at)]
-        return far, [(ins[0].at[mine], dst)]
 
 
 class ToSpots:
@@ -357,6 +339,46 @@
             copy.wait()
 
 
+class Trade:
+    def __init__(self, at, parts, out, send, recv, local, base):
+        self.at, self.parts, self.out, self.send, self.recv, self.base = at, parts, out, send, recv, base
+        self.me = at.spot(at.y, at.c)
+        self.own = pltpu.make_async_copy(parts.at[self.me], out.at[self.me], local)
+
+    @staticmethod
+    def peers(at):
+        return [(f"w{k}", {"wide": lax.rem(at.w + k, 8)}) for k in range(1, 8)]
+
+    def copy(self, b, place):
+        m, core, a = lax.rem(b, 2), lax.rem(lax.div(b, 2), 2), lax.div(b, 4)
+        y = 2 * lax.rem(m + self.at.n, 2) + lax.rem(a + m, 2)
+        send, recv = self.send.at[self.base + b], self.recv.at[self.base + place]
+        return remote(self.parts.at[b], self.out.at[place], send, recv, {"wide": y * 2 + core})
+
+    def give(self, b):
+        @pl.when(b == self.me)
+        def _():
+            self.own.start()
+
+        @pl.when(b != self.me)
+        def _():
+            self.copy(b, self.me).start()
+
+    def end(self):
+        def wait(b, carry):
+            @pl.when(b == self.me)
+            def _():
+                self.own.wait()
+
+            @pl.when(b != self.me)
+            def _():
+                self.copy(b, b).wait()
+
+            return carry
+
+        lax.fori_loop(0, 8, wait, 0)
+
+
 class Reduce:
     @staticmethod
     def scratch(deep, x_first, by_rows=False):
@@ -995,8 +1017,8 @@
 def forward_rest(number, attended, out_w, x, vectors, query_all, out_all, texts, all_down, expand_w, contract):
     def body(at, ins, outs, kept):
         mixed, out_own, out_got, x, vectors, query_all, out_all, texts, all_down, expand_own, expand_got, contract_own = ins
-        middle, after, normed_two, weights, all_rows, activated, grad, contract_out, keys_out, values_out = outs
-        *refs, normed, whole, downs, out_full, expand_full, contract_full, key_full, value_full, branch, send, recv, local = kept
+        middle, after, normed_two, weights, all_rows, activated, grad, contract_out, keys_out, values_out, traded = outs
+        *refs, normed, whole, downs, out_full, expand_full, contract_full, key_full, value_full, branch, scores_all, send, recv, local = kept
         half = at.half(at.n)
         weight = Whole(at, out_own, out_got, out_full, local.at[pl.ds(0, 2)], 1)
         swap = remote(contract_own, contract_full.at[:, half], send.at[21], recv.at[21], at.x())
@@ -1049,13 +1071,21 @@
 
         by_rows(BLOCK, 32, norm_two)
 
+        trade = Trade(at, weights, traded, send, recv, local.at[20], 22)
+
+        def score(rows, carry):
+            scores_all[rows] = dot_flip(key_full[rows], normed_two[...])
+
+        by_rows(D, QUARTER, score)
+
         def cross(b, carry):
             rows = pl.ds(pl.multiple_of(b * BLOCK, BLOCK), BLOCK)
-            scores = dot_flip(key_full[rows], normed_two[...]).reshape(HEADS, 64, BLOCK)
+            scores = scores_all[rows].reshape(HEADS, 64, BLOCK)
             raised = jnp.exp(scores - jnp.max(scores, axis=1, keepdims=True))
             p = raised / jnp.sum(raised, axis=1, keepdims=True)
             p = p.reshape(BLOCK, BLOCK).T.astype(bf16)
             weights[b] = p
+            trade.give(b)
             part = dot(p, value_full[rows])
 
             @pl.when(b == 0)
@@ -1102,6 +1132,7 @@
         at.flush()
         keep.wait()
         keep_contract.wait()
+        trade.end()
         for copy in made:
             copy.wait()
         scatter.end()
@@ -1122,6 +1153,7 @@
             shape(HALF, D),
             shape(D, D),
             shape(D, D),
+            shape(8, BLOCK, BLOCK),
         ],
         [
             *Scatter.scratch,
@@ -1134,12 +1166,13 @@
             VMEM((D, D), bf16),
             VMEM((D, D), bf16),
             VMEM((BLOCK, D), f32),
-            *sems(22),
+            VMEM((D, BLOCK), f32),
+            *sems(30),
         ],
         (),
-        lambda at: ring_peers(at) + [("x", at.x())],
+        lambda at: Trade.peers(at) + [("x", at.x())],
         spaces=[VMEM, ANY, ANY, VMEM, VMEM, ANY, ANY, VMEM, ANY, ANY, ANY, ANY],
-        out_spaces=[VMEM, VMEM, VMEM, VMEM, ANY, VMEM, VMEM, ANY, ANY, ANY],
+        out_spaces=[VMEM, VMEM, VMEM, VMEM, ANY, VMEM, VMEM, ANY, ANY, ANY, ANY],
     )
     return results
 
@@ -1149,11 +1182,11 @@
 ):
     def body(at, ins, outs, kept):
         grad, expand_own, expand_got, after, middle, vectors, down, keys, values, weights, out_own, out_got = ins[:12]
-        grad_rows, rounded_two, grad_scores, all_two, all_rows, grad_mixed, grad_vectors = outs[:7]
-        *refs, rounded, whole, second, out_full, expand_full, key_full, value_full, send, recv, local = kept
+        grad_rows, rounded_two, traded, all_two, all_rows, grad_mixed, grad_vectors = outs[:7]
+        *refs, rounded, whole, second, out_full, expand_full, key_full, value_full, grad_scores, grads_all, send, recv, local = kept
         reduces = [
             Reduce(at, ins[12], outs[7], refs[7:11], send, recv, local, 32, 16, False),
-            Reduce(at, ins[13], outs[8], refs[11:15], send, recv, local, 42, 18, True, True),
+            Reduce(at, ins[13], outs[8], refs[11:15], send, recv, local, 42, 18, True),
         ]
         refs = refs[:7]
         for reduce in reduces:
@@ -1190,13 +1223,21 @@
         grad_vectors[4:5] = gains
         grad_vectors[5:6] = shifts
 
+        trade = Trade(at, grad_scores, traded, send, recv, local.at[20], 52)
+
+        def score(rows, carry):
+            grads_all[rows] = dot_flip(value_full[rows], rounded_two[...])
+
+        by_rows(D, QUARTER, score)
+
         def cross(b, carry):
             rows = pl.ds(pl.multiple_of(b * BLOCK, BLOCK), BLOCK)
             p = weights[b].astype(f32).T.reshape(HEADS, 64, BLOCK)
-            dp = dot_flip(value_full[rows], rounded_two[...]).reshape(HEADS, 64, BLOCK)
+            dp = grads_all[rows].reshape(HEADS, 64, BLOCK)
             ds = p * (dp - jnp.sum(p * dp, axis=1, keepdims=True))
             ds = ds.reshape(BLOCK, BLOCK).T.astype(bf16)
             grad_scores[b] = ds
+            trade.give(b)
             part = dot(ds, key_full[rows])
 
             @pl.when(b == 0)
@@ -1219,7 +1260,7 @@
             return carry
 
         lax.fori_loop(0, 8, cross, 0)
-        at.flush(1, 2)
+        at.flush(1)
         for reduce in reduces:
             reduce.fourth()
 
@@ -1249,6 +1290,7 @@
         at.flush()
         before.got(4, 7, 8, 9, 10)
         before.end()
+        trade.end()
         keep.wait()
         scatter.end()
         for reduce in reduces:
@@ -1272,7 +1314,7 @@
         [
             *Scatter.scratch,
             *Reduce.scratch(96, False),
-            *Reduce.scratch(96, True, True),
+            *Reduce.scratch(96, True),
             VMEM((BLOCK, D), bf16),
             VMEM((D, D), bf16),
             VMEM((BLOCK, D), f32),
@@ -1280,12 +1322,14 @@
             VMEM((D, HALF), bf16),
             VMEM((D, D), bf16),
             VMEM((D, D), bf16),
-            *sems(52),
+            VMEM((8, BLOCK, BLOCK), bf16),
+            VMEM((D, BLOCK), f32),
+            *sems(60),
         ],
         beside,
-        lambda at: ring_peers(at) + Reduce.peers(at),
+        lambda at: Trade.peers(at) + Reduce.peers(at),
         spaces=[VMEM, ANY, ANY, VMEM, VMEM, VMEM, VMEM, ANY, ANY, VMEM, ANY, ANY, ANY, ANY],
-        out_spaces=[VMEM, VMEM, VMEM, ANY, ANY, VMEM, VMEM, ANY, ANY],
+        out_spaces=[VMEM, VMEM, ANY, ANY, ANY, VMEM, VMEM, ANY, ANY],
     )
 
 
@@ -1592,7 +1636,7 @@
     pair_t = jnp.concatenate((cross_key.T, cross_value.T), axis=0)
     n = lax.axis_index("narrow")
 
-    results, ((down,), (text_got,)) = enter(
+    results, ((down,), (out_got,), (text_got,)) = enter(
         1,
         layer_input,
         gains,
@@ -1601,20 +1645,19 @@
         cross_output,
         text_states,
         pair_t,
-        [Relay(cotangent), GiveClip(text_states)],
+        [Relay(cotangent), Give(output_weight), GiveClip(text_states)],
     )
     x, vectors, joined, all_one, qkv, query_all, out_quarter, text_pair = results
-    (attended, logs, all_down, out_all), ((texts,), (out_got,), (expand_got,)) = causal_forward(
-        2, qkv, down, out_quarter, [ToSpots(text_pair), Give(output_weight), Give(expand_weight)]
+    (attended, logs, all_down, out_all), ((texts,), (expand_got,)) = causal_forward(
+        2, qkv, down, out_quarter, [ToSpots(text_pair), Give(expand_weight)]
     )
     out_w, expand_w = (output_weight, out_got), (expand_weight, expand_got)
-    middle, after, normed_two, cross_p, all_three, activated, grad_expand, contract, all_keys, all_values = forward_rest(
-        3, attended, out_w, x, vectors, query_all, out_all, texts, all_down, expand_w, contract_weight
-    )
+    results = forward_rest(3, attended, out_w, x, vectors, query_all, out_all, texts, all_down, expand_w, contract_weight)
+    middle, after, normed_two, cross_p, all_three, activated, grad_expand, contract, all_keys, all_values, traded_p = results
 
     contract_part = outer(activated, all_down).astype(bf16).reshape(4, 2, 96, D)
-    expand_part = outer(all_three, grad_expand).astype(bf16).reshape(2, 4, 2, 96, HALF)
-    results, ((cross_p,), (query_got,), (cross_got,)) = backward_rest(
+    expand_part = outer(grad_expand, all_three).astype(bf16).reshape(4, 2, 96, D)
+    results, ((query_got,), (cross_got,)) = backward_rest(
         4,
         grad_expand,
         expand_w,
@@ -1628,7 +1671,7 @@
         out_w,
         contract_part,
         expand_part,
-        [Trade(cross_p), Give(query_t), Give(cross_output)],
+        [Give(query_t), Give(cross_output)],
     )
     grad_one, _, grad_scores, all_mid_two, all_mid_one, grad_attended, late, contract_grad, expand_grad = results
 
@@ -1642,12 +1685,12 @@
 
     text = whole(lax.dynamic_index_in_dim(text_states, n, 0, False), text_got)
     text_heads = text_pair.reshape(64, 2, HEADS, HDIM)
-    grad_values = outer(cross_p.reshape(D, COLS), all_mid_two).astype(bf16).reshape(HEADS, 64, D)
+    grad_values = outer(traded_p.reshape(D, COLS), all_mid_two).astype(bf16).reshape(HEADS, 64, D)
     heads_out = whole(cross_output, cross_got).reshape(HEADS, HDIM, D)
     grad_text_values = heads("hkf,hdf->khd", grad_values, heads_out).reshape(64, COLS).astype(bf16)
     grad_cross = heads("khd,hkf->hdf", text_heads[:, 1], grad_values).reshape(COLS, D)
     value_part = jnp.concatenate((grad_cross, outer(grad_text_values, text), outer(attended, all_mid_one)), axis=0)
-    (grad_qkv, layer_output, all_two, value_grad), ((grad_scores,), (pair_got,)) = causal_backward(
+    (grad_qkv, layer_output, all_two, value_grad), ((pair_got,),) = causal_backward(
         5,
         qkv,
         grad_attended,
@@ -1657,7 +1700,7 @@
         after,
         normed_two,
         value_part.astype(bf16).reshape(4, 2, 72, D),
-        [Trade(grad_scores), Give(pair_t)],
+        [Give(pair_t)],
     )
 
     joined_part = outer(grad_qkv, all_one).astype(bf16).reshape(4, 2, 72, D)
@@ -1702,7 +1745,7 @@
         value_grad[:COLS],
         parts[4],
         parts[5],
-        expand_grad,
+        expand_grad.T,
         contract_grad,
     )
 

time: 458 us -> 454 us (level)
  Pallas kernels: 398 us -> 392 us
    pallas_call x6, Pallas kernels: 398 us -> 392 us  [call(): pl.pallas_call(kernel, out_shape=tuple(outs) + tuple(side_outs), in_specs...]
where the time goes in v8:
time: 454 us; the launch traced here: 446 us
  Pallas kernels  392 us (86%)
  matrix products  33.7 us (7%)
  other arithmetic  11.5 us (3%)
  local copies, waits for them, and re-layouts  8.07 us (2%)
    pallas_call x6, Pallas kernels, call(): pl.pallas_call(kernel, out_shape=tuple(outs) + tuple(side_outs), in_specs...  392 us
    dot_general x8, matrix products, outer(): lax.dot_general(a, b, (((0,), (0,)), ((), ())), preferred_element_type=f32)  31.5 us

profile of v8, /device:TPU:0, one launch (start us, length us, event | category | flops | bytes accessed | tf_op | source)
XLA Modules:
  0.0 446.2 jit_solution(12215697080477985110)
XLA Ops:
  0.7 1.9 pad_maximum_fusion.2.refs_13_.refs_8_
  2.6 72.5 %shard_map.330 = (bf16[192,1536]{1,0:T(8,128)(2,1)}, f32[8,1536]{1,0:T(8,128)}, bf16[576,1536]{1,0:T(8,128)(2,1)}, bf16[1536,1536]{1,0:T(8,128)(2,1)}, bf16[1536...) custom-call(bf16[384,768]{1,0:T(8,128)(2,1)} %refs_0_.1, ...), custom_call_target="tpu_custom_call" | custom-call | tf_op jit(solution)/shard_map/pallas_call | solution.py:282
  75.1 36.3 %shard_map.331 = (bf16[1536,192]{1,0:T(8,128)(2,1)}, f32[8,1536]{1,0:T(8,128)}, bf16[1536,1536]{1,0:T(8,128)(2,1)}, bf16[1536,1536]{1,0:T(8,128)(2,1)}, bf16[8,6...) custom-call(bf16[1536,576]{1,0:T(8,128)(2,1)} %get-tuple-element.68.refs_0_, ...), custom_call_target="tpu_custom_call" | custom-call | tf_op jit(solution)/shard_map/pallas_call | solution.py:282
  111.4 64.2 %shard_map.332 = (f32[192,1536]{1,0:T(8,128)}, f32[192,1536]{1,0:T(8,128)}, bf16[192,1536]{1,0:T(8,128)(2,1)}, bf16[8,192,192]{2,1,0:T(8,128)(2,1)}, bf16[1536,1...) custom-call(bf16[1536,192]{1,0:T(8,128)(2,1)} %get-tuple-element.72., ...), custom_call_target="tpu_custom_call" | custom-call | tf_op jit(solution)/shard_map/pallas_call | solution.py:282
  175.6 8.5 %convolution_convert_fusion = bf16[768,1536]{1,0:T(8,128)(2,1)} fusion(bf16[1536,768]{1,0:T(8,128)(2,1)} %get-tuple-element.81.refs_0_, bf16[1536,1536]{1,0:T(8,128)(2,1)} %get-tuple-element.88), kind=kOutput, calls=%fused_computation | convolution fusion | flops 3625058304 | bytes 9437184 | tf_op jit(solution)/shard_map/dot_general | solution.py:36
  184.1 5.2 %convolution_convert_fusion.1 = bf16[768,1536]{1,0:T(8,128)(2,1)} fusion(bf16[1536,768]{1,0:T(8,128)(2,1)S(1)} %copy-done.3, bf16[1536,1536]{1,0:T(8,128)(2,1)S(1)} %bitcast.92), kind=kOutput, calls=%fused_computation.1 | convolution fusion | flops 3625058304 | bytes 9437184 | tf_op jit(solution)/shard_map/dot_general | solution.py:36
  189.3 89.3 %shard_map.333 = (f32[192,1536]{1,0:T(8,128)}, bf16[192,1536]{1,0:T(8,128)(2,1)}, bf16[8,192,192]{2,1,0:T(8,128)(2,1)}, bf16[1536,1536]{1,0:T(8,128)(2,1)}, bf16...) custom-call(bf16[1536,768]{1,0:T(8,128)(2,1)} %get-tuple-element.81., ...), custom_call_target="tpu_custom_call" | custom-call | tf_op jit(solution)/shard_map/pallas_call | solution.py:282
  278.5 3.4 bitcast_convert_fusion
  281.9 2.1 copy.43
  284.1 3.8 convolution_convert_fusion.8
  288.0 0.3 convolution_convert_fusion.7
  288.5 0.3 convolution_convert_fusion.10
  288.8 0.5 copy-done.5
  289.4 0.3 convolution_convert_fusion.6
  289.7 3.4 convolution_convert_fusion.5
  293.1 1.3 pad_maximum_fusion
  294.5 57.8 %shard_map.334 = (bf16[1536,576]{1,0:T(8,128)(2,1)}, bf16[192,1536]{1,0:T(8,128)(2,1)}, bf16[1536,1536]{1,0:T(8,128)(2,1)}, bf16[4,2,72,768]{3,2,1,0:T(8,128)(2,1)}, bf16[384,768]{1,0:T(8,128)(2,1)}) custom-call(bf16[1536,576]{1,0:T(8,128)(2,1)} %get-tuple-element.68.refs_0_, bf16[1536,192]{1,0:T(8,128)(2,1)} %get-tuple-element.89.refs_1_, ...), custom_call_target="tpu_custom_call" | custom-call | tf_op jit(solution)/shard_map/pallas_call | solution.py:282
  352.3 3.4 convolution_convert_fusion.4
  355.7 0.3 fusion
  356.1 0.3 fusion.5
  356.7 1.1 pad_maximum_fusion.1
  357.8 6.6 %convolution_convert_fusion.2 = bf16[576,1536]{1,0:T(8,128)(2,1)} fusion(bf16[1536,576]{1,0:T(8,128)(2,1)S(1)} %copy-done.4, bf16[1536,1536]{1,0:T(8,128)(2,1)} %get-tuple-element.106), kind=kOutput, calls=%fused_computation.2 | convolution fusion | flops 2718793728 | bytes 8257536 | tf_op jit(solution)/shard_map/dot_general | solution.py:36
  364.7 1.0 fusion.1.refs_6_
  365.7 71.5 %shard_map.335 = (bf16[384,768]{1,0:T(8,128)(2,1)}, bf16[4,2,72,768]{3,2,1,0:T(8,128)(2,1)}, bf16[4,2,48,768]{3,2,1,0:T(8,128)(2,1)}, f32[8,768]{1,0:T(8,128)}, ...) custom-call(bf16[1536,576]{1,0:T(8,128)(2,1)} %get-tuple-element.98.refs_0_, ...), custom_call_target="tpu_custom_call" | custom-call | tf_op jit(solution)/shard_map/pallas_call | solution.py:282
  437.2 1.3 bitcast_convert_fusion.3
  438.5 1.2 slice_bitcast_fusion.1
  439.8 1.1 fusion.13
  440.9 1.1 convert_element_type.95
  442.0 0.8 bitcast_convert_fusion.4
  442.8 0.6 slice_reduce_fusion
  443.6 1.2 fusion.12
  445.0 0.8 copy.46
  (52 shorter events, 1.3 us)
Async XLA Ops:
  111.4 72.7 %slice-start = ((s8[4718592]{0:T(1024)(128)(4,1)}), s8[524288]{0:T(1024)(128)(4,1)S(1)}, s32[]{:S(2)}) async-start(s8[4718592]{0:T(1024)(128)(4,1)} %bitcast.91), calls=%async_computation | async-start | bytes 1048576
  175.6 8.5 %slice-start.1 = ((s8[4718592]{0:T(1024)(128)(4,1)}), s8[4194304]{0:T(1024)(128)(4,1)S(1)}, s32[]{:S(2)}) async-start(s8[4718592]{0:T(1024)(128)(4,1)} %bitcast.91), calls=%async_computation.1 | async-start | bytes 8388608
  175.6 8.5 %copy-start.3 = (bf16[1536,768]{1,0:T(8,128)(2,1)S(1)}, bf16[1536,768]{1,0:T(8,128)(2,1)}, u32[]{:S(2)}) copy-start(bf16[1536,768]{1,0:T(8,128)(2,1)} %get-tuple-element.87.refs_3_) | copy-start | bytes 7077892
  284.1 3.8 copy-start.15
  284.1 4.3 copy-start
  284.1 4.3 copy-start.1
  284.1 4.3 copy-start.13
  284.1 4.3 copy-start.14
  288.4 0.9 copy-start.5
  288.4 1.0 copy-start.17
  288.5 1.2 copy-start.9
  294.5 57.8 %copy-start.19 = (bf16[8,192,192]{2,1,0:T(8,128)(2,1)S(1)}, bf16[8,192,192]{2,1,0:T(8,128)(2,1)}, u32[]{:S(2)}) copy-start(bf16[8,192,192]{2,1,0:T(8,128)(2,1)} %get-tuple-element.103) | copy-start | bytes 1769476
  356.1 1.7 copy-start.4
  357.8 6.6 %copy-start.6 = (bf16[768,192]{0,1:T(8,128)(2,1)S(1)}, bf16[768,192]{0,1:T(8,128)(2,1)}, u32[]{:S(2)}) copy-start(bf16[768,192]{0,1:T(8,128)(2,1)} %param.32) | copy-start | bytes 884740
  357.8 6.6 %copy-start.7 = (bf16[768,192]{0,1:T(8,128)(2,1)S(1)}, bf16[768,192]{0,1:T(8,128)(2,1)}, u32[]{:S(2)}) copy-start(bf16[768,192]{0,1:T(8,128)(2,1)} %param.31) | copy-start | bytes 884740
  357.8 6.6 %copy-start.10 = (bf16[384,768]{1,0:T(8,128)(2,1)S(1)}, bf16[384,768]{1,0:T(8,128)(2,1)}, u32[]{:S(2)}) copy-start(bf16[384,768]{1,0:T(8,128)(2,1)} %get-tuple-element.105) | copy-start | bytes 1769476
  438.5 1.3 copy-start.2
  438.5 2.4 copy-start.11
  439.8 2.3 copy-start.16
  439.8 3.0 copy-start.18
  439.8 3.6 copy-start.8
  443.6 1.3 copy-start.12

commit v9 on v8

--- a/solution.py
+++ b/solution.py
@@ -246,25 +246,27 @@
         for b, (i, o) in zip(beside, side_refs):
             if isinstance(b, Relay):
                 run = functools.partial(relay_run, b, at, i[0], o[0], send, recv, local.at[place], slot)
-                begin.append(functools.partial(run, False))
+                begin.append([functools.partial(run, False)])
                 todo.append(functools.partial(run, True))
                 slot, place = slot + 2, place + 1
                 continue
             far, near = b.moves(at, i, o)
+            begin.append([])
             for src, dst, peer in far:
                 copy = remote(src, dst, send.at[slot], recv.at[slot], peer)
-                begin.append(copy.start)
+                begin[-1].append(copy.start)
                 todo.append(copy.wait)
                 slot += 1
             for src, dst in near:
                 copy = pltpu.make_async_copy(src, dst, local.at[place])
-                begin.append(copy.start)
+                begin[-1].append(copy.start)
                 todo.append(copy.wait)
                 place += 1
 
-        def start():
-            for go in begin:
-                go()
+        def start(*which):
+            for i in which or range(len(begin)):
+                for go in begin[i]:
+                    go()
 
         at.start_beside = start
         if not late:
@@ -823,15 +825,26 @@
                 go.start()
                 stay.start()
 
-        stay, go = [], []
-        for i, (own, target) in enumerate(
-            [(own_vectors, vectors.at[:, half])]
-            + [(own, weight.at[j * COLS : (j + 1) * COLS, half]) for j, own in enumerate(own_weights)]
-        ):
-            stay.append(pltpu.make_async_copy(own, target, local.at[1 + i]))
-            go.append(remote(own, target, send.at[13 + i], recv.at[13 + i], at.x()))
-        stay[0].start()
-        go[0].start()
+        stay = [
+            pltpu.make_async_copy(own, target, local.at[1 + i])
+            for i, (own, target) in enumerate(
+                [(own_vectors, vectors.at[:, half])]
+                + [(own, weight.at[j * COLS : (j + 1) * COLS, half]) for j, own in enumerate(own_weights)]
+            )
+        ]
+        for copy in stay:
+            copy.start()
+        vectors_go = remote(own_vectors, vectors.at[:, half], send.at[13], recv.at[13], at.x())
+        vectors_go.start()
+        rows = pl.ds(pl.multiple_of(at.z * 144, 16), 144)
+        over = remote(weight.at[rows, half], weight.at[rows, half], send.at[14], recv.at[14], at.x())
+        other = weight.at[rows, at.half(1 - at.n)]
+        others = [
+            remote(other, other, send.at[slot], recv.at[slot], at.at_z(k)) for k, slot in ((1, 15), (2, 16), (3, 53))
+        ]
+        for copy in stay:
+            copy.wait()
+        over.start()
 
         @pl.when(holds)
         def _():
@@ -851,11 +864,12 @@
         queries = Gather(at, query_part, query_quarter, send, recv, local.at[16], 19)
         outputs = Gather(at, out_part, out_quarter, send, recv, local.at[17], 30)
         queries.begin()
-        stay[0].wait()
-        go[0].wait_recv()
+        vectors_go.wait_recv()
         moving(True)
-        for copy in stay[1:] + go[1:]:
+        over.wait_recv()
+        for copy in others:
             copy.start()
+        at.start_beside(1, 2)
         queries.pass_on()
         queries.pass_near()
 
@@ -880,11 +894,9 @@
 
             @pl.when(s == 4)
             def _():
-                for copy in stay[1:]:
-                    copy.wait()
-                for copy in go[1:]:
+                for copy in others:
                     copy.wait_recv()
-                at.start_beside()
+                at.start_beside(0)
                 at.flush(0, 1, 2)
 
             @pl.when(s >= 4)
@@ -913,7 +925,7 @@
         text_pair[...] = (text_parts[at.n] + text_got[...]).astype(bf16)
         outputs.got(4, 7, 8, 9, 10)
         keep.wait()
-        for copy in go:
+        for copy in [vectors_go, over] + others:
             copy.wait_send()
         outputs.end()
         queries.end()
@@ -942,10 +954,10 @@
             VMEM((2, 64, 2 * COLS), f32),
             VMEM((64, 2 * COLS), f32),
             VMEM((8, HALF), f32),
-            *sems(53),
+            *sems(54),
         ],
         beside,
-        lambda at: ring_peers(at) + relay.peers(at) + [("x", at.x())] + GatherZ.peers(at),
+        lambda at: ring_peers(at) + relay.peers(at) + [("x", at.x()), ("z2", at.at_z(2))] + GatherZ.peers(at),
         spaces=[ANY] + [PLAIN] * 6 + [VMEM] * 7,
         out_spaces=[VMEM, VMEM, VMEM, ANY, VMEM, ANY, VMEM, VMEM],
         late=True,
@@ -1186,7 +1198,7 @@
         *refs, rounded, whole, second, out_full, expand_full, key_full, value_full, grad_scores, grads_all, send, recv, local = kept
         reduces = [
             Reduce(at, ins[12], outs[7], refs[7:11], send, recv, local, 32, 16, False),
-            Reduce(at, ins[13], outs[8], refs[11:15], send, recv, local, 42, 18, True),
+            Reduce(at, ins[13], outs[8], refs[11:15], send, recv, local, 42, 18, True, True),
         ]
         refs = refs[:7]
         for reduce in reduces:
@@ -1220,6 +1232,7 @@
         before.begin()
         for reduce in reduces:
             reduce.second()
+        at.start_beside()
         grad_vectors[4:5] = gains
         grad_vectors[5:6] = shifts
 
@@ -1314,7 +1327,7 @@
         [
             *Scatter.scratch,
             *Reduce.scratch(96, False),
-            *Reduce.scratch(96, True),
+            *Reduce.scratch(96, True, True),
             VMEM((BLOCK, D), bf16),
             VMEM((D, D), bf16),
             VMEM((BLOCK, D), f32),
@@ -1330,6 +1343,7 @@
         lambda at: Trade.peers(at) + Reduce.peers(at),
         spaces=[VMEM, ANY, ANY, VMEM, VMEM, VMEM, VMEM, ANY, ANY, VMEM, ANY, ANY, ANY, ANY],
         out_spaces=[VMEM, VMEM, ANY, ANY, ANY, VMEM, VMEM, ANY, ANY],
+        late=True,
     )
 
 
@@ -1506,7 +1520,6 @@
             copy.start()
         scatter = Scatter(at, send, recv, refs)
         scatter.products(lambda rows: dot(grad[rows], weight[...]))
-        at.start_beside()
         scatter.middle()
         for reduce in reduces:
             reduce.second()
@@ -1521,6 +1534,7 @@
         for copy in texts:
             copy.start()
         scatter.arrive()
+        at.start_beside()
 
         def norm(rows, carry):
             incoming = scatter.total(rows)
@@ -1656,7 +1670,7 @@
     middle, after, normed_two, cross_p, all_three, activated, grad_expand, contract, all_keys, all_values, traded_p = results
 
     contract_part = outer(activated, all_down).astype(bf16).reshape(4, 2, 96, D)
-    expand_part = outer(grad_expand, all_three).astype(bf16).reshape(4, 2, 96, D)
+    expand_part = outer(all_three, grad_expand).astype(bf16).reshape(2, 4, 2, 96, HALF)
     results, ((query_got,), (cross_got,)) = backward_rest(
         4,
         grad_expand,
@@ -1745,7 +1759,7 @@
         value_grad[:COLS],
         parts[4],
         parts[5],
-        expand_grad.T,
+        expand_grad,
         contract_grad,
     )
 

time: 454 us -> 451 us (level)
  no operation moved by 1% of the time
where the time goes in v9:
time: 451 us; the launch traced here: 443 us
  Pallas kernels  392 us (87%)
  matrix products  31.1 us (7%)
  other arithmetic  12.4 us (3%)
  local copies, waits for them, and re-layouts  5.98 us (1%)
    pallas_call x6, Pallas kernels, call(): pl.pallas_call(kernel, out_shape=tuple(outs) + tuple(side_outs), in_specs...  392 us
    dot_general x8, matrix products, outer(): lax.dot_general(a, b, (((0,), (0,)), ((), ())), preferred_element_type=f32)  28.8 us

profile of v9, /device:TPU:0, one launch (start us, length us, event | category | flops | bytes accessed | tf_op | source)
XLA Modules:
  0.0 442.7 jit_solution(18403647369863533527)
XLA Ops:
  0.7 1.9 pad_maximum_fusion.2.refs_13_.refs_8_
  2.6 68.9 %shard_map.330 = (bf16[192,1536]{1,0:T(8,128)(2,1)}, f32[8,1536]{1,0:T(8,128)}, bf16[576,1536]{1,0:T(8,128)(2,1)}, bf16[1536,1536]{1,0:T(8,128)(2,1)}, bf16[1536...) custom-call(bf16[384,768]{1,0:T(8,128)(2,1)} %refs_0_.1, ...), custom_call_target="tpu_custom_call" | custom-call | tf_op jit(solution)/shard_map/pallas_call | solution.py:284
  71.5 42.0 %shard_map.331 = (bf16[1536,192]{1,0:T(8,128)(2,1)}, f32[8,1536]{1,0:T(8,128)}, bf16[1536,1536]{1,0:T(8,128)(2,1)}, bf16[1536,1536]{1,0:T(8,128)(2,1)}, bf16[8,6...) custom-call(bf16[1536,576]{1,0:T(8,128)(2,1)} %get-tuple-element.68.refs_0_, ...), custom_call_target="tpu_custom_call" | custom-call | tf_op jit(solution)/shard_map/pallas_call | solution.py:284
  113.4 64.3 %shard_map.332 = (f32[192,1536]{1,0:T(8,128)}, f32[192,1536]{1,0:T(8,128)}, bf16[192,1536]{1,0:T(8,128)(2,1)}, bf16[8,192,192]{2,1,0:T(8,128)(2,1)}, bf16[1536,1...) custom-call(bf16[1536,192]{1,0:T(8,128)(2,1)} %get-tuple-element.72., ...), custom_call_target="tpu_custom_call" | custom-call | tf_op jit(solution)/shard_map/pallas_call | solution.py:284
  177.7 8.5 %convolution_convert_fusion = bf16[1536,768]{1,0:T(8,128)(2,1)} fusion(bf16[1536,1536]{1,0:T(8,128)(2,1)} %get-tuple-element.88, bf16[1536,768]{1,0:T(8,128)(2,1)} %get-tuple-element.81.refs_0_), kind=kOutput, calls=%fused_computation | convolution fusion | flops 3625058304 | bytes 9437184 | tf_op jit(solution)/shard_map/dot_general | solution.py:36
  186.3 5.2 %convolution_convert_fusion.1 = bf16[768,1536]{1,0:T(8,128)(2,1)} fusion(bf16[1536,768]{1,0:T(8,128)(2,1)S(1)} %copy-done.3, bf16[1536,1536]{1,0:T(8,128)(2,1)S(1)} %bitcast.91), kind=kOutput, calls=%fused_computation.1 | convolution fusion | flops 3625058304 | bytes 9437184 | tf_op jit(solution)/shard_map/dot_general | solution.py:36
  191.4 89.6 %shard_map.333 = (f32[192,1536]{1,0:T(8,128)}, bf16[192,1536]{1,0:T(8,128)(2,1)}, bf16[8,192,192]{2,1,0:T(8,128)(2,1)}, bf16[1536,1536]{1,0:T(8,128)(2,1)}, bf16...) custom-call(bf16[1536,768]{1,0:T(8,128)(2,1)} %get-tuple-element.81., ...), custom_call_target="tpu_custom_call" | custom-call | tf_op jit(solution)/shard_map/pallas_call | solution.py:284
  281.1 4.3 bitcast_convert_fusion
  285.5 1.1 convolution_convert_fusion.8
  286.7 0.3 convolution_convert_fusion.7
  287.2 0.3 convolution_convert_fusion.10
  287.5 0.5 copy-done.5
  288.1 0.3 convolution_convert_fusion.6
  288.4 3.4 convolution_convert_fusion.5
  291.8 1.3 pad_maximum_fusion
  293.2 54.6 %shard_map.334 = (bf16[1536,576]{1,0:T(8,128)(2,1)}, bf16[192,1536]{1,0:T(8,128)(2,1)}, bf16[1536,1536]{1,0:T(8,128)(2,1)}, bf16[4,2,72,768]{3,2,1,0:T(8,128)(2,1)}, bf16[384,768]{1,0:T(8,128)(2,1)}) custom-call(bf16[1536,576]{1,0:T(8,128)(2,1)} %get-tuple-element.68.refs_0_, bf16[1536,192]{1,0:T(8,128)(2,1)} %get-tuple-element.89.refs_1_, ...), custom_call_target="tpu_custom_call" | custom-call | tf_op jit(solution)/shard_map/pallas_call | solution.py:284
  347.8 3.4 convolution_convert_fusion.4
  351.2 0.3 fusion
  351.6 0.3 fusion.5
  351.9 0.3 convolution_convert_fusion.3
  352.2 1.1 pad_maximum_fusion.1
  353.3 6.6 %convolution_convert_fusion.2 = bf16[576,1536]{1,0:T(8,128)(2,1)} fusion(bf16[1536,576]{1,0:T(8,128)(2,1)S(1)} %copy-done.4, bf16[1536,1536]{1,0:T(8,128)(2,1)} %get-tuple-element.106), kind=kOutput, calls=%fused_computation.2 | convolution fusion | flops 2718793728 | bytes 8257536 | tf_op jit(solution)/shard_map/dot_general | solution.py:36
  360.1 1.0 fusion.1.refs_6_
  361.1 72.5 %shard_map.335 = (bf16[384,768]{1,0:T(8,128)(2,1)}, bf16[4,2,72,768]{3,2,1,0:T(8,128)(2,1)}, bf16[4,2,48,768]{3,2,1,0:T(8,128)(2,1)}, f32[8,768]{1,0:T(8,128)}, ...) custom-call(bf16[1536,576]{1,0:T(8,128)(2,1)} %get-tuple-element.98.refs_0_, ...), custom_call_target="tpu_custom_call" | custom-call | tf_op jit(solution)/shard_map/pallas_call | solution.py:284
  433.7 1.3 bitcast_convert_fusion.3
  435.0 1.2 slice_bitcast_fusion.1
  436.3 1.1 fusion.13
  437.4 1.1 convert_element_type.97
  438.5 0.8 bitcast_convert_fusion.4
  439.3 0.6 slice_reduce_fusion
  440.1 1.2 fusion.12
  441.5 0.8 copy.44
  (55 shorter events, 1.1 us)
Async XLA Ops:
  113.4 72.8 %slice-start = ((s8[4718592]{0:T(1024)(128)(4,1)}), s8[524288]{0:T(1024)(128)(4,1)S(1)}, s32[]{:S(2)}) async-start(s8[4718592]{0:T(1024)(128)(4,1)} %bitcast.90), calls=%async_computation | async-start | bytes 1048576
  177.7 8.6 %slice-start.1 = ((s8[4718592]{0:T(1024)(128)(4,1)}), s8[4194304]{0:T(1024)(128)(4,1)S(1)}, s32[]{:S(2)}) async-start(s8[4718592]{0:T(1024)(128)(4,1)} %bitcast.90), calls=%async_computation.1 | async-start | bytes 8388608
  177.7 8.6 %copy-start.3 = (bf16[1536,768]{1,0:T(8,128)(2,1)S(1)}, bf16[1536,768]{1,0:T(8,128)(2,1)}, u32[]{:S(2)}) copy-start(bf16[1536,768]{1,0:T(8,128)(2,1)} %get-tuple-element.87.refs_3_) | copy-start | bytes 7077892
  281.1 4.3 copy-start.19
  281.1 4.3 copy-start.21
  285.4 1.2 copy-start.15
  285.4 1.6 copy-start
  285.4 1.6 copy-start.1
  285.4 1.6 copy-start.13
  285.4 1.6 copy-start.14
  287.1 0.9 copy-start.5
  287.1 1.0 copy-start.17
  287.2 1.2 copy-start.9
  293.2 54.6 %copy-start.20 = (bf16[8,192,192]{2,1,0:T(8,128)(2,1)S(1)}, bf16[8,192,192]{2,1,0:T(8,128)(2,1)}, u32[]{:S(2)}) copy-start(bf16[8,192,192]{2,1,0:T(8,128)(2,1)} %get-tuple-element.103) | copy-start | bytes 1769476
  351.6 1.7 copy-start.4
  353.3 6.6 %copy-start.6 = (bf16[768,192]{0,1:T(8,128)(2,1)S(1)}, bf16[768,192]{0,1:T(8,128)(2,1)}, u32[]{:S(2)}) copy-start(bf16[768,192]{0,1:T(8,128)(2,1)} %param.32) | copy-start | bytes 884740
  353.3 6.6 %copy-start.7 = (bf16[768,192]{0,1:T(8,128)(2,1)S(1)}, bf16[768,192]{0,1:T(8,128)(2,1)}, u32[]{:S(2)}) copy-start(bf16[768,192]{0,1:T(8,128)(2,1)} %param.31) | copy-start | bytes 884740
  353.3 6.6 %copy-start.10 = (bf16[384,768]{1,0:T(8,128)(2,1)S(1)}, bf16[384,768]{1,0:T(8,128)(2,1)}, u32[]{:S(2)}) copy-start(bf16[384,768]{1,0:T(8,128)(2,1)} %get-tuple-element.105) | copy-start | bytes 1769476
  435.0 1.3 copy-start.2
  436.2 1.2 copy-start.11
  436.3 2.2 copy-start.16
  436.3 3.0 copy-start.18
  436.3 3.6 copy-start.8
  440.1 1.3 copy-start.12

commit v10 on v9

--- a/solution.py
+++ b/solution.py
@@ -190,7 +190,7 @@
             arrive(1, land[1]).wait_recv()
 
 
-def call(body, number, ins, outs, scratch=(), beside=(), peers=None, spaces=None, out_spaces=None, late=False):
+def call(body, number, ins, outs, scratch=(), beside=(), peers=None, spaces=None, out_spaces=None, late=False, early=None):
     spaces = spaces or [VMEM] * len(ins)
     out_spaces = out_spaces or [VMEM] * len(outs)
     copies = sum(b.copies for b in beside)
@@ -230,6 +230,8 @@
                 waiting.pop(i).start()
 
         at.flush = flush
+        if early:
+            at.early = early(at, main_in, kept)
         known = dict(peers(at)) if peers else {}
         for b in beside:
             known.update(dict(b.peers(at)))
@@ -1032,7 +1034,7 @@
         middle, after, normed_two, weights, all_rows, activated, grad, contract_out, keys_out, values_out, traded = outs
         *refs, normed, whole, downs, out_full, expand_full, contract_full, key_full, value_full, branch, scores_all, send, recv, local = kept
         half = at.half(at.n)
-        weight = Whole(at, out_own, out_got, out_full, local.at[pl.ds(0, 2)], 1)
+        weight = at.early
         swap = remote(contract_own, contract_full.at[:, half], send.at[21], recv.at[21], at.x())
         swap.start()
         factors = [
@@ -1183,6 +1185,7 @@
         ],
         (),
         lambda at: Trade.peers(at) + [("x", at.x())],
+        early=lambda at, ins, kept: Whole(at, ins[1], ins[2], kept[len(Scatter.scratch) + 3], kept[-1].at[pl.ds(0, 2)], 1),
         spaces=[VMEM, ANY, ANY, VMEM, VMEM, ANY, ANY, VMEM, ANY, ANY, ANY, ANY],
         out_spaces=[VMEM, VMEM, VMEM, VMEM, ANY, VMEM, VMEM, ANY, ANY, ANY, ANY],
     )
@@ -1203,7 +1206,7 @@
         refs = refs[:7]
         for reduce in reduces:
             reduce.first()
-        weight = Whole(at, expand_own, expand_got, expand_full, local.at[pl.ds(0, 2)], 0)
+        weight = at.early
         later = [
             pltpu.make_async_copy(keys, key_full, local.at[2]),
             pltpu.make_async_copy(values, value_full, local.at[3]),
@@ -1232,7 +1235,6 @@
         before.begin()
         for reduce in reduces:
             reduce.second()
-        at.start_beside()
         grad_vectors[4:5] = gains
         grad_vectors[5:6] = shifts
 
@@ -1276,6 +1278,7 @@
         at.flush(1)
         for reduce in reduces:
             reduce.fourth()
+        at.start_beside()
 
         def norm_two(rows, carry):
             incoming = second[rows]
@@ -1341,6 +1344,7 @@
         ],
         beside,
         lambda at: Trade.peers(at) + Reduce.peers(at),
+        early=lambda at, ins, kept: Whole(at, ins[1], ins[2], kept[len(Scatter.scratch) + 12], kept[-1].at[pl.ds(0, 2)], 0),
         spaces=[VMEM, ANY, ANY, VMEM, VMEM, VMEM, VMEM, ANY, ANY, VMEM, ANY, ANY, ANY, ANY],
         out_spaces=[VMEM, VMEM, ANY, ANY, ANY, VMEM, VMEM, ANY, ANY],
         late=True,
@@ -1534,7 +1538,6 @@
         for copy in texts:
             copy.start()
         scatter.arrive()
-        at.start_beside()
 
         def norm(rows, carry):
             incoming = scatter.total(rows)
@@ -1567,6 +1570,7 @@
             copy.start()
         for reduce in reduces:
             reduce.fourth()
+        at.start_beside()
         x_own.wait()
         for copy in spreads:
             copy.wait_recv()

time: 451 us -> 439 us (0.973)
  Pallas kernels: 392 us -> 381 us
    pallas_call x6, Pallas kernels: 392 us -> 381 us  [call(): pl.pallas_call(kernel, out_shape=tuple(outs) + tuple(side_outs), in_specs...]
where the time goes in v10:
time: 439 us; the launch traced here: 432 us
  Pallas kernels  381 us (87%)
  matrix products  31.1 us (7%)
  other arithmetic  12.4 us (3%)
  local copies, waits for them, and re-layouts  5.98 us (1%)
    pallas_call x6, Pallas kernels, call(): pl.pallas_call(kernel, out_shape=tuple(outs) + tuple(side_outs), in_specs...  381 us
    dot_general x8, matrix products, outer(): lax.dot_general(a, b, (((0,), (0,)), ((), ())), preferred_element_type=f32)  28.9 us

profile of v10, /device:TPU:0, one launch (start us, length us, event | category | flops | bytes accessed | tf_op | source)
XLA Modules:
  0.0 431.9 jit_solution(2494388612022773597)
XLA Ops:
  0.7 1.9 pad_maximum_fusion.2.refs_13_.refs_8_
  2.6 68.9 %shard_map.330 = (bf16[192,1536]{1,0:T(8,128)(2,1)}, f32[8,1536]{1,0:T(8,128)}, bf16[576,1536]{1,0:T(8,128)(2,1)}, bf16[1536,1536]{1,0:T(8,128)(2,1)}, bf16[1536...) custom-call(bf16[384,768]{1,0:T(8,128)(2,1)} %refs_0_.1, ...), custom_call_target="tpu_custom_call" | custom-call | tf_op jit(solution)/shard_map/pallas_call | solution.py:286
  71.5 42.0 %shard_map.331 = (bf16[1536,192]{1,0:T(8,128)(2,1)}, f32[8,1536]{1,0:T(8,128)}, bf16[1536,1536]{1,0:T(8,128)(2,1)}, bf16[1536,1536]{1,0:T(8,128)(2,1)}, bf16[8,6...) custom-call(bf16[1536,576]{1,0:T(8,128)(2,1)} %get-tuple-element.68.refs_0_, ...), custom_call_target="tpu_custom_call" | custom-call | tf_op jit(solution)/shard_map/pallas_call | solution.py:286
  113.4 63.5 %shard_map.332 = (f32[192,1536]{1,0:T(8,128)}, f32[192,1536]{1,0:T(8,128)}, bf16[192,1536]{1,0:T(8,128)(2,1)}, bf16[8,192,192]{2,1,0:T(8,128)(2,1)}, bf16[1536,1...) custom-call(bf16[1536,192]{1,0:T(8,128)(2,1)} %get-tuple-element.72., ...), custom_call_target="tpu_custom_call" | custom-call | tf_op jit(solution)/shard_map/pallas_call | solution.py:286
  177.0 8.5 %convolution_convert_fusion = bf16[1536,768]{1,0:T(8,128)(2,1)} fusion(bf16[1536,1536]{1,0:T(8,128)(2,1)} %get-tuple-element.88, bf16[1536,768]{1,0:T(8,128)(2,1)} %get-tuple-element.81.refs_0_), kind=kOutput, calls=%fused_computation | convolution fusion | flops 3625058304 | bytes 9437184 | tf_op jit(solution)/shard_map/dot_general | solution.py:36
  185.5 5.2 %convolution_convert_fusion.1 = bf16[768,1536]{1,0:T(8,128)(2,1)} fusion(bf16[1536,768]{1,0:T(8,128)(2,1)S(1)} %copy-done.3, bf16[1536,1536]{1,0:T(8,128)(2,1)S(1)} %bitcast.91), kind=kOutput, calls=%fused_computation.1 | convolution fusion | flops 3625058304 | bytes 9437184 | tf_op jit(solution)/shard_map/dot_general | solution.py:36
  190.7 84.4 %shard_map.333 = (f32[192,1536]{1,0:T(8,128)}, bf16[192,1536]{1,0:T(8,128)(2,1)}, bf16[8,192,192]{2,1,0:T(8,128)(2,1)}, bf16[1536,1536]{1,0:T(8,128)(2,1)}, bf16...) custom-call(bf16[1536,768]{1,0:T(8,128)(2,1)} %get-tuple-element.81., ...), custom_call_target="tpu_custom_call" | custom-call | tf_op jit(solution)/shard_map/pallas_call | solution.py:286
  275.1 4.3 %bitcast_convert_fusion = (f32[768,768]{1,0:T(8,128)}, f32[768,768]{1,0:T(8,128)}) fusion(bf16[4,2,96,768]{3,2,1,0:T(8,128)(2,1)} %get-tuple-element.116, bf16[4,2,96,768]{3,2,1,0:T(8,128)(2,1)} %get-tuple-element.115), kind=kLoop, calls=%fused_computation.18 | loop fusion | flops 1179648 | bytes 7077888 | tf_op jit(solution)/shard_map/convert_element_type | solution.py:1746
  279.5 1.1 convolution_convert_fusion.8
  280.8 0.3 convolution_convert_fusion.7
  281.3 0.3 convolution_convert_fusion.10
  281.6 0.5 copy-done.5
  282.1 0.3 convolution_convert_fusion.6
  282.4 3.4 convolution_convert_fusion.5
  285.9 1.3 pad_maximum_fusion
  287.2 57.1 %shard_map.334 = (bf16[1536,576]{1,0:T(8,128)(2,1)}, bf16[192,1536]{1,0:T(8,128)(2,1)}, bf16[1536,1536]{1,0:T(8,128)(2,1)}, bf16[4,2,72,768]{3,2,1,0:T(8,128)(2,1)}, bf16[384,768]{1,0:T(8,128)(2,1)}) custom-call(bf16[1536,576]{1,0:T(8,128)(2,1)} %get-tuple-element.68.refs_0_, bf16[1536,192]{1,0:T(8,128)(2,1)} %get-tuple-element.89.refs_1_, ...), custom_call_target="tpu_custom_call" | custom-call | tf_op jit(solution)/shard_map/pallas_call | solution.py:286
  344.3 3.4 convolution_convert_fusion.4
  347.8 0.3 fusion
  348.1 0.3 fusion.5
  348.4 0.3 convolution_convert_fusion.3
  348.7 1.1 pad_maximum_fusion.1
  349.8 6.6 %convolution_convert_fusion.2 = bf16[576,1536]{1,0:T(8,128)(2,1)} fusion(bf16[1536,576]{1,0:T(8,128)(2,1)S(1)} %copy-done.4, bf16[1536,1536]{1,0:T(8,128)(2,1)} %get-tuple-element.106), kind=kOutput, calls=%fused_computation.2 | convolution fusion | flops 2718793728 | bytes 8257536 | tf_op jit(solution)/shard_map/dot_general | solution.py:36
  356.6 1.0 fusion.1.refs_6_
  357.7 65.1 %shard_map.335 = (bf16[384,768]{1,0:T(8,128)(2,1)}, bf16[4,2,72,768]{3,2,1,0:T(8,128)(2,1)}, bf16[4,2,48,768]{3,2,1,0:T(8,128)(2,1)}, f32[8,768]{1,0:T(8,128)}, ...) custom-call(bf16[1536,576]{1,0:T(8,128)(2,1)} %get-tuple-element.98.refs_0_, ...), custom_call_target="tpu_custom_call" | custom-call | tf_op jit(solution)/shard_map/pallas_call | solution.py:286
  422.8 1.3 bitcast_convert_fusion.3
  424.1 1.2 slice_bitcast_fusion.1
  425.4 1.1 fusion.13
  426.5 1.1 convert_element_type.97
  427.6 0.8 bitcast_convert_fusion.4
  428.4 0.6 slice_reduce_fusion
  429.3 1.2 fusion.12
  430.6 0.8 copy.44
  (55 shorter events, 1.1 us)
Async XLA Ops:
  113.4 72.1 %slice-start = ((s8[4718592]{0:T(1024)(128)(4,1)}), s8[524288]{0:T(1024)(128)(4,1)S(1)}, s32[]{:S(2)}) async-start(s8[4718592]{0:T(1024)(128)(4,1)} %bitcast.90), calls=%async_computation | async-start | bytes 1048576
  176.9 8.6 %slice-start.1 = ((s8[4718592]{0:T(1024)(128)(4,1)}), s8[4194304]{0:T(1024)(128)(4,1)S(1)}, s32[]{:S(2)}) async-start(s8[4718592]{0:T(1024)(128)(4,1)} %bitcast.90), calls=%async_computation.1 | async-start | bytes 8388608
  177.0 8.6 %copy-start.3 = (bf16[1536,768]{1,0:T(8,128)(2,1)S(1)}, bf16[1536,768]{1,0:T(8,128)(2,1)}, u32[]{:S(2)}) copy-start(bf16[1536,768]{1,0:T(8,128)(2,1)} %get-tuple-element.87.refs_3_) | copy-start | bytes 7077892
  275.1 4.3 %copy-start.19 = (bf16[1536,1536]{1,0:T(8,128)(2,1)S(1)}, bf16[1536,1536]{1,0:T(8,128)(2,1)}, u32[]{:S(2)}) copy-start(bf16[1536,1536]{1,0:T(8,128)(2,1)} %get-tuple-element.94) | copy-start | bytes 14155780
  275.1 4.3 %copy-start.21 = (bf16[8,192,192]{2,1,0:T(8,128)(2,1)S(1)}, bf16[8,192,192]{2,1,0:T(8,128)(2,1)}, u32[]{:S(2)}) copy-start(bf16[8,192,192]{2,1,0:T(8,128)(2,1)} %get-tuple-element.93) | copy-start | bytes 1769476
  279.5 1.2 copy-start.15
  279.5 1.6 copy-start
  279.5 1.6 copy-start.1
  279.5 1.6 copy-start.13
  279.5 1.6 copy-start.14
  281.1 0.9 copy-start.5
  281.1 1.0 copy-start.17
  281.2 1.2 copy-start.9
  287.2 57.1 %copy-start.20 = (bf16[8,192,192]{2,1,0:T(8,128)(2,1)S(1)}, bf16[8,192,192]{2,1,0:T(8,128)(2,1)}, u32[]{:S(2)}) copy-start(bf16[8,192,192]{2,1,0:T(8,128)(2,1)} %get-tuple-element.103) | copy-start | bytes 1769476
  348.1 1.7 copy-start.4
  349.8 6.6 %copy-start.6 = (bf16[768,192]{0,1:T(8,128)(2,1)S(1)}, bf16[768,192]{0,1:T(8,128)(2,1)}, u32[]{:S(2)}) copy-start(bf16[768,192]{0,1:T(8,128)(2,1)} %param.32) | copy-start | bytes 884740
  349.8 6.6 %copy-start.7 = (bf16[768,192]{0,1:T(8,128)(2,1)S(1)}, bf16[768,192]{0,1:T(8,128)(2,1)}, u32[]{:S(2)}) copy-start(bf16[768,192]{0,1:T(8,128)(2,1)} %param.31) | copy-start | bytes 884740
  349.8 6.6 %copy-start.10 = (bf16[384,768]{1,0:T(8,128)(2,1)S(1)}, bf16[384,768]{1,0:T(8,128)(2,1)}, u32[]{:S(2)}) copy-start(bf16[384,768]{1,0:T(8,128)(2,1)} %get-tuple-element.105) | copy-start | bytes 1769476
  424.1 1.3 copy-start.2
  425.3 1.2 copy-start.11
  425.4 2.2 copy-start.16
  425.4 3.0 copy-start.18
  425.4 3.6 copy-start.8
  429.3 1.3 copy-start.12

commit v11 on v10

--- a/solution.py
+++ b/solution.py
@@ -796,12 +796,12 @@
             pltpu.make_async_copy(self.whole.at[some], self.out.at[some], self.sem.at[self.base + s]).wait()
 
 
-def enter(number, layer_input, gains, weights, query_t, cross_out, texts, pair_t, beside):
+def enter(number, layer_input, gains, weights, query_t, cross_out, texts, pairs_t, beside):
     relay = Relay(layer_input)
 
     def body(at, ins, outs, kept):
         source, *gains = ins[:7]
-        *own_weights, query_own, out_own, own_texts, pair = ins[7:]
+        *own_weights, query_own, out_own, own_texts, text_key, text_value = ins[7:]
         x, vectors, weight, all_rows, qkv, query_all, out_quarter, text_pair = outs
         normed, whole, query_part, out_part, query_quarter, text_parts, text_got, own_vectors, send, recv, local = kept
         half = at.half(at.n)
@@ -860,7 +860,8 @@
                 far.wait_recv()
 
         for clip in range(2):
-            text_parts[clip] = dot_flip(own_texts[clip], pair[...])
+            text_parts[clip, :, :COLS] = dot_flip(own_texts[clip], text_key[...])
+            text_parts[clip, :, COLS:] = dot_flip(own_texts[clip], text_value[...])
         text_go = remote(text_parts.at[1 - at.n], text_got, send.at[52], recv.at[52], at.x())
         text_go.start()
         queries = Gather(at, query_part, query_quarter, send, recv, local.at[16], 19)
@@ -936,7 +937,7 @@
     return call(
         body,
         number,
-        [layer_input, *gains, *weights, query_t, cross_out, texts, pair_t],
+        [layer_input, *gains, *weights, query_t, cross_out, texts, *pairs_t],
         [
             shape(BLOCK, D),
             shape(8, D, dtype=f32),
@@ -960,7 +961,7 @@
         ],
         beside,
         lambda at: ring_peers(at) + relay.peers(at) + [("x", at.x()), ("z2", at.at_z(2))] + GatherZ.peers(at),
-        spaces=[ANY] + [PLAIN] * 6 + [VMEM] * 7,
+        spaces=[ANY] + [PLAIN] * 6 + [VMEM] * 8,
         out_spaces=[VMEM, VMEM, VMEM, ANY, VMEM, ANY, VMEM, VMEM],
         late=True,
     )
@@ -1651,7 +1652,7 @@
     gains = (first_gain, first_shift, second_gain, second_shift, third_gain, third_shift)
     weights = [query_weight.T, key_weight.T, value_weight.T]
     query_t = cross_query.T
-    pair_t = jnp.concatenate((cross_key.T, cross_value.T), axis=0)
+    pairs_t = cross_key.T, cross_value.T
     n = lax.axis_index("narrow")
 
     results, ((down,), (out_got,), (text_got,)) = enter(
@@ -1662,7 +1663,7 @@
         query_t,
         cross_output,
         text_states,
-        pair_t,
+        pairs_t,
         [Relay(cotangent), Give(output_weight), GiveClip(text_states)],
     )
     x, vectors, joined, all_one, qkv, query_all, out_quarter, text_pair = results
@@ -1708,7 +1709,7 @@
     grad_text_values = heads("hkf,hdf->khd", grad_values, heads_out).reshape(64, COLS).astype(bf16)
     grad_cross = heads("khd,hkf->hdf", text_heads[:, 1], grad_values).reshape(COLS, D)
     value_part = jnp.concatenate((grad_cross, outer(grad_text_values, text), outer(attended, all_mid_one)), axis=0)
-    (grad_qkv, layer_output, all_two, value_grad), ((pair_got,),) = causal_backward(
+    (grad_qkv, layer_output, all_two, value_grad), pairs_got = causal_backward(
         5,
         qkv,
         grad_attended,
@@ -1718,7 +1719,7 @@
         after,
         normed_two,
         value_part.astype(bf16).reshape(4, 2, 72, D),
-        [Give(pair_t)],
+        [Give(part) for part in pairs_t],
     )
 
     joined_part = outer(grad_qkv, all_one).astype(bf16).reshape(4, 2, 72, D)
@@ -1727,8 +1728,9 @@
     grad_text_keys = (heads("hkf,hdf->khd", grad_keys, heads_query) * EIGHTH).reshape(64, COLS).astype(bf16)
     grad_query = heads("khd,hkf->hdf", text_heads[:, 0], grad_keys).reshape(COLS, D) * EIGHTH
     key_part = jnp.concatenate((grad_query, outer(grad_text_keys, text)), axis=0).astype(bf16).reshape(4, 2, 48, D)
-    grad_pair = jnp.concatenate((grad_text_keys, grad_text_values), axis=1)
-    text_part = dot(grad_pair, whole(pair_t, pair_got)).astype(bf16).reshape(8, 8, D)
+    text_part = dot(grad_text_keys, whole(pairs_t[0], pairs_got[0][0]))
+    text_part += dot(grad_text_values, whole(pairs_t[1], pairs_got[1][0]))
+    text_part = text_part.astype(bf16).reshape(8, 8, D)
 
     (input_grad, joined_grad, key_grad, parts, text_grad), ((layer_output,),) = leave(
         6,

time: 439 us -> 438 us (level)
  no operation moved by 1% of the time
where the time goes in v11:
time: 438 us; the launch traced here: 431 us
  Pallas kernels  381 us (87%)
  matrix products  31.2 us (7%)
  other arithmetic  10.3 us (2%)
  local copies, waits for them, and re-layouts  6.68 us (2%)
    pallas_call x6, Pallas kernels, call(): pl.pallas_call(kernel, out_shape=tuple(outs) + tuple(side_outs), in_specs...  381 us
    dot_general x8, matrix products, outer(): lax.dot_general(a, b, (((0,), (0,)), ((), ())), preferred_element_type=f32)  28.9 us

profile of v11, /device:TPU:0, one launch (start us, length us, event | category | flops | bytes accessed | tf_op | source)
XLA Modules:
  0.0 430.8 jit_solution(707880482289779692)
XLA Ops:
  0.7 68.9 %shard_map.330 = (bf16[192,1536]{1,0:T(8,128)(2,1)}, f32[8,1536]{1,0:T(8,128)}, bf16[576,1536]{1,0:T(8,128)(2,1)}, bf16[1536,1536]{1,0:T(8,128)(2,1)}, bf16[1536...) custom-call(bf16[384,768]{1,0:T(8,128)(2,1)} %refs_0_.1, ...), custom_call_target="tpu_custom_call" | custom-call | tf_op jit(solution)/shard_map/pallas_call | solution.py:286
  69.6 42.0 %shard_map.331 = (bf16[1536,192]{1,0:T(8,128)(2,1)}, f32[8,1536]{1,0:T(8,128)}, bf16[1536,1536]{1,0:T(8,128)(2,1)}, bf16[1536,1536]{1,0:T(8,128)(2,1)}, bf16[8,6...) custom-call(bf16[1536,576]{1,0:T(8,128)(2,1)} %get-tuple-element.69.refs_0_, ...), custom_call_target="tpu_custom_call" | custom-call | tf_op jit(solution)/shard_map/pallas_call | solution.py:286
  111.6 63.5 %shard_map.332 = (f32[192,1536]{1,0:T(8,128)}, f32[192,1536]{1,0:T(8,128)}, bf16[192,1536]{1,0:T(8,128)(2,1)}, bf16[8,192,192]{2,1,0:T(8,128)(2,1)}, bf16[1536,1...) custom-call(bf16[1536,192]{1,0:T(8,128)(2,1)} %get-tuple-element.73., ...), custom_call_target="tpu_custom_call" | custom-call | tf_op jit(solution)/shard_map/pallas_call | solution.py:286
  175.1 8.5 %convolution_convert_fusion = bf16[1536,768]{1,0:T(8,128)(2,1)} fusion(bf16[1536,1536]{1,0:T(8,128)(2,1)} %get-tuple-element.89, bf16[1536,768]{1,0:T(8,128)(2,1)} %get-tuple-element.82.refs_0_), kind=kOutput, calls=%fused_computation | convolution fusion | flops 3625058304 | bytes 9437184 | tf_op jit(solution)/shard_map/dot_general | solution.py:36
  183.7 5.2 %convolution_convert_fusion.1 = bf16[768,1536]{1,0:T(8,128)(2,1)} fusion(bf16[1536,768]{1,0:T(8,128)(2,1)S(1)} %copy-done.5, bf16[1536,1536]{1,0:T(8,128)(2,1)S(1)} %bitcast.97), kind=kOutput, calls=%fused_computation.1 | convolution fusion | flops 3625058304 | bytes 9437184 | tf_op jit(solution)/shard_map/dot_general | solution.py:36
  188.9 84.3 %shard_map.333 = (f32[192,1536]{1,0:T(8,128)}, bf16[192,1536]{1,0:T(8,128)(2,1)}, bf16[8,192,192]{2,1,0:T(8,128)(2,1)}, bf16[1536,1536]{1,0:T(8,128)(2,1)}, bf16...) custom-call(bf16[1536,768]{1,0:T(8,128)(2,1)} %get-tuple-element.82., ...), custom_call_target="tpu_custom_call" | custom-call | tf_op jit(solution)/shard_map/pallas_call | solution.py:286
  273.2 4.3 %bitcast_convert_fusion = (f32[768,768]{1,0:T(8,128)}, f32[768,768]{1,0:T(8,128)}) fusion(bf16[4,2,96,768]{3,2,1,0:T(8,128)(2,1)} %get-tuple-element.118, bf16[4,2,96,768]{3,2,1,0:T(8,128)(2,1)} %get-tuple-element.117), kind=kLoop, calls=%fused_computation.16 | loop fusion | flops 1179648 | bytes 7077888 | tf_op jit(solution)/shard_map/convert_element_type | solution.py:1748
  277.6 1.1 convolution_convert_fusion.8
  278.9 0.3 convolution_convert_fusion.7
  279.4 0.3 convolution_convert_fusion.9
  279.7 0.5 copy-done.7
  280.2 0.3 convolution_convert_fusion.6
  280.5 3.4 convolution_convert_fusion.5
  284.0 1.3 pad_maximum_fusion
  285.3 57.1 %shard_map.334 = (bf16[1536,576]{1,0:T(8,128)(2,1)}, bf16[192,1536]{1,0:T(8,128)(2,1)}, bf16[1536,1536]{1,0:T(8,128)(2,1)}, bf16[4,2,72,768]{3,2,1,0:T(8,128)(2,...) custom-call(bf16[1536,576]{1,0:T(8,128)(2,1)} %get-tuple-element.69.refs_0_, ...), custom_call_target="tpu_custom_call" | custom-call | tf_op jit(solution)/shard_map/pallas_call | solution.py:286
  342.5 3.4 convolution_convert_fusion.4
  345.9 0.3 fusion
  346.3 0.3 fusion.3
  346.6 0.3 convolution_convert_fusion.3
  346.9 1.1 pad_maximum_fusion.1
  348.0 6.6 %convolution_convert_fusion.2 = bf16[576,1536]{1,0:T(8,128)(2,1)} fusion(bf16[1536,576]{1,0:T(8,128)(2,1)S(1)} %copy-done.6, bf16[1536,1536]{1,0:T(8,128)(2,1)} %get-tuple-element.108), kind=kOutput, calls=%fused_computation.2 | convolution fusion | flops 2718793728 | bytes 8257536 | tf_op jit(solution)/shard_map/dot_general | solution.py:36
  354.9 0.6 copy-done.1
  355.7 0.9 fusion.2.refs_6_
  356.6 65.1 %shard_map.335 = (bf16[384,768]{1,0:T(8,128)(2,1)}, bf16[4,2,72,768]{3,2,1,0:T(8,128)(2,1)}, bf16[4,2,48,768]{3,2,1,0:T(8,128)(2,1)}, f32[8,768]{1,0:T(8,128)}, ...) custom-call(bf16[1536,576]{1,0:T(8,128)(2,1)} %get-tuple-element.99.refs_0_, ...), custom_call_target="tpu_custom_call" | custom-call | tf_op jit(solution)/shard_map/pallas_call | solution.py:286
  421.7 1.3 bitcast_convert_fusion.3
  423.0 1.2 slice_bitcast_fusion.1
  424.4 1.1 fusion.16
  425.5 1.1 convert_element_type.97
  426.6 0.8 bitcast_convert_fusion.4
  427.3 0.6 slice_reduce_fusion
  428.2 1.2 fusion.15
  429.5 0.8 copy.44
  (58 shorter events, 1.2 us)
Async XLA Ops:
  111.6 72.1 %slice-start = ((s8[4718592]{0:T(1024)(128)(4,1)}), s8[524288]{0:T(1024)(128)(4,1)S(1)}, s32[]{:S(2)}) async-start(s8[4718592]{0:T(1024)(128)(4,1)} %bitcast.96), calls=%async_computation | async-start | bytes 1048576
  175.1 8.6 %slice-start.1 = ((s8[4718592]{0:T(1024)(128)(4,1)}), s8[4194304]{0:T(1024)(128)(4,1)S(1)}, s32[]{:S(2)}) async-start(s8[4718592]{0:T(1024)(128)(4,1)} %bitcast.96), calls=%async_computation.1 | async-start | bytes 8388608
  175.1 8.6 %copy-start.5 = (bf16[1536,768]{1,0:T(8,128)(2,1)S(1)}, bf16[1536,768]{1,0:T(8,128)(2,1)}, u32[]{:S(2)}) copy-start(bf16[1536,768]{1,0:T(8,128)(2,1)} %get-tuple-element.88.refs_3_) | copy-start | bytes 7077892
  273.2 4.3 %copy-start.20 = (bf16[1536,1536]{1,0:T(8,128)(2,1)S(1)}, bf16[1536,1536]{1,0:T(8,128)(2,1)}, u32[]{:S(2)}) copy-start(bf16[1536,1536]{1,0:T(8,128)(2,1)} %get-tuple-element.95) | copy-start | bytes 14155780
  273.2 4.3 %copy-start.22 = (bf16[8,192,192]{2,1,0:T(8,128)(2,1)S(1)}, bf16[8,192,192]{2,1,0:T(8,128)(2,1)}, u32[]{:S(2)}) copy-start(bf16[8,192,192]{2,1,0:T(8,128)(2,1)} %get-tuple-element.94) | copy-start | bytes 1769476
  277.6 1.2 copy-start.16
  277.6 1.6 copy-start.2
  277.6 1.6 copy-start.3
  277.6 1.6 copy-start.12
  277.6 1.6 copy-start.13
  279.2 0.9 copy-start.7
  279.2 1.0 copy-start.18
  279.3 1.2 copy-start.9
  285.3 57.2 %copy-start.21 = (bf16[8,192,192]{2,1,0:T(8,128)(2,1)S(1)}, bf16[8,192,192]{2,1,0:T(8,128)(2,1)}, u32[]{:S(2)}) copy-start(bf16[8,192,192]{2,1,0:T(8,128)(2,1)} %get-tuple-element.104) | copy-start | bytes 1769476
  346.3 1.7 copy-start.6
  348.0 6.6 %copy-start = (bf16[768,192]{0,1:T(8,128)(2,1)S(1)}, bf16[768,192]{0,1:T(8,128)(2,1)}, u32[]{:S(2)}) copy-start(bf16[768,192]{0,1:T(8,128)(2,1)} %param.31) | copy-start | bytes 884740
  348.0 6.6 %copy-start.15 = (bf16[192,768]{1,0:T(8,128)(2,1)S(1)}, bf16[192,768]{1,0:T(8,128)(2,1)}, u32[]{:S(2)}) copy-start(bf16[192,768]{1,0:T(8,128)(2,1)} %get-tuple-element.106) | copy-start | bytes 884740
  354.6 1.0 copy-start.1
  354.6 1.0 copy-start.14
  423.0 1.3 copy-start.4
  423.0 2.4 copy-start.10
  424.3 2.3 copy-start.17
  424.3 3.0 copy-start.19
  424.3 3.6 copy-start.8
  428.2 1.3 copy-start.11
